TPU v7x, 32 devices: a whole 2x2x4 slice. The times are simulated.
32 devices in a mesh: rep: 8 (over y, x, core), shard: 4 (over z).
Axes of the slice: x: 2, y: 2, z: 4, core: 2. Of those that a mesh axis runs over, the one named last changes fastest.
Arguments:
- tokens: bfloat16 [8, 1024, 768], P('rep', 'shard'), may hold values from -6 to 6
- cotangent: bfloat16 [8, 1024, 768], P('rep', 'shard'), may hold values from -6 to 6
- lengths: int32 [8, 4], P('rep'), may hold values from 1 to 512, 1024 in all within a row
- deal: int32 [8, 1024], P('rep'), may hold values from 0 to 1023, each once within a row
- attn_master: float32 [4, 768, 768], P(None, 'shard'), may hold values from -3 to 3
- ffin_master: float32 [2, 768, 2048], P(None, 'shard'), may hold values from -0.21875 to 0.21875
- ffout_master: float32 [2048, 768], P('shard'), may hold values from -0.125 to 0.125
- gain_master: float32 [2, 768], P(None, 'shard'), may hold values from 0.5 to 1.5
- bias_master: float32 [32, 12], P('shard'), may hold values from -4 to 4
- attn_first: float32 [4, 768, 768], P(None, 'shard'), may hold values from -286.72 to 286.72
- ffin_first: float32 [2, 768, 2048], P(None, 'shard'), may hold values from -30.320738 to 30.320738
- ffout_first: float32 [2048, 768], P('shard'), may hold values from -32.58348 to 32.58348
- gain_first: float32 [2, 768], P(None, 'shard'), may hold values from -75.57557 to 75.57557
- bias_first: float32 [32, 12], P('shard'), may hold values from -284.16 to 284.16
- attn_second: float32 [4, 768, 768], P(None, 'shard'), may hold values from 32.768 to 112721.92
- ffin_second: float32 [2, 768, 2048], P(None, 'shard'), may hold values from 155.648 to 1245.184
- ffout_second: float32 [2048, 768], P('shard'), may hold values from 181.8624 to 1458.176
- gain_second: float32 [2, 768], P(None, 'shard'), may hold values from 966.656 to 7782.4
- bias_second: float32 [32, 12], P('shard'), may hold values from 2097.152 to 16777.217
Outputs:
- layer_out: bfloat16 [8, 1024, 768], P('rep', 'shard')
- input_grad: bfloat16 [8, 1024, 768], P('rep', 'shard')
- attn_new: float32 [4, 768, 768], P(None, 'shard')
- ffin_new: float32 [2, 768, 2048], P(None, 'shard')
- ffout_new: float32 [2048, 768], P('shard')
- gain_step: float32 [2, 768], P(None, 'shard')
- bias_step: float32 [32, 12], P('shard')
- attn_first_new: float32 [4, 768, 768], P(None, 'shard')
- ffin_first_new: float32 [2, 768, 2048], P(None, 'shard')
- ffout_first_new: float32 [2048, 768], P('shard')
- gain_first_new: float32 [2, 768], P(None, 'shard')
- bias_first_new: float32 [32, 12], P('shard')
- attn_second_new: float32 [3, 768, 768], P(None, 'shard')
- wo_second_new: float32 [768, 768], P('shard')
- ffin_second_new: float32 [2, 768, 2048], P(None, 'shard')
- ffout_second_new: float32 [2048, 768], P('shard')
- gain_second_new: float32 [2, 768], P(None, 'shard')
- bias_second_new: float32 [32, 12], P('shard')
- attn_copy: bfloat16 [4, 768, 768], P(None, 'shard')
- ffin_copy: bfloat16 [2, 768, 2048], P(None, 'shard')
- ffout_copy: bfloat16 [2048, 768], P('shard')
Inputs may be any that keep to these rules, and one draw needn't show every extreme that they name: Each row holds the 4 lengths of one group's packed sequences; they sum to 1024 and the longest is exactly 512. `deal`: each row is a permutation of 0 to 1023.
All inputs are finite; a program needn't handle non-finite values.
Results may differ from a plain program's by a relative error of at most 0.03.
Values may be sent and summed in bfloat16 or wider, within the bound.
No kernel may reach another device: no remote copies, remote signals or barrier semaphores. Data moves between devices by JAX's collectives and lax.ppermute only.
A program may use at most 192 MiB of HBM per device.

v0:
```python
import jax
import jax.numpy as jnp
from jax import lax
from jax.sharding import PartitionSpec as P

norm_eps = 1e-06
far_below = -1e30
steps_beyond = (12, 16, 23, 32, 46, 64, 91)
first_rate = 0.9
second_rate = 0.95
learning = 0.05
shrink = 0.1
adam_eps = 1e-08
first_fix = 1.0 - 0.9**8
second_fix = 1.0 - 0.95**8


def bucket_of(relative):
    distance = jnp.abs(relative)
    beyond = 8 + sum(((distance >= threshold).astype(jnp.int32) for threshold in steps_beyond))
    near_part = jnp.where(distance < 8, distance, beyond)
    return near_part + 16 * (relative > 0).astype(jnp.int32)


def places(lengths_row, whole_len):
    starts = jnp.cumsum(lengths_row) - lengths_row
    index_all = jnp.arange(whole_len, dtype=jnp.int32)
    passed = index_all[:, None] >= starts[None, :]
    seg_ids = jnp.sum(passed.astype(jnp.int32), axis=1) - 1
    begins = jnp.max(jnp.where(passed, starts[None, :], 0), axis=1)
    return (seg_ids, index_all - begins)


def rms_scale(values, gain):
    return values * lax.rsqrt(jnp.mean(values * values, axis=-1, keepdims=True) + norm_eps) * gain


def tdot(left, right):
    return lax.dot_general(
        left, right, (((0,), (0,)), ((), ())), preferred_element_type=jnp.float32
    )


def ndot(left, right):
    return lax.dot_general(
        left, right, (((1,), (1,)), ((), ())), preferred_element_type=jnp.float32
    )


def split_heads(matrix, num_heads):
    return matrix.reshape(matrix.shape[0], num_heads, matrix.shape[1] // num_heads)


def pick_from(wanted, picked, shard_rows):
    inside = (wanted >= 0) & (wanted < shard_rows.shape[0])
    taken_rows = jnp.take(shard_rows, jnp.clip(wanted, 0, shard_rows.shape[0] - 1), axis=0)
    return jnp.where(inside[:, None], taken_rows, picked)


def block_scores(query_heads, key_heads, query_seg, query_pos, key_seg, key_pos, bias_rows):
    scores = jnp.einsum("qhd,khd->hqk", query_heads, key_heads, preferred_element_type=jnp.float32)
    buckets = bucket_of(key_pos[None, :] - query_pos[:, None])
    bucket_ids = jnp.arange(bias_rows.shape[0], dtype=jnp.int32)
    one_hot = (buckets[:, :, None] == bucket_ids[None, None, :]).astype(jnp.bfloat16)
    scores = scores + jnp.einsum(
        "qkb,bh->hqk", one_hot, bias_rows, preferred_element_type=jnp.float32
    )
    same_seq = query_seg[:, None] == key_seg[None, :]
    return (scores, same_seq, one_hot)


def weights_of(scores, same_seq, log_total):
    return jnp.exp(jnp.where(same_seq[None], scores - log_total[:, :, None], far_below))


def slice_keys(arrays, key_start, block_len):
    return tuple(
        (lax.dynamic_slice_in_dim(array_in, key_start, block_len, 0) for array_in in arrays)
    )


def log_totals(
    query_heads, query_seg, query_pos, key_heads, key_seg, key_pos, bias_rows, block_len
):
    num_rows, num_heads = (query_heads.shape[0], query_heads.shape[1])

    def log_visit_block(carried, block_idx):
        highest, sum_exp = carried
        key_blk, seg_blk, pos_blk = slice_keys(
            (key_heads, key_seg, key_pos), block_idx * block_len, block_len
        )
        scores, same_seq, _ = block_scores(
            query_heads, key_blk, query_seg, query_pos, seg_blk, pos_blk, bias_rows
        )
        scores = jnp.where(same_seq[None], scores, far_below)
        new_high = jnp.maximum(highest, jnp.max(scores, axis=-1))
        kept_exp = jnp.where(same_seq[None], jnp.exp(scores - new_high[:, :, None]), 0.0)
        sum_exp = sum_exp * jnp.exp(highest - new_high) + jnp.sum(kept_exp, axis=-1)
        return ((new_high, sum_exp), None)

    start_state = (
        jnp.full((num_heads, num_rows), far_below, jnp.float32),
        jnp.zeros((num_heads, num_rows), jnp.float32),
    )
    (highest, sum_exp), _ = lax.scan(
        log_visit_block, start_state, jnp.arange(key_heads.shape[0] // block_len)
    )
    return highest + jnp.log(sum_exp)


def attend(
    query_heads,
    query_seg,
    query_pos,
    key_heads,
    value_heads,
    key_seg,
    key_pos,
    bias_rows,
    log_total,
    block_len,
):

    def attend_visit_block(acc_out, block_idx):
        key_blk, value_blk, seg_blk, pos_blk = slice_keys(
            (key_heads, value_heads, key_seg, key_pos), block_idx * block_len, block_len
        )
        scores, same_seq, _ = block_scores(
            query_heads, key_blk, query_seg, query_pos, seg_blk, pos_blk, bias_rows
        )
        prob_vals = weights_of(scores, same_seq, log_total).astype(jnp.bfloat16)
        return (
            acc_out
            + jnp.einsum("hqk,khd->qhd", prob_vals, value_blk, preferred_element_type=jnp.float32),
            None,
        )

    acc_out, _ = lax.scan(
        attend_visit_block,
        jnp.zeros(query_heads.shape, jnp.float32),
        jnp.arange(key_heads.shape[0] // block_len),
    )
    return acc_out


def prob_dot(
    query_heads,
    grad_heads,
    query_seg,
    query_pos,
    key_heads,
    value_heads,
    key_seg,
    key_pos,
    bias_rows,
    log_total,
    block_len,
):

    def prob_visit_block(acc_delta, block_idx):
        key_blk, value_blk, seg_blk, pos_blk = slice_keys(
            (key_heads, value_heads, key_seg, key_pos), block_idx * block_len, block_len
        )
        scores, same_seq, _ = block_scores(
            query_heads, key_blk, query_seg, query_pos, seg_blk, pos_blk, bias_rows
        )
        prob_vals = weights_of(scores, same_seq, log_total)
        grad_probs = jnp.einsum(
            "qhd,khd->hqk", grad_heads, value_blk, preferred_element_type=jnp.float32
        )
        return (acc_delta + jnp.sum(prob_vals * grad_probs, axis=-1), None)

    acc_delta, _ = lax.scan(
        prob_visit_block,
        jnp.zeros(log_total.shape, jnp.float32),
        jnp.arange(key_heads.shape[0] // block_len),
    )
    return acc_delta


def pair_grads(
    query_heads,
    grad_heads,
    log_total,
    delta,
    query_seg,
    query_pos,
    key_heads,
    value_heads,
    key_seg,
    key_pos,
    bias_rows,
):
    scores, same_seq, one_hot = block_scores(
        query_heads, key_heads, query_seg, query_pos, key_seg, key_pos, bias_rows
    )
    prob_vals = weights_of(scores, same_seq, log_total)
    grad_probs = jnp.einsum(
        "qhd,khd->hqk", grad_heads, value_heads, preferred_element_type=jnp.float32
    )
    grad_scores = (prob_vals * (grad_probs - delta[:, :, None])).astype(jnp.bfloat16)
    part_q = jnp.einsum("hqk,khd->qhd", grad_scores, key_heads, preferred_element_type=jnp.float32)
    part_k = jnp.einsum(
        "hqk,qhd->khd", grad_scores, query_heads, preferred_element_type=jnp.float32
    )
    part_v = jnp.einsum(
        "hqk,qhd->khd",
        prob_vals.astype(jnp.bfloat16),
        grad_heads,
        preferred_element_type=jnp.float32,
    )
    part_table = jnp.einsum("hqk,qkb->bh", grad_scores, one_hot, preferred_element_type=jnp.float32)
    return (part_q, part_k, part_v, part_table)


def adam_step(master, first, second, grad, decayed):
    new_first = first_rate * first + (1.0 - first_rate) * grad
    new_second = second_rate * second + (1.0 - second_rate) * grad * grad
    update = new_first / first_fix / (jnp.sqrt(new_second / second_fix) + adam_eps)
    if decayed:
        update = update + shrink * master
    new_master = master - learning * update
    return (new_master, new_first, new_second, new_master.astype(jnp.bfloat16))


def body(
    tokens,
    cotangent,
    lengths,
    deal,
    attn_master,
    ffin_master,
    ffout_master,
    gain_master,
    bias_master,
    attn_first,
    ffin_first,
    ffout_first,
    gain_first,
    bias_first,
    attn_second,
    ffin_second,
    ffout_second,
    gain_second,
    bias_second,
):
    tok_rows = tokens.shape[1]
    model_width = tokens.shape[2]
    num_heads = bias_master.shape[1]
    whole_len = tok_rows * lax.axis_size("shard")
    block_len = min(512, whole_len)
    my_start = lax.axis_index("shard") * tok_rows
    deal_order = deal[0]
    seg_input, pos_input = places(lengths[0], whole_len)
    seg_dealt = jnp.take(seg_input, deal_order)
    pos_dealt = jnp.take(pos_input, deal_order)
    my_sources = lax.dynamic_slice_in_dim(deal_order, my_start, tok_rows)
    my_seg = lax.dynamic_slice_in_dim(seg_dealt, my_start, tok_rows)
    my_pos = lax.dynamic_slice_in_dim(pos_dealt, my_start, tok_rows)
    inverse = (
        jnp.zeros((whole_len,), jnp.int32)
        .at[deal_order]
        .set(jnp.arange(whole_len, dtype=jnp.int32))
    )
    my_slots = lax.dynamic_slice_in_dim(inverse, my_start, tok_rows)
    own_copies = (
        attn_master.astype(jnp.bfloat16),
        ffin_master.astype(jnp.bfloat16),
        ffout_master.astype(jnp.bfloat16),
        gain_master.astype(jnp.bfloat16),
        bias_master.astype(jnp.bfloat16),
    )
    w_attn, w_in, w_out, w_gain, w_bias = (
        lax.all_gather(own_copies[0], "shard", axis=1, tiled=True),
        lax.all_gather(own_copies[1], "shard", axis=1, tiled=True),
        lax.all_gather(own_copies[2], "shard", axis=0, tiled=True),
        lax.all_gather(own_copies[3], "shard", axis=1, tiled=True),
        lax.all_gather(own_copies[4], "shard", axis=0, tiled=True),
    )
    start_rows = jnp.zeros((tok_rows, model_width), jnp.bfloat16)
    dealt_in = pick_from(
        my_sources, start_rows, lax.all_gather(tokens[0], "shard", axis=0, tiled=True)
    )
    x_in = dealt_in.astype(jnp.float32)
    gain_one = w_gain[0].astype(jnp.float32)
    gain_two = w_gain[1].astype(jnp.float32)
    act_one = rms_scale(x_in, gain_one).astype(jnp.bfloat16)
    query_own = jnp.dot(act_one, w_attn[0], preferred_element_type=jnp.float32).astype(jnp.bfloat16)
    key_own = jnp.dot(act_one, w_attn[1], preferred_element_type=jnp.float32).astype(jnp.bfloat16)
    value_own = jnp.dot(act_one, w_attn[2], preferred_element_type=jnp.float32).astype(jnp.bfloat16)
    key_all, value_all = (
        lax.all_gather(key_own, "shard", axis=0, tiled=True),
        lax.all_gather(value_own, "shard", axis=0, tiled=True),
    )
    bias_rows = w_bias
    query_heads = split_heads(query_own, num_heads)
    key_heads = split_heads(key_all, num_heads)
    value_heads = split_heads(value_all, num_heads)
    log_total = log_totals(
        query_heads, my_seg, my_pos, key_heads, seg_dealt, pos_dealt, bias_rows, block_len
    )
    attn_acc = attend(
        query_heads,
        my_seg,
        my_pos,
        key_heads,
        value_heads,
        seg_dealt,
        pos_dealt,
        bias_rows,
        log_total,
        block_len,
    )
    attn_mix = attn_acc.reshape(tok_rows, model_width).astype(jnp.bfloat16)
    x_mid = x_in + jnp.dot(attn_mix, w_attn[3], preferred_element_type=jnp.float32)
    act_two = rms_scale(x_mid, gain_two).astype(jnp.bfloat16)
    gate_pre = jnp.dot(act_two, w_in[0], preferred_element_type=jnp.float32)
    up_pre = jnp.dot(act_two, w_in[1], preferred_element_type=jnp.float32)
    hidden = (jax.nn.gelu(gate_pre, approximate=True) * up_pre).astype(jnp.bfloat16)
    layer_y = x_mid + jnp.dot(hidden, w_out, preferred_element_type=jnp.float32)
    layer_out = layer_y.astype(jnp.bfloat16)[None]
    w_attn, w_in, w_out, w_gain, w_bias = (
        lax.all_gather(own_copies[0], "shard", axis=1, tiled=True),
        lax.all_gather(own_copies[1], "shard", axis=1, tiled=True),
        lax.all_gather(own_copies[2], "shard", axis=0, tiled=True),
        lax.all_gather(own_copies[3], "shard", axis=1, tiled=True),
        lax.all_gather(own_copies[4], "shard", axis=0, tiled=True),
    )
    bias_rows = w_bias
    grad_y = cotangent[0]
    d_out = tdot(hidden, grad_y)
    grad_hidden = ndot(grad_y, w_out)
    _, gelu_pull = jax.vjp(
        lambda gate_val, up_val: jax.nn.gelu(gate_val, approximate=True) * up_val, gate_pre, up_pre
    )
    grad_gate, grad_up = gelu_pull(grad_hidden)
    grad_gate = grad_gate.astype(jnp.bfloat16)
    grad_up = grad_up.astype(jnp.bfloat16)
    d_in_gate = tdot(act_two, grad_gate)
    d_in_up = tdot(act_two, grad_up)
    grad_act_two = ndot(grad_gate, w_in[0]) + ndot(grad_up, w_in[1])
    _, second_pull = jax.vjp(rms_scale, x_mid, gain_two)
    grad_mid_norm, d_gain_two = second_pull(grad_act_two)
    grad_mid = grad_y.astype(jnp.float32) + grad_mid_norm
    grad_attn_out = grad_mid.astype(jnp.bfloat16)
    d_wo = tdot(attn_mix, grad_attn_out)
    grad_mix = ndot(grad_attn_out, w_attn[3]).astype(jnp.bfloat16)
    grad_heads = split_heads(grad_mix, num_heads)
    delta = prob_dot(
        query_heads,
        grad_heads,
        my_seg,
        my_pos,
        key_heads,
        value_heads,
        seg_dealt,
        pos_dealt,
        bias_rows,
        log_total,
        block_len,
    )
    table_zero = jnp.zeros((bias_rows.shape[0], num_heads), jnp.float32)

    def visit_keys(carried, block_idx):
        grad_q, grad_k_all, grad_v_all, grad_table = carried
        key_start = block_idx * block_len
        key_blk, value_blk, seg_blk, pos_blk = slice_keys(
            (key_heads, value_heads, seg_dealt, pos_dealt), key_start, block_len
        )
        part_q, part_k, part_v, part_table = pair_grads(
            query_heads,
            grad_heads,
            log_total,
            delta,
            my_seg,
            my_pos,
            key_blk,
            value_blk,
            seg_blk,
            pos_blk,
            bias_rows,
        )
        grad_k_all = lax.dynamic_update_slice_in_dim(
            grad_k_all, part_k.reshape(block_len, model_width), key_start, 0
        )
        grad_v_all = lax.dynamic_update_slice_in_dim(
            grad_v_all, part_v.reshape(block_len, model_width), key_start, 0
        )
        return ((grad_q + part_q, grad_k_all, grad_v_all, grad_table + part_table), None)

    start_state = (
        jnp.zeros(query_heads.shape, jnp.float32),
        jnp.zeros((whole_len, model_width), jnp.float32),
        jnp.zeros((whole_len, model_width), jnp.float32),
        table_zero,
    )
    (grad_q, grad_k_all, grad_v_all, grad_table), _ = lax.scan(
        visit_keys, start_state, jnp.arange(whole_len // block_len)
    )
    grad_k, grad_v = (
        lax.psum_scatter(
            grad_k_all.astype(jnp.bfloat16), "shard", scatter_dimension=0, tiled=True
        ).astype(jnp.float32),
        lax.psum_scatter(
            grad_v_all.astype(jnp.bfloat16), "shard", scatter_dimension=0, tiled=True
        ).astype(jnp.float32),
    )
    grad_q = grad_q.reshape(tok_rows, model_width)
    grad_q_low = grad_q.astype(jnp.bfloat16)
    grad_k_low = grad_k.astype(jnp.bfloat16)
    grad_v_low = grad_v.astype(jnp.bfloat16)
    d_wq = tdot(act_one, grad_q_low)
    d_wk = tdot(act_one, grad_k_low)
    d_wv = tdot(act_one, grad_v_low)
    grad_act_one = (
        ndot(grad_q_low, w_attn[0]) + ndot(grad_k_low, w_attn[1]) + ndot(grad_v_low, w_attn[2])
    )
    _, first_pull = jax.vjp(rms_scale, x_in, gain_one)
    grad_in_norm, d_gain_one = first_pull(grad_act_one)
    grad_x = (grad_mid + grad_in_norm).astype(jnp.bfloat16)
    back_rows = pick_from(my_slots, start_rows, lax.all_gather(grad_x, "shard", axis=0, tiled=True))
    grad_list = (
        jnp.stack([d_wq, d_wk, d_wv, d_wo]),
        jnp.stack([d_in_gate, d_in_up]),
        d_out,
        jnp.stack([d_gain_one, d_gain_two]),
        grad_table,
    )
    shares = (
        lax.psum_scatter(
            grad_list[0].astype(jnp.bfloat16), "shard", scatter_dimension=1, tiled=True
        ).astype(jnp.float32),
        lax.psum_scatter(
            grad_list[1].astype(jnp.bfloat16), "shard", scatter_dimension=1, tiled=True
        ).astype(jnp.float32),
        lax.psum_scatter(
            grad_list[2].astype(jnp.bfloat16), "shard", scatter_dimension=0, tiled=True
        ).astype(jnp.float32),
        lax.psum_scatter(
            grad_list[3].astype(jnp.bfloat16), "shard", scatter_dimension=1, tiled=True
        ).astype(jnp.float32),
        lax.psum_scatter(
            grad_list[4].astype(jnp.bfloat16), "shard", scatter_dimension=0, tiled=True
        ).astype(jnp.float32),
    )
    totals = (
        lax.psum(shares[0].astype(jnp.bfloat16), "rep").astype(jnp.float32),
        lax.psum(shares[1].astype(jnp.bfloat16), "rep").astype(jnp.float32),
        lax.psum(shares[2].astype(jnp.bfloat16), "rep").astype(jnp.float32),
        lax.psum(shares[3].astype(jnp.bfloat16), "rep").astype(jnp.float32),
        lax.psum(shares[4].astype(jnp.bfloat16), "rep").astype(jnp.float32),
    )
    attn_res = adam_step(attn_master, attn_first, attn_second, totals[0], True)
    ffin_res = adam_step(ffin_master, ffin_first, ffin_second, totals[1], True)
    ffout_res = adam_step(ffout_master, ffout_first, ffout_second, totals[2], True)
    gain_res = adam_step(gain_master, gain_first, gain_second, totals[3], False)
    bias_res = adam_step(bias_master, bias_first, bias_second, totals[4], False)
    return (
        layer_out,
        back_rows[None],
        attn_res[0],
        ffin_res[0],
        ffout_res[0],
        gain_res[0] - gain_master,
        bias_res[0] - bias_master,
        attn_res[1],
        ffin_res[1],
        ffout_res[1],
        gain_res[1],
        bias_res[1],
        attn_res[2][:3],
        attn_res[2][3],
        ffin_res[2],
        ffout_res[2],
        gain_res[2],
        bias_res[2],
        attn_res[3],
        ffin_res[3],
        ffout_res[3],
    )


def solution(mesh):
    in_specs = (
        P("rep", "shard", None),
        P("rep", "shard", None),
        P("rep", None),
        P("rep", None),
        P(None, "shard", None),
        P(None, "shard", None),
        P("shard", None),
        P(None, "shard"),
        P("shard", None),
        P(None, "shard", None),
        P(None, "shard", None),
        P("shard", None),
        P(None, "shard"),
        P("shard", None),
        P(None, "shard", None),
        P(None, "shard", None),
        P("shard", None),
        P(None, "shard"),
        P("shard", None),
    )
    out_specs = (
        P("rep", "shard", None),
        P("rep", "shard", None),
        P(None, "shard", None),
        P(None, "shard", None),
        P("shard", None),
        P(None, "shard"),
        P("shard", None),
        P(None, "shard", None),
        P(None, "shard", None),
        P("shard", None),
        P(None, "shard"),
        P("shard", None),
        P(None, "shard", None),
        P("shard", None),
        P(None, "shard", None),
        P("shard", None),
        P(None, "shard"),
        P("shard", None),
        P(None, "shard", None),
        P(None, "shard", None),
        P("shard", None),
    )
    return jax.shard_map(body, mesh=mesh, in_specs=in_specs, out_specs=out_specs, check_vma=False)
```

profile of v0, /device:TPU:0, one launch (start us, length us, event | category | flops | bytes accessed | tf_op | source)
XLA Modules:
  0.0 1032.7 jit_solution(16688668092655022099)
XLA Ops:
  10.9 12.6 %all-gather.1 = bf16[4,192,2]{1,2,0:T(2,128)(2,1)S(1)} all-gather(bf16[1,192,2]{1,2,0:T(2,128)(2,1)S(1)} %convert_bitcast_fusion), channel_id=1, replica_groups=mesh['rep'=8,'shard'=4] {'shard'}, dimensions={0}, use_global_device_ids=true | all-gather | bytes 3840 | tf_op jit(solution)/shard_map/all_gather | solution.py:277
  24.3 25.1 %all-gather.22.cloned.1.call-done = bf16[1,1024,768]{2,1,0:T(8,128)(2,1)} async-done(((bf16[1,256,768]{2,1,0:T(8,128)(2,1)}), bf16[1,1024,768]{2,1,0:T(8,128)(2,1)}) %all-gather.22.cloned.1.call-update) | async-done | bytes 1572880 | tf_op jit(solution)/shard_map/all_gather | solution.py:282
  53.3 86.6 %all-gather.10.cloned.1.call-done = bf16[4,768,768]{2,1,0:T(8,128)(2,1)} async-done(((bf16[4,192,768]{2,1,0:T(8,128)(2,1)}), bf16[4,768,768]{2,1,0:T(8,128)(2,1)}) %all-gather.10.cloned.1.call-update) | async-done | bytes 4718608 | tf_op jit(solution)/shard_map/all_gather | solution.py:274
  149.7 4.5 gather_fusion.2
  154.9 4.5 gather_fusion.1
  162.6 12.0 %all_gather.36 = bf16[32,12]{1,0:T(8,128)(2,1)S(1)} all-gather(bf16[8,12]{1,0:T(8,128)(2,1)S(1)} %convert_element_type.352), channel_id=1, replica_groups=mesh['rep'=8,'shard'=4] {'shard'}, dimensions={0}, use_global_device_ids=true | all-gather | bytes 960 | tf_op jit(solution)/shard_map/all_gather | solution.py:278
  181.1 63.1 %while.52 = (s32[]{:T(128)}, f32[12,256]{1,0:T(8,128)S(1)}, f32[12,256]{1,0:T(8,128)S(1)}, s32[256]{0:T(256)}, s32[2]{0:T(128)S(1)}, /*index=5*/s32[1024]{0:T(10...) while((s32[]{:T(128)}, f32[12,256]{1,0:T(8,128)S(1)}, ...), condition=%wide.region_7.10_spmd.clone, body=%wide.region_4.9_spmd.clone.sunk | while | flops 319437824 | bytes 40545248 | solution.py:105
  184.3 6.6 fusion.250
  190.9 9.2 copy.153
  201.7 6.9 fusion.251
  215.8 6.6 fusion.250
  222.3 9.4 copy.153
  233.3 6.9 fusion.251
  240.3 3.9 select_reduce_fusion.3
  246.9 52.7 %while.53 = (s32[]{:T(128)}, f32[256,12,64]{0,2,1:T(8,128)S(1)}, s32[2]{0:T(128)S(1)}, bf16[1024,12,64]{0,2,1:T(8,128)(2,1)}, s32[256]{0:T(256)}, /*index=5*/s32...) while((s32[]{:T(128)}, f32[256,12,64]{0,2,1:T(8,128)S(1)}, ...), condition=%wide.region_9.12_spmd.clone, body=%wide.region_8.11_spmd.clone.sunk | while | flops 517996544 | bytes 30044648 | solution.py:138
  250.4 6.6 fusion.259
  256.9 9.2 copy.154
  267.7 5.6 fusion.260
  276.6 6.6 fusion.259
  283.2 9.2 copy.154
  293.9 5.6 fusion.260
  301.8 30.9 %all-gather.16.cloned.1.call-done = bf16[2,768,2048]{2,1,0:T(8,128)(2,1)} async-done(((bf16[2,192,2048]{2,1,0:T(8,128)(2,1)}), bf16[2,768,2048]{2,1,0:T(8,128)(2,1)}) %all-gather.16.cloned.1.call-update) | async-done | bytes 6291472 | tf_op jit(solution)/shard_map/all_gather | solution.py:275
  332.7 4.2 fusion.105
  336.9 4.2 fusion.107
  341.2 55.3 %all-gather.18.cloned.1.call-done = bf16[2048,768]{1,0:T(8,128)(2,1)} async-done(((bf16[512,768]{1,0:T(8,128)(2,1)}), bf16[2048,768]{1,0:T(8,128)(2,1)}) %all-gather.18.cloned.1.call-update) | async-done | bytes 3145744 | tf_op jit(solution)/shard_map/all_gather | solution.py:276
  396.4 6.7 multiply_convert_fusion
  414.5 54.6 %while.54 = (s32[]{:T(128)}, f32[12,256]{1,0:T(8,128)}, s32[256]{0:T(256)}, s32[2]{0:T(128)S(1)}, s32[1024]{0:T(1024)}, /*index=5*/bf16[1024,12,64]{0,2,1:T(8,12...) while((s32[]{:T(128)}, f32[12,256]{1,0:T(8,128)}, ...), condition=%wide.region_15.18_spmd.clone, body=%wide.region_13.17_spmd.clone.sunk | while | flops 519179264 | bytes 66661396 | solution.py:173
  417.8 6.6 fusion.267
  424.3 9.2 copy.155
  444.7 6.6 fusion.267
  451.3 9.2 copy.155
  472.3 62.4 %while.55 = (s32[]{:T(128)}, f32[256,12,64]{0,2,1:T(8,128)}, bf16[1024,768]{0,1:T(8,128)(2,1)}, bf16[1024,768]{0,1:T(8,128)(2,1)}, f32[32,12]{0,1:T(8,128)}, /*i...) while((s32[]{:T(128)}, f32[256,12,64]{0,2,1:T(8,128)}, ...), condition=%wide.region_17.20_spmd.clone, body=%wide.region_16.19_spmd.clone.sunk | while | flops 1231553280 | bytes 110684456 | solution.py:397
  481.2 5.8 fusion.284
  492.9 3.9 fusion.287
  512.1 5.8 fusion.284
  524.0 3.9 fusion.287
  542.8 26.0 %reduce-scatter.11.cloned.1.call-done = bf16[256,768]{0,1:T(8,128)(2,1)} async-done(((bf16[1024,768]{0,1:T(8,128)(2,1)}), bf16[256,768]{0,1:T(8,128)(2,1)}) %reduce-scatter.11.cloned.1.call-update) | async-done | bytes 393232 | tf_op jit(solution)/shard_map/reduce_scatter | solution.py:404
  571.5 34.5 %reduce-scatter.9.cloned.1.call-done = bf16[256,768]{0,1:T(8,128)(2,1)} async-done(((bf16[1024,768]{0,1:T(8,128)(2,1)}), bf16[256,768]{0,1:T(8,128)(2,1)}) %reduce-scatter.9.cloned.1.call-update) | async-done | bytes 393232 | tf_op jit(solution)/shard_map/reduce_scatter | solution.py:401
  629.8 38.4 %reduce-scatter.17.cloned.1.call-done = bf16[512,768]{1,0:T(8,128)(2,1)} async-done(((bf16[2048,768]{1,0:T(8,128)(2,1)}), bf16[512,768]{1,0:T(8,128)(2,1)}) %reduce-scatter.17.cloned.1.call-update) | async-done | bytes 786448 | tf_op jit(solution)/shard_map/reduce_scatter | solution.py:436
  668.1 87.5 %reduce-scatter.13.cloned.1.call-done = bf16[4,192,768]{2,1,0:T(8,128)(2,1)} async-done(((bf16[4,768,768]{2,1,0:T(8,128)(2,1)}), bf16[4,192,768]{2,1,0:T(8,128)(2,1)}) %reduce-scatter.13.cloned.1.call-update) | async-done | bytes 1179664 | tf_op jit(solution)/shard_map/reduce_scatter | solution.py:430
  755.6 113.6 %reduce-scatter.15.cloned.1.call-done = bf16[2,192,2048]{2,1,0:T(8,128)(2,1)} async-done(((bf16[2,768,2048]{2,1,0:T(8,128)(2,1)}), bf16[2,192,2048]{2,1,0:T(8,128)(2,1)}) %reduce-scatter.15.cloned.1.call-update) | async-done | bytes 1572880 | tf_op jit(solution)/shard_map/reduce_scatter | solution.py:433
  869.3 4.3 scatter_custom_fusion
  875.1 11.1 %all-reduce = bf16[32,12]{1,0:T(8,128)(2,1)S(1)} all-reduce(bf16[32,12]{1,0:T(8,128)(2,1)S(1)} %copy.134), channel_id=9, replica_groups=mesh['rep'=8,'shard'=4] {'shard'}, use_global_device_ids=true, to_apply=%region_31.34.clone | all-reduce | flops 384 | bytes 1536
  892.7 12.4 %all-reduce.1 = (bf16[2,192]{1,0:T(2,128)(2,1)S(1)}, bf16[8,12]{1,0:T(8,128)(2,1)S(1)}) all-reduce(bf16[2,192]{1,0:T(2,128)(2,1)S(1)} %copy.140, bf16[8,12]{1,0:T(8,128)(2,1)S(1)} %constant_dynamic-slice_fusion), channel_id=1, replica_groups=mesh['rep'=8,'shard'=4] {'rep'}, use_global_device_ids=true, to_apply=%region_30.33 | all-reduce | flops 480 | bytes 1920 | tf_op jit(solution)/shard_map/psum | solution.py:450
  906.3 23.0 %all-gather.20.cloned.1.call-done = bf16[1024,768]{1,0:T(8,128)(2,1)} async-done(((bf16[256,768]{1,0:T(8,128)(2,1)}), bf16[1024,768]{1,0:T(8,128)(2,1)}) %all-gather.20.cloned.1.call-update) | async-done | bytes 1572880 | tf_op jit(solution)/shard_map/all_gather | solution.py:421
  933.2 73.2 %all-reduce.5.cloned.1.call-done = (bf16[4,192,768]{2,1,0:T(8,128)(2,1)}, bf16[2,192,2048]{2,1,0:T(8,128)(2,1)}, bf16[512,768]{1,0:T(8,128)(2,1)}) async-done(((bf16[4,192,768]{2,1,0:T(8,128)(2,1)}, bf16[2,192,2048]{2,1,0:T(8,128)(2,1)}, bf16[512,768]{1,0:T(8,128)(2,1)}), (bf16[4,192,768]{2,1,0:T(8,128)(2,1)}, bf16[2,192,2048]{2,1,0:T(8,128)(2,1)}, bf16[512,768]{1,0:T(8,128)(2,1)})) %all-reduce.5.cloned.1.call-update) | async-done | bytes 3538960 | tf_op jit(solution)/shard_map/psum | solution.py:447
  1006.4 7.5 fusion.165
  1017.1 5.3 fusion.162
  (347 shorter events, 184.1 us)
Async XLA Ops:
  7.2 16.4 %copy-start.37 = (s32[1,1024]{1,0:T(1,128)S(1)}, s32[1,1024]{1,0:T(1,128)}, u32[]{:S(2)}) copy-start(s32[1,1024]{1,0:T(1,128)} %param.34) | copy-start | bytes 12292
  7.2 42.2 %all-gather.22.cloned.1.call-start = ((), (), s32[]{:S(2)}) async-start(), calls=%async_computation.17 | async-start | bytes 1966080 | tf_op jit(solution)/shard_map/all_gather | solution.py:282
  7.9 131.9 %all-gather.10.cloned.1.call-start = ((), (), s32[]{:S(2)}) async-start(), calls=%async_computation.6 | async-start | bytes 5898240 | tf_op jit(solution)/shard_map/all_gather | solution.py:274
  10.8 167.7 %all-gather.14.cloned.1.call-start = ((), (), s32[]{:S(2)}) async-start(), calls=%async_computation.8 | async-start | bytes 1966080 | tf_op jit(solution)/shard_map/all_gather | solution.py:292
  23.6 151.7 %copy-start.51 = (pred[256]{0:T(512)(128)(4,1)}, pred[256]{0:T(512)(128)(4,1)S(1)}, u32[]{:S(2)}) copy-start(pred[256]{0:T(512)(128)(4,1)S(1)} %and_reduce_fusion) | copy-start | bytes 772
  24.3 151.1 %copy-start.40 = (f32[768]{0:T(1024)}, f32[768]{0:T(1024)S(1)}, u32[]{:S(2)}) copy-start(f32[768]{0:T(1024)S(1)} %get-tuple-element.708) | copy-start | bytes 9220
  24.3 115.6 %copy-start.58 = (pred[256]{0:T(512)(128)(4,1)}, pred[256]{0:T(512)(128)(4,1)S(1)}, u32[]{:S(2)}) copy-start(pred[256]{0:T(512)(128)(4,1)S(1)} %compare_and_fusion.2) | copy-start | bytes 772
  52.5 122.9 %copy-start.17 = (bf16[256,768]{1,0:T(8,128)(2,1)}, bf16[256,768]{1,0:T(8,128)(2,1)S(1)}, u32[]{:S(2)}) copy-start(bf16[256,768]{1,0:T(8,128)(2,1)S(1)} %gather_fusion) | copy-start | bytes 1179652
  53.3 122.0 %copy-start.54 = (f32[256]{0:T(256)}, f32[256]{0:T(256)S(1)}, u32[]{:S(2)}) copy-start(f32[256]{0:T(256)S(1)} %fusion.151) | copy-start | bytes 3076
  139.9 5.5 copy-start.7
  142.7 101.6 %all-gather.12.cloned.1.call-start = ((), (), s32[]{:S(2)}) async-start(), calls=%async_computation.7 | async-start | bytes 1966080 | tf_op jit(solution)/shard_map/all_gather | solution.py:293
  145.3 187.4 %all-gather.16.cloned.1.call-start = ((), (), s32[]{:S(2)}) async-start(), calls=%async_computation.9 | async-start | bytes 7864320 | tf_op jit(solution)/shard_map/all_gather | solution.py:275
  146.8 249.7 %all-gather.18.cloned.1.call-start = ((), (), s32[]{:S(2)}) async-start(), calls=%async_computation.10 | async-start | bytes 3932160 | tf_op jit(solution)/shard_map/all_gather | solution.py:276
  149.3 419.5 %reduce-scatter.11.cloned.1.call-start = ((), (), s32[]{:S(2)}) async-start(), calls=%async_computation.12 | async-start | bytes 1966080 | tf_op jit(solution)/shard_map/reduce_scatter | solution.py:404
  154.3 8.4 copy-start.42
  154.3 21.1 %copy-start.59 = (pred[256]{0:T(512)(128)(4,1)S(1)}, pred[256]{0:T(512)(128)(4,1)}, u32[]{:S(2)}) copy-start(pred[256]{0:T(512)(128)(4,1)} %copy-done.58) | copy-start | bytes 772
  246.8 52.8 %copy-start.18 = (bf16[256,768]{1,0:T(8,128)(2,1)S(1)}, bf16[256,768]{1,0:T(8,128)(2,1)}, u32[]{:S(2)}) copy-start(bf16[256,768]{1,0:T(8,128)(2,1)} %copy-done.17) | copy-start | bytes 1179652
  246.9 52.8 %copy-start.52 = (pred[256]{0:T(512)(128)(4,1)S(1)}, pred[256]{0:T(512)(128)(4,1)}, u32[]{:S(2)}) copy-start(pred[256]{0:T(512)(128)(4,1)} %copy-done.51) | copy-start | bytes 772
  299.6 37.3 %copy-start.26 = (bf16[256,12,64]{0,2,1:T(8,128)(2,1)}, bf16[256,12,64]{0,2,1:T(8,128)(2,1)S(1)}, u32[]{:S(2)}) copy-start(bf16[256,12,64]{0,2,1:T(8,128)(2,1)S(1)} %convert_element_type.353) | copy-start | bytes 1179652
  301.6 109.1 %copy-start.20 = (f32[256,768]{1,0:T(8,128)}, f32[256,768]{1,0:T(8,128)S(1)}, u32[]{:S(2)}) copy-start(f32[256,768]{1,0:T(8,128)S(1)} %get-tuple-element.853) | copy-start | bytes 2359300
  301.8 39.3 %copy-start.35 = (bf16[256,768]{1,0:T(8,128)(2,1)}, bf16[256,768]{1,0:T(8,128)(2,1)S(1)}, u32[]{:S(2)}) copy-start(bf16[256,768]{1,0:T(8,128)(2,1)S(1)} %multiply_convert_fusion.2) | copy-start | bytes 1179652
  336.9 59.5 %copy-start.24 = (bf16[1,256,768]{2,1,0:T(8,128)(2,1)S(1)}, bf16[1,256,768]{2,1,0:T(8,128)(2,1)}, u32[]{:S(2)}) copy-start(bf16[1,256,768]{2,1,0:T(8,128)(2,1)} %param.32) | copy-start | bytes 1179652
  534.7 71.3 %reduce-scatter.9.cloned.1.call-start = ((), (), s32[]{:S(2)}) async-start(), calls=%async_computation.11 | async-start | bytes 1966080 | tf_op jit(solution)/shard_map/reduce_scatter | solution.py:401
  535.5 132.7 %reduce-scatter.17.cloned.1.call-start = ((), (), s32[]{:S(2)}) async-start(), calls=%async_computation.16 | async-start | bytes 3932160 | tf_op jit(solution)/shard_map/reduce_scatter | solution.py:436
  538.7 216.8 %reduce-scatter.13.cloned.1.call-start = ((), (), s32[]{:S(2)}) async-start(), calls=%async_computation.14 | async-start | bytes 5898240 | tf_op jit(solution)/shard_map/reduce_scatter | solution.py:430
  611.4 257.8 %reduce-scatter.15.cloned.1.call-start = ((), (), s32[]{:S(2)}) async-start(), calls=%async_computation.15 | async-start | bytes 7864320 | tf_op jit(solution)/shard_map/reduce_scatter | solution.py:433
  618.9 4.6 copy-start.64
  618.9 272.9 %reduce-scatter.19.cloned.1.call-start = ((), (), s32[]{:S(2)}) async-start(), calls=%async_computation.18 | async-start | bytes 245760
  627.3 302.1 %all-gather.20.cloned.1.call-start = ((), (), s32[]{:S(2)}) async-start(), calls=%async_computation.13 | async-start | bytes 1966080 | tf_op jit(solution)/shard_map/all_gather | solution.py:421
  627.3 242.0 %copy-start.38 = (s32[1,1024]{1,0:T(1,128)S(1)}, s32[1,1024]{1,0:T(1,128)}, u32[]{:S(2)}) copy-start(s32[1,1024]{1,0:T(1,128)} %param.34) | copy-start | bytes 12292
  627.3 246.4 %copy-start.66 = (u32[32]{0:T(128)S(1)}, u32[32]{0:T(128)}, u32[]{:S(2)}) copy-start(u32[32]{0:T(128)} %constant.188) | copy-start | bytes 388
  627.3 247.7 %copy-start.48 = (f32[32,12]{0,1:T(8,128)S(1)}, f32[32,12]{0,1:T(8,128)}, u32[]{:S(2)}) copy-start(f32[32,12]{0,1:T(8,128)} %get-tuple-element.307) | copy-start | bytes 4612
  627.3 258.9 %copy-start.16 = (bf16[256,2048]{1,0:T(8,128)(2,1)S(1)}, bf16[256,2048]{1,0:T(8,128)(2,1)}, u32[]{:S(2)}) copy-start(bf16[256,2048]{1,0:T(8,128)(2,1)} %get-tuple-element.850) | copy-start | bytes 3145732
  627.3 258.9 %copy-start.21 = (f32[256,768]{1,0:T(8,128)S(1)}, f32[256,768]{1,0:T(8,128)}, u32[]{:S(2)}) copy-start(f32[256,768]{1,0:T(8,128)} %copy-done.20) | copy-start | bytes 2359300
  629.7 376.6 %all-reduce.5.cloned.1.call-start = ((), (), s32[]{:S(2)}) async-start(), calls=%async_computation.19 | async-start | bytes 7077888 | tf_op jit(solution)/shard_map/psum | solution.py:447
  869.2 35.8 %copy-start.50 = (f32[2,192]{1,0:T(2,128)S(1)}, f32[2,192]{1,0:T(2,128)}, u32[]{:S(2)}) copy-start(f32[2,192]{1,0:T(2,128)} %param.38) | copy-start | bytes 4612
  869.2 35.8 %copy-start.62 = (f32[2,192]{1,0:T(2,128)S(1)}, f32[2,192]{1,0:T(2,128)}, u32[]{:S(2)}) copy-start(f32[2,192]{1,0:T(2,128)} %param.43) | copy-start | bytes 4612
  869.2 35.8 %copy-start.63 = (f32[2,192]{1,0:T(2,128)S(1)}, f32[2,192]{1,0:T(2,128)}, u32[]{:S(2)}) copy-start(f32[2,192]{1,0:T(2,128)} %param.48) | copy-start | bytes 4612
  869.3 36.4 %copy-start.43 = (f32[8,12]{1,0:T(8,128)S(1)}, f32[8,12]{1,0:T(8,128)}, u32[]{:S(2)}) copy-start(f32[8,12]{1,0:T(8,128)} %param.39) | copy-start | bytes 1156
  869.3 36.4 %copy-start.56 = (f32[8,12]{1,0:T(8,128)S(1)}, f32[8,12]{1,0:T(8,128)}, u32[]{:S(2)}) copy-start(f32[8,12]{1,0:T(8,128)} %param.44) | copy-start | bytes 1156
  869.3 36.4 %copy-start.57 = (f32[8,12]{1,0:T(8,128)S(1)}, f32[8,12]{1,0:T(8,128)}, u32[]{:S(2)}) copy-start(f32[8,12]{1,0:T(8,128)} %param.49) | copy-start | bytes 1156
  889.9 116.5 %copy-start.9 = (f32[4,192,768]{2,1,0:T(8,128)S(1)}, f32[4,192,768]{2,1,0:T(8,128)}, u32[]{:S(2)}) copy-start(f32[4,192,768]{2,1,0:T(8,128)} %param.35) | copy-start | bytes 7077892
  1006.4 9.7 copy-start.22
  1006.4 9.7 copy-start.23
  1017.1 5.3 copy-start.14
  1017.1 5.3 copy-start.30
  1017.1 5.3 copy-start.31
  1017.1 5.3 copy-start.33
  (46 other events, 108.0 us)
Sparse Core Ops, SparseCore 0:
  9.6 39.7 all-gather.21
  51.6 88.2 all-gather.9
  142.8 35.6 all-gather.13
  180.5 35.9 all-gather.11
  218.5 114.1 all-gather.15
  334.7 61.6 all-gather.17
  534.8 33.9 reduce-scatter.10
  571.7 34.2 reduce-scatter.8
  608.9 59.2 reduce-scatter.16
  670.3 85.2 reduce-scatter.12
  757.9 111.2 reduce-scatter.14
  871.9 19.8 reduce-scatter.18
  894.0 35.2 all-gather.19
  933.2 73.0 all-reduce.4
where the time goes:
time: 1040 us; the launch traced here: 1030 us
  waiting for transfers between devices  599 us (58%)
  matrix products  179 us (17%)
  local copies, waits for them, and re-layouts  121 us (12%)
  other arithmetic  63.5 us (6%)
  blocking collectives  48.1 us (5%)
  between operations  15.9 us (2%)
    reduce_scatter x1, waiting for transfers between devices, body(): lax.psum_scatter(grad_list[1].astype(jnp.bfloat16), 'shard', scatter_dime...  114 us
    reduce_scatter x1, waiting for transfers between devices, body(): lax.psum_scatter(grad_list[0].astype(jnp.bfloat16), 'shard', scatter_dime...  87.5 us
    all_gather x1, waiting for transfers between devices, body(): lax.all_gather(own_copies[0], 'shard', axis=1, tiled=True)  86.6 us
    psum x1, waiting for transfers between devices, body(): lax.psum(shares[0].astype(jnp.bfloat16), 'rep').astype(jnp.float32)  73.2 us
    dot_general x6, local copies, waits for them, and re-layouts, block_scores(): jnp.einsum('qkb,bh->hqk', one_hot, bias_rows, preferred_element_type=jnp....  55.3 us
    all_gather x1, waiting for transfers between devices, body(): lax.all_gather(own_copies[2], 'shard', axis=0, tiled=True)  55.3 us
    dot_general x8, matrix products, block_scores(): jnp.einsum('qkb,bh->hqk', one_hot, bias_rows, preferred_element_type=jnp....  45.8 us
    reduce_scatter x1, waiting for transfers between devices, body(): lax.psum_scatter(grad_list[2].astype(jnp.bfloat16), 'shard', scatter_dime...  38.4 us
  transfers between devices with their start and end apart: 14, of which 13 were waited for; matrix products, arithmetic and copies ran while one was open for 20% of the time, Pallas kernels for 0%

commit v1 on v0

v1 whole, which is shorter than its diff:
```python
import functools

import jax
import jax.numpy as jnp
from jax import lax
from jax.experimental import pallas as pl
from jax.experimental.pallas import tpu as pltpu
from jax.sharding import Mesh
from jax.sharding import PartitionSpec as P

norm_eps = 1e-06
far_below = -1e30
steps_beyond = (12, 16, 23, 32, 46, 64, 91)
first_rate = 0.9
second_rate = 0.95
learning = 0.05
shrink = 0.1
adam_eps = 1e-08
first_fix = 1.0 - 0.9**8
second_fix = 1.0 - 0.95**8
chips = ("plane", "shard")
low = jnp.bfloat16
full = jnp.float32


def bucket_of(relative):
    distance = jnp.abs(relative)
    beyond = 8 + sum(((distance >= threshold).astype(jnp.int32) for threshold in steps_beyond))
    near_part = jnp.where(distance < 8, distance, beyond)
    return near_part + 16 * (relative > 0).astype(jnp.int32)


def ndot(left, right):
    return lax.dot_general(left, right, (((1,), (1,)), ((), ())), preferred_element_type=full)


def tdot(left, right):
    return lax.dot_general(left, right, (((0,), (0,)), ((), ())), preferred_element_type=full)


def mdot(left, right):
    return jnp.dot(left, right, preferred_element_type=full)


def swap(value):
    return lax.ppermute(value, "core", [(0, 1), (1, 0)])


def both_cores(mine, other, core, axis):
    first = jnp.where(core == 0, mine, other)
    second = jnp.where(core == 0, other, mine)
    return jnp.concatenate([first, second], axis)


def toeplitz_of(vector_row):
    wide = jnp.broadcast_to(vector_row, (128, vector_row.shape[1]))
    return pltpu.roll(wide, 0, 1, stride=1, stride_axis=0)


def attend_kernel(rows, q_ref, k_ref, v_ref, qseg_ref, kseg_ref, vec_ref, o_ref, p_ref, s_ref):
    keys = k_ref.shape[0]
    lane = lax.broadcasted_iota(jnp.int32, (rows, 128), 1)
    parts = []
    for head in range(2):
        mine = (lane < 64) if head == 0 else (lane >= 64)
        q_head = jnp.where(mine, q_ref[...], jnp.zeros((), low))
        s_ref[...] = ndot(q_head, k_ref[...])
        table = toeplitz_of(vec_ref[0, head : head + 1, :])
        for blk in range(rows // 128):
            here = slice(128 * blk, 128 * blk + 128)
            at = rows - 128 * blk
            scores = s_ref[here, :] + table[:, at : at + keys]
            scores = jnp.where(qseg_ref[here, :] == kseg_ref[...], scores, far_below)
            highest = jnp.max(scores, axis=1, keepdims=True)
            raised = jnp.exp(scores - highest)
            total = jnp.sum(raised, axis=1, keepdims=True)
            p_ref[head, here, :] = (raised * (1.0 / total)).astype(low)
        parts.append(mdot(p_ref[head], v_ref[...]))
    o_ref[...] = jnp.where(lane < 64, parts[0], parts[1]).astype(low)


def attend_back_kernel(
    rows, q_ref, k_ref, v_ref, do_ref, p_ref, dq_ref, dk_ref, dv_ref, diag_ref, s_ref, ds_ref, acc_ref
):
    keys = k_ref.shape[0]
    lane = lax.broadcasted_iota(jnp.int32, (rows, 128), 1)
    q_turned = q_ref[...].astype(full).T.astype(low)
    do_turned = do_ref[...].astype(full).T.astype(low)
    dq_parts, dk_parts, dv_parts = [], [], []
    for head in range(2):
        mine = (lane < 64) if head == 0 else (lane >= 64)
        do_head = jnp.where(mine, do_ref[...], jnp.zeros((), low))
        s_ref[...] = ndot(do_head, v_ref[...])
        acc_ref[...] = jnp.zeros_like(acc_ref)
        for blk in range(rows // 128):
            here = slice(128 * blk, 128 * blk + 128)
            at = rows - 128 * blk
            prob = p_ref[head, here, :].astype(full)
            grad = s_ref[here, :]
            delta = jnp.sum(prob * grad, axis=1, keepdims=True)
            dscore = (prob * (grad - delta)).astype(low)
            ds_ref[here, :] = dscore
            acc_ref[:, at : at + keys] += dscore.astype(full)
        dq_parts.append(mdot(ds_ref[...], k_ref[...]))
        own = slice(64 * head, 64 * head + 64)
        dk_parts.append(mdot(q_turned[own, :], ds_ref[...]))
        dv_parts.append(mdot(do_turned[own, :], p_ref[head]))
        summed = acc_ref[...]
        count = 128
        while count > 8:
            count //= 2
            width = summed.shape[1]
            summed = summed[:count] + pltpu.roll(summed[count:], width - count, 1)
        diag_ref[0, head] = summed
    dq_ref[...] = jnp.where(lane < 64, dq_parts[0], dq_parts[1]).astype(low)
    dk_ref[...] = jnp.concatenate(dk_parts, 0).T.astype(low)
    dv_ref[...] = jnp.concatenate(dv_parts, 0).T.astype(low)


def attend(query, key, value, query_seg, key_seg, vectors):
    rows, width = query.shape
    keys = key.shape[0]
    pairs = width // 128
    span = vectors.shape[-1]
    tall = pl.BlockSpec((rows, 128), lambda i: (0, i))
    wide = pl.BlockSpec((keys, 128), lambda i: (0, i))
    return pl.pallas_call(
        functools.partial(attend_kernel, rows),
        grid=(pairs,),
        in_specs=[
            tall,
            wide,
            wide,
            pl.BlockSpec((rows, 1), lambda i: (0, 0)),
            pl.BlockSpec((1, keys), lambda i: (0, 0)),
            pl.BlockSpec((1, 2, span), lambda i: (i, 0, 0)),
        ],
        out_specs=[tall, pl.BlockSpec((2, rows, keys), lambda i: (i, 0, 0))],
        out_shape=[
            jax.ShapeDtypeStruct((rows, width), low),
            jax.ShapeDtypeStruct((2 * pairs, rows, keys), low),
        ],
        scratch_shapes=[pltpu.VMEM((rows, keys), full)],
        name="attend",
        cost_estimate=pl.CostEstimate(
            flops=8 * pairs * rows * keys * 128,
            bytes_accessed=4 * pairs * rows * keys,
            transcendentals=2 * pairs * rows * keys,
        ),
    )(query, key, value, query_seg, key_seg, vectors.reshape(pairs, 2, span))


def attend_back(query, key, value, grad_out, probs, span):
    rows, width = query.shape
    keys = key.shape[0]
    pairs = width // 128
    tall = pl.BlockSpec((rows, 128), lambda i: (0, i))
    wide = pl.BlockSpec((keys, 128), lambda i: (0, i))
    return pl.pallas_call(
        functools.partial(attend_back_kernel, rows),
        grid=(pairs,),
        in_specs=[tall, wide, wide, tall, pl.BlockSpec((2, rows, keys), lambda i: (i, 0, 0))],
        out_specs=[tall, wide, wide, pl.BlockSpec((1, 2, 8, span), lambda i: (i, 0, 0, 0))],
        out_shape=[
            jax.ShapeDtypeStruct((rows, width), low),
            jax.ShapeDtypeStruct((keys, width), low),
            jax.ShapeDtypeStruct((keys, width), low),
            jax.ShapeDtypeStruct((pairs, 2, 8, span), full),
        ],
        scratch_shapes=[
            pltpu.VMEM((rows, keys), full),
            pltpu.VMEM((rows, keys), low),
            pltpu.VMEM((128, span), full),
        ],
        name="attend_back",
        cost_estimate=pl.CostEstimate(
            flops=20 * pairs * rows * keys * 128,
            bytes_accessed=4 * pairs * rows * keys,
            transcendentals=0,
        ),
    )(query, key, value, grad_out, probs)


def adam_step(master, first, second, grad, decayed):
    new_first = first_rate * first + (1.0 - first_rate) * grad
    new_second = second_rate * second + (1.0 - second_rate) * grad * grad
    update = new_first / first_fix / (jnp.sqrt(new_second / second_fix) + adam_eps)
    if decayed:
        update = update + shrink * master
    new_master = master - learning * update
    return (new_master, new_first, new_second, new_master.astype(low))


def body(
    tokens,
    cotangent,
    lengths,
    deal,
    attn_master,
    ffin_master,
    ffout_master,
    gain_master,
    bias_master,
    attn_first,
    ffin_first,
    ffout_first,
    gain_first,
    bias_first,
    attn_second,
    ffin_second,
    ffout_second,
    gain_second,
    bias_second,
):
    shards = lax.axis_size("shard")
    core = lax.axis_index("core")
    shard = lax.axis_index("shard")
    tok_rows, model = tokens.shape[1], tokens.shape[2]
    heads = bias_master.shape[1]
    own_heads = heads // 2
    part = model // 2
    whole_len = tok_rows * shards
    half_len = whole_len // 2
    per_half = shards // 4
    rows = half_len // per_half
    place, sub = shard // per_half, shard % per_half
    group, rest = place // 2, place % 2
    mine = group == core
    siblings = [[a * per_half + b for b in range(per_half)] for a in range(4)]

    def join_half(value):
        if per_half == 1:
            return value
        return lax.all_gather(value, "shard", axis=0, tiled=True, axis_index_groups=siblings)

    table_own = jnp.concatenate([lengths[0], deal[0]])
    table = jnp.where(mine, table_own, swap(table_own))
    count = lengths.shape[1]
    lens, order = table[:count], table[count:]
    starts = jnp.cumsum(lens) - lens
    long_start = jnp.sum(jnp.where(lens == half_len, starts, 0))
    at_half = jnp.arange(half_len, dtype=jnp.int32)
    token_half = jnp.where(
        rest == 0, long_start + at_half, at_half + half_len * (at_half >= long_start)
    )
    seg_half = jnp.sum((token_half[:, None] >= starts[None, :]).astype(jnp.int32), axis=1)
    first_row = sub * rows
    token_here = lax.dynamic_slice_in_dim(token_half, first_row, rows)
    seg_here = lax.dynamic_slice_in_dim(seg_half, first_row, rows)

    def rows_here(place_of, own):
        gathered = lax.all_gather(own, "shard", axis=0, tiled=True)
        gathered = jnp.where(mine, gathered, swap(gathered))
        picked = (place_of[None, :] == token_here[:, None]).astype(low)
        return mdot(picked, gathered).astype(low)

    def rows_back(place_of, here):
        picked = (place_of[:, None] == token_here[None, :]) & mine
        spread = mdot(picked.astype(low), here).astype(low)
        return lax.psum_scatter(spread, "shard", scatter_dimension=0, tiled=True)

    ff_rows = ffout_master.shape[0]
    ff_part = ff_rows // 2
    attn_low = attn_master.astype(low)
    cols = lax.dynamic_slice_in_dim(attn_low[:3], core * part, part, 2)
    ffin_low = ffin_master.astype(low).reshape(2, -1, shards, 2, ff_part)
    ffin_low = lax.dynamic_index_in_dim(ffin_low, core, 3, keepdims=False)
    ffin_low = ffin_low.reshape(2, -1, shards * ff_part)
    ffout_low = lax.dynamic_slice_in_dim(ffout_master.astype(low), core * ff_part, ff_part, 0)
    w_qkv = lax.all_gather(cols, "shard", axis=1, tiled=True)
    w_o = lax.all_gather(attn_low[3], "shard", axis=0, tiled=True)
    w_in = lax.all_gather(ffin_low, "shard", axis=1, tiled=True)
    w_out = lax.all_gather(ffout_low, "shard", axis=0, tiled=True)
    gains = lax.all_gather(gain_master.astype(low), "shard", axis=1, tiled=True).astype(full)
    bias = lax.all_gather(bias_master.astype(low), "shard", axis=0, tiled=True).astype(full)

    token_index = jnp.arange(whole_len, dtype=jnp.int32)
    x_low = rows_here(token_index, tokens[0])
    grad_y = rows_here(order, cotangent[0])

    x_in = x_low.astype(full)
    scale_one = lax.rsqrt(jnp.mean(x_in * x_in, axis=-1, keepdims=True) + norm_eps)
    act_one = (x_in * scale_one * gains[0]).astype(low)
    query = mdot(act_one, w_qkv[0]).astype(low)
    key_own = mdot(act_one, w_qkv[1]).astype(low)
    value_own = mdot(act_one, w_qkv[2]).astype(low)
    key, value = join_half(key_own), join_half(value_own)
    span = rows + half_len
    relative = jnp.arange(span, dtype=jnp.int32) - rows - first_row
    ids = jnp.arange(bias.shape[0], dtype=jnp.int32)
    one_hot = (bucket_of(relative)[None, :] == ids[:, None]).astype(full)
    bias_own = lax.dynamic_slice_in_dim(bias, core * own_heads, own_heads, 1)
    vectors = lax.dot_general(
        bias_own, one_hot, (((0,), (0,)), ((), ())), precision=lax.Precision.HIGHEST
    )
    mix_own, probs = attend(
        query, key, value, seg_here[:, None], seg_half[None, :], vectors
    )
    mix = both_cores(mix_own, swap(mix_own), core, 1)
    x_mid = x_in + mdot(mix, w_o)
    scale_two = lax.rsqrt(jnp.mean(x_mid * x_mid, axis=-1, keepdims=True) + norm_eps)
    act_two = (x_mid * scale_two * gains[1]).astype(low)
    gate_pre = mdot(act_two, w_in[0])
    up_pre = mdot(act_two, w_in[1])
    gated, gelu_pull = jax.vjp(
        lambda gate_val, up_val: jax.nn.gelu(gate_val, approximate=True) * up_val, gate_pre, up_pre
    )
    hidden = gated.astype(low)
    y_part = mdot(hidden, w_out)
    y_here = (x_mid + y_part + swap(y_part)).astype(low)
    layer_out = rows_back(order, y_here)

    grad_gate, grad_up = gelu_pull(ndot(grad_y, w_out))
    grad_gate, grad_up = grad_gate.astype(low), grad_up.astype(low)
    d_out = tdot(hidden, grad_y).astype(low)
    d_in = jnp.stack([tdot(act_two, grad_gate), tdot(act_two, grad_up)]).astype(low)
    part_two = ndot(grad_gate, w_in[0]) + ndot(grad_up, w_in[1])
    grad_act_two = part_two + swap(part_two)
    turned = grad_act_two * gains[1]
    grad_mid = (
        grad_y.astype(full)
        + scale_two * turned
        - x_mid * scale_two**3 * jnp.mean(turned * x_mid, axis=-1, keepdims=True)
    )
    d_gain_two = jnp.sum(grad_act_two * x_mid * scale_two, axis=0)
    grad_attn = grad_mid.astype(low)
    w_o_own = lax.dynamic_slice_in_dim(w_o, core * part, part, 0)
    grad_mix = ndot(grad_attn, w_o_own).astype(low)
    d_wo = tdot(mix, lax.dynamic_slice_in_dim(grad_attn, core * part, part, 1)).astype(low)
    grad_q, grad_k, grad_v, diagonals = attend_back(query, key, value, grad_mix, probs, span)
    if per_half > 1:
        grad_k = lax.psum_scatter(
            grad_k, "shard", scatter_dimension=0, tiled=True, axis_index_groups=siblings
        )
        grad_v = lax.psum_scatter(
            grad_v, "shard", scatter_dimension=0, tiled=True, axis_index_groups=siblings
        )
    d_wq = tdot(act_one, grad_q).astype(low)
    d_wk = tdot(act_one, grad_k).astype(low)
    d_wv = tdot(act_one, grad_v).astype(low)
    part_one = ndot(grad_q, w_qkv[0]) + ndot(grad_k, w_qkv[1]) + ndot(grad_v, w_qkv[2])
    grad_act_one = part_one + swap(part_one)
    turned = grad_act_one * gains[0]
    grad_x = (
        grad_mid
        + scale_one * turned
        - x_in * scale_one**3 * jnp.mean(turned * x_in, axis=-1, keepdims=True)
    ).astype(low)
    d_gain_one = jnp.sum(grad_act_one * x_in * scale_one, axis=0)
    input_grad = rows_back(token_index, grad_x)

    folded = diagonals.reshape(own_heads, 8, span)
    lined = sum((jnp.roll(folded[:, i], -i, axis=1) for i in range(8)))
    table_own = lax.dot_general(
        one_hot, lined, (((1,), (1,)), ((), ())), precision=lax.Precision.HIGHEST
    )
    empty = jnp.zeros_like(table_own)
    grad_table = jnp.where(
        core == 0,
        jnp.concatenate([table_own, empty], 1),
        jnp.concatenate([empty, table_own], 1),
    )
    grad_gain = jnp.where(core == 0, jnp.stack([d_gain_one, d_gain_two]), 0.0)

    d_attn = jnp.stack([d_wq, d_wk, d_wv, d_wo])

    def reduced(grad, axis):
        share = lax.psum_scatter(grad, "shard", scatter_dimension=axis, tiled=True)
        return lax.psum(share, "plane")

    g_attn = reduced(d_attn, 1)
    g_attn = both_cores(g_attn, swap(g_attn), core, 2).astype(full)
    g_in = reduced(d_in, 1)
    g_in = g_in.reshape(2, -1, shards, 1, ff_part)
    g_in = both_cores(g_in, swap(g_in), core, 3).reshape(ffin_master.shape).astype(full)
    g_out = reduced(d_out, 0)
    g_out = both_cores(g_out, swap(g_out), core, 0).astype(full)
    g_gain, g_bias = lax.psum((grad_gain, grad_table), ("plane", "core", "shard"))
    own_gain = gain_master.shape[1]
    g_gain = lax.dynamic_slice_in_dim(g_gain, shard * own_gain, own_gain, 1)
    own_bias = bias_master.shape[0]
    g_bias = lax.dynamic_slice_in_dim(g_bias, shard * own_bias, own_bias, 0)

    attn_res = adam_step(attn_master, attn_first, attn_second, g_attn, True)
    ffin_res = adam_step(ffin_master, ffin_first, ffin_second, g_in, True)
    ffout_res = adam_step(ffout_master, ffout_first, ffout_second, g_out, True)
    gain_res = adam_step(gain_master, gain_first, gain_second, g_gain, False)
    bias_res = adam_step(bias_master, bias_first, bias_second, g_bias, False)
    return (
        layer_out[None],
        input_grad[None],
        attn_res[0],
        ffin_res[0],
        ffout_res[0],
        gain_res[0] - gain_master,
        bias_res[0] - bias_master,
        attn_res[1],
        ffin_res[1],
        ffout_res[1],
        gain_res[1],
        bias_res[1],
        attn_res[2][:3],
        attn_res[2][3],
        ffin_res[2],
        ffout_res[2],
        gain_res[2],
        bias_res[2],
        attn_res[3],
        ffin_res[3],
        ffout_res[3],
    )


def solution(mesh):
    reps, shards = mesh.devices.shape
    cores = Mesh(mesh.devices.reshape(reps // 2, 2, shards), ("plane", "core", "shard"))
    rep = ("plane", "core")
    tok = P(rep, "shard", None)
    row = P(rep, None)
    second = P(None, "shard", None)
    first = P("shard", None)
    gain = P(None, "shard")
    states = (second, second, first, gain, first)
    in_specs = (tok, tok, row, row) + states * 3
    out_specs = (
        (tok, tok) + states + states + (second, first, second, first, gain, first) + states[:3]
    )
    return jax.shard_map(body, mesh=cores, in_specs=in_specs, out_specs=out_specs, check_vma=False)
```

time: 1040 us -> 577 us (0.55)
  waiting for transfers between devices: 599 us -> 338 us
  matrix products: 179 us -> 51.3 us
  local copies, waits for them, and re-layouts: 121 us -> 38.7 us
  other arithmetic: 63.5 us -> 39.8 us
  Pallas kernels: 0 us -> 20.3 us
  blocking collectives: 48.1 us -> 64.7 us
    reduce_scatter x5, waiting for transfers between devices: 300 us -> 153 us  [the longest x3 110 us: reduced(): share = lax.psum_scatter(grad, 'shard', scatter_dimension=axis, tiled=True)]
    dot_general x35 -> x13, matrix products: 144 us -> 31.4 us  [the longest x11 31 us: mdot(): return jnp.dot(left, right, preferred_element_type=full)]
    psum x1, waiting for transfers between devices: 73.2 us -> 10.1 us  [reduced(): return lax.psum(share, 'plane')]
    dot_general x6 -> x0, local copies, waits for them, and re-layouts: 55.3 us -> none  [block_scores(): jnp.einsum('qkb,bh->hqk', one_hot, bias_rows, preferred_element_type=jnp....]
    all_gather x7 -> x6, waiting for transfers between devices: 222 us -> 170 us  [the longest x1 61.5 us: body(): w_in = lax.all_gather(ffin_low, 'shard', axis=1, tiled=True)]
    psum x1, blocking collectives: 12.4 us -> 40.3 us  [body(): lax.psum((grad_gain, grad_table), ('plane', 'core', 'shard'))]
    pallas_call x0 -> x2, Pallas kernels: none -> 20.3 us  [the longest x1 12.5 us: attend(): pl.pallas_call(functools.partial(attend_kernel, rows), grid=(pairs,), in_...]
    gather x4 -> x0, local copies, waits for them, and re-layouts: 15.1 us -> none  [the longest x2 6.01 us: pick_from(): jnp.take(shard_rows, jnp.clip(wanted, 0, shard_rows.shape[0] - 1), axis=0)]
  transfers between devices with their start and end apart: 14 -> 22, of which waited for: 13 -> 15; matrix products, arithmetic and copies ran while one was open for 20% -> 20% of each run, Pallas kernels for 0% -> 4%
where the time goes in v1:
time: 577 us; the launch traced here: 570 us
  waiting for transfers between devices  338 us (59%)
  blocking collectives  64.7 us (11%)
  matrix products  51.3 us (9%)
  other arithmetic  39.8 us (7%)
  local copies, waits for them, and re-layouts  38.7 us (7%)
  Pallas kernels  20.3 us (4%)
  between operations  15.2 us (3%)
    reduce_scatter x3, waiting for transfers between devices, reduced(): share = lax.psum_scatter(grad, 'shard', scatter_dimension=axis, tiled=True)  110 us
    all_gather x1, waiting for transfers between devices, body(): w_in = lax.all_gather(ffin_low, 'shard', axis=1, tiled=True)  61.5 us
    reduce_scatter x2, waiting for transfers between devices, rows_back(): return lax.psum_scatter(spread, 'shard', scatter_dimension=0, tiled=True)  43.6 us
    psum x1, blocking collectives, body(): lax.psum((grad_gain, grad_table), ('plane', 'core', 'shard'))  40.3 us
    all_gather x1, waiting for transfers between devices, body(): w_qkv = lax.all_gather(cols, 'shard', axis=1, tiled=True)  37.2 us
    all_gather x1, waiting for transfers between devices, body(): w_out = lax.all_gather(ffout_low, 'shard', axis=0, tiled=True)  31.6 us
    dot_general x11, matrix products, mdot(): return jnp.dot(left, right, preferred_element_type=full)  31 us
    all_gather x2, waiting for transfers between devices, rows_here(): gathered = lax.all_gather(own, 'shard', axis=0, tiled=True)  30.1 us
  transfers between devices with their start and end apart: 22, of which 15 were waited for; matrix products, arithmetic and copies ran while one was open for 20% of the time, Pallas kernels for 4%

profile of v1, /device:TPU:0, one launch (start us, length us, event | category | flops | bytes accessed | tf_op | source)
XLA Modules:
  0.0 570.0 jit_solution(2798199434570554328)
XLA Ops:
  8.7 1.8 convert_element_type.188
  12.5 2.1 constant_dynamic-slice_fusion.1
  14.7 1.7 slice.168
  17.8 2.9 reshape.181
  20.8 5.0 dynamic-slice_reduce_fusion
  27.9 1.9 dynamic-slice_convert_fusion
  29.9 12.3 %all-gather.3 = bf16[4,192,2]{1,2,0:T(2,128)(2,1)S(1)} all-gather(bf16[1,192,2]{1,2,0:T(2,128)(2,1)S(1)} %convert_bitcast_fusion), channel_id=1, replica_groups=mesh['plane'=4,'core'=2,'shard'=4] {'shard'}, dimensions={0}, use_global_device_ids=true | all-gather | bytes 3840 | tf_op jit(solution)/shard_map/all_gather | solution.py:274
  42.2 7.3 %all-gather.17.cloned.1.call-done = bf16[1,1024,768]{2,1,0:T(8,128)(2,1)} async-done(((bf16[1,256,768]{2,1,0:T(8,128)(2,1)}), bf16[1,1024,768]{2,1,0:T(8,128)(2,1)}) %all-gather.17.cloned.1.call-update) | async-done | bytes 1572880 | tf_op jit(solution)/shard_map/all_gather | solution.py:252
  49.6 12.1 %all_gather.27 = bf16[32,12]{1,0:T(8,128)(2,1)S(1)} all-gather(bf16[8,12]{1,0:T(8,128)(2,1)S(1)} %convert_element_type.193), channel_id=1, replica_groups=mesh['plane'=4,'core'=2,'shard'=4] {'shard'}, dimensions={0}, use_global_device_ids=true | all-gather | bytes 960 | tf_op jit(solution)/shard_map/all_gather | solution.py:275
  64.2 22.8 %all-gather.21.cloned.1.call-done = bf16[1,1024,768]{2,1,0:T(8,128)(2,1)} async-done(((bf16[1,256,768]{2,1,0:T(8,128)(2,1)}), bf16[1,1024,768]{2,1,0:T(8,128)(2,1)}) %all-gather.21.cloned.1.call-update) | async-done | bytes 1572880 | tf_op jit(solution)/shard_map/all_gather | solution.py:252
  88.0 2.6 fusion.27
  91.3 37.2 %all-gather.11.cloned.1.call-done = bf16[3,768,384]{2,1,0:T(8,128)(2,1)} async-done(((bf16[3,192,384]{2,1,0:T(8,128)(2,1)}), bf16[3,768,384]{2,1,0:T(8,128)(2,1)}) %all-gather.11.cloned.1.call-update) | async-done | bytes 1769488 | tf_op jit(solution)/shard_map/all_gather | solution.py:270
  128.5 2.5 convolution_convert_fusion.9.k_ref
  133.8 12.5 %attend.1 = (bf16[512,384]{1,0:T(8,128)(2,1)}, bf16[6,512,512]{2,1,0:T(8,128)(2,1)}) custom-call(bf16[512,384]{1,0:T(8,128)(2,1)} %convolution_convert_fusion.10.q_ref, bf16[512,384]{1,0:T(8,128)(2,1)} %convolution_convert_fusion.9.k_ref, bf16[512,384]{1,0:T(8,128)(2,1)} %convolution_convert_fusion.8.v_ref, s32[512,1]{1,0:T(8,128)} %copy.122.qseg_ref, ...), custom_call_target="tpu_custom_call" | custom-call | flops 805306368 | bytes 3145728 | tf_op jit(solution)/shard_map/attend/pallas_call | solution.py:127
  146.4 2.5 fusion.42
  149.9 9.9 %all-gather.19.cloned.1.call-done = bf16[1,768,768]{2,1,0:T(8,128)(2,1)} async-done(((bf16[1,192,768]{2,1,0:T(8,128)(2,1)}), bf16[1,768,768]{2,1,0:T(8,128)(2,1)}) %all-gather.19.cloned.1.call-update) | async-done | bytes 1179664 | tf_op jit(solution)/shard_map/all_gather | solution.py:271
  159.8 2.3 multiply_reduce_fusion.2
  162.9 61.5 %all-gather.13.cloned.1.call-done = bf16[2,768,1024]{2,1,0:T(8,128)(2,1)} async-done(((bf16[2,192,1024]{2,1,0:T(8,128)(2,1)}), bf16[2,768,1024]{2,1,0:T(8,128)(2,1)}) %all-gather.13.cloned.1.call-update) | async-done | bytes 3145744 | tf_op jit(solution)/shard_map/all_gather | solution.py:272
  224.5 3.9 fusion.52
  228.3 2.3 fusion.51
  230.6 31.6 %all-gather.15.cloned.1.call-done = bf16[1024,768]{1,0:T(8,128)(2,1)} async-done(((bf16[256,768]{1,0:T(8,128)(2,1)}), bf16[1024,768]{1,0:T(8,128)(2,1)}) %all-gather.15.cloned.1.call-update) | async-done | bytes 1572880 | tf_op jit(solution)/shard_map/all_gather | solution.py:273
  262.3 5.2 multiply_convert_fusion
  269.8 1.9 pad_maximum_fusion
  273.0 2.6 fusion.50
  277.5 2.2 convolution_convert_fusion
  280.3 2.5 multiply_reduce_fusion
  282.8 3.1 fusion.146
  288.5 7.8 %attend_back.1 = (bf16[512,384]{1,0:T(8,128)(2,1)}, bf16[512,384]{1,0:T(8,128)(2,1)}, bf16[512,384]{1,0:T(8,128)(2,1)}, f32[3,2,8,1024]{3,2,1,0:T(8,128)}) custom-call(bf16[512,384]{1,0:T(8,128)(2,1)} %convolution_convert_fusion.10.q_ref, bf16[512,384]{1,0:T(8,128)(2,1)} %convolution_convert_fusion.9.k_ref, ...), custom_call_target="tpu_custom_call" | custom-call | flops 2013265920 | bytes 3145728 | tf_op jit(solution)/shard_map/attend_back/pallas_call | solution.py:159
  296.4 1.7 fusion.53
  299.8 1.8 pad_maximum_fusion.1
  303.0 3.4 fusion.148
  306.5 24.6 %reduce-scatter.12.cloned.1.call-done = bf16[2,192,1024]{2,1,0:T(8,128)(2,1)} async-done(((bf16[2,768,1024]{2,1,0:T(8,128)(2,1)}), bf16[2,192,1024]{2,1,0:T(8,128)(2,1)}) %reduce-scatter.12.cloned.1.call-update) | async-done | bytes 786448 | tf_op jit(solution)/shard_map/reduce_scatter | solution.py:368
  331.1 1.9 reshape.183
  334.1 35.2 %reduce-scatter.14.cloned.1.call-done = bf16[256,768]{1,0:T(8,128)(2,1)} async-done(((bf16[1024,768]{1,0:T(8,128)(2,1)}), bf16[256,768]{1,0:T(8,128)(2,1)}) %reduce-scatter.14.cloned.1.call-update) | async-done | bytes 393232 | tf_op jit(solution)/shard_map/reduce_scatter | solution.py:368
  369.3 49.9 %reduce-scatter.10.cloned.1.call-done = bf16[4,192,384]{2,1,0:T(8,128)(2,1)} async-done(((bf16[4,768,384]{2,1,0:T(8,128)(2,1)}), bf16[4,192,384]{2,1,0:T(8,128)(2,1)}) %reduce-scatter.10.cloned.1.call-update) | async-done | bytes 589840 | tf_op jit(solution)/shard_map/reduce_scatter | solution.py:368
  419.3 4.4 fusion.22
  430.5 2.3 fusion.35
  432.8 40.3 %all-reduce.2 = (f32[2,768]{1,0:T(2,128)S(1)}, f32[32,12]{1,0:T(8,128)S(1)}) all-reduce(f32[2,768]{1,0:T(2,128)S(1)} %maximum_select_fusion, f32[32,12]{1,0:T(8,128)S(1)} %pad_select_fusion), channel_id=1, replica_groups=mesh['plane'=4,'core'=2,'shard'=4] {'plane','core','shard'}, use_global_device_ids=true, to_apply=%region_17.18 | all-reduce | flops 1920 | bytes 15360 | tf_op jit(solution)/shard_map/psum | solution.py:378
  473.2 4.4 fusion.19
  477.6 10.1 %all-reduce.6.cloned.1.call-done = (bf16[4,192,384]{2,1,0:T(8,128)(2,1)}, bf16[2,192,4,1,256]{4,1,3,2,0:T(8,128)(2,1)}, bf16[256,768]{1,0:T(8,128)(2,1)}) async-done(((bf16[4,192,384]{2,1,0:T(8,128)(2,1)}, bf16[2,192,4,1,256]{4,1,3,2,0:T(8,128)(2,1)}, bf16[256,768]{1,0:T(8,128)(2,1)}), (bf16[4,192,384]{2,1,0:T(8,128)(2,1)}, bf16[2,192,4,1,256]{4,1,3,2,0:T(8,128)(2,1)}, ...) | async-done | bytes 1769488 | tf_op jit(solution)/shard_map/psum | solution.py:369
  490.8 4.8 fusion.136
  495.7 1.8 copy-done.1
  497.5 4.7 fusion.141
  504.7 2.4 copy.125
  507.1 3.6 reshape.185
  510.8 8.6 %fusion.139 = (bf16[2,192,2048]{2,1,0:T(8,128)(2,1)}, f32[2,192,2048]{2,1,0:T(8,128)}, f32[2,192,2048]{2,1,0:T(8,128)}, f32[2,192,2048]{2,1,0:T(8,128)}) fusion(f32[2,192,2048]{2,1,0:T(8,128)} %param.24, f32[2,192,2048]{2,1,0:T(8,128)} %reshape.185, f32[2,192,2048]{2,1,0:T(8,128)} %param.29, f32[2,192,2048]{2,1,0:T(8,128)} %param.34), kind=kLoop, calls=%fused_computation.222 | loop fusion | flops 12582912 | bytes 23592960 | tf_op jit(solution)/shard_map/convert_element_type | solution.py:191
  519.4 6.6 %reduce-scatter.6.cloned.1.call-done = bf16[256,768]{1,0:T(8,128)(2,1)} async-done(((bf16[1024,768]{1,0:T(8,128)(2,1)}), bf16[256,768]{1,0:T(8,128)(2,1)}) %reduce-scatter.6.cloned.1.call-update) | async-done | bytes 393232 | tf_op jit(solution)/shard_map/reduce_scatter | solution.py:260
  526.0 37.0 %reduce-scatter.8.cloned.1.call-done = bf16[256,768]{1,0:T(8,128)(2,1)} async-done(((bf16[1024,768]{1,0:T(8,128)(2,1)}), bf16[256,768]{1,0:T(8,128)(2,1)}) %reduce-scatter.8.cloned.1.call-update) | async-done | bytes 393232 | tf_op jit(solution)/shard_map/reduce_scatter | solution.py:260
  (220 shorter events, 41.1 us)
Async XLA Ops:
  7.2 42.3 %all-gather.17.cloned.1.call-start = ((), (), s32[]{:S(2)}) async-start(), calls=%async_computation.13 | async-start | bytes 1966080 | tf_op jit(solution)/shard_map/all_gather | solution.py:252
  7.9 79.1 %all-gather.21.cloned.1.call-start = ((), (), s32[]{:S(2)}) async-start(), calls=%async_computation.15 | async-start | bytes 1966080 | tf_op jit(solution)/shard_map/all_gather | solution.py:252
  8.7 119.8 %all-gather.11.cloned.1.call-start = ((), (), s32[]{:S(2)}) async-start(), calls=%async_computation.5 | async-start | bytes 2211840 | tf_op jit(solution)/shard_map/all_gather | solution.py:270
  11.5 4.9 copy-start
  14.6 145.2 %all-gather.19.cloned.1.call-start = ((), (), s32[]{:S(2)}) async-start(), calls=%async_computation.14 | async-start | bytes 1474560 | tf_op jit(solution)/shard_map/all_gather | solution.py:271
  16.4 208.0 %all-gather.13.cloned.1.call-start = ((), (), s32[]{:S(2)}) async-start(), calls=%async_computation.6 | async-start | bytes 3932160 | tf_op jit(solution)/shard_map/all_gather | solution.py:272
  25.8 4.1 copy-start.36
  25.8 4.1 copy-start.29
  27.3 235.0 %all-gather.15.cloned.1.call-start = ((), (), s32[]{:S(2)}) async-start(), calls=%async_computation.7 | async-start | bytes 1966080 | tf_op jit(solution)/shard_map/all_gather | solution.py:273
  27.4 35.3 %collective-permute-start = (s32[1028]{0:T(1024)S(1)}, s32[1028]{0:T(1024)S(1)}, u32[]{:S(2)}, u32[]{:S(2)}) collective-permute-start(s32[1028]{0:T(1024)S(1)} %pad_add_fusion), channel_id=1, source_target_pairs={{0,4},{4,0},{1,5},{5,1},{2,6},{6,2},{3,7},{7,3},{8,12},{12,8},{9,1... | collective-permute-start | bytes 12344 | tf_op jit(solution)/shard_map/ppermute | solution.py:46
  29.8 301.3 %reduce-scatter.12.cloned.1.call-start = ((), (), s32[]{:S(2)}) async-start(), calls=%async_computation.11 | async-start | bytes 3932160 | tf_op jit(solution)/shard_map/reduce_scatter | solution.py:368
  49.5 38.5 %collective-permute-start.1 = (bf16[1024,768]{1,0:T(8,128)(2,1)}, bf16[1024,768]{1,0:T(8,128)(2,1)}, u32[]{:S(2)}, u32[]{:S(2)}) collective-permute-start(bf16[1024,768]{1,0:T(8,128)(2,1)} %bitcast.125), channel_id=1, source_target_pairs={{0,4},{4,0},{1,5},{5,1},{2,6},{6,2},{3,7},{7,3},{8,12},{12,8},{9,1... | collective-permute-start | bytes 4718600 | tf_op jit(solution)/shard_map/ppermute | solution.py:46
  64.2 82.1 %copy-start.25 = (s32[512]{0:T(512)}, s32[512]{0:T(512)S(1)}, u32[]{:S(2)}) copy-start(s32[512]{0:T(512)S(1)} %add_select_fusion) | copy-start | bytes 6148
  87.1 59.3 %collective-permute-start.4 = (bf16[1024,768]{1,0:T(8,128)(2,1)}, bf16[1024,768]{1,0:T(8,128)(2,1)}, u32[]{:S(2)}, u32[]{:S(2)}) collective-permute-start(bf16[1024,768]{1,0:T(8,128)(2,1)} %bitcast.124), channel_id=1, source_target_pairs={{0,4},{4,0},{1,5},{5,1},{2,6},{6,2},{3,7},{7,3},{8,12},{12,8},{9,1... | collective-permute-start | bytes 4718600 | tf_op jit(solution)/shard_map/ppermute | solution.py:46
  90.6 69.2 %copy-start.4 = (bf16[512,768]{1,0:T(8,128)(2,1)}, bf16[512,768]{1,0:T(8,128)(2,1)S(1)}, u32[]{:S(2)}) copy-start(bf16[512,768]{1,0:T(8,128)(2,1)S(1)} %get-tuple-element.174) | copy-start | bytes 2359300
  91.3 41.1 %copy-start.27 = (f32[512]{0:T(512)}, f32[512]{0:T(512)S(1)}, u32[]{:S(2)}) copy-start(f32[512]{0:T(512)S(1)} %get-tuple-element.170) | copy-start | bytes 6148
  146.3 2.7 collective-permute-start.2
  148.9 113.3 %copy-start.12 = (bf16[512,768]{1,0:T(8,128)(2,1)}, bf16[512,768]{1,0:T(8,128)(2,1)S(1)}, u32[]{:S(2)}) copy-start(bf16[512,768]{1,0:T(8,128)(2,1)S(1)} %fusion.42) | copy-start | bytes 2359300
  224.5 3.9 copy-start.44
  271.8 97.5 %reduce-scatter.14.cloned.1.call-start = ((), (), s32[]{:S(2)}) async-start(), calls=%async_computation.12 | async-start | bytes 1966080 | tf_op jit(solution)/shard_map/reduce_scatter | solution.py:368
  276.7 3.6 collective-permute-start.5
  279.7 139.6 %reduce-scatter.10.cloned.1.call-start = ((), (), s32[]{:S(2)}) async-start(), calls=%async_computation.10 | async-start | bytes 2949120 | tf_op jit(solution)/shard_map/reduce_scatter | solution.py:368
  288.5 7.8 %copy-start.5 = (bf16[512,768]{1,0:T(8,128)(2,1)S(1)}, bf16[512,768]{1,0:T(8,128)(2,1)}, u32[]{:S(2)}) copy-start(bf16[512,768]{1,0:T(8,128)(2,1)} %copy-done.4) | copy-start | bytes 2359300
  288.5 7.9 %copy-start.28 = (f32[512]{0:T(512)S(1)}, f32[512]{0:T(512)}, u32[]{:S(2)}) copy-start(f32[512]{0:T(512)} %copy-done.27) | copy-start | bytes 6148
  301.6 186.1 %all-reduce.6.cloned.1.call-start = ((), (), s32[]{:S(2)}) async-start(), calls=%async_computation.16 | async-start | bytes 3538944 | tf_op jit(solution)/shard_map/psum | solution.py:369
  306.4 112.9 %collective-permute-start.3 = (f32[512,768]{1,0:T(8,128)}, f32[512,768]{1,0:T(8,128)}, u32[]{:S(2)}, u32[]{:S(2)}) collective-permute-start(f32[512,768]{1,0:T(8,128)} %fusion.148), channel_id=1, source_target_pairs={{0,4},{4,0},{1,5},{5,1},{2,6},{6,2},{3,7},{7,3},{8,12},{12,8},{9,1... | collective-permute-start | bytes 4718600 | tf_op jit(solution)/shard_map/ppermute | solution.py:46
  333.0 86.2 %copy-start.26 = (s32[512]{0:T(512)S(1)}, s32[512]{0:T(512)}, u32[]{:S(2)}) copy-start(s32[512]{0:T(512)} %copy-done.25) | copy-start | bytes 6148
  333.1 86.2 %copy-start.33 = (s32[1024]{0:T(1024)S(1)}, s32[1024]{0:T(1024)}, u32[]{:S(2)}) copy-start(s32[1024]{0:T(1024)} %copy-done.32) | copy-start | bytes 12292
  419.2 106.7 %reduce-scatter.6.cloned.1.call-start = ((), (), s32[]{:S(2)}) async-start(), calls=%async_computation.8 | async-start | bytes 1966080 | tf_op jit(solution)/shard_map/reduce_scatter | solution.py:260
  419.3 4.7 copy-start.10
  423.7 139.2 %reduce-scatter.8.cloned.1.call-start = ((), (), s32[]{:S(2)}) async-start(), calls=%async_computation.9 | async-start | bytes 1966080 | tf_op jit(solution)/shard_map/reduce_scatter | solution.py:260
  426.9 3.6 collective-permute-start.6
  429.0 44.1 %copy-start.2 = (f32[512,768]{1,0:T(8,128)S(1)}, f32[512,768]{1,0:T(8,128)}, u32[]{:S(2)}) copy-start(f32[512,768]{1,0:T(8,128)} %get-tuple-element.147) | copy-start | bytes 4718596
  429.0 44.1 %copy-start.38 = (f32[512]{0:T(512)S(1)}, f32[512]{0:T(512)}, u32[]{:S(2)}) copy-start(f32[512]{0:T(512)} %get-tuple-element.169) | copy-start | bytes 6148
  477.6 10.2 %copy-start.37 = (f32[2,192]{1,0:T(2,128)S(1)}, f32[2,192]{1,0:T(2,128)}, u32[]{:S(2)}) copy-start(f32[2,192]{1,0:T(2,128)} %param.26) | copy-start | bytes 4612
  477.6 10.2 %copy-start.42 = (f32[2,192]{1,0:T(2,128)S(1)}, f32[2,192]{1,0:T(2,128)}, u32[]{:S(2)}) copy-start(f32[2,192]{1,0:T(2,128)} %param.31) | copy-start | bytes 4612
  477.6 10.2 %copy-start.43 = (f32[2,192]{1,0:T(2,128)S(1)}, f32[2,192]{1,0:T(2,128)}, u32[]{:S(2)}) copy-start(f32[2,192]{1,0:T(2,128)} %param.36) | copy-start | bytes 4612
  477.6 10.9 %copy-start.30 = (f32[8,12]{1,0:T(8,128)S(1)}, f32[8,12]{1,0:T(8,128)}, u32[]{:S(2)}) copy-start(f32[8,12]{1,0:T(8,128)} %param.27) | copy-start | bytes 1156
  477.6 10.9 %copy-start.39 = (f32[8,12]{1,0:T(8,128)S(1)}, f32[8,12]{1,0:T(8,128)}, u32[]{:S(2)}) copy-start(f32[8,12]{1,0:T(8,128)} %param.32) | copy-start | bytes 1156
  477.6 10.9 %copy-start.40 = (f32[8,12]{1,0:T(8,128)S(1)}, f32[8,12]{1,0:T(8,128)}, u32[]{:S(2)}) copy-start(f32[8,12]{1,0:T(8,128)} %param.37) | copy-start | bytes 1156
  477.6 13.2 %copy-start.6 = (f32[512,768]{1,0:T(8,128)S(1)}, f32[512,768]{1,0:T(8,128)}, u32[]{:S(2)}) copy-start(f32[512,768]{1,0:T(8,128)} %param.25) | copy-start | bytes 4718596
  477.6 13.1 %copy-start.11 = (f32[512,768]{1,0:T(8,128)S(1)}, f32[512,768]{1,0:T(8,128)}, u32[]{:S(2)}) copy-start(f32[512,768]{1,0:T(8,128)} %param.30) | copy-start | bytes 4718596
  487.8 1.9 collective-permute-start.9
  489.1 6.5 %collective-permute-start.7 = (bf16[4,192,384]{2,1,0:T(8,128)(2,1)}, bf16[4,192,384]{2,1,0:T(8,128)(2,1)S(1)}, u32[]{:S(2)}, u32[]{:S(2)}) collective-permute-start(bf16[4,192,384]{2,1,0:T(8,128)(2,1)} %get-tuple-element.125), channel_id=1, source_target_pairs={{0,4},{4,0},{1,5},{5,1},{2,6},{6,2},{3,7},{7,3},{8,12},{12,8},{9,1... | collective-permute-start | bytes 1769480 | tf_op jit(solution)/shard_map/ppermute | solution.py:46
  489.6 14.8 %collective-permute-start.8 = (bf16[2,192,4,1,256]{4,1,3,2,0:T(8,128)(2,1)}, bf16[2,192,4,1,256]{4,1,3,2,0:T(8,128)(2,1)S(1)}, u32[]{:S(2)}, u32[]{:S(2)}) collective-permute-start(bf16[2,192,4,1,256]{4,1,3,2,0:T(8,128)(2,1)} %get-tuple-element.126), channel_id=1, source_target_pairs={{0,4},{4,0},{1,5},{5,1},{2,6},{6,2},{3,7},{7,3},{8,12},{12,8},{9,1... | collective-permute-start | bytes 2359304 | tf_op jit(solution)/shard_map/ppermute | solution.py:46
  490.8 4.8 copy-start.16
  490.8 4.9 copy-start.7
  490.8 4.9 copy-start.8
  (27 other events, 50.5 us)
Sparse Core Ops, SparseCore 0:
  9.6 39.8 all-gather.16
  51.1 35.9 all-gather.20
  89.2 39.2 all-gather.10
  130.5 29.3 all-gather.18
  161.8 62.5 all-gather.12
  226.4 35.7 all-gather.14
  271.9 59.1 reduce-scatter.11
  334.0 35.2 reduce-scatter.13
  372.2 46.9 reduce-scatter.9
  423.1 64.6 all-reduce.5
  490.6 35.2 reduce-scatter.5
  528.7 34.2 reduce-scatter.7

commit v2 on v1

--- a/solution.py
+++ b/solution.py
@@ -50,6 +50,16 @@
     first = jnp.where(core == 0, mine, other)
     second = jnp.where(core == 0, other, mine)
     return jnp.concatenate([first, second], axis)
+
+
+def adam_step(master, first, second, grad, decayed):
+    new_first = first_rate * first + (1.0 - first_rate) * grad
+    new_second = second_rate * second + (1.0 - second_rate) * grad * grad
+    update = new_first / first_fix / (jnp.sqrt(new_second / second_fix) + adam_eps)
+    if decayed:
+        update = update + shrink * master
+    new_master = master - learning * update
+    return (new_master, new_first, new_second, new_master.astype(low))
 
 
 def toeplitz_of(vector_row):
@@ -111,7 +121,11 @@
             count //= 2
             width = summed.shape[1]
             summed = summed[:count] + pltpu.roll(summed[count:], width - count, 1)
-        diag_ref[0, head] = summed
+        row = lax.broadcasted_iota(jnp.int32, summed.shape, 0)
+        for bit in (1, 2, 4):
+            turned = pltpu.roll(summed, summed.shape[1] - bit, 1)
+            summed = jnp.where(jnp.bitwise_and(row, bit) > 0, turned, summed)
+        diag_ref[0, head : head + 1, :] = jnp.sum(summed, axis=0, keepdims=True)
     dq_ref[...] = jnp.where(lane < 64, dq_parts[0], dq_parts[1]).astype(low)
     dk_ref[...] = jnp.concatenate(dk_parts, 0).T.astype(low)
     dv_ref[...] = jnp.concatenate(dv_parts, 0).T.astype(low)
@@ -160,12 +174,12 @@
         functools.partial(attend_back_kernel, rows),
         grid=(pairs,),
         in_specs=[tall, wide, wide, tall, pl.BlockSpec((2, rows, keys), lambda i: (i, 0, 0))],
-        out_specs=[tall, wide, wide, pl.BlockSpec((1, 2, 8, span), lambda i: (i, 0, 0, 0))],
+        out_specs=[tall, wide, wide, pl.BlockSpec((1, 2, span), lambda i: (i, 0, 0))],
         out_shape=[
             jax.ShapeDtypeStruct((rows, width), low),
             jax.ShapeDtypeStruct((keys, width), low),
             jax.ShapeDtypeStruct((keys, width), low),
-            jax.ShapeDtypeStruct((pairs, 2, 8, span), full),
+            jax.ShapeDtypeStruct((pairs, 2, span), full),
         ],
         scratch_shapes=[
             pltpu.VMEM((rows, keys), full),
@@ -181,17 +195,800 @@
     )(query, key, value, grad_out, probs)
 
 
-def adam_step(master, first, second, grad, decayed):
-    new_first = first_rate * first + (1.0 - first_rate) * grad
-    new_second = second_rate * second + (1.0 - second_rate) * grad * grad
-    update = new_first / first_fix / (jnp.sqrt(new_second / second_fix) + adam_eps)
-    if decayed:
-        update = update + shrink * master
-    new_master = master - learning * update
-    return (new_master, new_first, new_second, new_master.astype(low))
-
-
-def body(
+def xor(left, right):
+    return jnp.bitwise_xor(left, right)
+
+
+def by_shard(value, shard):
+    pairs = value.reshape((2, 2) + value.shape[1:])
+    pairs = jnp.where(shard % 2 == 1, pairs[:, ::-1], pairs)
+    return jnp.where(shard // 2 == 1, pairs[::-1], pairs).reshape(value.shape)
+
+
+def after(value, *others):
+    return lax.optimization_barrier((value,) + others)[0]
+
+
+def send(value, pairs):
+    return lax.ppermute(
+        value,
+        ("plane", "core", "shard"),
+        [((p * 2 + c) * 4 + z, (q * 2 + d) * 4 + w) for (p, c, z), (q, d, w) in pairs],
+    )
+
+
+ALL = [(p, c, z) for p in range(4) for c in range(2) for z in range(4)]
+
+
+def plane_first(value):
+    return send(value, [((p, c, z), (p ^ (1 + c), c, z)) for p, c, z in ALL])
+
+
+def plane_second(value):
+    return send(value, [((p, c, z), (p ^ (2 - c), c, z)) for p, c, z in ALL])
+
+
+def across(value, step):
+    return send(value, [((p, c, z), (p, c, z ^ step)) for p, c, z in ALL])
+
+
+def turns(core):
+    return (0, 1 + core, 2 - core, 3)
+
+
+def stack_at(turn, core):
+    return jnp.where((core == 1) & ((turn == 1) | (turn == 2)), 3 - turn, turn)
+
+
+def tile_at(start, size):
+    return pl.ds(pl.multiple_of(start, size), size)
+
+
+vmem = pl.BlockSpec(memory_space=pltpu.VMEM)
+anywhere = pl.BlockSpec(memory_space=pl.ANY)
+fixed = pl.BlockSpec(memory_space=pltpu.HBM)
+
+
+def call(kernel, spot, inputs, outputs, scratch, name, flops=0, grant=16):
+    arrays = [item[0] if isinstance(item, (tuple, list)) else item for item in inputs]
+    specs = [
+        anywhere if isinstance(item, tuple) else fixed if isinstance(item, list) else vmem for item in inputs
+    ]
+    return pl.pallas_call(
+        kernel,
+        in_specs=[pl.BlockSpec(memory_space=pltpu.SMEM)] + specs,
+        out_specs=[vmem for _ in outputs],
+        scratch_shapes=scratch,
+        out_shape=[jax.ShapeDtypeStruct(shape, kind) for shape, kind in outputs],
+        name=name,
+        cost_estimate=pl.CostEstimate(flops=0, bytes_accessed=0, transcendentals=0),
+        compiler_params=pltpu.CompilerParams(vmem_limit_bytes=grant << 20),
+    )(spot, *arrays)
+
+
+def fetch_part(source, target, sem):
+    copy = pltpu.make_async_copy(source, target, sem)
+    copy.start()
+    return copy
+
+
+def bring(pieces, near_ref, far_ref, sems, scalars):
+    plane, core, shard = scalars[0], scalars[1], scalars[2]
+    copies = []
+    for k, turn in enumerate(turns(core)):
+        quarter = xor(plane, turn)
+        for step in (1, 2, 3):
+            source = (near_ref, far_ref)[k // 2].at[3 * (k % 2) + step - 1]
+            for part, target in pieces(source, quarter, xor(shard, step)):
+                copies.append(fetch_part(part, target, sems.at[len(copies)]))
+    return copies
+
+
+def attend_all_kernel(scalars, q_ref, k_ref, v_ref, qseg_ref, kseg_ref, vec_ref, o_ref, p_ref, s_ref):
+    def one(pair, _):
+        lanes = tile_at(128 * pair, 128)
+        attend_kernel(
+            512, q_ref.at[:, lanes], k_ref.at[:, lanes], v_ref.at[:, lanes], qseg_ref, kseg_ref,
+            vec_ref.at[pl.ds(pair, 1)], o_ref.at[:, lanes], p_ref.at[pl.ds(2 * pair, 2)], s_ref,
+        )
+        return 0
+
+    lax.fori_loop(0, 3, one, 0)
+
+
+def hot_buckets():
+    relative = lax.broadcasted_iota(jnp.int32, (32, 1024), 1) - 512
+    return jnp.where(bucket_of(relative) == lax.broadcasted_iota(jnp.int32, (32, 1024), 0), 1.0, 0.0)
+
+
+def unpack_kernel(scalars, r0, r1, r2, r3, gain_ref, vec_ref, bias_ref):
+    core, shard = scalars[1], scalars[2]
+    for z in range(4):
+        rows = jnp.zeros((16, 384), full)
+        for step, ref in enumerate((r0, r1, r2, r3)):
+            rows = rows + jnp.where(xor(shard, step) == z, ref[192:208, :].astype(full), 0.0)
+        gain_ref[:, 192 * z : 192 * z + 192] = rows[0:2, :192]
+        bias_ref[8 * z : 8 * z + 8, :] = rows[2:10, :12]
+    found = lax.dot_general(
+        bias_ref[...], hot_buckets(), (((0,), (0,)), ((), ())),
+        precision=lax.Precision.HIGHEST, preferred_element_type=full,
+    )
+    own = jnp.where(core == 0, found[0:6], found[6:12])
+    for i in range(6):
+        vec_ref[i // 2, i % 2 : i % 2 + 1, :] = own[i : i + 1]
+
+
+def cat_kernel(rows, scalars, *refs):
+    at = 0
+    for ref in refs[:-1]:
+        value = ref[...]
+        if len(value.shape) == 2:
+            value = value[None]
+        refs[-1][at : at + value.shape[0]] = value[:, :rows]
+        at += value.shape[0]
+
+
+def cat(spot, pieces, rows, name):
+    count = sum(1 if len(piece.shape) == 2 else piece.shape[0] for piece in pieces)
+    shape = (count, rows, pieces[0].shape[-1])
+    return call(functools.partial(cat_kernel, rows), spot, pieces, [(shape, pieces[0].dtype)], [], name, 0, 4)[0]
+
+
+def pass_ffn_kernel(scalars, keep, first, out):
+    def one(i, _):
+        rows, later = tile_at(576 * i, 576), tile_at(2304 + 576 * i, 576)
+        out[rows, :] = (wide(keep[later, :]) + wide(first[later, :])).astype(low)
+        return 0
+
+    lax.fori_loop(0, 4, one, 0)
+
+
+def sum_ffn_kernel(scalars, keep, first, second, *outs):
+    for step, out in enumerate(outs):
+        rows = tile_at(576 * xor(scalars[2], step), 576)
+        total = wide(keep[rows, :]) + wide(first[rows, :]) + wide(second[rows, :])
+        out[...] = total.astype(out.dtype)
+
+
+def pass_attn_kernel(scalars, keep, sent, first, out):
+    out[0:768, :] = (wide(keep[768:1536, :]) + wide(first[768:1536, :])).astype(low)
+    out[768:784, :] = (wide(sent[1536:1552, :]) + wide(first[1536:1552, :])).astype(low)
+
+
+def sum_attn_kernel(scalars, keep, passed, first, second, *outs):
+    for step, out in enumerate(outs):
+        rows = tile_at(192 * xor(scalars[2], step), 192)
+        total = wide(keep[rows, :]) + wide(first[rows, :]) + wide(second[rows, :])
+        out[0:192, :] = total.astype(out.dtype)
+        small = wide(passed[768:784, :]) + wide(second[768:784, :])
+        out[192:208, :] = small.astype(out.dtype)
+
+
+def total_kernel(scalars, own, r1, r2, r3, out, *rest):
+    total = own[...] + wide(r1[...]) + wide(r2[...]) + wide(r3[...])
+    out[...] = total[: out.shape[0]].astype(low)
+    if rest:
+        rest[0][...] = total[out.shape[0] :]
+
+
+def pack_attn_kernel(scalars, master_ref, gain_ref, bias_ref, out_ref, part_ref, gain_part, bias_part, sems):
+    columns = tile_at(384 * scalars[1], 384)
+    copies = [
+        fetch_part(master_ref.at[scalars[0], :, columns], part_ref, sems.at[0]),
+        fetch_part(gain_ref, gain_part, sems.at[1]),
+        fetch_part(bias_ref, bias_part, sems.at[2]),
+    ]
+    for copy in copies:
+        copy.wait()
+    gains = jnp.concatenate([gain_part[...], jnp.zeros((2, 192), full)], 1)
+    bias = jnp.concatenate([bias_part[...], jnp.zeros((8, 372), full)], 1)
+    out_ref[192:208, :] = jnp.concatenate([gains, bias, jnp.zeros((6, 384), full)], 0).astype(low)
+    out_ref[0:192, :] = part_ref[...].astype(low)
+
+
+def pack_ffn_kernel(scalars, in_ref, out_ref, unit_ref, part_ref, rows_ref, sems):
+    plane, core = scalars[0], scalars[1]
+    copies = []
+    for k in range(2):
+        columns = tile_at(1024 * (plane % 2) + 512 * k + 256 * core, 256)
+        copies.append(fetch_part(in_ref.at[plane // 2, :, columns], part_ref.at[k], sems.at[k]))
+    rows = tile_at(256 * core + 64 * plane, 64)
+    copies.append(fetch_part(out_ref.at[rows, :], rows_ref, sems.at[2]))
+    for copy in copies:
+        copy.wait()
+    unit_ref[0:192, :] = part_ref[0].astype(low)
+    unit_ref[192:384, :] = part_ref[1].astype(low)
+    for i in range(3):
+        unit_ref[384 + 64 * i : 448 + 64 * i, :] = rows_ref[:, 256 * i : 256 * i + 256].astype(low)
+
+
+def project_kernel(
+    scalars, x_ref, gain_ref, master_ref, near_ref, far_ref, w_ref, act_ref, q_ref, k_ref, v_ref, own_ref, sems
+):
+    columns = tile_at(384 * scalars[1], 384)
+    own_copy = fetch_part(master_ref.at[:, :, columns], own_ref, sems.at[12])
+
+    def pieces(source, quarter, shard):
+        return [(source, w_ref.at[quarter, tile_at(192 * shard, 192), :])]
+
+    copies = bring(pieces, near_ref, far_ref, sems, scalars)
+    x_in = x_ref[...].astype(full)
+    scale = lax.rsqrt(jnp.mean(x_in * x_in, axis=-1, keepdims=True) + norm_eps)
+    act_ref[...] = (x_in * scale * gain_ref[0:1, :]).astype(low)
+    own_copy.wait()
+    for quarter in range(4):
+        w_ref[quarter, tile_at(192 * scalars[2], 192), :] = own_ref[quarter].astype(low)
+    for copy in copies:
+        copy.wait()
+    for quarter, out in enumerate((q_ref, k_ref, v_ref)):
+        out[...] = mdot(act_ref[...], w_ref[quarter]).astype(low)
+
+
+def gelu_parts(gate):
+    inner = 0.7978845608028654 * (gate + 0.044715 * gate * gate * gate)
+    bent = jnp.tanh(inner)
+    slope = 0.7978845608028654 * (1.0 + 3.0 * 0.044715 * gate * gate)
+    value = 0.5 * gate * (1.0 + bent)
+    return value, 0.5 * (1.0 + bent) + 0.5 * gate * (1.0 - bent * bent) * slope
+
+
+def feed_kernel(
+    scalars, x_ref, mix_own, mix_other, w_attn, wo_other, gain_ref, gy_ref, in_master, out_master, near_ref, far_ref,
+    mid_ref, act_ref, hid_ref, part_ref, y_ref, grad_ref,
+    mix_ref, wo_ref, win_ref, wout_ref, own_ref, gate_ref, up_ref, sems,
+):
+    core, shard = scalars[1], scalars[2]
+    own_copy = fetch_part(out_master.at[tile_at(256 * core, 256), :], own_ref, sems.at[60])
+
+    def pieces(source, quarter, shard):
+        rows = tile_at(192 * shard, 192)
+        found = []
+        for k in range(2):
+            columns = tile_at(512 * (quarter % 2) + 256 * k, 256)
+            found.append((source.at[192 * k : 192 * k + 192, :], win_ref.at[quarter // 2, rows, columns]))
+        rows = tile_at(256 * shard + 64 * quarter, 64)
+        for i in range(3):
+            part = source.at[384 + 64 * i : 448 + 64 * i, :]
+            found.append((part, wout_ref.at[rows, 256 * i : 256 * i + 256]))
+        return found
+
+    copies = bring(pieces, near_ref, far_ref, sems, scalars)
+    here, there = tile_at(384 * core, 384), tile_at(384 * (1 - core), 384)
+    mix_ref[:, here] = mix_own[...]
+    mix_ref[:, there] = mix_other[...]
+    wo_ref[:, here] = w_attn[3]
+    wo_ref[:, there] = wo_other[...]
+
+    def middle(half, _):
+        rows = tile_at(256 * half, 256)
+        x_mid = x_ref[rows, :].astype(full) + mdot(mix_ref[rows, :], wo_ref[...])
+        mid_ref[rows, :] = x_mid
+        scale = lax.rsqrt(jnp.mean(x_mid * x_mid, axis=-1, keepdims=True) + norm_eps)
+        act_ref[rows, :] = (x_mid * scale * gain_ref[1:2, :]).astype(low)
+        return 0
+
+    lax.fori_loop(0, 2, middle, 0)
+    for i in range(2):
+        for k in range(4):
+            pair = in_master[i, :, 512 * k : 512 * k + 512]
+            win_ref[i, tile_at(192 * shard, 192), 256 * k : 256 * k + 256] = jnp.where(
+                core == 0, pair[:, :256], pair[:, 256:]
+            ).astype(low)
+    own_copy.wait()
+    wout_ref[tile_at(256 * shard, 256), :] = own_ref[...].astype(low)
+    for copy in copies:
+        copy.wait()
+
+    def hidden(at, _):
+        rows, columns = tile_at(256 * (at // 2), 256), tile_at(512 * (at % 2), 512)
+        gate = mdot(act_ref[rows, :], win_ref[0, :, columns])
+        up = mdot(act_ref[rows, :], win_ref[1, :, columns])
+        value, slope = gelu_parts(gate)
+        hid_ref[rows, columns] = (value * up).astype(low)
+        gate_ref[rows, columns] = slope * up
+        up_ref[rows, columns] = value
+        return 0
+
+    lax.fori_loop(0, 4, hidden, 0)
+
+    def inner(half, _):
+        rows = tile_at(256 * half, 256)
+        part = jnp.zeros((256, 768), full)
+        for h in range(2):
+            columns = slice(512 * h, 512 * h + 512)
+            grad_hid = ndot(gy_ref[rows, :], wout_ref[columns, :])
+            grad_gate = (grad_hid * gate_ref[rows, columns]).astype(low)
+            grad_up = (grad_hid * up_ref[rows, columns]).astype(low)
+            grad_ref[h, rows, :] = grad_gate
+            grad_ref[2 + h, rows, :] = grad_up
+            part = part + ndot(grad_gate, win_ref[0, :, columns]) + ndot(grad_up, win_ref[1, :, columns])
+        part_ref[rows, :] = part
+        y_ref[rows, :] = mdot(hid_ref[rows, :], wout_ref[...])
+        return 0
+
+    lax.fori_loop(0, 2, inner, 0)
+
+
+def outer_kernel(scalars, act_ref, grad_ref, hid_ref, gy_ref, send_ref, keep_ref, turned_ref, sum_ref):
+    plane, core = scalars[0], scalars[1]
+    turned_ref[...] = act_ref[...].astype(full).T.astype(low)
+
+    def outer(j, _):
+        for odd, out in enumerate((keep_ref, send_ref)):
+            turn = odd * (1 + core) + j * (2 - core)
+            found = mdot(turned_ref[...], grad_ref[xor(plane, turn)]).astype(low)
+            for z in range(4):
+                for i in range(2):
+                    out[tile_at(2304 * j + 576 * z + 192 * i, 192), :] = found[
+                        192 * z : 192 * z + 192, 256 * i : 256 * i + 256
+                    ]
+        return 0
+
+    lax.fori_loop(0, 2, outer, 0)
+
+    def last(z, _):
+        sum_ref[...] = tdot(hid_ref[:, tile_at(256 * z, 256)], gy_ref[...])
+        for k, turn in enumerate(turns(core)):
+            out = (keep_ref, send_ref)[k % 2]
+            found = sum_ref[tile_at(64 * xor(plane, turn), 64), :].astype(low)
+            for i in range(3):
+                out[tile_at(2304 * (k // 2) + 576 * z + 384 + 64 * i, 64), :] = found[:, 256 * i : 256 * i + 256]
+        return 0
+
+    lax.fori_loop(0, 4, last, 0)
+
+
+def pick_kernel(scalars, b0, b1, b2, b3, place_ref, token_ref, out_ref):
+    def rows_of(half, _):
+        rows = tile_at(256 * half, 256)
+        total = jnp.zeros((256, 768), full)
+        for i, ref in enumerate((b0, b1, b2, b3)):
+            same = place_ref[:, 256 * i : 256 * i + 256] == token_ref[rows, :]
+            total = total + mdot(jnp.where(same, 1.0, 0.0).astype(low), ref[...])
+        out_ref[rows, :] = total.astype(low)
+        return 0
+
+    lax.fori_loop(0, 2, rows_of, 0)
+
+
+def spread(wanted_ref, token_ref, value, outs):
+    for i, out in enumerate(outs):
+        same = wanted_ref[256 * i : 256 * i + 256, :] == token_ref[...]
+        out[...] = mdot(jnp.where(same, 1.0, 0.0).astype(low), value).astype(low)
+
+
+def spread_y_kernel(scalars, mid_ref, own_ref, other_ref, wanted_ref, token_ref, o0, o1, o2, o3, value_ref):
+    value_ref[...] = (mid_ref[...] + own_ref[...] + other_ref[...]).astype(low)
+    spread(wanted_ref, token_ref, value_ref[...], (o0, o1, o2, o3))
+
+
+def spread_x_kernel(
+    scalars, own_ref, other_ref, x_ref, gain_ref, mid_ref, wanted_ref, token_ref, o0, o1, o2, o3, value_ref
+):
+    x_in = x_ref[...].astype(full)
+    scale = lax.rsqrt(jnp.mean(x_in * x_in, axis=-1, keepdims=True) + norm_eps)
+    turned = (own_ref[...] + other_ref[...]) * gain_ref[0:1, :]
+    lean = jnp.mean(turned * x_in, axis=-1, keepdims=True)
+    value_ref[...] = (mid_ref[...] + scale * turned - x_in * (scale * scale * scale * lean)).astype(low)
+    spread(wanted_ref, token_ref, value_ref[...], (o0, o1, o2, o3))
+
+
+def back_kernel(
+    scalars, own_part, other_part, mid_ref, gy_ref, gain_ref, w_ref, wo_other, q_ref, k_ref, v_ref, p_ref,
+    grad_ref, right_ref, lined_ref, gain_out, attn_ref, mixed_ref, s_ref, ds_ref, acc_ref, *rest
+):
+    core = scalars[1]
+    here, there = tile_at(384 * core, 384), tile_at(384 * (1 - core), 384)
+    late = (q_ref, k_ref, v_ref, p_ref)
+    copies = [fetch_part(ref, held, rest[-1].at[i]) for i, (ref, held) in enumerate(zip(late, rest[:-1]))]
+    q_ref, k_ref, v_ref, p_ref = rest[:-1]
+    x_mid = mid_ref[...]
+    scale = lax.rsqrt(jnp.mean(x_mid * x_mid, axis=-1, keepdims=True) + norm_eps)
+    gain_out[...] = jnp.sum(own_part[...] * x_mid * scale, axis=0, keepdims=True)
+    turned = (own_part[...] + other_part[...]) * gain_ref[1:2, :]
+    lean = jnp.mean(turned * x_mid, axis=-1, keepdims=True)
+    grad_mid = gy_ref[...].astype(full) + scale * turned - x_mid * (scale * scale * scale * lean)
+    grad_ref[...] = grad_mid
+    attn_ref[...] = grad_mid.astype(low)
+    mixed_ref[...] = (
+        ndot(attn_ref[:, here], w_ref[3, here, :]) + ndot(attn_ref[:, there], wo_other[here, :])
+    ).astype(low)
+    for copy in copies:
+        copy.wait()
+
+    def one(pair, _):
+        lanes = tile_at(128 * pair, 128)
+        attend_back_kernel(
+            512, *[ref.at[:, lanes] for ref in (q_ref, k_ref, v_ref, mixed_ref)], p_ref.at[pl.ds(2 * pair, 2)],
+            *[right_ref.at[i, :, lanes] for i in range(3)], lined_ref.at[pl.ds(pair, 1)], s_ref, ds_ref, acc_ref,
+        )
+        return 0
+
+    lax.fori_loop(0, 3, one, 0)
+    right_ref[3] = attn_ref[:, here]
+
+
+def last_kernel(
+    scalars, act_ref, mix_own, mix_other, right_ref, w_ref, x_ref, lined_ref, other_ref,
+    send_ref, keep_ref, part_ref, turned_ref, *rest
+):
+    plane, core = scalars[0], scalars[1]
+    here, there = tile_at(384 * core, 384), tile_at(384 * (1 - core), 384)
+    late = (act_ref, mix_own, mix_other, right_ref, w_ref, x_ref)
+    copies = [fetch_part(ref, held, rest[-1].at[i]) for i, (ref, held) in enumerate(zip(late, rest[:-1]))]
+    act_ref, mix_own, mix_other, right_ref, w_ref, x_ref = rest[:-1]
+    for copy in copies:
+        copy.wait()
+    turned_ref[0] = act_ref[...].astype(full).T.astype(low)
+    turned_ref[1, here, :] = mix_own[...].astype(full).T.astype(low)
+    turned_ref[1, there, :] = mix_other[...].astype(full).T.astype(low)
+
+    def outer(j, _):
+        for odd, out in enumerate((keep_ref, send_ref)):
+            quarter = xor(plane, odd * (1 + core) + j * (2 - core))
+            out[tile_at(768 * j, 768), :] = mdot(turned_ref[quarter // 3], right_ref[quarter]).astype(low)
+        return 0
+
+    lax.fori_loop(0, 2, outer, 0)
+    part = ndot(right_ref[0], w_ref[0]) + ndot(right_ref[1], w_ref[1]) + ndot(right_ref[2], w_ref[2])
+    part_ref[...] = part
+    x_in = x_ref[...].astype(full)
+    scale = lax.rsqrt(jnp.mean(x_in * x_in, axis=-1, keepdims=True) + norm_eps)
+    gain = jnp.sum(part * x_in * scale, axis=0, keepdims=True)
+    lined = jnp.concatenate([lined_ref[0], lined_ref[1], lined_ref[2]], 0)
+    table = lax.dot_general(
+        lined, hot_buckets(), (((1,), (1,)), ((), ())),
+        precision=lax.Precision.HIGHEST, preferred_element_type=full,
+    )
+    table = jnp.concatenate([table, jnp.zeros((6, 352), full)], 1)
+    other = other_ref[...]
+    send_ref[1536:1552, :] = jnp.concatenate(
+        [gain[:, :384], gain[:, 384:], other[:, :384], other[:, 384:], table, jnp.zeros((6, 384), full)], 0
+    ).astype(low)
+
+
+def wide(value):
+    return value.astype(full)
+
+
+def adam_kernel(join, scalars, master, first, second, own, other, *outs):
+    lower = scalars[1] == 0
+    left = jnp.where(lower, own[0], other[0]).astype(full)
+    right = jnp.where(lower, other[0], own[0]).astype(full)
+    grad = join(left, right).reshape(master.shape)
+    new_master, new_first, new_second, copy = adam_step(master[...], first[...], second[...], grad, True)
+    outs[0][...] = new_master
+    outs[1][...] = new_first
+    outs[2][...] = copy
+    if len(outs) == 4:
+        outs[3][...] = new_second
+    else:
+
+        @pl.when(pl.program_id(0) < 3)
+        def _():
+            outs[3][...] = new_second
+
+        @pl.when(pl.program_id(0) == 3)
+        def _():
+            outs[4][...] = new_second[0]
+
+
+def adam_call(grid, join, state, quarter_of, states, grads, spot, name, sizes, rows_at, second=None):
+
+    def grad_spec(other):
+        def where(*idx):
+            scalars = idx[-1]
+            core = 1 - scalars[1] if other else scalars[1]
+            return (stack_at(xor(scalars[0], quarter_of(*idx[:-1])), core), rows_at, 0)
+
+        return pl.BlockSpec(sizes, where)
+
+    shape = states[0].shape
+    kinds = [full, full, low] + ([full] if second is None else [])
+    count = functools.reduce(lambda a, b: a * b, shape)
+    return pl.pallas_call(
+        functools.partial(adam_kernel, join),
+        grid_spec=pltpu.PrefetchScalarGridSpec(
+            num_scalar_prefetch=1,
+            grid=grid,
+            in_specs=[state] * 3 + [grad_spec(False), grad_spec(True)],
+            out_specs=[state] * len(kinds) + ([] if second is None else second[0]),
+        ),
+        out_shape=[jax.ShapeDtypeStruct(shape, kind) for kind in kinds]
+        + ([] if second is None else second[1]),
+        name=name,
+        cost_estimate=pl.CostEstimate(flops=0, bytes_accessed=0, transcendentals=0),
+    )(spot, *states, *grads)
+
+
+def body_fast(
+    tokens,
+    cotangent,
+    lengths,
+    deal,
+    attn_master,
+    ffin_master,
+    ffout_master,
+    gain_master,
+    bias_master,
+    attn_first,
+    ffin_first,
+    ffout_first,
+    gain_first,
+    bias_first,
+    attn_second,
+    ffin_second,
+    ffout_second,
+    gain_second,
+    bias_second,
+):
+    plane, core, shard = (lax.axis_index(name) for name in ("plane", "core", "shard"))
+    spot = jnp.stack([plane, core, shard])
+    group, rest = shard // 2, shard % 2
+    mine = group == core
+
+    quarter = call(
+        pack_attn_kernel, spot, [[attn_master], [gain_master], [bias_master]], [((208, 384), low)],
+        [
+            pltpu.VMEM((192, 384), full), pltpu.VMEM((2, 192), full), pltpu.VMEM((8, 12), full),
+            pltpu.SemaphoreType.DMA((3,)),
+        ],
+        "pack_attn", 0, 60,
+    )[0]
+    attn_came = [across(quarter, step) for step in (1, 2, 3)]
+
+    unit = call(
+        pack_ffn_kernel, spot, [[ffin_master], [ffout_master]], [((576, 256), low)],
+        [pltpu.VMEM((2, 192, 256), full), pltpu.VMEM((64, 768), full), pltpu.SemaphoreType.DMA((3,))],
+        "pack_ffn", 0, 60,
+    )[0]
+    attn_came = [after(value, unit) for value in attn_came]
+
+    def fetch(own, gates=(None, None)):
+        up = lambda pairs: [((p, 1, z), (p, 1, w)) for p in range(4) for z, w in pairs]
+        down = lambda pairs: [((p, 0, 3 - z), (p, 0, 3 - w)) for p in range(4) for z, w in pairs]
+        pairs = lambda *which: up(which) + down(which)
+        held = lambda value, gate: value if gate is None else after(value, gate())
+        one = held(send(own, pairs((0, 1), (1, 2), (2, 3))), gates[0])
+        two = held(send(one, pairs((1, 2), (2, 3))), gates[1])
+        three = send(jnp.where(at_end, own, two), pairs((2, 3), (3, 2)))
+        return own, one, two, three
+
+    way = 1 - 2 * core
+    at_end = shard == 3 * core
+    blocks = jnp.stack(
+        [shard, shard + way, shard + 2 * way, jnp.where(at_end, shard + 3 * way, shard - way)]
+    )
+    blocks = jnp.clip(blocks, 0, 3)
+    tok_blocks = fetch(tokens[0])
+
+    table_own = jnp.concatenate([lengths[0], deal[0]])
+    table = jnp.where(mine, table_own, swap(table_own))
+    lens, order = table[:4], table[4:]
+    starts = jnp.cumsum(lens) - lens
+    long_start = jnp.sum(jnp.where(lens == 512, starts, 0))
+    at_half = jnp.arange(512, dtype=jnp.int32)
+    token_here = jnp.where(rest == 0, long_start + at_half, at_half + 512 * (at_half >= long_start))
+    seg_here = jnp.sum((token_here[:, None] >= starts[None, :]).astype(jnp.int32), axis=1)
+    token_index = jnp.arange(1024, dtype=jnp.int32)
+
+    token_column = token_here[:, None]
+    token_row = jnp.where(mine, token_here, -1)[None, :]
+
+    def rows_here(place_of, pieces, gate=None):
+        place = [lax.dynamic_slice_in_dim(place_of, blocks[i] * 256, 256) for i in range(4)]
+        place = jnp.concatenate(place).reshape(1, 1024)
+        chosen = call(
+            pick_kernel, spot, [*pieces, place, token_column], [((512, 768), low)], [], "pick", 0, 8
+        )[0]
+        chosen = chosen if gate is None else after(chosen, *gate)
+        return jnp.where(mine, chosen, swap(chosen))
+
+    def wanted_by(place_of):
+        return by_shard(place_of.reshape(4, 256), shard).reshape(1024, 1)
+
+    def rows_back(rows, gate):
+        pairs = lambda step: [((p, c, z), (p, c, z ^ step)) for p, c, z in ALL if z // 2 == c]
+        return [after(send(rows[step], pairs(step)), gate) for step in (1, 2, 3)]
+
+    wanted_y = wanted_by(order)
+    wanted_x = wanted_by(token_index)
+
+    gains, vectors = call(
+        unpack_kernel, spot, [quarter, *attn_came], [((2, 768), full), ((3, 2, 1024), full)],
+        [pltpu.VMEM((32, 12), full)], "unpack", 0, 8,
+    )
+
+    def spread_plane(pieces, rows, gate=None, late=None):
+        near = cat(spot, pieces, rows, "near")
+        arrived = plane_first(near)
+        if gate is not None:
+            arrived = after(arrived, gate)
+        near = cat(spot, [near, arrived], rows, "nearest")
+        return near, plane_second(near if late is None else after(near, late))
+
+    near, far = spread_plane(attn_came, 192)
+    unit = after(unit, near, tok_blocks[2], gains)
+    ffn_came = [across(unit, step) for step in (1, 2, 3)]
+    x_low = rows_here(token_index, tok_blocks, (far, ffn_came[0]))
+    w_attn, act_one, query, key, value = call(
+        project_kernel, spot,
+        [x_low, gains, [attn_master], (near,), (far,)],
+        [((4, 768, 384), low), ((512, 768), low)] + [((512, 384), low)] * 3,
+        [pltpu.VMEM((4, 192, 384), full), pltpu.SemaphoreType.DMA((13,))], "project", 0, 60,
+    )
+    wo_other = swap(w_attn[3])
+
+
+    mix_own, probs = call(
+        attend_all_kernel, spot, [query, key, value, seg_here[:, None], seg_here[None, :], vectors],
+        [((512, 384), low), ((6, 512, 512), low)], [pltpu.VMEM((512, 512), full)], "attend", 0, 8,
+    )
+    ffn_came = [after(piece, mix_own) for piece in ffn_came]
+    ffn_near, ffn_far = spread_plane(ffn_came, 576)
+    cot_blocks = fetch(after(cotangent[0], *ffn_came), (lambda: ffn_near, None))
+    grad_y = rows_here(order, cot_blocks)
+    mix_other = swap(mix_own)
+    x_mid, act_two, hidden, part_two, y_part, grads_up = call(
+        feed_kernel, spot,
+        [
+            x_low, mix_own, mix_other, w_attn, wo_other, gains, grad_y, ffin_master, [ffout_master],
+            (ffn_near,), (ffn_far,),
+        ],
+        [
+            ((512, 768), full), ((512, 768), low), ((512, 1024), low), ((512, 768), full), ((512, 768), full),
+            ((4, 512, 512), low),
+        ],
+        [
+            pltpu.VMEM((512, 768), low), pltpu.VMEM((768, 768), low), pltpu.VMEM((2, 768, 1024), low),
+            pltpu.VMEM((1024, 768), low), pltpu.VMEM((256, 768), full), pltpu.VMEM((512, 1024), full),
+            pltpu.VMEM((512, 1024), full), pltpu.SemaphoreType.DMA((61,)),
+        ],
+        "feed", 0, 24,
+    )
+    ffn_send, ffn_keep = call(
+        outer_kernel, spot, [act_two, grads_up, hidden, grad_y], [((4608, 256), low)] * 2,
+        [pltpu.VMEM((768, 512), low), pltpu.VMEM((256, 768), full)], "outer", 0, 12,
+    )
+    part_other = after(swap(part_two), ffn_send)
+    ffn_first = plane_first(ffn_send)
+
+    y_other = swap(after(y_part, part_other))
+    y_rows = call(
+        spread_y_kernel, spot, [x_mid, y_part, y_other, wanted_y, token_row], [((256, 768), low)] * 4,
+        [pltpu.VMEM((512, 768), low)], "spread_y", 0, 10,
+    )
+    grad_mid, right, lined, gain_two = call(
+        back_kernel, spot,
+        [
+            after(part_two, *y_rows), part_other, x_mid, grad_y, gains, w_attn, wo_other,
+            (query,), (key,), (value,), (probs,),
+        ],
+        [
+            ((512, 768), full), ((4, 512, 384), low), ((3, 2, 1024), full), ((1, 768), full),
+        ],
+        [
+            pltpu.VMEM((512, 768), low), pltpu.VMEM((512, 384), low), pltpu.VMEM((512, 512), full), pltpu.VMEM((512, 512), low),
+            pltpu.VMEM((128, 1024), full), *[pltpu.VMEM((512, 384), low)] * 3, pltpu.VMEM((6, 512, 512), low),
+            pltpu.SemaphoreType.DMA((4,)),
+        ],
+        "back", 0, 24,
+    )
+    ffn_first = after(ffn_first, right)
+    one_out = lambda kernel, inputs, shape, name: call(kernel, spot, inputs, [(shape, low)], [], name, 0, 8)[0]
+    ffn_passed = one_out(pass_ffn_kernel, [ffn_keep, ffn_first], (2304, 256), "pass_ffn")
+    ffn_second = plane_second(ffn_passed)
+    attn_send, attn_keep, part_one = call(
+        last_kernel, spot,
+        [
+            (after(act_one, ffn_passed),), (mix_own,), (mix_other,), (right,), (w_attn,), (x_low,), lined, gain_two,
+        ],
+        [((1552, 384), low), ((1536, 384), low), ((512, 768), full)],
+        [
+            pltpu.VMEM((2, 768, 512), low), pltpu.VMEM((512, 768), low), *[pltpu.VMEM((512, 384), low)] * 2,
+            pltpu.VMEM((4, 512, 384), low), pltpu.VMEM((4, 768, 384), low), pltpu.VMEM((512, 768), low),
+            pltpu.SemaphoreType.DMA((6,)),
+        ],
+        "last", 0, 24,
+    )
+    y_came = rows_back(y_rows, part_one)
+    ffn_second = after(ffn_second, part_one, *y_came)
+    layer_out = y_rows[0] + y_came[0] + y_came[1] + y_came[2]
+    ffn_own, *ffn_outs = call(
+        sum_ffn_kernel, spot, [ffn_keep, ffn_first, ffn_second],
+        [((576, 256), full)] + [((576, 256), low)] * 3, [], "sum_ffn", 0, 8,
+    )
+    ffn_came = [across(out, step) for step, out in zip((1, 2, 3), ffn_outs)]
+    attn_first_came = after(plane_first(after(attn_send, ffn_second)), *ffn_came[:2])
+    passed = one_out(pass_attn_kernel, [attn_keep, attn_send, attn_first_came], (784, 384), "pass_attn")
+    attn_second_came = plane_second(passed)
+    attn_own, *attn_outs = call(
+        sum_attn_kernel, spot, [attn_keep, passed, attn_first_came, attn_second_came],
+        [((208, 384), full)] + [((208, 384), low)] * 3, [], "sum_attn", 0, 8,
+    )
+    x_rows = call(
+        spread_x_kernel, spot, [part_one, swap(part_one), x_low, gains, grad_mid, wanted_x, token_row],
+        [((256, 768), low)] * 4, [pltpu.VMEM((512, 768), low)], "spread_x", 0, 10,
+    )
+
+    ffn_came = [after(value, attn_second_came) for value in ffn_came]
+    attn_outs = [across(out, step) for step, out in zip((1, 2, 3), attn_outs)]
+    ffn_sum = one_out(total_kernel, [ffn_own, *ffn_came], (576, 256), "total_ffn")
+    ffn_pair = cat(spot, [ffn_sum, after(plane_first(ffn_sum), attn_outs[0])], 576, "pair_ffn")
+    ffn_stack = cat(spot, [ffn_pair, after(plane_second(ffn_pair), attn_outs[1], attn_outs[2])], 576, "stack_ffn")
+    ffn_sum = (ffn_stack, swap(ffn_stack))
+    ffout_state = pl.BlockSpec((2, 1, 64, 768), lambda q, s: (0, q, 0, 0))
+    unfold = lambda value: jnp.concatenate([value[:64], value[64:128], value[128:]], 1)
+    ffout_res = adam_call(
+        (4,), lambda left, right: jnp.stack([unfold(left), unfold(right)]), ffout_state, lambda q: q,
+        [state.reshape(2, 4, 64, 768) for state in (ffout_master, ffout_first, ffout_second)],
+        ffn_sum, spot, "adam_ffout", (1, 192, 256), 2,
+    )
+    ffout_res = [value.reshape(512, 768) for value in ffout_res]
+    ffin_res = adam_call(
+        (2, 2),
+        lambda left, right: jnp.concatenate(
+            [left[:192], right[:192], left[192:], right[192:]], 1
+        ),
+        pl.BlockSpec((1, 192, 1024), lambda i, h, s: (i, 0, h)), lambda i, h: 2 * i + h,
+        [ffin_master, ffin_first, ffin_second], ffn_sum, spot, "adam_ffin", (1, 384, 256), 0,
+    )
+    attn_outs = [after(value, ffn_stack) for value in attn_outs]
+    attn_sum, small = call(
+        total_kernel, spot, [attn_own, *attn_outs], [((192, 384), low), ((16, 384), full)], [], "total_attn", 0, 8
+    )
+    attn_near = cat(spot, [attn_sum, after(plane_first(attn_sum), ffin_res[0])], 192, "pair_attn")
+    attn_stack = cat(spot, [attn_near, after(plane_second(attn_near), ffout_res[0])], 192, "stack_attn")
+    attn_sum = (attn_stack, swap(attn_stack))
+    x_rows = [after(value, small) for value in x_rows]
+    x_came = rows_back(x_rows, attn_stack)
+    input_grad = x_rows[0] + x_came[0] + x_came[1] + x_came[2]
+    small_other = swap(small)
+    gain_sum = (small[:4] + small_other[:4]).reshape(2, 768)
+    g_gain = lax.dynamic_slice_in_dim(gain_sum, shard * 192, 192, 1)
+    g_bias = both_cores(small[4:10, :32], small_other[4:10, :32], core, 0)
+    g_bias = lax.dynamic_slice_in_dim(g_bias, shard * 8, 8, 1).T
+
+    attn_res = adam_call(
+        (4,), lambda left, right: jnp.concatenate([left, right], 1),
+        pl.BlockSpec((1, 192, 768), lambda m, s: (m, 0, 0)), lambda m: m,
+        [attn_master, attn_first, attn_second], attn_sum, spot, "adam_attn", (1, 192, 384), 0,
+        (
+            [
+                pl.BlockSpec((1, 192, 768), lambda m, s: (jnp.minimum(m, 2), 0, 0)),
+                pl.BlockSpec((192, 768), lambda m, s: (0, 0)),
+            ],
+            [jax.ShapeDtypeStruct((3, 192, 768), full), jax.ShapeDtypeStruct((192, 768), full)],
+        ),
+    )
+    gain_res = adam_step(gain_master, gain_first, gain_second, g_gain, False)
+    bias_res = adam_step(bias_master, bias_first, bias_second, g_bias, False)
+    return (
+        layer_out[None],
+        input_grad[None],
+        attn_res[0],
+        ffin_res[0],
+        ffout_res[0],
+        gain_res[0] - gain_master,
+        bias_res[0] - bias_master,
+        attn_res[1],
+        ffin_res[1],
+        ffout_res[1],
+        gain_res[1],
+        bias_res[1],
+        attn_res[3],
+        attn_res[4],
+        ffin_res[3],
+        ffout_res[3],
+        gain_res[2],
+        bias_res[2],
+        attn_res[2],
+        ffin_res[2],
+        ffout_res[2],
+    )
+
+
+def body_any(
     tokens,
     cotangent,
     lengths,
@@ -349,8 +1146,7 @@
     d_gain_one = jnp.sum(grad_act_one * x_in * scale_one, axis=0)
     input_grad = rows_back(token_index, grad_x)
 
-    folded = diagonals.reshape(own_heads, 8, span)
-    lined = sum((jnp.roll(folded[:, i], -i, axis=1) for i in range(8)))
+    lined = diagonals.reshape(own_heads, span)
     table_own = lax.dot_general(
         one_hot, lined, (((1,), (1,)), ((), ())), precision=lax.Precision.HIGHEST
     )
@@ -425,4 +1221,5 @@
     out_specs = (
         (tok, tok) + states + states + (second, first, second, first, gain, first) + states[:3]
     )
+    body = body_fast if (reps, shards) == (8, 4) else body_any
     return jax.shard_map(body, mesh=cores, in_specs=in_specs, out_specs=out_specs, check_vma=False)

time: 577 us -> 313 us (0.54)
  waiting for transfers between devices: 338 us -> 91.5 us
  Pallas kernels: 20.3 us -> 105 us
  starting transfers between devices: 2.32 us -> 74.1 us
  blocking collectives: 64.7 us -> 0 us
  matrix products: 51.3 us -> 0 us
  other arithmetic: 39.8 us -> 13 us
  local copies, waits for them, and re-layouts: 38.7 us -> 24 us
  between operations: 15.2 us -> 4.28 us
    all_gather x6 -> x0, waiting for transfers between devices: 170 us -> none  [the longest x1 61.5 us: body(): w_in = lax.all_gather(ffin_low, 'shard', axis=1, tiled=True)]
    reduce_scatter x5 -> x0, waiting for transfers between devices: 153 us -> none  [the longest x3 110 us: reduced(): share = lax.psum_scatter(grad, 'shard', scatter_dimension=axis, tiled=True)]
    ppermute x0 -> x36, waiting for transfers between devices: none -> 87.9 us  [send(): lax.ppermute(value, ('plane', 'core', 'shard'), [((p * 2 + c) * 4 + z, (q...]
    pallas_call x2 -> x30, Pallas kernels: 20.3 us -> 105 us  [the longest x27 79.3 us: call(): pl.pallas_call(kernel, in_specs=[pl.BlockSpec(memory_space=pltpu.SMEM)] +...]
    ppermute x0 -> x36, starting transfers between devices: none -> 71.9 us  [send(): lax.ppermute(value, ('plane', 'core', 'shard'), [((p * 2 + c) * 4 + z, (q...]
    dot_general x27 -> x0, matrix products: 51.3 us -> none  [the longest x11 31 us: mdot(): return jnp.dot(left, right, preferred_element_type=full)]
    psum x1 -> x0, blocking collectives: 40.3 us -> none  [body(): lax.psum((grad_gain, grad_table), ('plane', 'core', 'shard'))]
    convert_element_type x10 -> x0, other arithmetic: 24.7 us -> none  [the longest x3 18.1 us: adam_step(): return (new_master, new_first, new_second, new_master.astype(low))]
  transfers between devices with their start and end apart: 22 -> 47, of which waited for: 15 -> 20; matrix products, arithmetic and copies ran while one was open for 20% -> 6% of each run, Pallas kernels for 4% -> 26%
where the time goes in v2:
time: 313 us; the launch traced here: 311 us
  Pallas kernels  105 us (34%)
  waiting for transfers between devices  91.5 us (29%)
  starting transfers between devices  74.1 us (24%)
  local copies, waits for them, and re-layouts  24 us (8%)
  other arithmetic  13 us (4%)
  between operations  4.28 us (1%)
    ppermute x36, waiting for transfers between devices, send(): lax.ppermute(value, ('plane', 'core', 'shard'), [((p * 2 + c) * 4 + z, (q...  87.9 us
    pallas_call x27, Pallas kernels, call(): pl.pallas_call(kernel, in_specs=[pl.BlockSpec(memory_space=pltpu.SMEM)] +...  79.3 us
    ppermute x36, starting transfers between devices, send(): lax.ppermute(value, ('plane', 'core', 'shard'), [((p * 2 + c) * 4 + z, (q...  71.9 us
    pallas_call x3, Pallas kernels, adam_call(): pl.pallas_call(functools.partial(adam_kernel, join), grid_spec=pltpu.Pref...  25.3 us
    unnamed x136, local copies, waits for them, and re-layouts  20.4 us
  transfers between devices with their start and end apart: 47, of which 20 were waited for; matrix products, arithmetic and copies ran while one was open for 6% of the time, Pallas kernels for 26%

profile of v2, /device:TPU:0, one launch (start us, length us, event | category | flops | bytes accessed | tf_op | source)
XLA Modules:
  0.0 311.4 jit_solution(14340050835497479452)
XLA Ops:
  2.6 2.3 pack_attn.1.r0
  5.0 6.9 %collective-permute-start.6 = (bf16[208,384]{1,0:T(8,128)(2,1)}, bf16[208,384]{1,0:T(8,128)(2,1)S(1)}, u32[]{:S(2)}, u32[]{:S(2)}) collective-permute-start(bf16[208,384]{1,0:T(8,128)(2,1)} %pack_attn.1.r0), channel_id=1, source_target_pairs={{0,3},{1,2},{2,1},{3,0},{4,7},{5,6},{6,5},{7,4},{8,11},{9,10},{10,... | collective-permute-start | bytes 479240 | tf_op jit(solution)/shard_map/ppermute | solution.py:213
  12.6 2.6 pack_ffn.1
  15.1 2.7 collective-permute-done.6.refs_2_.r3
  17.9 8.8 %collective-permute-done.5.refs_1_.r2 = bf16[208,384]{1,0:T(8,128)(2,1)S(1)} collective-permute-done((bf16[208,384]{1,0:T(8,128)(2,1)}, bf16[208,384]{1,0:T(8,128)(2,1)S(1)}, u32[]{:S(2)}, u32[]{:S(2)}) %collective-permute-start.5) | collective-permute-done | bytes 159776 | tf_op jit(solution)/shard_map/ppermute | solution.py:213
  33.9 1.8 collective-permute-done.7.refs_1_
  39.7 1.9 collective-permute-start.2
  42.7 2.1 collective-permute-start.9
  46.1 3.5 %collective-permute-done.2.b3 = bf16[256,768]{1,0:T(8,128)(2,1)S(1)} collective-permute-done((bf16[256,768]{1,0:T(8,128)(2,1)}, bf16[256,768]{1,0:T(8,128)(2,1)S(1)}, u32[]{:S(2)}, u32[]{:S(2)}) %collective-permute-start.2) | collective-permute-done | bytes 393248 | tf_op jit(solution)/shard_map/ppermute | solution.py:213
  49.6 2.3 pick.2
  54.1 2.9 collective-permute-start.14
  58.3 5.2 %project.1 = (bf16[4,768,384]{2,1,0:T(8,128)(2,1)}, bf16[512,768]{1,0:T(8,128)(2,1)}, bf16[512,384]{1,0:T(8,128)(2,1)}, bf16[512,384]{1,0:T(8,128)(2,1)}, bf16[512,384]{1,0:T(8,128)(2,1)}) custom-call(s32[3]{0:T(128)} %pad_add_fusion.3.scalars, bf16[512,768]{1,0:T(8,128)(2,1)} %broadcast_select_fusion.1.x_ref, f32[2,768]{1,0:T(2,128)} %copy-done.49, ...), custom_call_target="tpu_custom_call" | custom-call | tf_op jit(solution)/shard_map/project/pallas_call | solution.py:257
  66.5 11.0 %attend.1 = (bf16[512,384]{1,0:T(8,128)(2,1)S(1)}, bf16[6,512,512]{2,1,0:T(8,128)(2,1)S(1)}) custom-call(s32[3]{0:T(128)S(1)} %copy-done.38, bf16[512,384]{1,0:T(8,128)(2,1)S(1)} %copy-done.21, bf16[512,384]{1,0:T(8,128)(2,1)S(1)} %copy-done.23, bf16[512,384]{1,0:T(8,128)(2,1)S(1)} %copy-done.25, s32[512,1]{1,0:T(8,128)S(1)} %copy.67.qseg_ref, ...), custom_call_target="tpu_custom_call" | custom-call | tf_op jit(solution)/shard_map/attend/pallas_call | solution.py:257
  77.5 4.7 %collective-permute-done.13.refs_1_ = bf16[576,256]{1,0:T(8,128)(2,1)S(1)} collective-permute-done((bf16[576,256]{1,0:T(8,128)(2,1)}, bf16[576,256]{1,0:T(8,128)(2,1)S(1)}, u32[]{:S(2)}, u32[]{:S(2)}) %collective-permute-start.13) | collective-permute-done | bytes 294944 | tf_op jit(solution)/shard_map/ppermute | solution.py:213
  85.0 10.9 %collective-permute-done.16.refs_1_ = bf16[3,576,256]{2,1,0:T(8,128)(2,1)S(1)} collective-permute-done((bf16[3,576,256]{2,1,0:T(8,128)(2,1)S(1)}, bf16[3,576,256]{2,1,0:T(8,128)(2,1)S(1)}, u32[]{:S(2)}, u32[]{:S(2)}) %collective-permute-start.16) | collective-permute-done | bytes 884768 | tf_op jit(solution)/shard_map/ppermute | solution.py:213
  99.5 6.8 %collective-permute-done.17.b2 = bf16[256,768]{1,0:T(8,128)(2,1)S(1)} collective-permute-done((bf16[256,768]{1,0:T(8,128)(2,1)S(1)}, bf16[256,768]{1,0:T(8,128)(2,1)S(1)}, u32[]{:S(2)}, u32[]{:S(2)}) %collective-permute-start.17) | collective-permute-done | bytes 393248 | tf_op jit(solution)/shard_map/ppermute | solution.py:213
  106.4 2.4 collective-permute-start.18
  108.9 7.4 %collective-permute-done.18.b3 = bf16[256,768]{1,0:T(8,128)(2,1)S(1)} collective-permute-done((bf16[256,768]{1,0:T(8,128)(2,1)S(1)}, bf16[256,768]{1,0:T(8,128)(2,1)S(1)}, u32[]{:S(2)}, u32[]{:S(2)}) %collective-permute-start.18) | collective-permute-done | bytes 393248 | tf_op jit(solution)/shard_map/ppermute | solution.py:213
  116.3 1.8 pick.3
  121.9 11.2 %feed.1 = (f32[512,768]{1,0:T(8,128)S(1)}, bf16[512,768]{1,0:T(8,128)(2,1)S(1)}, bf16[512,1024]{1,0:T(8,128)(2,1)S(1)}, f32[512,768]{1,0:T(8,128)S(1)}, f32[512,...) custom-call(s32[3]{0:T(128)S(1)} %copy-done.38, bf16[512,768]{1,0:T(8,128)(2,1)S(1)} %copy-done.3, ...), custom_call_target="tpu_custom_call" | custom-call | tf_op jit(solution)/shard_map/feed/pallas_call | solution.py:257
  133.4 6.1 %outer.1 = (bf16[4608,256]{1,0:T(8,128)(2,1)}, bf16[4608,256]{1,0:T(8,128)(2,1)S(1)}) custom-call(s32[3]{0:T(128)S(1)} %copy-done.38, bf16[512,768]{1,0:T(8,128)(2,1)S(1)} %get-tuple-element.134.act_ref, bf16[4,512,512]{2,1,0:T(8,128)(2,1)S(1)} %get-tuple-element.135.grad_ref, bf16[512,1024]{1,0:T(8,128)(2,1)S(1)} %get-tuple-element.136.hid_ref, ...), custom_call_target="tpu_custom_call" | custom-call | tf_op jit(solution)/shard_map/outer/pallas_call | solution.py:257
  148.1 3.1 spread_y.1
  152.0 1.9 copy-done.14
  158.7 9.4 %back.1 = (f32[512,768]{1,0:T(8,128)S(1)}, bf16[4,512,384]{2,1,0:T(8,128)(2,1)S(1)}, f32[3,2,1024]{2,1,0:T(2,128)S(1)}, f32[1,768]{1,0:T(1,128)S(1)}) custom-call(s32[3]{0:T(128)S(1)} %copy-done.38, f32[512,768]{1,0:T(8,128)S(1)} %copy-done.28, f32[512,768]{1,0:T(8,128)S(1)} %copy-done.30, f32[512,768]{1,0:T(8,128)S(1)} %copy-done.11, ...), custom_call_target="tpu_custom_call" | custom-call | tf_op jit(solution)/shard_map/back/pallas_call | solution.py:257
  168.7 2.1 pass_ffn.1
  172.4 1.8 collective-permute-start.26
  175.5 2.7 collective-permute-start.23
  178.3 6.4 %last.1 = (bf16[1552,384]{1,0:T(8,128)(2,1)S(1)}, bf16[1536,384]{1,0:T(8,128)(2,1)S(1)}, f32[512,768]{1,0:T(8,128)}) custom-call(s32[3]{0:T(128)S(1)} %copy-done.38, bf16[512,768]{1,0:T(8,128)(2,1)S(1)} %copy-done.35, bf16[512,384]{1,0:T(8,128)(2,1)S(1)} %get-tuple-element.124.mix_own, bf16[512,384]{1,0:T(8,128)(2,1)S(1)} %copy-done.20, ...), custom_call_target="tpu_custom_call" | custom-call | tf_op jit(solution)/shard_map/last/pallas_call | solution.py:257
  184.8 3.2 %collective-permute-done.23 = bf16[256,768]{1,0:T(8,128)(2,1)S(1)} collective-permute-done((bf16[256,768]{1,0:T(8,128)(2,1)S(1)}, bf16[256,768]{1,0:T(8,128)(2,1)S(1)}, u32[]{:S(2)}, u32[]{:S(2)}) %collective-permute-start.23) | collective-permute-done | bytes 393248 | tf_op jit(solution)/shard_map/ppermute | solution.py:213
  189.3 2.1 sum_ffn.1
  191.4 4.9 %collective-permute-start.30 = (bf16[576,256]{1,0:T(8,128)(2,1)S(1)}, bf16[576,256]{1,0:T(8,128)(2,1)S(1)}, u32[]{:S(2)}, u32[]{:S(2)}) collective-permute-start(bf16[576,256]{1,0:T(8,128)(2,1)S(1)} %get-tuple-element.163), channel_id=1, source_target_pairs={{0,1},{1,0},{2,3},{3,2},{4,5},{5,4},{6,7},{7,6},{8,9},{9,8},{10,11... | collective-permute-start | bytes 884744 | tf_op jit(solution)/shard_map/ppermute | solution.py:213
  196.2 3.4 %collective-permute-start.31 = (bf16[576,256]{1,0:T(8,128)(2,1)S(1)}, bf16[576,256]{1,0:T(8,128)(2,1)S(1)}, u32[]{:S(2)}, u32[]{:S(2)}) collective-permute-start(bf16[576,256]{1,0:T(8,128)(2,1)S(1)} %get-tuple-element.164), channel_id=1, source_target_pairs={{0,2},{1,3},{2,0},{3,1},{4,6},{5,7},{6,4},{7,5},{8,10},{9,11},{10,... | collective-permute-start | bytes 884744 | tf_op jit(solution)/shard_map/ppermute | solution.py:213
  199.6 7.6 %collective-permute-done.30.r1 = bf16[576,256]{1,0:T(8,128)(2,1)S(1)} collective-permute-done((bf16[576,256]{1,0:T(8,128)(2,1)S(1)}, bf16[576,256]{1,0:T(8,128)(2,1)S(1)}, u32[]{:S(2)}, u32[]{:S(2)}) %collective-permute-start.30) | collective-permute-done | bytes 294944 | tf_op jit(solution)/shard_map/ppermute | solution.py:213
  207.3 5.6 %collective-permute-done.31.r2 = bf16[576,256]{1,0:T(8,128)(2,1)S(1)} collective-permute-done((bf16[576,256]{1,0:T(8,128)(2,1)S(1)}, bf16[576,256]{1,0:T(8,128)(2,1)S(1)}, u32[]{:S(2)}, u32[]{:S(2)}) %collective-permute-start.31) | collective-permute-done | bytes 294944 | tf_op jit(solution)/shard_map/ppermute | solution.py:213
  215.9 8.4 %collective-permute-done.34.r3 = bf16[576,256]{1,0:T(8,128)(2,1)S(1)} collective-permute-done((bf16[576,256]{1,0:T(8,128)(2,1)S(1)}, bf16[576,256]{1,0:T(8,128)(2,1)S(1)}, u32[]{:S(2)}, u32[]{:S(2)}) %collective-permute-start.34) | collective-permute-done | bytes 294944 | tf_op jit(solution)/shard_map/ppermute | solution.py:213
  227.0 4.2 %collective-permute-start.33 = (bf16[208,384]{1,0:T(8,128)(2,1)S(1)}, bf16[208,384]{1,0:T(8,128)(2,1)S(1)}, u32[]{:S(2)}, u32[]{:S(2)}) collective-permute-start(bf16[208,384]{1,0:T(8,128)(2,1)S(1)} %get-tuple-element.167), channel_id=1, source_target_pairs={{0,1},{1,0},{2,3},{3,2},{4,5},{5,4},{6,7},{7,6},{8,9},{9,8},{10,11... | collective-permute-start | bytes 479240 | tf_op jit(solution)/shard_map/ppermute | solution.py:213
  231.1 3.4 %collective-permute-done.33.r1 = bf16[208,384]{1,0:T(8,128)(2,1)S(1)} collective-permute-done((bf16[208,384]{1,0:T(8,128)(2,1)S(1)}, bf16[208,384]{1,0:T(8,128)(2,1)S(1)}, u32[]{:S(2)}, u32[]{:S(2)}) %collective-permute-start.33) | collective-permute-done | bytes 159776 | tf_op jit(solution)/shard_map/ppermute | solution.py:213
  236.0 3.2 %collective-permute-start.37 = (bf16[208,384]{1,0:T(8,128)(2,1)S(1)}, bf16[208,384]{1,0:T(8,128)(2,1)S(1)}, u32[]{:S(2)}, u32[]{:S(2)}) collective-permute-start(bf16[208,384]{1,0:T(8,128)(2,1)S(1)} %get-tuple-element.174), channel_id=1, source_target_pairs={{0,2},{1,3},{2,0},{3,1},{4,6},{5,7},{6,4},{7,5},{8,10},{9,11},{10,... | collective-permute-start | bytes 479240 | tf_op jit(solution)/shard_map/ppermute | solution.py:213
  240.4 10.6 %collective-permute-done.37.r2 = bf16[208,384]{1,0:T(8,128)(2,1)S(1)} collective-permute-done((bf16[208,384]{1,0:T(8,128)(2,1)S(1)}, bf16[208,384]{1,0:T(8,128)(2,1)S(1)}, u32[]{:S(2)}, u32[]{:S(2)}) %collective-permute-start.37) | collective-permute-done | bytes 159776 | tf_op jit(solution)/shard_map/ppermute | solution.py:213
  259.1 2.1 add_bitcast_fusion.1
  261.2 4.2 %spread_x.1 = (bf16[256,768]{1,0:T(8,128)(2,1)S(1)}, bf16[256,768]{1,0:T(8,128)(2,1)}, bf16[256,768]{1,0:T(8,128)(2,1)}, bf16[256,768]{1,0:T(8,128)(2,1)}) custom-call(s32[3]{0:T(128)S(1)} %copy-done.38, f32[512,768]{1,0:T(8,128)} %get-tuple-element.153.own_ref, f32[512,768]{1,0:T(8,128)} %collective-permute-done.27.other_ref, ...), custom_call_target="tpu_custom_call" | custom-call | tf_op jit(solution)/shard_map/spread_x/pallas_call | solution.py:257
  265.4 4.4 %collective-permute-start.44 = (bf16[256,768]{1,0:T(8,128)(2,1)}, bf16[256,768]{1,0:T(8,128)(2,1)S(1)}, u32[]{:S(2)}, u32[]{:S(2)}) collective-permute-start(bf16[256,768]{1,0:T(8,128)(2,1)} %get-tuple-element.194), channel_id=1, source_target_pairs={{0,3},{1,2},{6,5},{7,4},{8,11},{9,10},{14,13},{15,12},{16,19},{17,... | collective-permute-start | bytes 1179656 | tf_op jit(solution)/shard_map/ppermute | solution.py:213
  269.8 4.2 %collective-permute-start.43 = (bf16[256,768]{1,0:T(8,128)(2,1)}, bf16[256,768]{1,0:T(8,128)(2,1)}, u32[]{:S(2)}, u32[]{:S(2)}) collective-permute-start(bf16[256,768]{1,0:T(8,128)(2,1)} %get-tuple-element.191), channel_id=1, source_target_pairs={{0,2},{1,3},{6,4},{7,5},{8,10},{9,11},{14,12},{15,13},{16,18},{17,... | collective-permute-start | bytes 1179656 | tf_op jit(solution)/shard_map/ppermute | solution.py:213
  274.0 2.5 collective-permute-start.39
  276.5 9.7 %adam_ffin.1 = (f32[2,192,2048]{2,1,0:T(8,128)}, f32[2,192,2048]{2,1,0:T(8,128)}, bf16[2,192,2048]{2,1,0:T(8,128)(2,1)}, f32[2,192,2048]{2,1,0:T(8,128)}) custom-call(s32[3]{0:T(128)} %pad_add_fusion.3.scalars, f32[2,192,2048]{2,1,0:T(8,128)} %master.2, f32[2,192,2048]{2,1,0:T(8,128)} %first.2, f32[2,192,2048]{2,1,0:T(8,128)} %second.2, ...), custom_call_target="tpu_custom_call" | custom-call | tf_op jit(solution)/shard_map/adam_ffin/pallas_call | solution.py:689
  289.0 6.8 %adam_ffout.1 = (f32[2,4,64,768]{3,2,1,0:T(8,128)}, f32[2,4,64,768]{3,2,1,0:T(8,128)}, bf16[2,4,64,768]{3,2,1,0:T(8,128)(2,1)}, f32[2,4,64,768]{3,2,1,0:T(8,128)}) custom-call(s32[3]{0:T(128)} %pad_add_fusion.3.scalars, f32[2,4,64,768]{3,2,1,0:T(8,128)} %bitcast.45, f32[2,4,64,768]{3,2,1,0:T(8,128)} %bitcast.55, f32[2,4,64,768]{3,2,1,0:T(8,128)} %bitcast.56, ...), custom_call_target="tpu_custom_call" | custom-call | tf_op jit(solution)/shard_map/adam_ffout/pallas_call | solution.py:689
  300.0 1.8 add_bitcast_fusion
  302.7 8.8 %adam_attn.1 = (f32[4,192,768]{2,1,0:T(8,128)}, f32[4,192,768]{2,1,0:T(8,128)}, bf16[4,192,768]{2,1,0:T(8,128)(2,1)}, f32[3,192,768]{2,1,0:T(8,128)}, f32[192,768]{1,0:T(8,128)}) custom-call(s32[3]{0:T(128)} %pad_add_fusion.3.scalars, f32[4,192,768]{2,1,0:T(8,128)} %master.3, f32[4,192,768]{2,1,0:T(8,128)} %first.3, f32[4,192,768]{2,1,0:T(8,128)} %second.3, ...), custom_call_target="tpu_custom_call" | custom-call | tf_op jit(solution)/shard_map/adam_attn/pallas_call | solution.py:689
  (258 shorter events, 73.4 us)
Async XLA Ops:
  0.7 28.4 %collective-permute-start = (bf16[256,768]{1,0:T(8,128)(2,1)}, bf16[256,768]{1,0:T(8,128)(2,1)}, u32[]{:S(2)}, u32[]{:S(2)}) collective-permute-start(bf16[256,768]{1,0:T(8,128)(2,1)} %bitcast.46), channel_id=1, source_target_pairs={{4,5},{5,6},{6,7},{12,13},{13,14},{14,15},{20,21},{21,22},{22,23},... | collective-permute-start | bytes 1179656 | tf_op jit(solution)/shard_map/ppermute | solution.py:213
  5.0 12.9 %collective-permute-start.6 = (bf16[208,384]{1,0:T(8,128)(2,1)}, bf16[208,384]{1,0:T(8,128)(2,1)S(1)}, u32[]{:S(2)}, u32[]{:S(2)}) collective-permute-start(bf16[208,384]{1,0:T(8,128)(2,1)} %pack_attn.1.r0), channel_id=1, source_target_pairs={{0,3},{1,2},{2,1},{3,0},{4,7},{5,6},{6,5},{7,4},{8,11},{9,10},{10,... | collective-permute-start | bytes 479240 | tf_op jit(solution)/shard_map/ppermute | solution.py:213
  11.9 14.8 %collective-permute-start.5 = (bf16[208,384]{1,0:T(8,128)(2,1)}, bf16[208,384]{1,0:T(8,128)(2,1)S(1)}, u32[]{:S(2)}, u32[]{:S(2)}) collective-permute-start(bf16[208,384]{1,0:T(8,128)(2,1)} %pack_attn.1.r0), channel_id=1, source_target_pairs={{0,2},{1,3},{2,0},{3,1},{4,6},{5,7},{6,4},{7,5},{8,10},{9,11},{10,... | collective-permute-start | bytes 479240 | tf_op jit(solution)/shard_map/ppermute | solution.py:213
  11.9 14.8 %collective-permute-start.4 = (bf16[208,384]{1,0:T(8,128)(2,1)}, bf16[208,384]{1,0:T(8,128)(2,1)S(1)}, u32[]{:S(2)}, u32[]{:S(2)}) collective-permute-start(bf16[208,384]{1,0:T(8,128)(2,1)} %pack_attn.1.r0), channel_id=1, source_target_pairs={{0,1},{1,0},{2,3},{3,2},{4,5},{5,4},{6,7},{7,6},{8,9},{9,8},{10,11... | collective-permute-start | bytes 479240 | tf_op jit(solution)/shard_map/ppermute | solution.py:213
  27.3 8.4 %collective-permute-start.7 = (bf16[3,192,384]{2,1,0:T(8,128)(2,1)S(1)}, bf16[3,192,384]{2,1,0:T(8,128)(2,1)S(1)}, u32[]{:S(2)}, u32[]{:S(2)}) collective-permute-start(bf16[3,192,384]{2,1,0:T(8,128)(2,1)S(1)} %near.2.refs_0_), channel_id=1, source_target_pairs={{0,8},{1,9},{2,10},{3,11},{4,20},{5,21},{6,22},{7,23},{8,0},{9,1},... | collective-permute-start | bytes 1327112 | tf_op jit(solution)/shard_map/ppermute | solution.py:213
  28.9 9.0 %collective-permute-start.3 = (s32[1028]{0:T(1024)S(1)}, s32[1028]{0:T(1024)S(1)}, u32[]{:S(2)}, u32[]{:S(2)}) collective-permute-start(s32[1028]{0:T(1024)S(1)} %pad_add_fusion), channel_id=1, source_target_pairs={{0,4},{4,0},{1,5},{5,1},{2,6},{6,2},{3,7},{7,3},{8,12},{12,8},{9,1... | collective-permute-start | bytes 12344 | tf_op jit(solution)/shard_map/ppermute | solution.py:46
  29.0 9.9 %collective-permute-start.1 = (bf16[256,768]{1,0:T(8,128)(2,1)}, bf16[256,768]{1,0:T(8,128)(2,1)S(1)}, u32[]{:S(2)}, u32[]{:S(2)}) collective-permute-start(bf16[256,768]{1,0:T(8,128)(2,1)} %collective-permute-done.b1), channel_id=1, source_target_pairs={{5,6},{6,7},{13,14},{14,15},{21,22},{22,23},{29,30},{30,31},{2,1},... | collective-permute-start | bytes 1179656 | tf_op jit(solution)/shard_map/ppermute | solution.py:213
  36.3 17.2 %collective-permute-start.8 = (bf16[6,192,384]{2,1,0:T(8,128)(2,1)S(1)}, bf16[6,192,384]{2,1,0:T(8,128)(2,1)}, u32[]{:S(2)}, u32[]{:S(2)}) collective-permute-start(bf16[6,192,384]{2,1,0:T(8,128)(2,1)S(1)} %nearest.2.near_ref), channel_id=1, source_target_pairs={{0,16},{1,17},{2,18},{3,19},{4,12},{5,13},{6,14},{7,15},{8,24},{9,... | collective-permute-start | bytes 2654216 | tf_op jit(solution)/shard_map/ppermute | solution.py:213
  39.7 9.9 %collective-permute-start.2 = (bf16[256,768]{1,0:T(8,128)(2,1)}, bf16[256,768]{1,0:T(8,128)(2,1)S(1)}, u32[]{:S(2)}, u32[]{:S(2)}) collective-permute-start(bf16[256,768]{1,0:T(8,128)(2,1)} %broadcast_select_fusion.3), channel_id=1, source_target_pairs={{6,7},{7,6},{14,15},{15,14},{22,23},{23,22},{30,31},{31,30},{1,0},... | collective-permute-start | bytes 1179656 | tf_op jit(solution)/shard_map/ppermute | solution.py:213
  42.7 10.1 %collective-permute-start.9 = (bf16[576,256]{1,0:T(8,128)(2,1)}, bf16[576,256]{1,0:T(8,128)(2,1)S(1)}, u32[]{:S(2)}, u32[]{:S(2)}) collective-permute-start(bf16[576,256]{1,0:T(8,128)(2,1)} %pack_ffn.1), channel_id=1, source_target_pairs={{0,1},{1,0},{2,3},{3,2},{4,5},{5,4},{6,7},{7,6},{8,9},{9,8},{10,11... | collective-permute-start | bytes 884744 | tf_op jit(solution)/shard_map/ppermute | solution.py:213
  53.5 3.9 %collective-permute-start.10 = (bf16[512,768]{1,0:T(8,128)(2,1)S(1)}, bf16[512,768]{1,0:T(8,128)(2,1)S(1)}, u32[]{:S(2)}, u32[]{:S(2)}) collective-permute-start(bf16[512,768]{1,0:T(8,128)(2,1)S(1)} %pick.2), channel_id=1, source_target_pairs={{0,4},{4,0},{1,5},{5,1},{2,6},{6,2},{3,7},{7,3},{8,12},{12,8},{9,1... | collective-permute-start | bytes 2359304 | tf_op jit(solution)/shard_map/ppermute | solution.py:46
  54.1 23.4 %collective-permute-start.14 = (bf16[576,256]{1,0:T(8,128)(2,1)}, bf16[576,256]{1,0:T(8,128)(2,1)S(1)}, u32[]{:S(2)}, u32[]{:S(2)}) collective-permute-start(bf16[576,256]{1,0:T(8,128)(2,1)} %pack_ffn.1), channel_id=1, source_target_pairs={{0,3},{1,2},{2,1},{3,0},{4,7},{5,6},{6,5},{7,4},{8,11},{9,10},{10,... | collective-permute-start | bytes 884744 | tf_op jit(solution)/shard_map/ppermute | solution.py:213
  57.1 25.2 %collective-permute-start.13 = (bf16[576,256]{1,0:T(8,128)(2,1)}, bf16[576,256]{1,0:T(8,128)(2,1)S(1)}, u32[]{:S(2)}, u32[]{:S(2)}) collective-permute-start(bf16[576,256]{1,0:T(8,128)(2,1)} %pack_ffn.1), channel_id=1, source_target_pairs={{0,2},{1,3},{2,0},{3,1},{4,6},{5,7},{6,4},{7,5},{8,10},{9,11},{10,... | collective-permute-start | bytes 884744 | tf_op jit(solution)/shard_map/ppermute | solution.py:213
  82.8 13.1 %collective-permute-start.16 = (bf16[3,576,256]{2,1,0:T(8,128)(2,1)S(1)}, bf16[3,576,256]{2,1,0:T(8,128)(2,1)S(1)}, u32[]{:S(2)}, u32[]{:S(2)}) collective-permute-start(bf16[3,576,256]{2,1,0:T(8,128)(2,1)S(1)} %near.3.refs_0_), channel_id=1, source_target_pairs={{0,8},{1,9},{2,10},{3,11},{4,20},{5,21},{6,22},{7,23},{8,0},{9,1},... | collective-permute-start | bytes 2654216 | tf_op jit(solution)/shard_map/ppermute | solution.py:213
  83.8 12.9 %collective-permute-start.15 = (bf16[256,768]{1,0:T(8,128)(2,1)S(1)}, bf16[256,768]{1,0:T(8,128)(2,1)S(1)}, u32[]{:S(2)}, u32[]{:S(2)}) collective-permute-start(bf16[256,768]{1,0:T(8,128)(2,1)S(1)} %bitcast.48), channel_id=1, source_target_pairs={{4,5},{5,6},{6,7},{12,13},{13,14},{14,15},{20,21},{21,22},{22,23},... | collective-permute-start | bytes 1179656 | tf_op jit(solution)/shard_map/ppermute | solution.py:213
  96.6 9.7 %collective-permute-start.17 = (bf16[256,768]{1,0:T(8,128)(2,1)S(1)}, bf16[256,768]{1,0:T(8,128)(2,1)S(1)}, u32[]{:S(2)}, u32[]{:S(2)}) collective-permute-start(bf16[256,768]{1,0:T(8,128)(2,1)S(1)} %collective-permute-done.15.b1), channel_id=1, source_target_pairs={{5,6},{6,7},{13,14},{14,15},{21,22},{22,23},{29,30},{30,31},{2,1},... | collective-permute-start | bytes 1179656 | tf_op jit(solution)/shard_map/ppermute | solution.py:213
  97.9 24.0 %collective-permute-start.20 = (bf16[6,576,256]{2,1,0:T(8,128)(2,1)S(1)}, bf16[6,576,256]{2,1,0:T(8,128)(2,1)S(1)}, u32[]{:S(2)}, u32[]{:S(2)}) collective-permute-start(bf16[6,576,256]{2,1,0:T(8,128)(2,1)S(1)} %nearest.3.near_ref), channel_id=1, source_target_pairs={{0,16},{1,17},{2,18},{3,19},{4,12},{5,13},{6,14},{7,15},{8,24},{9,... | collective-permute-start | bytes 5308424 | tf_op jit(solution)/shard_map/ppermute | solution.py:213
  106.4 9.9 %collective-permute-start.18 = (bf16[256,768]{1,0:T(8,128)(2,1)S(1)}, bf16[256,768]{1,0:T(8,128)(2,1)S(1)}, u32[]{:S(2)}, u32[]{:S(2)}) collective-permute-start(bf16[256,768]{1,0:T(8,128)(2,1)S(1)} %broadcast_select_fusion.2), channel_id=1, source_target_pairs={{6,7},{7,6},{14,15},{15,14},{22,23},{23,22},{30,31},{31,30},{1,0},... | collective-permute-start | bytes 1179656 | tf_op jit(solution)/shard_map/ppermute | solution.py:213
  118.1 2.4 collective-permute-start.19
  118.3 3.6 %collective-permute-start.12 = (bf16[768,384]{1,0:T(8,128)(2,1)S(1)}, bf16[768,384]{1,0:T(8,128)(2,1)S(1)}, u32[]{:S(2)}, u32[]{:S(2)}) collective-permute-start(bf16[768,384]{1,0:T(8,128)(2,1)S(1)} %slice_bitcast_fusion), channel_id=1, source_target_pairs={{0,4},{4,0},{1,5},{5,1},{2,6},{6,2},{3,7},{7,3},{8,12},{12,8},{9,1... | collective-permute-start | bytes 1769480 | tf_op jit(solution)/shard_map/ppermute | solution.py:46
  118.8 3.0 collective-permute-start.11
  133.2 7.2 %collective-permute-start.21 = (f32[512,768]{1,0:T(8,128)S(1)}, f32[512,768]{1,0:T(8,128)S(1)}, u32[]{:S(2)}, u32[]{:S(2)}) collective-permute-start(f32[512,768]{1,0:T(8,128)S(1)} %get-tuple-element.146.own_part), channel_id=1, source_target_pairs={{0,4},{4,0},{1,5},{5,1},{2,6},{6,2},{3,7},{7,3},{8,12},{12,8},{9,1... | collective-permute-start | bytes 4718600 | tf_op jit(solution)/shard_map/ppermute | solution.py:46
  139.5 29.2 %collective-permute-start.24 = (bf16[4608,256]{1,0:T(8,128)(2,1)}, bf16[4608,256]{1,0:T(8,128)(2,1)}, u32[]{:S(2)}, u32[]{:S(2)}) collective-permute-start(bf16[4608,256]{1,0:T(8,128)(2,1)} %get-tuple-element.137), channel_id=1, source_target_pairs={{0,8},{1,9},{2,10},{3,11},{4,20},{5,21},{6,22},{7,23},{8,0},{9,1},... | collective-permute-start | bytes 7077896 | tf_op jit(solution)/shard_map/ppermute | solution.py:213
  141.5 4.1 %collective-permute-start.22 = (f32[512,768]{1,0:T(8,128)}, f32[512,768]{1,0:T(8,128)}, u32[]{:S(2)}, u32[]{:S(2)}) collective-permute-start(f32[512,768]{1,0:T(8,128)} %get-tuple-element.139.own_ref), channel_id=1, source_target_pairs={{0,4},{4,0},{1,5},{5,1},{2,6},{6,2},{3,7},{7,3},{8,12},{12,8},{9,1... | collective-permute-start | bytes 4718600 | tf_op jit(solution)/shard_map/ppermute | solution.py:46
  170.8 17.2 %collective-permute-start.28 = (bf16[2304,256]{1,0:T(8,128)(2,1)S(1)}, bf16[2304,256]{1,0:T(8,128)(2,1)S(1)}, u32[]{:S(2)}, u32[]{:S(2)}) collective-permute-start(bf16[2304,256]{1,0:T(8,128)(2,1)S(1)} %pass_ffn.1), channel_id=1, source_target_pairs={{0,16},{1,17},{2,18},{3,19},{4,12},{5,13},{6,14},{7,15},{8,24},{9,... | collective-permute-start | bytes 3538952 | tf_op jit(solution)/shard_map/ppermute | solution.py:213
  172.4 12.3 %collective-permute-start.26 = (bf16[256,768]{1,0:T(8,128)(2,1)S(1)}, bf16[256,768]{1,0:T(8,128)(2,1)S(1)}, u32[]{:S(2)}, u32[]{:S(2)}) collective-permute-start(bf16[256,768]{1,0:T(8,128)(2,1)S(1)} %get-tuple-element.145), channel_id=1, source_target_pairs={{0,3},{1,2},{6,5},{7,4},{8,11},{9,10},{14,13},{15,12},{16,19},{17,... | collective-permute-start | bytes 1179656 | tf_op jit(solution)/shard_map/ppermute | solution.py:213
  174.2 10.5 %collective-permute-start.25 = (bf16[256,768]{1,0:T(8,128)(2,1)S(1)}, bf16[256,768]{1,0:T(8,128)(2,1)S(1)}, u32[]{:S(2)}, u32[]{:S(2)}) collective-permute-start(bf16[256,768]{1,0:T(8,128)(2,1)S(1)} %get-tuple-element.144), channel_id=1, source_target_pairs={{0,2},{1,3},{6,4},{7,5},{8,10},{9,11},{14,12},{15,13},{16,18},{17,... | collective-permute-start | bytes 1179656 | tf_op jit(solution)/shard_map/ppermute | solution.py:213
  175.5 12.4 %collective-permute-start.23 = (bf16[256,768]{1,0:T(8,128)(2,1)S(1)}, bf16[256,768]{1,0:T(8,128)(2,1)S(1)}, u32[]{:S(2)}, u32[]{:S(2)}) collective-permute-start(bf16[256,768]{1,0:T(8,128)(2,1)S(1)} %get-tuple-element.141), channel_id=1, source_target_pairs={{0,1},{1,0},{6,7},{7,6},{8,9},{9,8},{14,15},{15,14},{16,17},{17,16... | collective-permute-start | bytes 1179656 | tf_op jit(solution)/shard_map/ppermute | solution.py:213
  184.7 28.9 %copy-start.52 = (bf16[256,768]{1,0:T(8,128)(2,1)}, bf16[256,768]{1,0:T(8,128)(2,1)S(1)}, u32[]{:S(2)}) copy-start(bf16[256,768]{1,0:T(8,128)(2,1)S(1)} %collective-permute-done.26) | copy-start | bytes 1179652
  187.9 24.9 %collective-permute-start.29 = (bf16[1552,384]{1,0:T(8,128)(2,1)S(1)}, bf16[1552,384]{1,0:T(8,128)(2,1)S(1)}, u32[]{:S(2)}, u32[]{:S(2)}) collective-permute-start(bf16[1552,384]{1,0:T(8,128)(2,1)S(1)} %get-tuple-element.162.sent), channel_id=1, source_target_pairs={{0,8},{1,9},{2,10},{3,11},{4,20},{5,21},{6,22},{7,23},{8,0},{9,1},... | collective-permute-start | bytes 3575816 | tf_op jit(solution)/shard_map/ppermute | solution.py:213
  191.4 15.9 %collective-permute-start.30 = (bf16[576,256]{1,0:T(8,128)(2,1)S(1)}, bf16[576,256]{1,0:T(8,128)(2,1)S(1)}, u32[]{:S(2)}, u32[]{:S(2)}) collective-permute-start(bf16[576,256]{1,0:T(8,128)(2,1)S(1)} %get-tuple-element.163), channel_id=1, source_target_pairs={{0,1},{1,0},{2,3},{3,2},{4,5},{5,4},{6,7},{7,6},{8,9},{9,8},{10,11... | collective-permute-start | bytes 884744 | tf_op jit(solution)/shard_map/ppermute | solution.py:213
  196.2 16.7 %collective-permute-start.31 = (bf16[576,256]{1,0:T(8,128)(2,1)S(1)}, bf16[576,256]{1,0:T(8,128)(2,1)S(1)}, u32[]{:S(2)}, u32[]{:S(2)}) collective-permute-start(bf16[576,256]{1,0:T(8,128)(2,1)S(1)} %get-tuple-element.164), channel_id=1, source_target_pairs={{0,2},{1,3},{2,0},{3,1},{4,6},{5,7},{6,4},{7,5},{8,10},{9,11},{10,... | collective-permute-start | bytes 884744 | tf_op jit(solution)/shard_map/ppermute | solution.py:213
  213.6 10.6 %collective-permute-start.32 = (bf16[784,384]{1,0:T(8,128)(2,1)S(1)}, bf16[784,384]{1,0:T(8,128)(2,1)S(1)}, u32[]{:S(2)}, u32[]{:S(2)}) collective-permute-start(bf16[784,384]{1,0:T(8,128)(2,1)S(1)} %pass_attn.1.passed), channel_id=1, source_target_pairs={{0,16},{1,17},{2,18},{3,19},{4,12},{5,13},{6,14},{7,15},{8,24},{9,... | collective-permute-start | bytes 1806344 | tf_op jit(solution)/shard_map/ppermute | solution.py:213
  214.5 9.7 %collective-permute-start.34 = (bf16[576,256]{1,0:T(8,128)(2,1)S(1)}, bf16[576,256]{1,0:T(8,128)(2,1)S(1)}, u32[]{:S(2)}, u32[]{:S(2)}) collective-permute-start(bf16[576,256]{1,0:T(8,128)(2,1)S(1)} %get-tuple-element.171), channel_id=1, source_target_pairs={{0,3},{1,2},{2,1},{3,0},{4,7},{5,6},{6,5},{7,4},{8,11},{9,10},{10,... | collective-permute-start | bytes 884744 | tf_op jit(solution)/shard_map/ppermute | solution.py:213
  224.9 9.6 %collective-permute-start.35 = (bf16[576,256]{1,0:T(8,128)(2,1)S(1)}, bf16[576,256]{1,0:T(8,128)(2,1)S(1)}, u32[]{:S(2)}, u32[]{:S(2)}) collective-permute-start(bf16[576,256]{1,0:T(8,128)(2,1)S(1)} %total_ffn.1.refs_0_), channel_id=1, source_target_pairs={{0,8},{1,9},{2,10},{3,11},{4,20},{5,21},{6,22},{7,23},{8,0},{9,1},... | collective-permute-start | bytes 884744 | tf_op jit(solution)/shard_map/ppermute | solution.py:213
  227.0 7.6 %collective-permute-start.33 = (bf16[208,384]{1,0:T(8,128)(2,1)S(1)}, bf16[208,384]{1,0:T(8,128)(2,1)S(1)}, u32[]{:S(2)}, u32[]{:S(2)}) collective-permute-start(bf16[208,384]{1,0:T(8,128)(2,1)S(1)} %get-tuple-element.167), channel_id=1, source_target_pairs={{0,1},{1,0},{2,3},{3,2},{4,5},{5,4},{6,7},{7,6},{8,9},{9,8},{10,11... | collective-permute-start | bytes 479240 | tf_op jit(solution)/shard_map/ppermute | solution.py:213
  235.1 16.6 %collective-permute-start.36 = (bf16[2,576,256]{2,1,0:T(8,128)(2,1)S(1)}, bf16[2,576,256]{2,1,0:T(8,128)(2,1)S(1)}, u32[]{:S(2)}, u32[]{:S(2)}) collective-permute-start(bf16[2,576,256]{2,1,0:T(8,128)(2,1)S(1)} %pair_ffn.1.refs_0_), channel_id=1, source_target_pairs={{0,16},{1,17},{2,18},{3,19},{4,12},{5,13},{6,14},{7,15},{8,24},{9,... | collective-permute-start | bytes 1769480 | tf_op jit(solution)/shard_map/ppermute | solution.py:213
  236.0 25.2 %collective-permute-start.27 = (f32[512,768]{1,0:T(8,128)}, f32[512,768]{1,0:T(8,128)}, u32[]{:S(2)}, u32[]{:S(2)}) collective-permute-start(f32[512,768]{1,0:T(8,128)} %get-tuple-element.153.own_ref), channel_id=1, source_target_pairs={{0,4},{4,0},{1,5},{5,1},{2,6},{6,2},{3,7},{7,3},{8,12},{12,8},{9,1... | collective-permute-start | bytes 4718600 | tf_op jit(solution)/shard_map/ppermute | solution.py:46
  236.0 15.0 %collective-permute-start.37 = (bf16[208,384]{1,0:T(8,128)(2,1)S(1)}, bf16[208,384]{1,0:T(8,128)(2,1)S(1)}, u32[]{:S(2)}, u32[]{:S(2)}) collective-permute-start(bf16[208,384]{1,0:T(8,128)(2,1)S(1)} %get-tuple-element.174), channel_id=1, source_target_pairs={{0,2},{1,3},{2,0},{3,1},{4,6},{5,7},{6,4},{7,5},{8,10},{9,11},{10,... | collective-permute-start | bytes 479240 | tf_op jit(solution)/shard_map/ppermute | solution.py:213
  239.2 11.8 %collective-permute-start.38 = (bf16[208,384]{1,0:T(8,128)(2,1)S(1)}, bf16[208,384]{1,0:T(8,128)(2,1)S(1)}, u32[]{:S(2)}, u32[]{:S(2)}) collective-permute-start(bf16[208,384]{1,0:T(8,128)(2,1)S(1)} %get-tuple-element.175), channel_id=1, source_target_pairs={{0,3},{1,2},{2,1},{3,0},{4,7},{5,6},{6,5},{7,4},{8,11},{9,10},{10,... | collective-permute-start | bytes 479240 | tf_op jit(solution)/shard_map/ppermute | solution.py:213
  252.3 21.6 %collective-permute-start.41 = (bf16[4,576,256]{2,1,0:T(8,128)(2,1)S(1)}, bf16[4,576,256]{2,1,0:T(8,128)(2,1)}, u32[]{:S(2)}, u32[]{:S(2)}) collective-permute-start(bf16[4,576,256]{2,1,0:T(8,128)(2,1)S(1)} %stack_ffn.1.own), channel_id=1, source_target_pairs={{0,4},{4,0},{1,5},{5,1},{2,6},{6,2},{3,7},{7,3},{8,12},{12,8},{9,1... | collective-permute-start | bytes 3538952 | tf_op jit(solution)/shard_map/ppermute | solution.py:46
  257.3 30.9 %collective-permute-start.46 = (f32[16,384]{1,0:T(8,128)}, f32[16,384]{1,0:T(8,128)S(1)}, u32[]{:S(2)}, u32[]{:S(2)}) collective-permute-start(f32[16,384]{1,0:T(8,128)} %get-tuple-element.180), channel_id=1, source_target_pairs={{0,4},{4,0},{1,5},{5,1},{2,6},{6,2},{3,7},{7,3},{8,12},{12,8},{9,1... | collective-permute-start | bytes 73736 | tf_op jit(solution)/shard_map/ppermute | solution.py:46
  257.7 28.5 %collective-permute-start.40 = (bf16[192,384]{1,0:T(8,128)(2,1)}, bf16[192,384]{1,0:T(8,128)(2,1)S(1)}, u32[]{:S(2)}, u32[]{:S(2)}) collective-permute-start(bf16[192,384]{1,0:T(8,128)(2,1)} %get-tuple-element.184.refs_0_), channel_id=1, source_target_pairs={{0,8},{1,9},{2,10},{3,11},{4,20},{5,21},{6,22},{7,23},{8,0},{9,1},... | collective-permute-start | bytes 442376 | tf_op jit(solution)/shard_map/ppermute | solution.py:213
  265.4 34.6 %collective-permute-start.44 = (bf16[256,768]{1,0:T(8,128)(2,1)}, bf16[256,768]{1,0:T(8,128)(2,1)S(1)}, u32[]{:S(2)}, u32[]{:S(2)}) collective-permute-start(bf16[256,768]{1,0:T(8,128)(2,1)} %get-tuple-element.194), channel_id=1, source_target_pairs={{0,3},{1,2},{6,5},{7,4},{8,11},{9,10},{14,13},{15,12},{16,19},{17,... | collective-permute-start | bytes 1179656 | tf_op jit(solution)/shard_map/ppermute | solution.py:213
  269.8 30.2 %collective-permute-start.43 = (bf16[256,768]{1,0:T(8,128)(2,1)}, bf16[256,768]{1,0:T(8,128)(2,1)}, u32[]{:S(2)}, u32[]{:S(2)}) collective-permute-start(bf16[256,768]{1,0:T(8,128)(2,1)} %get-tuple-element.191), channel_id=1, source_target_pairs={{0,2},{1,3},{6,4},{7,5},{8,10},{9,11},{14,12},{15,13},{16,18},{17,... | collective-permute-start | bytes 1179656 | tf_op jit(solution)/shard_map/ppermute | solution.py:213
  274.0 26.0 %collective-permute-start.39 = (bf16[256,768]{1,0:T(8,128)(2,1)}, bf16[256,768]{1,0:T(8,128)(2,1)S(1)}, u32[]{:S(2)}, u32[]{:S(2)}) collective-permute-start(bf16[256,768]{1,0:T(8,128)(2,1)} %get-tuple-element.183), channel_id=1, source_target_pairs={{0,1},{1,0},{6,7},{7,6},{8,9},{9,8},{14,15},{15,14},{16,17},{17,16... | collective-permute-start | bytes 1179656 | tf_op jit(solution)/shard_map/ppermute | solution.py:213
  287.2 8.7 %collective-permute-start.42 = (bf16[2,192,384]{2,1,0:T(8,128)(2,1)S(1)}, bf16[2,192,384]{2,1,0:T(8,128)(2,1)S(1)}, u32[]{:S(2)}, u32[]{:S(2)}) collective-permute-start(bf16[2,192,384]{2,1,0:T(8,128)(2,1)S(1)} %pair_attn.1.refs_0_), channel_id=1, source_target_pairs={{0,16},{1,17},{2,18},{3,19},{4,12},{5,13},{6,14},{7,15},{8,24},{9,... | collective-permute-start | bytes 884744 | tf_op jit(solution)/shard_map/ppermute | solution.py:213
  296.4 5.4 %collective-permute-start.45 = (bf16[4,192,384]{2,1,0:T(8,128)(2,1)S(1)}, bf16[4,192,384]{2,1,0:T(8,128)(2,1)S(1)}, u32[]{:S(2)}, u32[]{:S(2)}) collective-permute-start(bf16[4,192,384]{2,1,0:T(8,128)(2,1)S(1)} %stack_attn.1.own), channel_id=1, source_target_pairs={{0,4},{4,0},{1,5},{5,1},{2,6},{6,2},{3,7},{7,3},{8,12},{12,8},{9,1... | collective-permute-start | bytes 1769480 | tf_op jit(solution)/shard_map/ppermute | solution.py:46
  (64 other events, 693.3 us)

commit v3 on v2

--- a/solution.py
+++ b/solution.py
@@ -249,7 +249,7 @@
 fixed = pl.BlockSpec(memory_space=pltpu.HBM)
 
 
-def call(kernel, spot, inputs, outputs, scratch, name, flops=0, grant=16):
+def call(kernel, spot, inputs, outputs, scratch, name, flops=0, grant=16, loose=()):
     arrays = [item[0] if isinstance(item, (tuple, list)) else item for item in inputs]
     specs = [
         anywhere if isinstance(item, tuple) else fixed if isinstance(item, list) else vmem for item in inputs
@@ -257,7 +257,7 @@
     return pl.pallas_call(
         kernel,
         in_specs=[pl.BlockSpec(memory_space=pltpu.SMEM)] + specs,
-        out_specs=[vmem for _ in outputs],
+        out_specs=[anywhere if i in loose else vmem for i in range(len(outputs))],
         scratch_shapes=scratch,
         out_shape=[jax.ShapeDtypeStruct(shape, kind) for shape, kind in outputs],
         name=name,
@@ -284,16 +284,23 @@
     return copies
 
 
-def attend_all_kernel(scalars, q_ref, k_ref, v_ref, qseg_ref, kseg_ref, vec_ref, o_ref, p_ref, s_ref):
+def attend_all_kernel(scalars, q_ref, k_ref, v_ref, qseg_ref, kseg_ref, vec_ref, o_ref, p_out, s_ref, p_ref, sems):
+    def leave(pair):
+        here = pl.ds(2 * pair, 2)
+        return pltpu.make_async_copy(p_ref.at[here], p_out.at[here], sems.at[pair])
+
     def one(pair, _):
         lanes = tile_at(128 * pair, 128)
         attend_kernel(
             512, q_ref.at[:, lanes], k_ref.at[:, lanes], v_ref.at[:, lanes], qseg_ref, kseg_ref,
             vec_ref.at[pl.ds(pair, 1)], o_ref.at[:, lanes], p_ref.at[pl.ds(2 * pair, 2)], s_ref,
         )
+        leave(pair).start()
         return 0
 
     lax.fori_loop(0, 3, one, 0)
+    for pair in range(3):
+        leave(pair).wait()
 
 
 def hot_buckets():
@@ -551,26 +558,42 @@
     lax.fori_loop(0, 2, rows_of, 0)
 
 
-def spread(wanted_ref, token_ref, value, outs):
-    for i, out in enumerate(outs):
-        same = wanted_ref[256 * i : 256 * i + 256, :] == token_ref[...]
+def spread(wanted_ref, token_ref, value, near_ref, own_ref, far_ref):
+    for step, out in enumerate((own_ref, near_ref.at[0:256], far_ref, near_ref.at[256:512])):
+        same = wanted_ref[256 * step : 256 * step + 256, :] == token_ref[...]
         out[...] = mdot(jnp.where(same, 1.0, 0.0).astype(low), value).astype(low)
 
 
-def spread_y_kernel(scalars, mid_ref, own_ref, other_ref, wanted_ref, token_ref, o0, o1, o2, o3, value_ref):
-    value_ref[...] = (mid_ref[...] + own_ref[...] + other_ref[...]).astype(low)
-    spread(wanted_ref, token_ref, value_ref[...], (o0, o1, o2, o3))
+def spread_y_kernel(
+    scalars, mid_ref, own_part, other_part, wanted_ref, token_ref, near_ref, own_ref, far_ref, value_ref, *rest
+):
+    parts = (mid_ref, own_part, other_part)
+    copies = [fetch_part(ref, held, rest[-1].at[i]) for i, (ref, held) in enumerate(zip(parts, rest[:-1]))]
+    for copy in copies:
+        copy.wait()
+    value_ref[...] = (rest[0][...] + rest[1][...] + rest[2][...]).astype(low)
+    spread(wanted_ref, token_ref, value_ref[...], near_ref, own_ref, far_ref)
 
 
 def spread_x_kernel(
-    scalars, own_ref, other_ref, x_ref, gain_ref, mid_ref, wanted_ref, token_ref, o0, o1, o2, o3, value_ref
+    scalars, own_part, other_part, x_ref, gain_ref, mid_ref, wanted_ref, token_ref, near_ref, own_ref, far_ref,
+    value_ref, *rest
 ):
+    parts = (own_part, other_part, mid_ref, x_ref)
+    copies = [fetch_part(ref, held, rest[-1].at[i]) for i, (ref, held) in enumerate(zip(parts, rest[:-1]))]
+    for copy in copies:
+        copy.wait()
+    own_part, other_part, mid_ref, x_ref = rest[:-1]
     x_in = x_ref[...].astype(full)
     scale = lax.rsqrt(jnp.mean(x_in * x_in, axis=-1, keepdims=True) + norm_eps)
-    turned = (own_ref[...] + other_ref[...]) * gain_ref[0:1, :]
+    turned = (own_part[...] + other_part[...]) * gain_ref[0:1, :]
     lean = jnp.mean(turned * x_in, axis=-1, keepdims=True)
     value_ref[...] = (mid_ref[...] + scale * turned - x_in * (scale * scale * scale * lean)).astype(low)
-    spread(wanted_ref, token_ref, value_ref[...], (o0, o1, o2, o3))
+    spread(wanted_ref, token_ref, value_ref[...], near_ref, own_ref, far_ref)
+
+
+def add_kernel(scalars, value_ref, more_ref, out_ref):
+    out_ref[...] = value_ref[...] + more_ref[256:512, :]
 
 
 def back_kernel(
@@ -579,9 +602,11 @@
 ):
     core = scalars[1]
     here, there = tile_at(384 * core, 384), tile_at(384 * (1 - core), 384)
-    late = (q_ref, k_ref, v_ref, p_ref)
+    late = (own_part, other_part, mid_ref, gy_ref, wo_other, w_ref.at[3], q_ref, k_ref, v_ref, p_ref)
     copies = [fetch_part(ref, held, rest[-1].at[i]) for i, (ref, held) in enumerate(zip(late, rest[:-1]))]
-    q_ref, k_ref, v_ref, p_ref = rest[:-1]
+    own_part, other_part, mid_ref, gy_ref, wo_other, wo_own, q_ref, k_ref, v_ref, p_ref = rest[:-1]
+    for copy in copies[:4]:
+        copy.wait()
     x_mid = mid_ref[...]
     scale = lax.rsqrt(jnp.mean(x_mid * x_mid, axis=-1, keepdims=True) + norm_eps)
     gain_out[...] = jnp.sum(own_part[...] * x_mid * scale, axis=0, keepdims=True)
@@ -590,11 +615,11 @@
     grad_mid = gy_ref[...].astype(full) + scale * turned - x_mid * (scale * scale * scale * lean)
     grad_ref[...] = grad_mid
     attn_ref[...] = grad_mid.astype(low)
+    for copy in copies[4:]:
+        copy.wait()
     mixed_ref[...] = (
-        ndot(attn_ref[:, here], w_ref[3, here, :]) + ndot(attn_ref[:, there], wo_other[here, :])
+        ndot(attn_ref[:, here], wo_own[here, :]) + ndot(attn_ref[:, there], wo_other[here, :])
     ).astype(low)
-    for copy in copies:
-        copy.wait()
 
     def one(pair, _):
         lanes = tile_at(128 * pair, 128)
@@ -744,14 +769,14 @@
     )[0]
     attn_came = [after(value, unit) for value in attn_came]
 
-    def fetch(own, gates=(None, None)):
-        up = lambda pairs: [((p, 1, z), (p, 1, w)) for p in range(4) for z, w in pairs]
-        down = lambda pairs: [((p, 0, 3 - z), (p, 0, 3 - w)) for p in range(4) for z, w in pairs]
-        pairs = lambda *which: up(which) + down(which)
-        held = lambda value, gate: value if gate is None else after(value, gate())
-        one = held(send(own, pairs((0, 1), (1, 2), (2, 3))), gates[0])
-        two = held(send(one, pairs((1, 2), (2, 3))), gates[1])
-        three = send(jnp.where(at_end, own, two), pairs((2, 3), (3, 2)))
+    up_pairs = lambda pairs: [((p, 1, z), (p, 1, w)) for p in range(4) for z, w in pairs]
+    down_pairs = lambda pairs: [((p, 0, 3 - z), (p, 0, 3 - w)) for p in range(4) for z, w in pairs]
+    along = lambda value, *which: send(value, up_pairs(which) + down_pairs(which))
+
+    def fetch_rest(own, one, gate=None):
+        two = along(one, (1, 2), (2, 3))
+        two = two if gate is None else after(two, gate)
+        three = along(jnp.where(at_end, own, two), (2, 3), (3, 2))
         return own, one, two, three
 
     way = 1 - 2 * core
@@ -760,7 +785,7 @@
         [shard, shard + way, shard + 2 * way, jnp.where(at_end, shard + 3 * way, shard - way)]
     )
     blocks = jnp.clip(blocks, 0, 3)
-    tok_blocks = fetch(tokens[0])
+    tok_blocks = fetch_rest(tokens[0], along(tokens[0], (0, 1), (1, 2), (2, 3)))
 
     table_own = jnp.concatenate([lengths[0], deal[0]])
     table = jnp.where(mine, table_own, swap(table_own))
@@ -775,24 +800,30 @@
     token_column = token_here[:, None]
     token_row = jnp.where(mine, token_here, -1)[None, :]
 
+    def wanted_by(place_of):
+        rows = [lax.dynamic_slice_in_dim(place_of, 256 * xor(shard, step), 256) for step in range(4)]
+        return jnp.concatenate(rows).reshape(1024, 1)
+
+    wanted_y = wanted_by(order)
+    wanted_x = wanted_by(token_index)
+
     def rows_here(place_of, pieces, gate=None):
         place = [lax.dynamic_slice_in_dim(place_of, blocks[i] * 256, 256) for i in range(4)]
         place = jnp.concatenate(place).reshape(1, 1024)
         chosen = call(
-            pick_kernel, spot, [*pieces, place, token_column], [((512, 768), low)], [], "pick", 0, 8
+            pick_kernel, spot, [*pieces, after(place, wanted_y, wanted_x, token_row), token_column], [((512, 768), low)], [], "pick", 0, 8
         )[0]
         chosen = chosen if gate is None else after(chosen, *gate)
         return jnp.where(mine, chosen, swap(chosen))
 
-    def wanted_by(place_of):
-        return by_shard(place_of.reshape(4, 256), shard).reshape(1024, 1)
-
-    def rows_back(rows, gate):
+    def rows_back(rows, first_gate, second_gate):
         pairs = lambda step: [((p, c, z), (p, c, z ^ step)) for p, c, z in ALL if z // 2 == c]
-        return [after(send(rows[step], pairs(step)), gate) for step in (1, 2, 3)]
-
-    wanted_y = wanted_by(order)
-    wanted_x = wanted_by(token_index)
+        near, own, far = rows
+        came = after(send(near, pairs(1)), first_gate)
+        far = call(add_kernel, spot, [far, came], [((256, 768), low)], [], "add_rows", 0, 4)[0]
+        last = after(send(far, pairs(2)), second_gate)
+        return own + came[:256] + last, last
+
 
     gains, vectors = call(
         unpack_kernel, spot, [quarter, *attn_came], [((2, 768), full), ((3, 2, 1024), full)],
@@ -807,10 +838,11 @@
         near = cat(spot, [near, arrived], rows, "nearest")
         return near, plane_second(near if late is None else after(near, late))
 
-    near, far = spread_plane(attn_came, 192)
-    unit = after(unit, near, tok_blocks[2], gains)
+    unit = after(unit, *attn_came)
     ffn_came = [across(unit, step) for step in (1, 2, 3)]
-    x_low = rows_here(token_index, tok_blocks, (far, ffn_came[0]))
+    attn_came = [after(value, ffn_came[0]) for value in attn_came]
+    near, far = spread_plane(attn_came, 192, ffn_came[1])
+    x_low = rows_here(token_index, tok_blocks, (far, *ffn_came))
     w_attn, act_one, query, key, value = call(
         project_kernel, spot,
         [x_low, gains, [attn_master], (near,), (far,)],
@@ -820,13 +852,18 @@
     wo_other = swap(w_attn[3])
 
 
+    ffn_near, ffn_far = spread_plane(ffn_came, 576, query)
+    cot_own = after(cotangent[0], *ffn_came)
+    cot_one = after(along(cot_own, (0, 1), (1, 2), (2, 3)), query)
+    cot_two = along(cot_one, (1, 2), (2, 3))
     mix_own, probs = call(
-        attend_all_kernel, spot, [query, key, value, seg_here[:, None], seg_here[None, :], vectors],
-        [((512, 384), low), ((6, 512, 512), low)], [pltpu.VMEM((512, 512), full)], "attend", 0, 8,
-    )
-    ffn_came = [after(piece, mix_own) for piece in ffn_came]
-    ffn_near, ffn_far = spread_plane(ffn_came, 576)
-    cot_blocks = fetch(after(cotangent[0], *ffn_came), (lambda: ffn_near, None))
+        attend_all_kernel, spot, [after(query, ffn_near, cot_two), key, value, seg_here[:, None], seg_here[None, :], vectors],
+        [((512, 384), low), ((6, 512, 512), low)],
+        [pltpu.VMEM((512, 512), full), pltpu.VMEM((6, 512, 512), low), pltpu.SemaphoreType.DMA((3,))],
+        "attend", 0, 60, (1,),
+    )
+    cot_three = after(along(jnp.where(at_end, cot_own, cot_two), (2, 3), (3, 2)), mix_own)
+    cot_blocks = (cot_own, cot_one, cot_two, cot_three)
     grad_y = rows_here(order, cot_blocks)
     mix_other = swap(mix_own)
     x_mid, act_two, hidden, part_two, y_part, grads_up = call(
@@ -855,13 +892,15 @@
 
     y_other = swap(after(y_part, part_other))
     y_rows = call(
-        spread_y_kernel, spot, [x_mid, y_part, y_other, wanted_y, token_row], [((256, 768), low)] * 4,
-        [pltpu.VMEM((512, 768), low)], "spread_y", 0, 10,
+        spread_y_kernel, spot, [(x_mid,), (y_part,), (y_other,), wanted_y, token_row],
+        [((512, 768), low), ((256, 768), low), ((256, 768), low)],
+        [pltpu.VMEM((512, 768), low), *[pltpu.VMEM((512, 768), full)] * 3, pltpu.SemaphoreType.DMA((3,))],
+        "spread_y", 0, 60,
     )
     grad_mid, right, lined, gain_two = call(
         back_kernel, spot,
         [
-            after(part_two, *y_rows), part_other, x_mid, grad_y, gains, w_attn, wo_other,
+            (after(part_two, *y_rows),), (part_other,), (x_mid,), (grad_y,), gains, (w_attn,), (wo_other,),
             (query,), (key,), (value,), (probs,),
         ],
         [
@@ -869,10 +908,11 @@
         ],
         [
             pltpu.VMEM((512, 768), low), pltpu.VMEM((512, 384), low), pltpu.VMEM((512, 512), full), pltpu.VMEM((512, 512), low),
-            pltpu.VMEM((128, 1024), full), *[pltpu.VMEM((512, 384), low)] * 3, pltpu.VMEM((6, 512, 512), low),
-            pltpu.SemaphoreType.DMA((4,)),
-        ],
-        "back", 0, 24,
+            pltpu.VMEM((128, 1024), full), *[pltpu.VMEM((512, 768), full)] * 3, pltpu.VMEM((512, 768), low),
+            *[pltpu.VMEM((768, 384), low)] * 2, *[pltpu.VMEM((512, 384), low)] * 3, pltpu.VMEM((6, 512, 512), low),
+            pltpu.SemaphoreType.DMA((10,)),
+        ],
+        "back", 0, 60,
     )
     ffn_first = after(ffn_first, right)
     one_out = lambda kernel, inputs, shape, name: call(kernel, spot, inputs, [(shape, low)], [], name, 0, 8)[0]
@@ -889,28 +929,32 @@
             pltpu.VMEM((4, 512, 384), low), pltpu.VMEM((4, 768, 384), low), pltpu.VMEM((512, 768), low),
             pltpu.SemaphoreType.DMA((6,)),
         ],
-        "last", 0, 24,
-    )
-    y_came = rows_back(y_rows, part_one)
-    ffn_second = after(ffn_second, part_one, *y_came)
-    layer_out = y_rows[0] + y_came[0] + y_came[1] + y_came[2]
+        "last", 0, 60,
+    )
+    layer_out, y_last = rows_back(y_rows, right, part_one)
+    ffn_second = after(ffn_second, part_one, y_last)
+    x_rows = call(
+        spread_x_kernel, spot,
+        [(part_one,), (swap(part_one),), (x_low,), gains, (grad_mid,), wanted_x, token_row],
+        [((512, 768), low), ((256, 768), low), ((256, 768), low)],
+        [
+            pltpu.VMEM((512, 768), low), *[pltpu.VMEM((512, 768), full)] * 3, pltpu.VMEM((512, 768), low),
+            pltpu.SemaphoreType.DMA((4,)),
+        ],
+        "spread_x", 0, 60,
+    )
     ffn_own, *ffn_outs = call(
         sum_ffn_kernel, spot, [ffn_keep, ffn_first, ffn_second],
         [((576, 256), full)] + [((576, 256), low)] * 3, [], "sum_ffn", 0, 8,
     )
     ffn_came = [across(out, step) for step, out in zip((1, 2, 3), ffn_outs)]
-    attn_first_came = after(plane_first(after(attn_send, ffn_second)), *ffn_came[:2])
+    attn_first_came = after(plane_first(after(attn_send, ffn_second)), *ffn_came[:2], *x_rows)
     passed = one_out(pass_attn_kernel, [attn_keep, attn_send, attn_first_came], (784, 384), "pass_attn")
     attn_second_came = plane_second(passed)
     attn_own, *attn_outs = call(
         sum_attn_kernel, spot, [attn_keep, passed, attn_first_came, attn_second_came],
         [((208, 384), full)] + [((208, 384), low)] * 3, [], "sum_attn", 0, 8,
     )
-    x_rows = call(
-        spread_x_kernel, spot, [part_one, swap(part_one), x_low, gains, grad_mid, wanted_x, token_row],
-        [((256, 768), low)] * 4, [pltpu.VMEM((512, 768), low)], "spread_x", 0, 10,
-    )
-
     ffn_came = [after(value, attn_second_came) for value in ffn_came]
     attn_outs = [across(out, step) for step, out in zip((1, 2, 3), attn_outs)]
     ffn_sum = one_out(total_kernel, [ffn_own, *ffn_came], (576, 256), "total_ffn")
@@ -941,8 +985,7 @@
     attn_stack = cat(spot, [attn_near, after(plane_second(attn_near), ffout_res[0])], 192, "stack_attn")
     attn_sum = (attn_stack, swap(attn_stack))
     x_rows = [after(value, small) for value in x_rows]
-    x_came = rows_back(x_rows, attn_stack)
-    input_grad = x_rows[0] + x_came[0] + x_came[1] + x_came[2]
+    input_grad, _ = rows_back(x_rows, ffin_res[0], ffout_res[0])
     small_other = swap(small)
     gain_sum = (small[:4] + small_other[:4]).reshape(2, 768)
     g_gain = lax.dynamic_slice_in_dim(gain_sum, shard * 192, 192, 1)

time: 313 us -> 285 us (0.911)
  waiting for transfers between devices: 91.5 us -> 66.9 us
  Pallas kernels: 105 us -> 121 us
  starting transfers between devices: 74.1 us -> 65.5 us
  local copies, waits for them, and re-layouts: 24 us -> 16.4 us
  other arithmetic: 13 us -> 9.54 us
    ppermute x36 -> x34, waiting for transfers between devices: 87.9 us -> 61.7 us  [send(): lax.ppermute(value, ('plane', 'core', 'shard'), [((p * 2 + c) * 4 + z, (q...]
    pallas_call x27 -> x29, Pallas kernels: 79.3 us -> 95.6 us  [call(): pl.pallas_call(kernel, in_specs=[pl.BlockSpec(memory_space=pltpu.SMEM)] +...]
    ppermute x36 -> x34, starting transfers between devices: 71.9 us -> 62.1 us  [send(): lax.ppermute(value, ('plane', 'core', 'shard'), [((p * 2 + c) * 4 + z, (q...]
    unnamed x136 -> x120, local copies, waits for them, and re-layouts: 20.4 us -> 11.4 us
  transfers between devices with their start and end apart: 47 -> 45, of which waited for: 20 -> 21; matrix products, arithmetic and copies ran while one was open for 6% -> 6% of each run, Pallas kernels for 26% -> 34%
where the time goes in v3:
time: 285 us; the launch traced here: 284 us
  Pallas kernels  121 us (42%)
  waiting for transfers between devices  66.9 us (23%)
  starting transfers between devices  65.5 us (23%)
  local copies, waits for them, and re-layouts  16.4 us (6%)
  other arithmetic  9.54 us (3%)
  between operations  4.18 us (1%)
    pallas_call x29, Pallas kernels, call(): pl.pallas_call(kernel, in_specs=[pl.BlockSpec(memory_space=pltpu.SMEM)] +...  95.6 us
    ppermute x34, starting transfers between devices, send(): lax.ppermute(value, ('plane', 'core', 'shard'), [((p * 2 + c) * 4 + z, (q...  62.1 us
    ppermute x34, waiting for transfers between devices, send(): lax.ppermute(value, ('plane', 'core', 'shard'), [((p * 2 + c) * 4 + z, (q...  61.7 us
    pallas_call x3, Pallas kernels, adam_call(): pl.pallas_call(functools.partial(adam_kernel, join), grid_spec=pltpu.Pref...  25.4 us
    unnamed x120, local copies, waits for them, and re-layouts  11.4 us
  transfers between devices with their start and end apart: 45, of which 21 were waited for; matrix products, arithmetic and copies ran while one was open for 6% of the time, Pallas kernels for 34%

profile of v3, /device:TPU:0, one launch (start us, length us, event | category | flops | bytes accessed | tf_op | source)
XLA Modules:
  0.0 283.6 jit_solution(12750947979677711404)
XLA Ops:
  1.4 2.3 pack_attn.1.r0
  3.7 5.1 %collective-permute-start.6 = (bf16[208,384]{1,0:T(8,128)(2,1)}, bf16[208,384]{1,0:T(8,128)(2,1)S(1)}, u32[]{:S(2)}, u32[]{:S(2)}) collective-permute-start(bf16[208,384]{1,0:T(8,128)(2,1)} %pack_attn.1.r0), channel_id=1, source_target_pairs={{0,3},{1,2},{2,1},{3,0},{4,7},{5,6},{6,5},{7,4},{8,11},{9,10},{10,... | collective-permute-start | bytes 479240 | tf_op jit(solution)/shard_map/ppermute | solution.py:213
  11.2 2.7 pack_ffn.1
  14.1 8.6 %collective-permute-done.5.refs_1_.r2 = bf16[208,384]{1,0:T(8,128)(2,1)S(1)} collective-permute-done((bf16[208,384]{1,0:T(8,128)(2,1)}, bf16[208,384]{1,0:T(8,128)(2,1)S(1)}, u32[]{:S(2)}, u32[]{:S(2)}) %collective-permute-start.5) | collective-permute-done | bytes 159776 | tf_op jit(solution)/shard_map/ppermute | solution.py:213
  27.7 3.3 %collective-permute-start.9 = (bf16[576,256]{1,0:T(8,128)(2,1)}, bf16[576,256]{1,0:T(8,128)(2,1)}, u32[]{:S(2)}, u32[]{:S(2)}) collective-permute-start(bf16[576,256]{1,0:T(8,128)(2,1)} %pack_ffn.1), channel_id=1, source_target_pairs={{0,2},{1,3},{2,0},{3,1},{4,6},{5,7},{6,4},{7,5},{8,10},{9,11},{10,... | collective-permute-start | bytes 884744 | tf_op jit(solution)/shard_map/ppermute | solution.py:213
  31.0 1.7 collective-permute-done.7.refs_0_
  33.3 1.6 collective-permute-start.8
  36.5 6.1 %collective-permute-done.9.refs_1_ = bf16[576,256]{1,0:T(8,128)(2,1)} collective-permute-done((bf16[576,256]{1,0:T(8,128)(2,1)}, bf16[576,256]{1,0:T(8,128)(2,1)}, u32[]{:S(2)}, u32[]{:S(2)}) %collective-permute-start.9) | collective-permute-done | bytes 294944 | tf_op jit(solution)/shard_map/ppermute | solution.py:213
  43.2 1.6 collective-permute-start.10
  46.6 2.5 collective-permute-start.2
  52.7 4.9 %collective-permute-done.2.b3 = bf16[256,768]{1,0:T(8,128)(2,1)S(1)} collective-permute-done((bf16[256,768]{1,0:T(8,128)(2,1)S(1)}, bf16[256,768]{1,0:T(8,128)(2,1)S(1)}, u32[]{:S(2)}, u32[]{:S(2)}) %collective-permute-start.2) | collective-permute-done | bytes 393248 | tf_op jit(solution)/shard_map/ppermute | solution.py:213
  57.6 1.8 pick.2
  59.5 1.9 collective-permute-done.11.refs_2_
  68.3 5.2 %project.1 = (bf16[4,768,384]{2,1,0:T(8,128)(2,1)}, bf16[512,768]{1,0:T(8,128)(2,1)}, bf16[512,384]{1,0:T(8,128)(2,1)}, bf16[512,384]{1,0:T(8,128)(2,1)}, bf16[512,384]{1,0:T(8,128)(2,1)}) custom-call(s32[3]{0:T(128)} %pad_add_fusion.5.scalars, bf16[512,768]{1,0:T(8,128)(2,1)} %broadcast_select_fusion.1.x_ref, f32[2,768]{1,0:T(2,128)} %copy-done.38, ...), custom_call_target="tpu_custom_call" | custom-call | tf_op jit(solution)/shard_map/project/pallas_call | solution.py:257
  76.7 1.9 nearest.3.near_ref
  80.1 4.5 %collective-permute-done.15.b2 = bf16[256,768]{1,0:T(8,128)(2,1)S(1)} collective-permute-done((bf16[256,768]{1,0:T(8,128)(2,1)S(1)}, bf16[256,768]{1,0:T(8,128)(2,1)S(1)}, u32[]{:S(2)}, u32[]{:S(2)}) %collective-permute-start.15) | collective-permute-done | bytes 393248 | tf_op jit(solution)/shard_map/ppermute | solution.py:213
  84.7 4.1 %collective-permute-start.18 = (bf16[256,768]{1,0:T(8,128)(2,1)S(1)}, bf16[256,768]{1,0:T(8,128)(2,1)S(1)}, u32[]{:S(2)}, u32[]{:S(2)}) collective-permute-start(bf16[256,768]{1,0:T(8,128)(2,1)S(1)} %broadcast_select_fusion.2), channel_id=1, source_target_pairs={{6,7},{7,6},{14,15},{15,14},{22,23},{23,22},{30,31},{31,30},{1,0},... | collective-permute-start | bytes 1179656 | tf_op jit(solution)/shard_map/ppermute | solution.py:213
  90.4 13.3 %attend.1 = (bf16[512,384]{1,0:T(8,128)(2,1)}, bf16[6,512,512]{2,1,0:T(8,128)(2,1)}) custom-call(s32[3]{0:T(128)} %pad_add_fusion.5.scalars, bf16[512,384]{1,0:T(8,128)(2,1)} %get-tuple-element.130.q_ref, bf16[512,384]{1,0:T(8,128)(2,1)} %get-tuple-element.131.k_ref, bf16[512,384]{1,0:T(8,128)(2,1)} %get-tuple-element.132.v_ref, s32[512,1]{1,0:T(8,128)} %copy.67.qseg_ref, ...), custom_call_target="tpu_custom_call" | custom-call | tf_op jit(solution)/shard_map/attend/pallas_call | solution.py:257
  103.7 1.8 pick.3
  112.0 11.1 %feed.1 = (f32[512,768]{1,0:T(8,128)S(1)}, bf16[512,768]{1,0:T(8,128)(2,1)S(1)}, bf16[512,1024]{1,0:T(8,128)(2,1)S(1)}, f32[512,768]{1,0:T(8,128)S(1)}, f32[512,...) custom-call(s32[3]{0:T(128)S(1)} %copy-done.24, bf16[512,768]{1,0:T(8,128)(2,1)S(1)} %copy-done.2, ...), custom_call_target="tpu_custom_call" | custom-call | tf_op jit(solution)/shard_map/feed/pallas_call | solution.py:257
  123.3 6.1 %outer.1 = (bf16[4608,256]{1,0:T(8,128)(2,1)}, bf16[4608,256]{1,0:T(8,128)(2,1)S(1)}) custom-call(s32[3]{0:T(128)S(1)} %copy-done.24, bf16[512,768]{1,0:T(8,128)(2,1)S(1)} %get-tuple-element.141.act_ref, bf16[4,512,512]{2,1,0:T(8,128)(2,1)S(1)} %get-tuple-element.142.grad_ref, bf16[512,1024]{1,0:T(8,128)(2,1)S(1)} %get-tuple-element.143.hid_ref, ...), custom_call_target="tpu_custom_call" | custom-call | tf_op jit(solution)/shard_map/outer/pallas_call | solution.py:257
  133.2 2.4 collective-permute-done.22.other_part
  135.6 5.4 %spread_y.1 = (bf16[512,768]{1,0:T(8,128)(2,1)}, bf16[256,768]{1,0:T(8,128)(2,1)}, bf16[256,768]{1,0:T(8,128)(2,1)}) custom-call(s32[3]{0:T(128)} %pad_add_fusion.5.scalars, f32[512,768]{1,0:T(8,128)} %copy-done.6, f32[512,768]{1,0:T(8,128)} %get-tuple-element.146.own_part, f32[512,768]{1,0:T(8,128)} %collective-permute-done.22.other_part, ...), custom_call_target="tpu_custom_call" | custom-call | tf_op jit(solution)/shard_map/spread_y/pallas_call | solution.py:257
  141.0 2.1 collective-permute-start.23
  143.1 13.4 %back.1 = (f32[512,768]{1,0:T(8,128)}, bf16[4,512,384]{2,1,0:T(8,128)(2,1)}, f32[3,2,1024]{2,1,0:T(2,128)}, f32[1,768]{1,0:T(1,128)}) custom-call(s32[3]{0:T(128)} %pad_add_fusion.5.scalars, f32[512,768]{1,0:T(8,128)} %copy-done.15, f32[512,768]{1,0:T(8,128)} %copy-done.43, f32[512,768]{1,0:T(8,128)} %copy-done.6, bf16[512,768]{1,0:T(8,128)(2,1)} %copy-done.4, ...), custom_call_target="tpu_custom_call" | custom-call | tf_op jit(solution)/shard_map/back/pallas_call | solution.py:257
  156.5 2.0 collective-permute-done.25.first
  158.6 3.0 %pass_ffn.1 = bf16[2304,256]{1,0:T(8,128)(2,1)} custom-call(s32[3]{0:T(128)S(1)} %copy-done.25, bf16[4608,256]{1,0:T(8,128)(2,1)S(1)} %get-tuple-element.155.keep, bf16[4608,256]{1,0:T(8,128)(2,1)} %collective-permute-done.25.first), custom_call_target="tpu_custom_call" | custom-call | tf_op jit(solution)/shard_map/pass_ffn/pallas_call | solution.py:257
  163.7 2.1 collective-permute-start.24
  165.8 9.0 %last.1 = (bf16[1552,384]{1,0:T(8,128)(2,1)}, bf16[1536,384]{1,0:T(8,128)(2,1)}, f32[512,768]{1,0:T(8,128)}) custom-call(s32[3]{0:T(128)} %pad_add_fusion.5.scalars, bf16[512,768]{1,0:T(8,128)(2,1)} %get-tuple-element.157.act_ref, bf16[512,384]{1,0:T(8,128)(2,1)} %get-tuple-element.134.mix_own, bf16[512,384]{1,0:T(8,128)(2,1)} %copy-done.14, ...), custom_call_target="tpu_custom_call" | custom-call | tf_op jit(solution)/shard_map/last/pallas_call | solution.py:257
  175.0 3.1 %collective-permute-done.27.second = bf16[2304,256]{1,0:T(8,128)(2,1)} collective-permute-done((bf16[2304,256]{1,0:T(8,128)(2,1)}, bf16[2304,256]{1,0:T(8,128)(2,1)}, u32[]{:S(2)}, u32[]{:S(2)}) %collective-permute-start.27) | collective-permute-done | bytes 1179680 | tf_op jit(solution)/shard_map/ppermute | solution.py:213
  178.7 3.1 %sum_ffn.1 = (f32[576,256]{1,0:T(8,128)S(1)}, bf16[576,256]{1,0:T(8,128)(2,1)}, bf16[576,256]{1,0:T(8,128)(2,1)}, bf16[576,256]{1,0:T(8,128)(2,1)S(1)}) custom-call(s32[3]{0:T(128)S(1)} %copy-done.26, bf16[4608,256]{1,0:T(8,128)(2,1)S(1)} %get-tuple-element.155.keep, bf16[4608,256]{1,0:T(8,128)(2,1)} %collective-permute-done.25.first, ...), custom_call_target="tpu_custom_call" | custom-call | tf_op jit(solution)/shard_map/sum_ffn/pallas_call | solution.py:257
  183.5 2.1 collective-permute-start.30
  185.7 1.7 copy.69.wanted_ref
  187.4 6.2 %spread_x.1 = (bf16[512,768]{1,0:T(8,128)(2,1)}, bf16[256,768]{1,0:T(8,128)(2,1)}, bf16[256,768]{1,0:T(8,128)(2,1)}) custom-call(s32[3]{0:T(128)} %pad_add_fusion.5.scalars, f32[512,768]{1,0:T(8,128)} %get-tuple-element.160.own_part, f32[512,768]{1,0:T(8,128)} %collective-permute-done.26.other_part, bf16[512,768]{1,0:T(8,128)(2,1)} %broadcast_select_fusion.1.x_ref, ...), custom_call_target="tpu_custom_call" | custom-call | tf_op jit(solution)/shard_map/spread_x/pallas_call | solution.py:257
  193.6 2.9 %collective-permute-done.29.r1 = bf16[576,256]{1,0:T(8,128)(2,1)S(1)} collective-permute-done((bf16[576,256]{1,0:T(8,128)(2,1)}, bf16[576,256]{1,0:T(8,128)(2,1)S(1)}, u32[]{:S(2)}, u32[]{:S(2)}) %collective-permute-start.29) | collective-permute-done | bytes 294944 | tf_op jit(solution)/shard_map/ppermute | solution.py:213
  197.2 1.9 collective-permute-done.30.r2
  203.8 7.2 %collective-permute-done.33.r3 = bf16[576,256]{1,0:T(8,128)(2,1)S(1)} collective-permute-done((bf16[576,256]{1,0:T(8,128)(2,1)S(1)}, bf16[576,256]{1,0:T(8,128)(2,1)S(1)}, u32[]{:S(2)}, u32[]{:S(2)}) %collective-permute-start.33) | collective-permute-done | bytes 294944 | tf_op jit(solution)/shard_map/ppermute | solution.py:213
  214.7 3.4 %collective-permute-start.32 = (bf16[208,384]{1,0:T(8,128)(2,1)S(1)}, bf16[208,384]{1,0:T(8,128)(2,1)S(1)}, u32[]{:S(2)}, u32[]{:S(2)}) collective-permute-start(bf16[208,384]{1,0:T(8,128)(2,1)S(1)} %get-tuple-element.174), channel_id=1, source_target_pairs={{0,1},{1,0},{2,3},{3,2},{4,5},{5,4},{6,7},{7,6},{8,9},{9,8},{10,11... | collective-permute-start | bytes 479240 | tf_op jit(solution)/shard_map/ppermute | solution.py:213
  218.1 3.3 %collective-permute-done.32.r1 = bf16[208,384]{1,0:T(8,128)(2,1)S(1)} collective-permute-done((bf16[208,384]{1,0:T(8,128)(2,1)S(1)}, bf16[208,384]{1,0:T(8,128)(2,1)S(1)}, u32[]{:S(2)}, u32[]{:S(2)}) %collective-permute-start.32) | collective-permute-done | bytes 159776 | tf_op jit(solution)/shard_map/ppermute | solution.py:213
  222.6 3.4 %collective-permute-start.36 = (bf16[208,384]{1,0:T(8,128)(2,1)S(1)}, bf16[208,384]{1,0:T(8,128)(2,1)S(1)}, u32[]{:S(2)}, u32[]{:S(2)}) collective-permute-start(bf16[208,384]{1,0:T(8,128)(2,1)S(1)} %get-tuple-element.181), channel_id=1, source_target_pairs={{0,2},{1,3},{2,0},{3,1},{4,6},{5,7},{6,4},{7,5},{8,10},{9,11},{10,... | collective-permute-start | bytes 479240 | tf_op jit(solution)/shard_map/ppermute | solution.py:213
  226.9 9.3 %collective-permute-done.36.r2 = bf16[208,384]{1,0:T(8,128)(2,1)S(1)} collective-permute-done((bf16[208,384]{1,0:T(8,128)(2,1)S(1)}, bf16[208,384]{1,0:T(8,128)(2,1)S(1)}, u32[]{:S(2)}, u32[]{:S(2)}) %collective-permute-start.36) | collective-permute-done | bytes 159776 | tf_op jit(solution)/shard_map/ppermute | solution.py:213
  237.5 5.1 %collective-permute-start.38 = (bf16[512,768]{1,0:T(8,128)(2,1)}, bf16[512,768]{1,0:T(8,128)(2,1)S(1)}, u32[]{:S(2)}, u32[]{:S(2)}) collective-permute-start(bf16[512,768]{1,0:T(8,128)(2,1)} %get-tuple-element.189), channel_id=1, source_target_pairs={{0,1},{1,0},{6,7},{7,6},{8,9},{9,8},{14,15},{15,14},{16,17},{17,16... | collective-permute-start | bytes 2359304 | tf_op jit(solution)/shard_map/ppermute | solution.py:213
  243.7 1.8 add_bitcast_fusion.1
  245.6 9.9 %adam_ffin.1 = (f32[2,192,2048]{2,1,0:T(8,128)}, f32[2,192,2048]{2,1,0:T(8,128)}, bf16[2,192,2048]{2,1,0:T(8,128)(2,1)}, f32[2,192,2048]{2,1,0:T(8,128)}) custom-call(s32[3]{0:T(128)} %pad_add_fusion.5.scalars, f32[2,192,2048]{2,1,0:T(8,128)} %master.2, f32[2,192,2048]{2,1,0:T(8,128)} %first.2, f32[2,192,2048]{2,1,0:T(8,128)} %second.2, ...), custom_call_target="tpu_custom_call" | custom-call | tf_op jit(solution)/shard_map/adam_ffin/pallas_call | solution.py:714
  256.0 2.6 collective-permute-start.42
  259.3 3.5 %collective-permute-start.40 = (bf16[256,768]{1,0:T(8,128)(2,1)S(1)}, bf16[256,768]{1,0:T(8,128)(2,1)S(1)}, u32[]{:S(2)}, u32[]{:S(2)}) collective-permute-start(bf16[256,768]{1,0:T(8,128)(2,1)S(1)} %add_rows.3), channel_id=1, source_target_pairs={{0,2},{1,3},{6,4},{7,5},{8,10},{9,11},{14,12},{15,13},{16,18},{17,... | collective-permute-start | bytes 1179656 | tf_op jit(solution)/shard_map/ppermute | solution.py:213
  262.9 6.8 %adam_ffout.1 = (f32[2,4,64,768]{3,2,1,0:T(8,128)}, f32[2,4,64,768]{3,2,1,0:T(8,128)}, bf16[2,4,64,768]{3,2,1,0:T(8,128)(2,1)}, f32[2,4,64,768]{3,2,1,0:T(8,128)}) custom-call(s32[3]{0:T(128)} %pad_add_fusion.5.scalars, f32[2,4,64,768]{3,2,1,0:T(8,128)} %bitcast.47, f32[2,4,64,768]{3,2,1,0:T(8,128)} %bitcast.55, f32[2,4,64,768]{3,2,1,0:T(8,128)} %bitcast.56, ...), custom_call_target="tpu_custom_call" | custom-call | tf_op jit(solution)/shard_map/adam_ffout/pallas_call | solution.py:714
  274.8 8.8 %adam_attn.1 = (f32[4,192,768]{2,1,0:T(8,128)}, f32[4,192,768]{2,1,0:T(8,128)}, bf16[4,192,768]{2,1,0:T(8,128)(2,1)}, f32[3,192,768]{2,1,0:T(8,128)}, f32[192,768]{1,0:T(8,128)}) custom-call(s32[3]{0:T(128)} %pad_add_fusion.5.scalars, f32[4,192,768]{2,1,0:T(8,128)} %master.3, f32[4,192,768]{2,1,0:T(8,128)} %first.3, f32[4,192,768]{2,1,0:T(8,128)} %second.3, ...), custom_call_target="tpu_custom_call" | custom-call | tf_op jit(solution)/shard_map/adam_attn/pallas_call | solution.py:714
  (242 shorter events, 61.9 us)
Async XLA Ops:
  3.7 10.4 %collective-permute-start.6 = (bf16[208,384]{1,0:T(8,128)(2,1)}, bf16[208,384]{1,0:T(8,128)(2,1)S(1)}, u32[]{:S(2)}, u32[]{:S(2)}) collective-permute-start(bf16[208,384]{1,0:T(8,128)(2,1)} %pack_attn.1.r0), channel_id=1, source_target_pairs={{0,3},{1,2},{2,1},{3,0},{4,7},{5,6},{6,5},{7,4},{8,11},{9,10},{10,... | collective-permute-start | bytes 479240 | tf_op jit(solution)/shard_map/ppermute | solution.py:213
  8.8 13.8 %collective-permute-start.5 = (bf16[208,384]{1,0:T(8,128)(2,1)}, bf16[208,384]{1,0:T(8,128)(2,1)S(1)}, u32[]{:S(2)}, u32[]{:S(2)}) collective-permute-start(bf16[208,384]{1,0:T(8,128)(2,1)} %pack_attn.1.r0), channel_id=1, source_target_pairs={{0,2},{1,3},{2,0},{3,1},{4,6},{5,7},{6,4},{7,5},{8,10},{9,11},{10,... | collective-permute-start | bytes 479240 | tf_op jit(solution)/shard_map/ppermute | solution.py:213
  8.8 13.8 %collective-permute-start.4 = (bf16[208,384]{1,0:T(8,128)(2,1)}, bf16[208,384]{1,0:T(8,128)(2,1)S(1)}, u32[]{:S(2)}, u32[]{:S(2)}) collective-permute-start(bf16[208,384]{1,0:T(8,128)(2,1)} %pack_attn.1.r0), channel_id=1, source_target_pairs={{0,1},{1,0},{2,3},{3,2},{4,5},{5,4},{6,7},{7,6},{8,9},{9,8},{10,11... | collective-permute-start | bytes 479240 | tf_op jit(solution)/shard_map/ppermute | solution.py:213
  9.5 25.3 %collective-permute-start.3 = (s32[1028]{0:T(1024)S(1)}, s32[1028]{0:T(1024)S(1)}, u32[]{:S(2)}, u32[]{:S(2)}) collective-permute-start(s32[1028]{0:T(1024)S(1)} %pad_add_fusion), channel_id=1, source_target_pairs={{0,4},{4,0},{1,5},{5,1},{2,6},{6,2},{3,7},{7,3},{8,12},{12,8},{9,1... | collective-permute-start | bytes 12344 | tf_op jit(solution)/shard_map/ppermute | solution.py:46
  9.6 25.4 %collective-permute-start = (bf16[256,768]{1,0:T(8,128)(2,1)S(1)}, bf16[256,768]{1,0:T(8,128)(2,1)S(1)}, u32[]{:S(2)}, u32[]{:S(2)}) collective-permute-start(bf16[256,768]{1,0:T(8,128)(2,1)S(1)} %bitcast.48), channel_id=1, source_target_pairs={{4,5},{5,6},{6,7},{12,13},{13,14},{14,15},{20,21},{21,22},{22,23},... | collective-permute-start | bytes 1179656 | tf_op jit(solution)/shard_map/ppermute | solution.py:213
  11.2 21.5 %copy-start.22 = (s32[3]{0:T(128)S(1)}, s32[3]{0:T(128)}, u32[]{:S(2)}) copy-start(s32[3]{0:T(128)} %pad_add_fusion.5.scalars) | copy-start | bytes 40
  22.7 10.0 %collective-permute-start.7 = (bf16[576,256]{1,0:T(8,128)(2,1)}, bf16[576,256]{1,0:T(8,128)(2,1)S(1)}, u32[]{:S(2)}, u32[]{:S(2)}) collective-permute-start(bf16[576,256]{1,0:T(8,128)(2,1)} %pack_ffn.1), channel_id=1, source_target_pairs={{0,1},{1,0},{2,3},{3,2},{4,5},{5,4},{6,7},{7,6},{8,9},{9,8},{10,11... | collective-permute-start | bytes 884744 | tf_op jit(solution)/shard_map/ppermute | solution.py:213
  27.7 14.9 %collective-permute-start.9 = (bf16[576,256]{1,0:T(8,128)(2,1)}, bf16[576,256]{1,0:T(8,128)(2,1)}, u32[]{:S(2)}, u32[]{:S(2)}) collective-permute-start(bf16[576,256]{1,0:T(8,128)(2,1)} %pack_ffn.1), channel_id=1, source_target_pairs={{0,2},{1,3},{2,0},{3,1},{4,6},{5,7},{6,4},{7,5},{8,10},{9,11},{10,... | collective-permute-start | bytes 884744 | tf_op jit(solution)/shard_map/ppermute | solution.py:213
  33.3 9.3 %collective-permute-start.8 = (bf16[3,192,384]{2,1,0:T(8,128)(2,1)S(1)}, bf16[3,192,384]{2,1,0:T(8,128)(2,1)S(1)}, u32[]{:S(2)}, u32[]{:S(2)}) collective-permute-start(bf16[3,192,384]{2,1,0:T(8,128)(2,1)S(1)} %near.2.refs_0_), channel_id=1, source_target_pairs={{0,8},{1,9},{2,10},{3,11},{4,20},{5,21},{6,22},{7,23},{8,0},{9,1},... | collective-permute-start | bytes 1327112 | tf_op jit(solution)/shard_map/ppermute | solution.py:213
  35.0 11.5 %collective-permute-start.1 = (bf16[256,768]{1,0:T(8,128)(2,1)S(1)}, bf16[256,768]{1,0:T(8,128)(2,1)S(1)}, u32[]{:S(2)}, u32[]{:S(2)}) collective-permute-start(bf16[256,768]{1,0:T(8,128)(2,1)S(1)} %collective-permute-done.b1), channel_id=1, source_target_pairs={{5,6},{6,7},{13,14},{14,15},{21,22},{22,23},{29,30},{30,31},{2,1},... | collective-permute-start | bytes 1179656 | tf_op jit(solution)/shard_map/ppermute | solution.py:213
  43.2 18.1 %collective-permute-start.10 = (bf16[6,192,384]{2,1,0:T(8,128)(2,1)S(1)}, bf16[6,192,384]{2,1,0:T(8,128)(2,1)S(1)}, u32[]{:S(2)}, u32[]{:S(2)}) collective-permute-start(bf16[6,192,384]{2,1,0:T(8,128)(2,1)S(1)} %nearest.2.near_ref), channel_id=1, source_target_pairs={{0,16},{1,17},{2,18},{3,19},{4,12},{5,13},{6,14},{7,15},{8,24},{9,... | collective-permute-start | bytes 2654216 | tf_op jit(solution)/shard_map/ppermute | solution.py:213
  46.6 11.0 %collective-permute-start.2 = (bf16[256,768]{1,0:T(8,128)(2,1)S(1)}, bf16[256,768]{1,0:T(8,128)(2,1)S(1)}, u32[]{:S(2)}, u32[]{:S(2)}) collective-permute-start(bf16[256,768]{1,0:T(8,128)(2,1)S(1)} %broadcast_select_fusion.3), channel_id=1, source_target_pairs={{6,7},{7,6},{14,15},{15,14},{22,23},{23,22},{30,31},{31,30},{1,0},... | collective-permute-start | bytes 1179656 | tf_op jit(solution)/shard_map/ppermute | solution.py:213
  49.2 12.1 %collective-permute-start.11 = (bf16[576,256]{1,0:T(8,128)(2,1)}, bf16[576,256]{1,0:T(8,128)(2,1)S(1)}, u32[]{:S(2)}, u32[]{:S(2)}) collective-permute-start(bf16[576,256]{1,0:T(8,128)(2,1)} %pack_ffn.1), channel_id=1, source_target_pairs={{0,3},{1,2},{2,1},{3,0},{4,7},{5,6},{6,5},{7,4},{8,11},{9,10},{10,... | collective-permute-start | bytes 884744 | tf_op jit(solution)/shard_map/ppermute | solution.py:213
  61.3 6.0 %collective-permute-start.12 = (bf16[512,768]{1,0:T(8,128)(2,1)S(1)}, bf16[512,768]{1,0:T(8,128)(2,1)S(1)}, u32[]{:S(2)}, u32[]{:S(2)}) collective-permute-start(bf16[512,768]{1,0:T(8,128)(2,1)S(1)} %pick.2), channel_id=1, source_target_pairs={{0,4},{4,0},{1,5},{5,1},{2,6},{6,2},{3,7},{7,3},{8,12},{12,8},{9,1... | collective-permute-start | bytes 2359304 | tf_op jit(solution)/shard_map/ppermute | solution.py:46
  63.6 13.1 %collective-permute-start.13 = (bf16[3,576,256]{2,1,0:T(8,128)(2,1)S(1)}, bf16[3,576,256]{2,1,0:T(8,128)(2,1)S(1)}, u32[]{:S(2)}, u32[]{:S(2)}) collective-permute-start(bf16[3,576,256]{2,1,0:T(8,128)(2,1)S(1)} %near.3.refs_0_), channel_id=1, source_target_pairs={{0,8},{1,9},{2,10},{3,11},{4,20},{5,21},{6,22},{7,23},{8,0},{9,1},... | collective-permute-start | bytes 2654216 | tf_op jit(solution)/shard_map/ppermute | solution.py:213
  65.1 9.8 %collective-permute-start.14 = (bf16[256,768]{1,0:T(8,128)(2,1)S(1)}, bf16[256,768]{1,0:T(8,128)(2,1)S(1)}, u32[]{:S(2)}, u32[]{:S(2)}) collective-permute-start(bf16[256,768]{1,0:T(8,128)(2,1)S(1)} %bitcast.50), channel_id=1, source_target_pairs={{4,5},{5,6},{6,7},{12,13},{13,14},{14,15},{20,21},{21,22},{22,23},... | collective-permute-start | bytes 1179656 | tf_op jit(solution)/shard_map/ppermute | solution.py:213
  74.9 9.7 %collective-permute-start.15 = (bf16[256,768]{1,0:T(8,128)(2,1)S(1)}, bf16[256,768]{1,0:T(8,128)(2,1)S(1)}, u32[]{:S(2)}, u32[]{:S(2)}) collective-permute-start(bf16[256,768]{1,0:T(8,128)(2,1)S(1)} %collective-permute-done.14.b1), channel_id=1, source_target_pairs={{5,6},{6,7},{13,14},{14,15},{21,22},{22,23},{29,30},{30,31},{2,1},... | collective-permute-start | bytes 1179656 | tf_op jit(solution)/shard_map/ppermute | solution.py:213
  78.6 25.1 %copy-start.24 = (s32[3]{0:T(128)S(1)}, s32[3]{0:T(128)}, u32[]{:S(2)}) copy-start(s32[3]{0:T(128)} %pad_add_fusion.5.scalars) | copy-start | bytes 40
  78.6 30.7 %collective-permute-start.20 = (bf16[6,576,256]{2,1,0:T(8,128)(2,1)}, bf16[6,576,256]{2,1,0:T(8,128)(2,1)}, u32[]{:S(2)}, u32[]{:S(2)}) collective-permute-start(bf16[6,576,256]{2,1,0:T(8,128)(2,1)} %nearest.3.near_ref), channel_id=1, source_target_pairs={{0,16},{1,17},{2,18},{3,19},{4,12},{5,13},{6,14},{7,15},{8,24},{9,... | collective-permute-start | bytes 5308424 | tf_op jit(solution)/shard_map/ppermute | solution.py:213
  80.1 23.6 %copy-start.33 = (bf16[256,768]{1,0:T(8,128)(2,1)S(1)}, bf16[256,768]{1,0:T(8,128)(2,1)}, u32[]{:S(2)}) copy-start(bf16[256,768]{1,0:T(8,128)(2,1)} %copy-done.32) | copy-start | bytes 1179652
  84.7 19.0 %collective-permute-start.18 = (bf16[256,768]{1,0:T(8,128)(2,1)S(1)}, bf16[256,768]{1,0:T(8,128)(2,1)S(1)}, u32[]{:S(2)}, u32[]{:S(2)}) collective-permute-start(bf16[256,768]{1,0:T(8,128)(2,1)S(1)} %broadcast_select_fusion.2), channel_id=1, source_target_pairs={{6,7},{7,6},{14,15},{15,14},{22,23},{23,22},{30,31},{31,30},{1,0},... | collective-permute-start | bytes 1179656 | tf_op jit(solution)/shard_map/ppermute | solution.py:213
  105.5 2.4 collective-permute-start.19
  105.7 3.0 %collective-permute-start.17 = (bf16[768,384]{1,0:T(8,128)(2,1)S(1)}, bf16[768,384]{1,0:T(8,128)(2,1)S(1)}, u32[]{:S(2)}, u32[]{:S(2)}) collective-permute-start(bf16[768,384]{1,0:T(8,128)(2,1)S(1)} %slice_bitcast_fusion), channel_id=1, source_target_pairs={{0,4},{4,0},{1,5},{5,1},{2,6},{6,2},{3,7},{7,3},{8,12},{12,8},{9,1... | collective-permute-start | bytes 1769480 | tf_op jit(solution)/shard_map/ppermute | solution.py:46
  106.2 3.0 %collective-permute-start.16 = (bf16[512,384]{1,0:T(8,128)(2,1)S(1)}, bf16[512,384]{1,0:T(8,128)(2,1)S(1)}, u32[]{:S(2)}, u32[]{:S(2)}) collective-permute-start(bf16[512,384]{1,0:T(8,128)(2,1)S(1)} %copy-done.13), channel_id=1, source_target_pairs={{0,4},{4,0},{1,5},{5,1},{2,6},{6,2},{3,7},{7,3},{8,12},{12,8},{9,1... | collective-permute-start | bytes 1179656 | tf_op jit(solution)/shard_map/ppermute | solution.py:46
  123.1 6.8 %collective-permute-start.21 = (f32[512,768]{1,0:T(8,128)S(1)}, f32[512,768]{1,0:T(8,128)S(1)}, u32[]{:S(2)}, u32[]{:S(2)}) collective-permute-start(f32[512,768]{1,0:T(8,128)S(1)} %get-tuple-element.150.own_part), channel_id=1, source_target_pairs={{0,4},{4,0},{1,5},{5,1},{2,6},{6,2},{3,7},{7,3},{8,12},{12,8},{9,1... | collective-permute-start | bytes 4718600 | tf_op jit(solution)/shard_map/ppermute | solution.py:46
  129.4 29.2 %collective-permute-start.25 = (bf16[4608,256]{1,0:T(8,128)(2,1)}, bf16[4608,256]{1,0:T(8,128)(2,1)}, u32[]{:S(2)}, u32[]{:S(2)}) collective-permute-start(bf16[4608,256]{1,0:T(8,128)(2,1)} %get-tuple-element.144), channel_id=1, source_target_pairs={{0,8},{1,9},{2,10},{3,11},{4,20},{5,21},{6,22},{7,23},{8,0},{9,1},... | collective-permute-start | bytes 7077896 | tf_op jit(solution)/shard_map/ppermute | solution.py:213
  131.1 4.5 %collective-permute-start.22 = (f32[512,768]{1,0:T(8,128)}, f32[512,768]{1,0:T(8,128)}, u32[]{:S(2)}, u32[]{:S(2)}) collective-permute-start(f32[512,768]{1,0:T(8,128)} %get-tuple-element.146.own_part), channel_id=1, source_target_pairs={{0,4},{4,0},{1,5},{5,1},{2,6},{6,2},{3,7},{7,3},{8,12},{12,8},{9,1... | collective-permute-start | bytes 4718600 | tf_op jit(solution)/shard_map/ppermute | solution.py:46
  141.0 22.2 %collective-permute-start.23 = (bf16[512,768]{1,0:T(8,128)(2,1)}, bf16[512,768]{1,0:T(8,128)(2,1)S(1)}, u32[]{:S(2)}, u32[]{:S(2)}) collective-permute-start(bf16[512,768]{1,0:T(8,128)(2,1)} %get-tuple-element.148), channel_id=1, source_target_pairs={{0,1},{1,0},{6,7},{7,6},{8,9},{9,8},{14,15},{15,14},{16,17},{17,16... | collective-permute-start | bytes 2359304 | tf_op jit(solution)/shard_map/ppermute | solution.py:213
  161.6 16.5 %collective-permute-start.27 = (bf16[2304,256]{1,0:T(8,128)(2,1)}, bf16[2304,256]{1,0:T(8,128)(2,1)}, u32[]{:S(2)}, u32[]{:S(2)}) collective-permute-start(bf16[2304,256]{1,0:T(8,128)(2,1)} %pass_ffn.1), channel_id=1, source_target_pairs={{0,16},{1,17},{2,18},{3,19},{4,12},{5,13},{6,14},{7,15},{8,24},{9,... | collective-permute-start | bytes 3538952 | tf_op jit(solution)/shard_map/ppermute | solution.py:213
  163.7 11.2 %collective-permute-start.24 = (bf16[256,768]{1,0:T(8,128)(2,1)S(1)}, bf16[256,768]{1,0:T(8,128)(2,1)}, u32[]{:S(2)}, u32[]{:S(2)}) collective-permute-start(bf16[256,768]{1,0:T(8,128)(2,1)S(1)} %add_rows.2), channel_id=1, source_target_pairs={{0,2},{1,3},{6,4},{7,5},{8,10},{9,11},{14,12},{15,13},{16,18},{17,... | collective-permute-start | bytes 1179656 | tf_op jit(solution)/shard_map/ppermute | solution.py:213
  174.9 12.5 %collective-permute-start.26 = (f32[512,768]{1,0:T(8,128)}, f32[512,768]{1,0:T(8,128)}, u32[]{:S(2)}, u32[]{:S(2)}) collective-permute-start(f32[512,768]{1,0:T(8,128)} %get-tuple-element.160.own_part), channel_id=1, source_target_pairs={{0,4},{4,0},{1,5},{5,1},{2,6},{6,2},{3,7},{7,3},{8,12},{12,8},{9,1... | collective-permute-start | bytes 4718600 | tf_op jit(solution)/shard_map/ppermute | solution.py:46
  178.1 21.7 %collective-permute-start.28 = (bf16[1552,384]{1,0:T(8,128)(2,1)}, bf16[1552,384]{1,0:T(8,128)(2,1)S(1)}, u32[]{:S(2)}, u32[]{:S(2)}) collective-permute-start(bf16[1552,384]{1,0:T(8,128)(2,1)} %get-tuple-element.167.sent), channel_id=1, source_target_pairs={{0,8},{1,9},{2,10},{3,11},{4,20},{5,21},{6,22},{7,23},{8,0},{9,1},... | collective-permute-start | bytes 3575816 | tf_op jit(solution)/shard_map/ppermute | solution.py:213
  183.3 13.2 %collective-permute-start.29 = (bf16[576,256]{1,0:T(8,128)(2,1)}, bf16[576,256]{1,0:T(8,128)(2,1)S(1)}, u32[]{:S(2)}, u32[]{:S(2)}) collective-permute-start(bf16[576,256]{1,0:T(8,128)(2,1)} %get-tuple-element.168), channel_id=1, source_target_pairs={{0,1},{1,0},{2,3},{3,2},{4,5},{5,4},{6,7},{7,6},{8,9},{9,8},{10,11... | collective-permute-start | bytes 884744 | tf_op jit(solution)/shard_map/ppermute | solution.py:213
  183.5 15.5 %collective-permute-start.30 = (bf16[576,256]{1,0:T(8,128)(2,1)}, bf16[576,256]{1,0:T(8,128)(2,1)S(1)}, u32[]{:S(2)}, u32[]{:S(2)}) collective-permute-start(bf16[576,256]{1,0:T(8,128)(2,1)} %get-tuple-element.169), channel_id=1, source_target_pairs={{0,2},{1,3},{2,0},{3,1},{4,6},{5,7},{6,4},{7,5},{8,10},{9,11},{10,... | collective-permute-start | bytes 884744 | tf_op jit(solution)/shard_map/ppermute | solution.py:213
  201.8 10.3 %collective-permute-start.31 = (bf16[784,384]{1,0:T(8,128)(2,1)S(1)}, bf16[784,384]{1,0:T(8,128)(2,1)S(1)}, u32[]{:S(2)}, u32[]{:S(2)}) collective-permute-start(bf16[784,384]{1,0:T(8,128)(2,1)S(1)} %pass_attn.1.passed), channel_id=1, source_target_pairs={{0,16},{1,17},{2,18},{3,19},{4,12},{5,13},{6,14},{7,15},{8,24},{9,... | collective-permute-start | bytes 1806344 | tf_op jit(solution)/shard_map/ppermute | solution.py:213
  202.4 8.6 %collective-permute-start.33 = (bf16[576,256]{1,0:T(8,128)(2,1)S(1)}, bf16[576,256]{1,0:T(8,128)(2,1)S(1)}, u32[]{:S(2)}, u32[]{:S(2)}) collective-permute-start(bf16[576,256]{1,0:T(8,128)(2,1)S(1)} %copy-done.42), channel_id=1, source_target_pairs={{0,3},{1,2},{2,1},{3,0},{4,7},{5,6},{6,5},{7,4},{8,11},{9,10},{10,... | collective-permute-start | bytes 884744 | tf_op jit(solution)/shard_map/ppermute | solution.py:213
  212.8 8.5 %collective-permute-start.34 = (bf16[576,256]{1,0:T(8,128)(2,1)S(1)}, bf16[576,256]{1,0:T(8,128)(2,1)S(1)}, u32[]{:S(2)}, u32[]{:S(2)}) collective-permute-start(bf16[576,256]{1,0:T(8,128)(2,1)S(1)} %total_ffn.1.refs_0_), channel_id=1, source_target_pairs={{0,8},{1,9},{2,10},{3,11},{4,20},{5,21},{6,22},{7,23},{8,0},{9,1},... | collective-permute-start | bytes 884744 | tf_op jit(solution)/shard_map/ppermute | solution.py:213
  214.7 6.7 %collective-permute-start.32 = (bf16[208,384]{1,0:T(8,128)(2,1)S(1)}, bf16[208,384]{1,0:T(8,128)(2,1)S(1)}, u32[]{:S(2)}, u32[]{:S(2)}) collective-permute-start(bf16[208,384]{1,0:T(8,128)(2,1)S(1)} %get-tuple-element.174), channel_id=1, source_target_pairs={{0,1},{1,0},{2,3},{3,2},{4,5},{5,4},{6,7},{7,6},{8,9},{9,8},{10,11... | collective-permute-start | bytes 479240 | tf_op jit(solution)/shard_map/ppermute | solution.py:213
  221.9 14.3 %collective-permute-start.35 = (bf16[2,576,256]{2,1,0:T(8,128)(2,1)S(1)}, bf16[2,576,256]{2,1,0:T(8,128)(2,1)S(1)}, u32[]{:S(2)}, u32[]{:S(2)}) collective-permute-start(bf16[2,576,256]{2,1,0:T(8,128)(2,1)S(1)} %pair_ffn.1.refs_0_), channel_id=1, source_target_pairs={{0,16},{1,17},{2,18},{3,19},{4,12},{5,13},{6,14},{7,15},{8,24},{9,... | collective-permute-start | bytes 1769480 | tf_op jit(solution)/shard_map/ppermute | solution.py:213
  222.6 13.6 %collective-permute-start.36 = (bf16[208,384]{1,0:T(8,128)(2,1)S(1)}, bf16[208,384]{1,0:T(8,128)(2,1)S(1)}, u32[]{:S(2)}, u32[]{:S(2)}) collective-permute-start(bf16[208,384]{1,0:T(8,128)(2,1)S(1)} %get-tuple-element.181), channel_id=1, source_target_pairs={{0,2},{1,3},{2,0},{3,1},{4,6},{5,7},{6,4},{7,5},{8,10},{9,11},{10,... | collective-permute-start | bytes 479240 | tf_op jit(solution)/shard_map/ppermute | solution.py:213
  226.0 10.1 %collective-permute-start.37 = (bf16[208,384]{1,0:T(8,128)(2,1)S(1)}, bf16[208,384]{1,0:T(8,128)(2,1)S(1)}, u32[]{:S(2)}, u32[]{:S(2)}) collective-permute-start(bf16[208,384]{1,0:T(8,128)(2,1)S(1)} %get-tuple-element.182), channel_id=1, source_target_pairs={{0,3},{1,2},{2,1},{3,0},{4,7},{5,6},{6,5},{7,4},{8,11},{9,10},{10,... | collective-permute-start | bytes 479240 | tf_op jit(solution)/shard_map/ppermute | solution.py:213
  236.8 8.7 %collective-permute-start.39 = (bf16[4,576,256]{2,1,0:T(8,128)(2,1)S(1)}, bf16[4,576,256]{2,1,0:T(8,128)(2,1)}, u32[]{:S(2)}, u32[]{:S(2)}) collective-permute-start(bf16[4,576,256]{2,1,0:T(8,128)(2,1)S(1)} %stack_ffn.1.own), channel_id=1, source_target_pairs={{0,4},{4,0},{1,5},{5,1},{2,6},{6,2},{3,7},{7,3},{8,12},{12,8},{9,1... | collective-permute-start | bytes 3538952 | tf_op jit(solution)/shard_map/ppermute | solution.py:46
  237.5 21.2 %collective-permute-start.38 = (bf16[512,768]{1,0:T(8,128)(2,1)}, bf16[512,768]{1,0:T(8,128)(2,1)S(1)}, u32[]{:S(2)}, u32[]{:S(2)}) collective-permute-start(bf16[512,768]{1,0:T(8,128)(2,1)} %get-tuple-element.189), channel_id=1, source_target_pairs={{0,1},{1,0},{6,7},{7,6},{8,9},{9,8},{14,15},{15,14},{16,17},{17,16... | collective-permute-start | bytes 2359304 | tf_op jit(solution)/shard_map/ppermute | solution.py:213
  242.9 15.7 %collective-permute-start.44 = (f32[16,384]{1,0:T(8,128)S(1)}, f32[16,384]{1,0:T(8,128)S(1)}, u32[]{:S(2)}, u32[]{:S(2)}) collective-permute-start(f32[16,384]{1,0:T(8,128)S(1)} %get-tuple-element.187), channel_id=1, source_target_pairs={{0,4},{4,0},{1,5},{5,1},{2,6},{6,2},{3,7},{7,3},{8,12},{12,8},{9,1... | collective-permute-start | bytes 73736 | tf_op jit(solution)/shard_map/ppermute | solution.py:46
  242.9 12.5 %collective-permute-start.41 = (bf16[192,384]{1,0:T(8,128)(2,1)S(1)}, bf16[192,384]{1,0:T(8,128)(2,1)S(1)}, u32[]{:S(2)}, u32[]{:S(2)}) collective-permute-start(bf16[192,384]{1,0:T(8,128)(2,1)S(1)} %get-tuple-element.195.refs_0_), channel_id=1, source_target_pairs={{0,8},{1,9},{2,10},{3,11},{4,20},{5,21},{6,22},{7,23},{8,0},{9,1},... | collective-permute-start | bytes 442376 | tf_op jit(solution)/shard_map/ppermute | solution.py:213
  256.0 13.7 %collective-permute-start.42 = (bf16[2,192,384]{2,1,0:T(8,128)(2,1)S(1)}, bf16[2,192,384]{2,1,0:T(8,128)(2,1)S(1)}, u32[]{:S(2)}, u32[]{:S(2)}) collective-permute-start(bf16[2,192,384]{2,1,0:T(8,128)(2,1)S(1)} %pair_attn.1.refs_0_), channel_id=1, source_target_pairs={{0,16},{1,17},{2,18},{3,19},{4,12},{5,13},{6,14},{7,15},{8,24},{9,... | collective-permute-start | bytes 884744 | tf_op jit(solution)/shard_map/ppermute | solution.py:213
  259.3 13.8 %collective-permute-start.40 = (bf16[256,768]{1,0:T(8,128)(2,1)S(1)}, bf16[256,768]{1,0:T(8,128)(2,1)S(1)}, u32[]{:S(2)}, u32[]{:S(2)}) collective-permute-start(bf16[256,768]{1,0:T(8,128)(2,1)S(1)} %add_rows.3), channel_id=1, source_target_pairs={{0,2},{1,3},{6,4},{7,5},{8,10},{9,11},{14,12},{15,13},{16,18},{17,... | collective-permute-start | bytes 1179656 | tf_op jit(solution)/shard_map/ppermute | solution.py:213
  270.3 3.6 %collective-permute-start.43 = (bf16[4,192,384]{2,1,0:T(8,128)(2,1)S(1)}, bf16[4,192,384]{2,1,0:T(8,128)(2,1)S(1)}, u32[]{:S(2)}, u32[]{:S(2)}) collective-permute-start(bf16[4,192,384]{2,1,0:T(8,128)(2,1)S(1)} %stack_attn.1.own), channel_id=1, source_target_pairs={{0,4},{4,0},{1,5},{5,1},{2,6},{6,2},{3,7},{7,3},{8,12},{12,8},{9,1... | collective-permute-start | bytes 1769480 | tf_op jit(solution)/shard_map/ppermute | solution.py:46
  (54 other events, 442.5 us)

commit v4 on v3

--- a/solution.py
+++ b/solution.py
@@ -308,11 +308,11 @@
     return jnp.where(bucket_of(relative) == lax.broadcasted_iota(jnp.int32, (32, 1024), 0), 1.0, 0.0)
 
 
-def unpack_kernel(scalars, r0, r1, r2, r3, gain_ref, vec_ref, bias_ref):
+def unpack_kernel(scalars, r0, pair, r3, gain_ref, vec_ref, bias_ref):
     core, shard = scalars[1], scalars[2]
     for z in range(4):
         rows = jnp.zeros((16, 384), full)
-        for step, ref in enumerate((r0, r1, r2, r3)):
+        for step, ref in enumerate((r0, pair.at[0], pair.at[1], r3)):
             rows = rows + jnp.where(xor(shard, step) == z, ref[192:208, :].astype(full), 0.0)
         gain_ref[:, 192 * z : 192 * z + 192] = rows[0:2, :192]
         bias_ref[8 * z : 8 * z + 8, :] = rows[2:10, :12]
@@ -344,14 +344,14 @@
 def pass_ffn_kernel(scalars, keep, first, out):
     def one(i, _):
         rows, later = tile_at(576 * i, 576), tile_at(2304 + 576 * i, 576)
-        out[rows, :] = (wide(keep[later, :]) + wide(first[later, :])).astype(low)
+        out[rows, :] = keep[later, :] + first[later, :]
         return 0
 
     lax.fori_loop(0, 4, one, 0)
 
 
-def sum_ffn_kernel(scalars, keep, first, second, *outs):
-    for step, out in enumerate(outs):
+def sum_ffn_kernel(scalars, keep, first, second, own, pair, far):
+    for step, out in enumerate((own, pair.at[0:576], pair.at[576:1152], far)):
         rows = tile_at(576 * xor(scalars[2], step), 576)
         total = wide(keep[rows, :]) + wide(first[rows, :]) + wide(second[rows, :])
         out[...] = total.astype(out.dtype)
@@ -362,8 +362,8 @@
     out[768:784, :] = (wide(sent[1536:1552, :]) + wide(first[1536:1552, :])).astype(low)
 
 
-def sum_attn_kernel(scalars, keep, passed, first, second, *outs):
-    for step, out in enumerate(outs):
+def sum_attn_kernel(scalars, keep, passed, first, second, own, pair, far):
+    for step, out in enumerate((own, pair.at[0:208], pair.at[208:416], far)):
         rows = tile_at(192 * xor(scalars[2], step), 192)
         total = wide(keep[rows, :]) + wide(first[rows, :]) + wide(second[rows, :])
         out[0:192, :] = total.astype(out.dtype)
@@ -371,8 +371,13 @@
         out[192:208, :] = small.astype(out.dtype)
 
 
-def total_kernel(scalars, own, r1, r2, r3, out, *rest):
-    total = own[...] + wide(r1[...]) + wide(r2[...]) + wide(r3[...])
+def far_kernel(scalars, far, came, out):
+    count = far.shape[0]
+    out[...] = (far[...] + wide(came[count : 2 * count, :])).astype(low)
+
+
+def total_kernel(scalars, own, near, far, out, *rest):
+    total = own[...] + wide(near[0 : own.shape[0], :]) + wide(far[...])
     out[...] = total[: out.shape[0]].astype(low)
     if rest:
         rest[0][...] = total[out.shape[0] :]
@@ -463,7 +468,7 @@
     here, there = tile_at(384 * core, 384), tile_at(384 * (1 - core), 384)
     mix_ref[:, here] = mix_own[...]
     mix_ref[:, there] = mix_other[...]
-    wo_ref[:, here] = w_attn[3]
+    wo_ref[:, here] = w_attn[...]
     wo_ref[:, there] = wo_other[...]
 
     def middle(half, _):
@@ -516,33 +521,48 @@
     lax.fori_loop(0, 2, inner, 0)
 
 
-def outer_kernel(scalars, act_ref, grad_ref, hid_ref, gy_ref, send_ref, keep_ref, turned_ref, sum_ref):
+def inner_part(turned_ref, grad_ref, plane, core, odd, out):
+    def one(j, _):
+        turn = odd * (1 + core) + j * (2 - core)
+        found = mdot(turned_ref[...], grad_ref[xor(plane, turn)]).astype(low)
+        for z in range(4):
+            for i in range(2):
+                out[tile_at(2304 * j + 576 * z + 192 * i, 192), :] = found[
+                    192 * z : 192 * z + 192, 256 * i : 256 * i + 256
+                ]
+        return 0
+
+    lax.fori_loop(0, 2, one, 0)
+
+
+def sent_kernel(scalars, act_ref, grad_ref, hid_ref, gy_ref, send_ref, kept_ref, turned_ref, sum_ref):
     plane, core = scalars[0], scalars[1]
     turned_ref[...] = act_ref[...].astype(full).T.astype(low)
-
-    def outer(j, _):
-        for odd, out in enumerate((keep_ref, send_ref)):
-            turn = odd * (1 + core) + j * (2 - core)
-            found = mdot(turned_ref[...], grad_ref[xor(plane, turn)]).astype(low)
-            for z in range(4):
-                for i in range(2):
-                    out[tile_at(2304 * j + 576 * z + 192 * i, 192), :] = found[
-                        192 * z : 192 * z + 192, 256 * i : 256 * i + 256
-                    ]
-        return 0
-
-    lax.fori_loop(0, 2, outer, 0)
+    inner_part(turned_ref, grad_ref, plane, core, 1, send_ref)
 
     def last(z, _):
         sum_ref[...] = tdot(hid_ref[:, tile_at(256 * z, 256)], gy_ref[...])
         for k, turn in enumerate(turns(core)):
-            out = (keep_ref, send_ref)[k % 2]
             found = sum_ref[tile_at(64 * xor(plane, turn), 64), :].astype(low)
             for i in range(3):
-                out[tile_at(2304 * (k // 2) + 576 * z + 384 + 64 * i, 64), :] = found[:, 256 * i : 256 * i + 256]
+                part = found[:, 256 * i : 256 * i + 256]
+                if k % 2:
+                    send_ref[tile_at(2304 * (k // 2) + 576 * z + 384 + 64 * i, 64), :] = part
+                else:
+                    kept_ref[tile_at(768 * (k // 2) + 192 * z + 64 * i, 64), :] = part
         return 0
 
     lax.fori_loop(0, 4, last, 0)
+
+
+def kept_kernel(scalars, act_ref, grad_ref, kept_ref, keep_ref, turned_ref):
+    plane, core = scalars[0], scalars[1]
+    turned_ref[...] = act_ref[...].astype(full).T.astype(low)
+    inner_part(turned_ref, grad_ref, plane, core, 0, keep_ref)
+    for j in range(2):
+        for z in range(4):
+            at = 2304 * j + 576 * z + 384
+            keep_ref[at : at + 192, :] = kept_ref[768 * j + 192 * z : 768 * j + 192 * z + 192, :]
 
 
 def pick_kernel(scalars, b0, b1, b2, b3, place_ref, token_ref, out_ref):
@@ -602,7 +622,7 @@
 ):
     core = scalars[1]
     here, there = tile_at(384 * core, 384), tile_at(384 * (1 - core), 384)
-    late = (own_part, other_part, mid_ref, gy_ref, wo_other, w_ref.at[3], q_ref, k_ref, v_ref, p_ref)
+    late = (own_part, other_part, mid_ref, gy_ref, wo_other, w_ref, q_ref, k_ref, v_ref, p_ref)
     copies = [fetch_part(ref, held, rest[-1].at[i]) for i, (ref, held) in enumerate(zip(late, rest[:-1]))]
     own_part, other_part, mid_ref, gy_ref, wo_other, wo_own, q_ref, k_ref, v_ref, p_ref = rest[:-1]
     for copy in copies[:4]:
@@ -676,54 +696,136 @@
     return value.astype(full)
 
 
-def adam_kernel(join, scalars, master, first, second, own, other, *outs):
-    lower = scalars[1] == 0
-    left = jnp.where(lower, own[0], other[0]).astype(full)
-    right = jnp.where(lower, other[0], own[0]).astype(full)
-    grad = join(left, right).reshape(master.shape)
-    new_master, new_first, new_second, copy = adam_step(master[...], first[...], second[...], grad, True)
-    outs[0][...] = new_master
-    outs[1][...] = new_first
-    outs[2][...] = copy
-    if len(outs) == 4:
-        outs[3][...] = new_second
-    else:
-
-        @pl.when(pl.program_id(0) < 3)
-        def _():
-            outs[3][...] = new_second
-
-        @pl.when(pl.program_id(0) == 3)
-        def _():
-            outs[4][...] = new_second[0]
-
-
-def adam_call(grid, join, state, quarter_of, states, grads, spot, name, sizes, rows_at, second=None):
-
-    def grad_spec(other):
-        def where(*idx):
-            scalars = idx[-1]
-            core = 1 - scalars[1] if other else scalars[1]
-            return (stack_at(xor(scalars[0], quarter_of(*idx[:-1])), core), rows_at, 0)
-
-        return pl.BlockSpec(sizes, where)
-
-    shape = states[0].shape
-    kinds = [full, full, low] + ([full] if second is None else [])
-    count = functools.reduce(lambda a, b: a * b, shape)
-    return pl.pallas_call(
-        functools.partial(adam_kernel, join),
-        grid_spec=pltpu.PrefetchScalarGridSpec(
-            num_scalar_prefetch=1,
-            grid=grid,
-            in_specs=[state] * 3 + [grad_spec(False), grad_spec(True)],
-            out_specs=[state] * len(kinds) + ([] if second is None else second[0]),
-        ),
-        out_shape=[jax.ShapeDtypeStruct(shape, kind) for kind in kinds]
-        + ([] if second is None else second[1]),
-        name=name,
-        cost_estimate=pl.CostEstimate(flops=0, bytes_accessed=0, transcendentals=0),
-    )(spot, *states, *grads)
+def adam_kernel(steps, count, scalars, *refs):
+    plane, core = scalars[0], scalars[1]
+    lower = core == 0
+    states, grads, outs = refs[:3], refs[3:5], refs[5 : 5 + count]
+    own, other, brought, held, sems = refs[5 + count], refs[6 + count], refs[7 + count : 10 + count], refs[-5:-1], refs[-1]
+    arrive = [fetch_part(grads[0], own, sems.at[8]), fetch_part(grads[1], other, sems.at[9])]
+    loads = []
+    for number, (where, _, _, _) in enumerate(steps):
+        loads.append(
+            [fetch_part(where(state), brought[i].at[number], sems.at[10 + 3 * number + i]) for i, state in enumerate(states)]
+        )
+    for copy in arrive:
+        copy.wait()
+
+    def place(own, other, quarter):
+        turn = xor(plane, quarter)
+        return own.at[stack_at(turn, core)], other.at[stack_at(turn, 1 - core)]
+
+    flying = []
+    for number, (_, quarter, read, targets) in enumerate(steps):
+        slot = number % 2
+        if number >= 2:
+            for copy in flying[number - 2]:
+                copy.wait()
+        if quarter is None:
+            grad = read(own, other, place, lower).astype(full)
+        else:
+            grad = read(*place(own, other, quarter), lower).astype(full)
+        for copy in loads[number]:
+            copy.wait()
+        new = adam_step(brought[0][number], brought[1][number], brought[2][number], grad, True)
+        copies = []
+        for i, value in enumerate(new):
+            order = (0, 1, 3, 2)[i]
+            held[order][slot] = value
+            copies.append(fetch_part(held[order].at[slot], targets(outs, i), sems.at[4 * slot + i]))
+        flying.append(copies)
+    for copies in flying[-2:]:
+        for copy in copies:
+            copy.wait()
+
+
+def adam_call(spot, steps, block, states, grads, outputs, name):
+    return call(
+        functools.partial(adam_kernel, steps, len(outputs)), spot,
+        [*[[state] for state in states], *[(grad,) for grad in grads]], outputs,
+        [
+            *[pltpu.VMEM(grads[0].shape, low)] * 2, *[pltpu.VMEM((len(steps),) + block, full)] * 3,
+            *[pltpu.VMEM((2,) + block, full)] * 2, pltpu.VMEM((2,) + block, low), pltpu.VMEM((2,) + block, full),
+            pltpu.SemaphoreType.DMA((10 + 3 * len(steps),)),
+        ],
+        name, 0, 60, range(len(outputs)),
+    )
+
+
+def small_kernel(
+    scalars, own, other, gm_ref, gf_ref, gs_ref, bm_ref, bf_ref, bs_ref, gain_step, gain_first, gain_second,
+    bias_step, bias_first, bias_second, table_ref,
+):
+    core, shard = scalars[1], scalars[2]
+    total = own[...] + other[...]
+    grads = []
+    for j in range(2):
+        row = jnp.where(shard // 2 == 1, total[2 * j + 1 : 2 * j + 2], total[2 * j : 2 * j + 1])
+        grads.append(jnp.where(shard % 2 == 1, row[:, 192:], row[:, :192]))
+    new = adam_step(gm_ref[...], gf_ref[...], gs_ref[...], jnp.concatenate(grads, 0), False)
+    gain_step[...], gain_first[...], gain_second[...] = new[0] - gm_ref[...], new[1], new[2]
+    mine, theirs = own[4:10, :32], other[4:10, :32]
+    table = jnp.concatenate(chosen(core == 0, mine, theirs), 0)
+    same = lax.broadcasted_iota(jnp.int32, (32, 32), 0) == lax.broadcasted_iota(jnp.int32, (32, 32), 1)
+    table_ref[...] = lax.dot_general(
+        jnp.where(same, 1.0, 0.0), table, (((1,), (1,)), ((), ())),
+        precision=lax.Precision.HIGHEST, preferred_element_type=full,
+    )
+    grad = table_ref[tile_at(8 * shard, 8), :]
+    new = adam_step(bm_ref[...], bf_ref[...], bs_ref[...], grad, False)
+    bias_step[...], bias_first[...], bias_second[...] = new[0] - bm_ref[...], new[1], new[2]
+
+
+def chosen(lower, mine, theirs):
+    return jnp.where(lower, mine, theirs), jnp.where(lower, theirs, mine)
+
+
+def attn_steps():
+    def one(m):
+        where = lambda ref: ref.at[m]
+
+        def read(mine, theirs, lower):
+            return jnp.concatenate(chosen(lower, mine[...], theirs[...]), 1)
+
+        def targets(outs, i):
+            if i == 2:
+                return outs[2].at[m] if m < 3 else outs[3]
+            return outs[(0, 1, 2, 4)[i]].at[m]
+
+        return where, m, read, targets
+
+    return [one(m) for m in range(4)]
+
+
+def ffin_steps():
+    def one(i, h):
+        columns = slice(1024 * h, 1024 * h + 1024)
+        where = lambda ref: ref.at[i, :, columns]
+
+        def read(mine, theirs, lower):
+            left, right = chosen(lower, mine[0:384, :], theirs[0:384, :])
+            return jnp.concatenate([left[:192], right[:192], left[192:], right[192:]], 1)
+
+        return where, 2 * i + h, read, lambda outs, n: where(outs[n])
+
+    return [one(i, h) for i in range(2) for h in range(2)]
+
+
+def ffout_steps():
+    def one(c):
+        rows = slice(256 * c, 256 * c + 256)
+        where = lambda ref: ref.at[rows, :]
+
+        def read(own, other, place, lower):
+            found = []
+            for q in range(4):
+                mine, theirs = place(own, other, q)
+                value = chosen(lower, mine[384:576, :], theirs[384:576, :])[c]
+                found.append(jnp.concatenate([value[:64], value[64:128], value[128:]], 1))
+            return jnp.concatenate(found, 0)
+
+        return where, None, read, lambda outs, n: where(outs[n])
+
+    return [one(c) for c in range(2)]
 
 
 def body_fast(
@@ -760,14 +862,15 @@
         ],
         "pack_attn", 0, 60,
     )[0]
-    attn_came = [across(quarter, step) for step in (1, 2, 3)]
+    attn_third = across(quarter, 3)
 
     unit = call(
         pack_ffn_kernel, spot, [[ffin_master], [ffout_master]], [((576, 256), low)],
         [pltpu.VMEM((2, 192, 256), full), pltpu.VMEM((64, 768), full), pltpu.SemaphoreType.DMA((3,))],
         "pack_ffn", 0, 60,
     )[0]
-    attn_came = [after(value, unit) for value in attn_came]
+    attn_third = after(attn_third, unit)
+    attn_pair = across(cat(spot, [quarter, attn_third], 208, "pair_attn_in"), 1)
 
     up_pairs = lambda pairs: [((p, 1, z), (p, 1, w)) for p in range(4) for z, w in pairs]
     down_pairs = lambda pairs: [((p, 0, 3 - z), (p, 0, 3 - w)) for p in range(4) for z, w in pairs]
@@ -816,6 +919,15 @@
         chosen = chosen if gate is None else after(chosen, *gate)
         return jnp.where(mine, chosen, swap(chosen))
 
+    def rows_near(rows, *gates):
+        pairs = [((p, c, z), (p, c, z ^ 1)) for p, c, z in ALL if z // 2 == c]
+        return after(send(rows[0], pairs), *gates)
+
+    def rows_far(rows, came, *gates):
+        pairs = [((p, c, z), (p, c, z ^ 2)) for p, c, z in ALL if z // 2 == c]
+        far = call(add_kernel, spot, [rows[2], came], [((256, 768), low)], [], "add_rows", 0, 4)[0]
+        return after(send(far, pairs), *gates)
+
     def rows_back(rows, first_gate, second_gate):
         pairs = lambda step: [((p, c, z), (p, c, z ^ step)) for p, c, z in ALL if z // 2 == c]
         near, own, far = rows
@@ -826,7 +938,7 @@
 
 
     gains, vectors = call(
-        unpack_kernel, spot, [quarter, *attn_came], [((2, 768), full), ((3, 2, 1024), full)],
+        unpack_kernel, spot, [quarter, attn_pair, attn_third], [((2, 768), full), ((3, 2, 1024), full)],
         [pltpu.VMEM((32, 12), full)], "unpack", 0, 8,
     )
 
@@ -834,14 +946,16 @@
         near = cat(spot, pieces, rows, "near")
         arrived = plane_first(near)
         if gate is not None:
-            arrived = after(arrived, gate)
+            arrived = after(arrived, *gate)
         near = cat(spot, [near, arrived], rows, "nearest")
         return near, plane_second(near if late is None else after(near, late))
 
-    unit = after(unit, *attn_came)
-    ffn_came = [across(unit, step) for step in (1, 2, 3)]
-    attn_came = [after(value, ffn_came[0]) for value in attn_came]
-    near, far = spread_plane(attn_came, 192, ffn_came[1])
+    unit = after(unit, attn_third)
+    ffn_third = across(unit, 3)
+    ffn_two = cat(spot, [unit, ffn_third], 576, "pair_ffn_in")
+    near, far = spread_plane([attn_pair, attn_third], 192, [ffn_two])
+    ffn_pair_in = across(ffn_two, 1)
+    ffn_came = [ffn_pair_in, ffn_third]
     x_low = rows_here(token_index, tok_blocks, (far, *ffn_came))
     w_attn, act_one, query, key, value = call(
         project_kernel, spot,
@@ -849,27 +963,28 @@
         [((4, 768, 384), low), ((512, 768), low)] + [((512, 384), low)] * 3,
         [pltpu.VMEM((4, 192, 384), full), pltpu.SemaphoreType.DMA((13,))], "project", 0, 60,
     )
-    wo_other = swap(w_attn[3])
-
-
-    ffn_near, ffn_far = spread_plane(ffn_came, 576, query)
+    wo_own = w_attn[3]
+    wo_other = swap(wo_own)
+
+
     cot_own = after(cotangent[0], *ffn_came)
-    cot_one = after(along(cot_own, (0, 1), (1, 2), (2, 3)), query)
-    cot_two = along(cot_one, (1, 2), (2, 3))
+    cot_one = along(cot_own, (1, 2), (2, 3))
+    cot_two = along(cot_own, (0, 2), (1, 3))
+    cot_three = along(cot_own, (0, 3), (3, 2))
+    ffn_near, ffn_far = spread_plane(ffn_came, 576, [query, cot_one])
     mix_own, probs = call(
-        attend_all_kernel, spot, [after(query, ffn_near, cot_two), key, value, seg_here[:, None], seg_here[None, :], vectors],
+        attend_all_kernel, spot, [after(query, ffn_near), key, value, seg_here[:, None], seg_here[None, :], vectors],
         [((512, 384), low), ((6, 512, 512), low)],
         [pltpu.VMEM((512, 512), full), pltpu.VMEM((6, 512, 512), low), pltpu.SemaphoreType.DMA((3,))],
         "attend", 0, 60, (1,),
     )
-    cot_three = after(along(jnp.where(at_end, cot_own, cot_two), (2, 3), (3, 2)), mix_own)
-    cot_blocks = (cot_own, cot_one, cot_two, cot_three)
+    cot_blocks = (cot_own, *[after(piece, mix_own) for piece in (cot_one, cot_two, cot_three)])
     grad_y = rows_here(order, cot_blocks)
     mix_other = swap(mix_own)
     x_mid, act_two, hidden, part_two, y_part, grads_up = call(
         feed_kernel, spot,
         [
-            x_low, mix_own, mix_other, w_attn, wo_other, gains, grad_y, ffin_master, [ffout_master],
+            x_low, mix_own, mix_other, wo_own, wo_other, gains, grad_y, ffin_master, [ffout_master],
             (ffn_near,), (ffn_far,),
         ],
         [
@@ -883,24 +998,21 @@
         ],
         "feed", 0, 24,
     )
-    ffn_send, ffn_keep = call(
-        outer_kernel, spot, [act_two, grads_up, hidden, grad_y], [((4608, 256), low)] * 2,
-        [pltpu.VMEM((768, 512), low), pltpu.VMEM((256, 768), full)], "outer", 0, 12,
-    )
-    part_other = after(swap(part_two), ffn_send)
+    ffn_send, out_kept = call(
+        sent_kernel, spot, [act_two, grads_up, hidden, grad_y], [((4608, 256), low), ((1536, 256), low)],
+        [pltpu.VMEM((768, 512), low), pltpu.VMEM((256, 768), full)], "sent", 0, 12,
+    )
     ffn_first = plane_first(ffn_send)
-
-    y_other = swap(after(y_part, part_other))
-    y_rows = call(
-        spread_y_kernel, spot, [(x_mid,), (y_part,), (y_other,), wanted_y, token_row],
-        [((512, 768), low), ((256, 768), low), ((256, 768), low)],
-        [pltpu.VMEM((512, 768), low), *[pltpu.VMEM((512, 768), full)] * 3, pltpu.SemaphoreType.DMA((3,))],
-        "spread_y", 0, 60,
-    )
+    ffn_keep = call(
+        kept_kernel, spot, [act_two, after(grads_up, ffn_send), out_kept], [((4608, 256), low)],
+        [pltpu.VMEM((768, 512), low)], "kept", 0, 12,
+    )[0]
+    part_other = after(swap(part_two), ffn_keep)
+
     grad_mid, right, lined, gain_two = call(
         back_kernel, spot,
         [
-            (after(part_two, *y_rows),), (part_other,), (x_mid,), (grad_y,), gains, (w_attn,), (wo_other,),
+            (part_two,), (part_other,), (x_mid,), (grad_y,), gains, (wo_own,), (wo_other,),
             (query,), (key,), (value,), (probs,),
         ],
         [
@@ -914,7 +1026,14 @@
         ],
         "back", 0, 60,
     )
-    ffn_first = after(ffn_first, right)
+    y_other = swap(after(y_part, part_other))
+    y_rows = call(
+        spread_y_kernel, spot, [(x_mid,), (after(y_part, right),), (y_other,), wanted_y, token_row],
+        [((512, 768), low), ((256, 768), low), ((256, 768), low)],
+        [pltpu.VMEM((512, 768), low), *[pltpu.VMEM((512, 768), full)] * 3, pltpu.SemaphoreType.DMA((3,))],
+        "spread_y", 0, 60,
+    )
+    ffn_first = after(ffn_first, right, y_rows[0])
     one_out = lambda kernel, inputs, shape, name: call(kernel, spot, inputs, [(shape, low)], [], name, 0, 8)[0]
     ffn_passed = one_out(pass_ffn_kernel, [ffn_keep, ffn_first], (2304, 256), "pass_ffn")
     ffn_second = plane_second(ffn_passed)
@@ -931,8 +1050,14 @@
         ],
         "last", 0, 60,
     )
-    layer_out, y_last = rows_back(y_rows, right, part_one)
-    ffn_second = after(ffn_second, part_one, y_last)
+    y_near = rows_near([after(y_rows[0], ffn_passed)], part_one)
+    ffn_second = after(ffn_second, part_one, y_near)
+    ffn_own, ffn_two, ffn_far = call(
+        sum_ffn_kernel, spot, [ffn_keep, ffn_first, ffn_second],
+        [((576, 256), full), ((1152, 256), low), ((576, 256), full)], [], "sum_ffn", 0, 8,
+    )
+    ffn_near = across(ffn_two, 1)
+    y_far = rows_far(y_rows, after(y_near, ffn_two))
     x_rows = call(
         spread_x_kernel, spot,
         [(part_one,), (swap(part_one),), (x_low,), gains, (grad_mid,), wanted_x, token_row],
@@ -943,43 +1068,38 @@
         ],
         "spread_x", 0, 60,
     )
-    ffn_own, *ffn_outs = call(
-        sum_ffn_kernel, spot, [ffn_keep, ffn_first, ffn_second],
-        [((576, 256), full)] + [((576, 256), low)] * 3, [], "sum_ffn", 0, 8,
-    )
-    ffn_came = [across(out, step) for step, out in zip((1, 2, 3), ffn_outs)]
-    attn_first_came = after(plane_first(after(attn_send, ffn_second)), *ffn_came[:2], *x_rows)
+    ffn_send = call(far_kernel, spot, [ffn_far, after(ffn_near, *x_rows)], [((576, 256), low)], [], "far_ffn", 0, 8)[0]
+    ffn_last = across(ffn_send, 3)
+    y_far = after(y_far, ffn_send)
+    attn_first_came = after(plane_first(after(attn_send, ffn_second)), ffn_send, y_far, *x_rows)
     passed = one_out(pass_attn_kernel, [attn_keep, attn_send, attn_first_came], (784, 384), "pass_attn")
+    layer_out = y_rows[1] + y_near[:256] + y_far
     attn_second_came = plane_second(passed)
-    attn_own, *attn_outs = call(
+    attn_own, attn_two, attn_far = call(
         sum_attn_kernel, spot, [attn_keep, passed, attn_first_came, attn_second_came],
-        [((208, 384), full)] + [((208, 384), low)] * 3, [], "sum_attn", 0, 8,
-    )
-    ffn_came = [after(value, attn_second_came) for value in ffn_came]
-    attn_outs = [across(out, step) for step, out in zip((1, 2, 3), attn_outs)]
-    ffn_sum = one_out(total_kernel, [ffn_own, *ffn_came], (576, 256), "total_ffn")
-    ffn_pair = cat(spot, [ffn_sum, after(plane_first(ffn_sum), attn_outs[0])], 576, "pair_ffn")
-    ffn_stack = cat(spot, [ffn_pair, after(plane_second(ffn_pair), attn_outs[1], attn_outs[2])], 576, "stack_ffn")
+        [((208, 384), full), ((416, 384), low), ((208, 384), full)], [], "sum_attn", 0, 8,
+    )
+
+    attn_near_came = across(attn_two, 1)
+    ffn_last = after(ffn_last, attn_two)
+    ffn_sum = one_out(total_kernel, [ffn_own, ffn_near, ffn_last], (576, 256), "total_ffn")
+    attn_far_send = call(far_kernel, spot, [attn_far, attn_near_came], [((208, 384), low)], [], "far_attn", 0, 8)[0]
+    attn_last = across(attn_far_send, 3)
+    ffn_pair = cat(spot, [ffn_sum, after(plane_first(ffn_sum), attn_far_send)], 576, "pair_ffn")
+    ffn_stack = cat(spot, [ffn_pair, after(plane_second(ffn_pair), attn_last)], 576, "stack_ffn")
     ffn_sum = (ffn_stack, swap(ffn_stack))
-    ffout_state = pl.BlockSpec((2, 1, 64, 768), lambda q, s: (0, q, 0, 0))
-    unfold = lambda value: jnp.concatenate([value[:64], value[64:128], value[128:]], 1)
+    flat, wide_in = (512, 768), (2, 192, 2048)
+    ffin_res = adam_call(
+        spot, ffin_steps(), (192, 1024), [ffin_master, ffin_first, ffin_second], ffn_sum,
+        [(wide_in, full), (wide_in, full), (wide_in, full), (wide_in, low)], "adam_ffin",
+    )
     ffout_res = adam_call(
-        (4,), lambda left, right: jnp.stack([unfold(left), unfold(right)]), ffout_state, lambda q: q,
-        [state.reshape(2, 4, 64, 768) for state in (ffout_master, ffout_first, ffout_second)],
-        ffn_sum, spot, "adam_ffout", (1, 192, 256), 2,
-    )
-    ffout_res = [value.reshape(512, 768) for value in ffout_res]
-    ffin_res = adam_call(
-        (2, 2),
-        lambda left, right: jnp.concatenate(
-            [left[:192], right[:192], left[192:], right[192:]], 1
-        ),
-        pl.BlockSpec((1, 192, 1024), lambda i, h, s: (i, 0, h)), lambda i, h: 2 * i + h,
-        [ffin_master, ffin_first, ffin_second], ffn_sum, spot, "adam_ffin", (1, 384, 256), 0,
-    )
-    attn_outs = [after(value, ffn_stack) for value in attn_outs]
+        spot, ffout_steps(), (256, 768), [ffout_master, ffout_first, ffout_second], ffn_sum,
+        [(flat, full), (flat, full), (flat, full), (flat, low)], "adam_ffout",
+    )
     attn_sum, small = call(
-        total_kernel, spot, [attn_own, *attn_outs], [((192, 384), low), ((16, 384), full)], [], "total_attn", 0, 8
+        total_kernel, spot, [attn_own, attn_near_came, after(attn_last, ffn_stack)],
+        [((192, 384), low), ((16, 384), full)], [], "total_attn", 0, 8,
     )
     attn_near = cat(spot, [attn_sum, after(plane_first(attn_sum), ffin_res[0])], 192, "pair_attn")
     attn_stack = cat(spot, [attn_near, after(plane_second(attn_near), ffout_res[0])], 192, "stack_attn")
@@ -987,47 +1107,38 @@
     x_rows = [after(value, small) for value in x_rows]
     input_grad, _ = rows_back(x_rows, ffin_res[0], ffout_res[0])
     small_other = swap(small)
-    gain_sum = (small[:4] + small_other[:4]).reshape(2, 768)
-    g_gain = lax.dynamic_slice_in_dim(gain_sum, shard * 192, 192, 1)
-    g_bias = both_cores(small[4:10, :32], small_other[4:10, :32], core, 0)
-    g_bias = lax.dynamic_slice_in_dim(g_bias, shard * 8, 8, 1).T
-
+    square = (4, 192, 768)
     attn_res = adam_call(
-        (4,), lambda left, right: jnp.concatenate([left, right], 1),
-        pl.BlockSpec((1, 192, 768), lambda m, s: (m, 0, 0)), lambda m: m,
-        [attn_master, attn_first, attn_second], attn_sum, spot, "adam_attn", (1, 192, 384), 0,
-        (
-            [
-                pl.BlockSpec((1, 192, 768), lambda m, s: (jnp.minimum(m, 2), 0, 0)),
-                pl.BlockSpec((192, 768), lambda m, s: (0, 0)),
-            ],
-            [jax.ShapeDtypeStruct((3, 192, 768), full), jax.ShapeDtypeStruct((192, 768), full)],
-        ),
-    )
-    gain_res = adam_step(gain_master, gain_first, gain_second, g_gain, False)
-    bias_res = adam_step(bias_master, bias_first, bias_second, g_bias, False)
+        spot, attn_steps(), (192, 768), [attn_master, attn_first, attn_second], attn_sum,
+        [(square, full), (square, full), ((3, 192, 768), full), ((192, 768), full), (square, low)], "adam_attn",
+    )
+    smalls = call(
+        small_kernel, spot,
+        [small, small_other, gain_master, gain_first, gain_second, bias_master, bias_first, bias_second],
+        [((2, 192), full)] * 3 + [((8, 12), full)] * 3, [pltpu.VMEM((32, 12), full)], "adam_small", 0, 4,
+    )
     return (
         layer_out[None],
         input_grad[None],
         attn_res[0],
         ffin_res[0],
         ffout_res[0],
-        gain_res[0] - gain_master,
-        bias_res[0] - bias_master,
+        smalls[0],
+        smalls[3],
         attn_res[1],
         ffin_res[1],
         ffout_res[1],
-        gain_res[1],
-        bias_res[1],
+        smalls[1],
+        smalls[4],
+        attn_res[2],
         attn_res[3],
+        ffin_res[2],
+        ffout_res[2],
+        smalls[2],
+        smalls[5],
         attn_res[4],
         ffin_res[3],
         ffout_res[3],
-        gain_res[2],
-        bias_res[2],
-        attn_res[2],
-        ffin_res[2],
-        ffout_res[2],
     )
 
 

time: 285 us -> 274 us (0.961)
  local copies, waits for them, and re-layouts: 16.4 us -> 11.6 us
  starting transfers between devices: 65.5 us -> 61.2 us
  waiting for transfers between devices: 66.9 us -> 63.8 us
    pallas_call x29 -> x38, Pallas kernels: 95.6 us -> 123 us  [call(): pl.pallas_call(kernel, in_specs=[pl.BlockSpec(memory_space=pltpu.SMEM)] +...]
    pallas_call x3 -> x0, Pallas kernels: 25.4 us -> none  [adam_call(): pl.pallas_call(functools.partial(adam_kernel, join), grid_spec=pltpu.Pref...]
    unnamed x120 -> x112, local copies, waits for them, and re-layouts: 11.4 us -> 6.03 us
    ppermute x34 -> x30, starting transfers between devices: 62.1 us -> 59.2 us  [send(): lax.ppermute(value, ('plane', 'core', 'shard'), [((p * 2 + c) * 4 + z, (q...]
    ppermute x34 -> x30, waiting for transfers between devices: 61.7 us -> 61.1 us  [send(): lax.ppermute(value, ('plane', 'core', 'shard'), [((p * 2 + c) * 4 + z, (q...]
  transfers between devices with their start and end apart: 45 -> 41, of which waited for: 21 -> 19; matrix products, arithmetic and copies ran while one was open for 6% -> 5% of each run, Pallas kernels for 34% -> 35%
where the time goes in v4:
time: 274 us; the launch traced here: 273 us
  Pallas kernels  123 us (45%)
  waiting for transfers between devices  63.8 us (23%)
  starting transfers between devices  61.2 us (22%)
  local copies, waits for them, and re-layouts  11.6 us (4%)
  other arithmetic  8.69 us (3%)
  between operations  4.56 us (2%)
    pallas_call x38, Pallas kernels, call(): pl.pallas_call(kernel, in_specs=[pl.BlockSpec(memory_space=pltpu.SMEM)] +...  123 us
    ppermute x30, waiting for transfers between devices, send(): lax.ppermute(value, ('plane', 'core', 'shard'), [((p * 2 + c) * 4 + z, (q...  61.1 us
    ppermute x30, starting transfers between devices, send(): lax.ppermute(value, ('plane', 'core', 'shard'), [((p * 2 + c) * 4 + z, (q...  59.2 us
    unnamed x112, local copies, waits for them, and re-layouts  6.03 us
  transfers between devices with their start and end apart: 41, of which 19 were waited for; matrix products, arithmetic and copies ran while one was open for 5% of the time, Pallas kernels for 35%

profile of v4, /device:TPU:0, one launch (start us, length us, event | category | flops | bytes accessed | tf_op | source)
XLA Modules:
  0.0 273.1 jit_solution(14817011087754837239)
XLA Ops:
  1.3 2.3 pack_attn.1.refs_0_.r0
  3.7 5.1 %collective-permute-start.4 = (bf16[208,384]{1,0:T(8,128)(2,1)}, bf16[208,384]{1,0:T(8,128)(2,1)S(1)}, u32[]{:S(2)}, u32[]{:S(2)}) collective-permute-start(bf16[208,384]{1,0:T(8,128)(2,1)} %pack_attn.1.refs_0_.r0), channel_id=1, source_target_pairs={{0,3},{1,2},{2,1},{3,0},{4,7},{5,6},{6,5},{7,4},{8,11},{9,10},{10,... | collective-permute-start | bytes 479240 | tf_op jit(solution)/shard_map/ppermute | solution.py:213
  10.6 2.7 pack_ffn.1.refs_0_
  14.2 3.0 %collective-permute-start.5 = (bf16[2,208,384]{2,1,0:T(8,128)(2,1)S(1)}, bf16[2,208,384]{2,1,0:T(8,128)(2,1)S(1)}, u32[]{:S(2)}, u32[]{:S(2)}) collective-permute-start(bf16[2,208,384]{2,1,0:T(8,128)(2,1)S(1)} %pair_attn_in.1), channel_id=1, source_target_pairs={{0,1},{1,0},{2,3},{3,2},{4,5},{5,4},{6,7},{7,6},{8,9},{9,8},{10,11... | collective-permute-start | bytes 958472 | tf_op jit(solution)/shard_map/ppermute | solution.py:213
  21.4 3.3 %collective-permute-start.7 = (bf16[576,256]{1,0:T(8,128)(2,1)}, bf16[576,256]{1,0:T(8,128)(2,1)S(1)}, u32[]{:S(2)}, u32[]{:S(2)}) collective-permute-start(bf16[576,256]{1,0:T(8,128)(2,1)} %pack_ffn.1.refs_0_), channel_id=1, source_target_pairs={{0,3},{1,2},{2,1},{3,0},{4,7},{5,6},{6,5},{7,4},{8,11},{9,10},{10,... | collective-permute-start | bytes 884744 | tf_op jit(solution)/shard_map/ppermute | solution.py:213
  26.8 1.6 collective-permute-start.6
  29.9 2.0 collective-permute-done.7.refs_1_
  32.5 2.8 %collective-permute-done.6.refs_1_ = bf16[3,192,384]{2,1,0:T(8,128)(2,1)} collective-permute-done((bf16[3,192,384]{2,1,0:T(8,128)(2,1)S(1)}, bf16[3,192,384]{2,1,0:T(8,128)(2,1)}, u32[]{:S(2)}, u32[]{:S(2)}) %collective-permute-start.6) | collective-permute-done | bytes 442400 | tf_op jit(solution)/shard_map/ppermute | solution.py:213
  36.4 1.6 collective-permute-start.8
  38.6 2.4 collective-permute-start.9
  41.0 1.9 collective-permute-start.2
  45.1 11.5 %collective-permute-done.2.b3 = bf16[256,768]{1,0:T(8,128)(2,1)S(1)} collective-permute-done((bf16[256,768]{1,0:T(8,128)(2,1)S(1)}, bf16[256,768]{1,0:T(8,128)(2,1)S(1)}, u32[]{:S(2)}, u32[]{:S(2)}) %collective-permute-start.2) | collective-permute-done | bytes 393248 | tf_op jit(solution)/shard_map/ppermute | solution.py:213
  56.6 2.3 pick.2
  63.4 5.2 %project.1 = (bf16[4,768,384]{2,1,0:T(8,128)(2,1)}, bf16[512,768]{1,0:T(8,128)(2,1)}, bf16[512,384]{1,0:T(8,128)(2,1)}, bf16[512,384]{1,0:T(8,128)(2,1)}, bf16[512,384]{1,0:T(8,128)(2,1)}) custom-call(s32[3]{0:T(128)} %pad_add_fusion.5.scalars, bf16[512,768]{1,0:T(8,128)(2,1)} %broadcast_select_fusion.1.x_ref, f32[2,768]{1,0:T(2,128)} %copy-done.35, ...), custom_call_target="tpu_custom_call" | custom-call | tf_op jit(solution)/shard_map/project/pallas_call | solution.py:257
  68.5 1.5 collective-permute-done.12.b1
  70.1 2.6 collective-permute-done.11.refs_1_
  72.7 1.9 nearest.3.near_ref
  74.6 1.5 collective-permute-start.18
  76.1 3.6 %collective-permute-start.16 = (bf16[256,768]{1,0:T(8,128)(2,1)}, bf16[256,768]{1,0:T(8,128)(2,1)S(1)}, u32[]{:S(2)}, u32[]{:S(2)}) collective-permute-start(bf16[256,768]{1,0:T(8,128)(2,1)} %bitcast.18.b0), channel_id=1, source_target_pairs={{4,7},{7,6},{12,15},{15,14},{20,23},{23,22},{28,31},{31,30},{3,0},... | collective-permute-start | bytes 1179656 | tf_op jit(solution)/shard_map/ppermute | solution.py:213
  82.8 13.3 %attend.1 = (bf16[512,384]{1,0:T(8,128)(2,1)}, bf16[6,512,512]{2,1,0:T(8,128)(2,1)}) custom-call(s32[3]{0:T(128)} %pad_add_fusion.5.scalars, bf16[512,384]{1,0:T(8,128)(2,1)} %get-tuple-element.124.q_ref, bf16[512,384]{1,0:T(8,128)(2,1)} %get-tuple-element.125.k_ref, bf16[512,384]{1,0:T(8,128)(2,1)} %get-tuple-element.126.v_ref, s32[512,1]{1,0:T(8,128)} %copy.43.qseg_ref, ...), custom_call_target="tpu_custom_call" | custom-call | tf_op jit(solution)/shard_map/attend/pallas_call | solution.py:257
  96.2 2.4 pick.3
  101.1 1.7 collective-permute-done.13.mix_other
  102.8 11.1 %feed.1 = (f32[512,768]{1,0:T(8,128)S(1)}, bf16[512,768]{1,0:T(8,128)(2,1)S(1)}, bf16[512,1024]{1,0:T(8,128)(2,1)S(1)}, f32[512,768]{1,0:T(8,128)S(1)}, f32[512,...) custom-call(s32[3]{0:T(128)S(1)} %copy-done.23, bf16[512,768]{1,0:T(8,128)(2,1)S(1)} %copy-done.1, ...), custom_call_target="tpu_custom_call" | custom-call | tf_op jit(solution)/shard_map/feed/pallas_call | solution.py:257
  114.4 5.3 %sent.1 = (bf16[4608,256]{1,0:T(8,128)(2,1)}, bf16[1536,256]{1,0:T(8,128)(2,1)S(1)}) custom-call(s32[3]{0:T(128)S(1)} %copy-done.23, bf16[512,768]{1,0:T(8,128)(2,1)S(1)} %get-tuple-element.137.act_ref, bf16[4,512,512]{2,1,0:T(8,128)(2,1)S(1)} %get-tuple-element.141.grad_ref, bf16[512,1024]{1,0:T(8,128)(2,1)S(1)} %get-tuple-element.139.hid_ref, ...), custom_call_target="tpu_custom_call" | custom-call | tf_op jit(solution)/shard_map/sent/pallas_call | solution.py:257
  120.2 2.0 kept.1.keep
  124.5 13.6 %back.1 = (f32[512,768]{1,0:T(8,128)}, bf16[4,512,384]{2,1,0:T(8,128)(2,1)}, f32[3,2,1024]{2,1,0:T(2,128)}, f32[1,768]{1,0:T(1,128)}) custom-call(s32[3]{0:T(128)} %pad_add_fusion.5.scalars, f32[512,768]{1,0:T(8,128)} %copy-done.17, f32[512,768]{1,0:T(8,128)} %copy-done.44, f32[512,768]{1,0:T(8,128)} %copy-done.5, bf16[512,768]{1,0:T(8,128)(2,1)} %copy-done.3, ...), custom_call_target="tpu_custom_call" | custom-call | tf_op jit(solution)/shard_map/back/pallas_call | solution.py:257
  138.1 5.4 %spread_y.1 = (bf16[512,768]{1,0:T(8,128)(2,1)}, bf16[256,768]{1,0:T(8,128)(2,1)}, bf16[256,768]{1,0:T(8,128)(2,1)}) custom-call(s32[3]{0:T(128)} %pad_add_fusion.5.scalars, f32[512,768]{1,0:T(8,128)} %copy-done.5, f32[512,768]{1,0:T(8,128)} %get-tuple-element.147.own_part, f32[512,768]{1,0:T(8,128)} %collective-permute-done.20.other_part, ...), custom_call_target="tpu_custom_call" | custom-call | tf_op jit(solution)/shard_map/spread_y/pallas_call | solution.py:257
  143.5 5.4 %collective-permute-done.21.first = bf16[4608,256]{1,0:T(8,128)(2,1)} collective-permute-done((bf16[4608,256]{1,0:T(8,128)(2,1)}, bf16[4608,256]{1,0:T(8,128)(2,1)}, u32[]{:S(2)}, u32[]{:S(2)}) %collective-permute-start.21) | collective-permute-done | bytes 2359328 | tf_op jit(solution)/shard_map/ppermute | solution.py:213
  148.9 2.8 %pass_ffn.1 = bf16[2304,256]{1,0:T(8,128)(2,1)} custom-call(s32[3]{0:T(128)S(1)} %copy-done.24, bf16[4608,256]{1,0:T(8,128)(2,1)S(1)} %kept.1.keep, bf16[4608,256]{1,0:T(8,128)(2,1)} %collective-permute-done.21.first), custom_call_target="tpu_custom_call" | custom-call | tf_op jit(solution)/shard_map/pass_ffn/pallas_call | solution.py:257
  152.2 1.9 collective-permute-start.22
  154.1 9.0 %last.1 = (bf16[1552,384]{1,0:T(8,128)(2,1)}, bf16[1536,384]{1,0:T(8,128)(2,1)}, f32[512,768]{1,0:T(8,128)}) custom-call(s32[3]{0:T(128)} %pad_add_fusion.5.scalars, bf16[512,768]{1,0:T(8,128)(2,1)} %get-tuple-element.153.act_ref, bf16[512,384]{1,0:T(8,128)(2,1)} %get-tuple-element.128.mix_own, bf16[512,384]{1,0:T(8,128)(2,1)} %copy-done.15, ...), custom_call_target="tpu_custom_call" | custom-call | tf_op jit(solution)/shard_map/last/pallas_call | solution.py:257
  163.3 3.0 %collective-permute-done.22.more_ref = bf16[512,768]{1,0:T(8,128)(2,1)S(1)} collective-permute-done((bf16[512,768]{1,0:T(8,128)(2,1)}, bf16[512,768]{1,0:T(8,128)(2,1)S(1)}, u32[]{:S(2)}, u32[]{:S(2)}) %collective-permute-start.22) | collective-permute-done | bytes 786464 | tf_op jit(solution)/shard_map/ppermute | solution.py:213
  168.8 3.1 %sum_ffn.1 = (f32[576,256]{1,0:T(8,128)S(1)}, bf16[1152,256]{1,0:T(8,128)(2,1)}, f32[576,256]{1,0:T(8,128)S(1)}) custom-call(s32[3]{0:T(128)S(1)} %copy-done.25, bf16[4608,256]{1,0:T(8,128)(2,1)S(1)} %kept.1.keep, bf16[4608,256]{1,0:T(8,128)(2,1)} %collective-permute-done.21.first, bf16[2304,256]{1,0:T(8,128)(2,1)} %collective-permute-done.23.second), custom_call_target="tpu_custom_call" | custom-call | tf_op jit(solution)/shard_map/sum_ffn/pallas_call | solution.py:257
  172.9 5.5 %collective-permute-start.24 = (bf16[256,768]{1,0:T(8,128)(2,1)S(1)}, bf16[256,768]{1,0:T(8,128)(2,1)S(1)}, u32[]{:S(2)}, u32[]{:S(2)}) collective-permute-start(bf16[256,768]{1,0:T(8,128)(2,1)S(1)} %add_rows.2), channel_id=1, source_target_pairs={{0,2},{1,3},{6,4},{7,5},{8,10},{9,11},{14,12},{15,13},{16,18},{17,... | collective-permute-start | bytes 1179656 | tf_op jit(solution)/shard_map/ppermute | solution.py:213
  179.4 8.9 %collective-permute-done.24 = bf16[256,768]{1,0:T(8,128)(2,1)S(1)} collective-permute-done((bf16[256,768]{1,0:T(8,128)(2,1)S(1)}, bf16[256,768]{1,0:T(8,128)(2,1)S(1)}, u32[]{:S(2)}, u32[]{:S(2)}) %collective-permute-start.24) | collective-permute-done | bytes 393248 | tf_op jit(solution)/shard_map/ppermute | solution.py:213
  189.0 6.1 %spread_x.1 = (bf16[512,768]{1,0:T(8,128)(2,1)}, bf16[256,768]{1,0:T(8,128)(2,1)}, bf16[256,768]{1,0:T(8,128)(2,1)}) custom-call(s32[3]{0:T(128)} %pad_add_fusion.5.scalars, f32[512,768]{1,0:T(8,128)} %get-tuple-element.156.own_part, f32[512,768]{1,0:T(8,128)} %collective-permute-done.26.other_part, bf16[512,768]{1,0:T(8,128)(2,1)} %broadcast_select_fusion.1.x_ref, ...), custom_call_target="tpu_custom_call" | custom-call | tf_op jit(solution)/shard_map/spread_x/pallas_call | solution.py:257
  199.3 9.2 %collective-permute-done.28.second = bf16[784,384]{1,0:T(8,128)(2,1)S(1)} collective-permute-done((bf16[784,384]{1,0:T(8,128)(2,1)S(1)}, bf16[784,384]{1,0:T(8,128)(2,1)S(1)}, u32[]{:S(2)}, u32[]{:S(2)}) %collective-permute-start.28) | collective-permute-done | bytes 602144 | tf_op jit(solution)/shard_map/ppermute | solution.py:213
  210.9 2.0 collective-permute-start.32
  212.9 5.4 %collective-permute-done.29.came.near = bf16[416,384]{1,0:T(8,128)(2,1)S(1)} collective-permute-done((bf16[416,384]{1,0:T(8,128)(2,1)S(1)}, bf16[416,384]{1,0:T(8,128)(2,1)S(1)}, u32[]{:S(2)}, u32[]{:S(2)}) %collective-permute-start.29) | collective-permute-done | bytes 319520 | tf_op jit(solution)/shard_map/ppermute | solution.py:213
  219.8 4.8 %collective-permute-start.30 = (bf16[208,384]{1,0:T(8,128)(2,1)S(1)}, bf16[208,384]{1,0:T(8,128)(2,1)S(1)}, u32[]{:S(2)}, u32[]{:S(2)}) collective-permute-start(bf16[208,384]{1,0:T(8,128)(2,1)S(1)} %far_attn.1), channel_id=1, source_target_pairs={{0,3},{1,2},{2,1},{3,0},{4,7},{5,6},{6,5},{7,4},{8,11},{9,10},{10,... | collective-permute-start | bytes 479240 | tf_op jit(solution)/shard_map/ppermute | solution.py:213
  224.6 4.7 %collective-permute-done.30.far = bf16[208,384]{1,0:T(8,128)(2,1)S(1)} collective-permute-done((bf16[208,384]{1,0:T(8,128)(2,1)S(1)}, bf16[208,384]{1,0:T(8,128)(2,1)S(1)}, u32[]{:S(2)}, u32[]{:S(2)}) %collective-permute-start.30) | collective-permute-done | bytes 159776 | tf_op jit(solution)/shard_map/ppermute | solution.py:213
  230.9 7.2 %collective-permute-start.34 = (bf16[512,768]{1,0:T(8,128)(2,1)S(1)}, bf16[512,768]{1,0:T(8,128)(2,1)S(1)}, u32[]{:S(2)}, u32[]{:S(2)}) collective-permute-start(bf16[512,768]{1,0:T(8,128)(2,1)S(1)} %copy-done.55), channel_id=1, source_target_pairs={{0,1},{1,0},{6,7},{7,6},{8,9},{9,8},{14,15},{15,14},{16,17},{17,16... | collective-permute-start | bytes 2359304 | tf_op jit(solution)/shard_map/ppermute | solution.py:213
  238.2 1.5 collective-permute-start.37
  239.7 8.5 %adam_ffin.1 = (f32[2,192,2048]{2,1,0:T(8,128)}, f32[2,192,2048]{2,1,0:T(8,128)}, f32[2,192,2048]{2,1,0:T(8,128)}, bf16[2,192,2048]{2,1,0:T(8,128)(2,1)}) custom-call(s32[3]{0:T(128)} %pad_add_fusion.5.scalars, f32[2,192,2048]{2,1,0:T(8,128)} %refs_0_.3, f32[2,192,2048]{2,1,0:T(8,128)} %refs_1_.3, f32[2,192,2048]{2,1,0:T(8,128)} %refs_2_.3, ...), custom_call_target="tpu_custom_call" | custom-call | tf_op jit(solution)/shard_map/adam_ffin/pallas_call | solution.py:257
  250.1 2.8 %collective-permute-start.36 = (bf16[256,768]{1,0:T(8,128)(2,1)S(1)}, bf16[256,768]{1,0:T(8,128)(2,1)}, u32[]{:S(2)}, u32[]{:S(2)}) collective-permute-start(bf16[256,768]{1,0:T(8,128)(2,1)S(1)} %add_rows.3), channel_id=1, source_target_pairs={{0,2},{1,3},{6,4},{7,5},{8,10},{9,11},{14,12},{15,13},{16,18},{17,... | collective-permute-start | bytes 1179656 | tf_op jit(solution)/shard_map/ppermute | solution.py:213
  252.9 6.2 %adam_ffout.1 = (f32[512,768]{1,0:T(8,128)}, f32[512,768]{1,0:T(8,128)}, f32[512,768]{1,0:T(8,128)}, bf16[512,768]{1,0:T(8,128)(2,1)}) custom-call(s32[3]{0:T(128)} %pad_add_fusion.5.scalars, f32[512,768]{1,0:T(8,128)} %refs_0_.4, f32[512,768]{1,0:T(8,128)} %refs_1_.4, f32[512,768]{1,0:T(8,128)} %refs_2_.4, bf16[4,576,256]{2,1,0:T(8,128)(2,1)} %copy-done.4, ...), custom_call_target="tpu_custom_call" | custom-call | tf_op jit(solution)/shard_map/adam_ffout/pallas_call | solution.py:257
  263.3 1.8 add_bitcast_fusion
  265.9 7.0 %adam_attn.1 = (f32[4,192,768]{2,1,0:T(8,128)}, f32[4,192,768]{2,1,0:T(8,128)}, f32[3,192,768]{2,1,0:T(8,128)}, f32[192,768]{1,0:T(8,128)}, bf16[4,192,768]{2,1,0:T(8,128)(2,1)}) custom-call(s32[3]{0:T(128)} %pad_add_fusion.5.scalars, f32[4,192,768]{2,1,0:T(8,128)} %refs_0_.5, f32[4,192,768]{2,1,0:T(8,128)} %refs_1_.5, f32[4,192,768]{2,1,0:T(8,128)} %refs_2_.5, ...), custom_call_target="tpu_custom_call" | custom-call | tf_op jit(solution)/shard_map/adam_attn/pallas_call | solution.py:257
  (226 shorter events, 47.9 us)
Async XLA Ops:
  3.7 9.9 %collective-permute-start.4 = (bf16[208,384]{1,0:T(8,128)(2,1)}, bf16[208,384]{1,0:T(8,128)(2,1)S(1)}, u32[]{:S(2)}, u32[]{:S(2)}) collective-permute-start(bf16[208,384]{1,0:T(8,128)(2,1)} %pack_attn.1.refs_0_.r0), channel_id=1, source_target_pairs={{0,3},{1,2},{2,1},{3,0},{4,7},{5,6},{6,5},{7,4},{8,11},{9,10},{10,... | collective-permute-start | bytes 479240 | tf_op jit(solution)/shard_map/ppermute | solution.py:213
  8.9 19.5 %collective-permute-start.3 = (s32[1028]{0:T(1024)S(1)}, s32[1028]{0:T(1024)S(1)}, u32[]{:S(2)}, u32[]{:S(2)}) collective-permute-start(s32[1028]{0:T(1024)S(1)} %pad_add_fusion), channel_id=1, source_target_pairs={{0,4},{4,0},{1,5},{5,1},{2,6},{6,2},{3,7},{7,3},{8,12},{12,8},{9,1... | collective-permute-start | bytes 12344 | tf_op jit(solution)/shard_map/ppermute | solution.py:46
  8.9 19.5 %collective-permute-start = (bf16[256,768]{1,0:T(8,128)(2,1)S(1)}, bf16[256,768]{1,0:T(8,128)(2,1)}, u32[]{:S(2)}, u32[]{:S(2)}) collective-permute-start(bf16[256,768]{1,0:T(8,128)(2,1)S(1)} %bitcast.32), channel_id=1, source_target_pairs={{4,5},{5,6},{6,7},{12,13},{13,14},{14,15},{20,21},{21,22},{22,23},... | collective-permute-start | bytes 1179656 | tf_op jit(solution)/shard_map/ppermute | solution.py:213
  13.3 18.6 %copy-start.20 = (bf16[576,256]{1,0:T(8,128)(2,1)S(1)}, bf16[576,256]{1,0:T(8,128)(2,1)}, u32[]{:S(2)}) copy-start(bf16[576,256]{1,0:T(8,128)(2,1)} %pack_ffn.1.refs_0_) | copy-start | bytes 884740
  14.2 12.0 %collective-permute-start.5 = (bf16[2,208,384]{2,1,0:T(8,128)(2,1)S(1)}, bf16[2,208,384]{2,1,0:T(8,128)(2,1)S(1)}, u32[]{:S(2)}, u32[]{:S(2)}) collective-permute-start(bf16[2,208,384]{2,1,0:T(8,128)(2,1)S(1)} %pair_attn_in.1), channel_id=1, source_target_pairs={{0,1},{1,0},{2,3},{3,2},{4,5},{5,4},{6,7},{7,6},{8,9},{9,8},{10,11... | collective-permute-start | bytes 958472 | tf_op jit(solution)/shard_map/ppermute | solution.py:213
  21.4 10.5 %collective-permute-start.7 = (bf16[576,256]{1,0:T(8,128)(2,1)}, bf16[576,256]{1,0:T(8,128)(2,1)S(1)}, u32[]{:S(2)}, u32[]{:S(2)}) collective-permute-start(bf16[576,256]{1,0:T(8,128)(2,1)} %pack_ffn.1.refs_0_), channel_id=1, source_target_pairs={{0,3},{1,2},{2,1},{3,0},{4,7},{5,6},{6,5},{7,4},{8,11},{9,10},{10,... | collective-permute-start | bytes 884744 | tf_op jit(solution)/shard_map/ppermute | solution.py:213
  26.8 8.5 %collective-permute-start.6 = (bf16[3,192,384]{2,1,0:T(8,128)(2,1)S(1)}, bf16[3,192,384]{2,1,0:T(8,128)(2,1)}, u32[]{:S(2)}, u32[]{:S(2)}) collective-permute-start(bf16[3,192,384]{2,1,0:T(8,128)(2,1)S(1)} %near.2.refs_0_), channel_id=1, source_target_pairs={{0,8},{1,9},{2,10},{3,11},{4,20},{5,21},{6,22},{7,23},{8,0},{9,1},... | collective-permute-start | bytes 1327112 | tf_op jit(solution)/shard_map/ppermute | solution.py:213
  28.4 12.6 %collective-permute-start.1 = (bf16[256,768]{1,0:T(8,128)(2,1)}, bf16[256,768]{1,0:T(8,128)(2,1)S(1)}, u32[]{:S(2)}, u32[]{:S(2)}) collective-permute-start(bf16[256,768]{1,0:T(8,128)(2,1)} %collective-permute-done.b1), channel_id=1, source_target_pairs={{5,6},{6,7},{13,14},{14,15},{21,22},{22,23},{29,30},{30,31},{2,1},... | collective-permute-start | bytes 1179656 | tf_op jit(solution)/shard_map/ppermute | solution.py:213
  36.4 22.5 %copy-start.8 = (bf16[6,192,384]{2,1,0:T(8,128)(2,1)}, bf16[6,192,384]{2,1,0:T(8,128)(2,1)S(1)}, u32[]{:S(2)}) copy-start(bf16[6,192,384]{2,1,0:T(8,128)(2,1)S(1)} %nearest.2.near_ref) | copy-start | bytes 2654212
  36.4 22.5 %collective-permute-start.8 = (bf16[6,192,384]{2,1,0:T(8,128)(2,1)S(1)}, bf16[6,192,384]{2,1,0:T(8,128)(2,1)S(1)}, u32[]{:S(2)}, u32[]{:S(2)}) collective-permute-start(bf16[6,192,384]{2,1,0:T(8,128)(2,1)S(1)} %nearest.2.near_ref), channel_id=1, source_target_pairs={{0,16},{1,17},{2,18},{3,19},{4,12},{5,13},{6,14},{7,15},{8,24},{9,... | collective-permute-start | bytes 2654216 | tf_op jit(solution)/shard_map/ppermute | solution.py:213
  38.6 20.3 %collective-permute-start.9 = (bf16[2,576,256]{2,1,0:T(8,128)(2,1)S(1)}, bf16[2,576,256]{2,1,0:T(8,128)(2,1)S(1)}, u32[]{:S(2)}, u32[]{:S(2)}) collective-permute-start(bf16[2,576,256]{2,1,0:T(8,128)(2,1)S(1)} %pair_ffn_in.1), channel_id=1, source_target_pairs={{0,1},{1,0},{2,3},{3,2},{4,5},{5,4},{6,7},{7,6},{8,9},{9,8},{10,11... | collective-permute-start | bytes 1769480 | tf_op jit(solution)/shard_map/ppermute | solution.py:213
  41.0 15.6 %collective-permute-start.2 = (bf16[256,768]{1,0:T(8,128)(2,1)S(1)}, bf16[256,768]{1,0:T(8,128)(2,1)S(1)}, u32[]{:S(2)}, u32[]{:S(2)}) collective-permute-start(bf16[256,768]{1,0:T(8,128)(2,1)S(1)} %broadcast_select_fusion.2), channel_id=1, source_target_pairs={{6,7},{7,6},{14,15},{15,14},{22,23},{23,22},{30,31},{31,30},{1,0},... | collective-permute-start | bytes 1179656 | tf_op jit(solution)/shard_map/ppermute | solution.py:213
  58.9 3.4 %collective-permute-start.10 = (bf16[512,768]{1,0:T(8,128)(2,1)S(1)}, bf16[512,768]{1,0:T(8,128)(2,1)S(1)}, u32[]{:S(2)}, u32[]{:S(2)}) collective-permute-start(bf16[512,768]{1,0:T(8,128)(2,1)S(1)} %pick.2), channel_id=1, source_target_pairs={{0,4},{4,0},{1,5},{5,1},{2,6},{6,2},{3,7},{7,3},{8,12},{12,8},{9,1... | collective-permute-start | bytes 2359304 | tf_op jit(solution)/shard_map/ppermute | solution.py:46
  59.6 13.1 %collective-permute-start.11 = (bf16[3,576,256]{2,1,0:T(8,128)(2,1)S(1)}, bf16[3,576,256]{2,1,0:T(8,128)(2,1)S(1)}, u32[]{:S(2)}, u32[]{:S(2)}) collective-permute-start(bf16[3,576,256]{2,1,0:T(8,128)(2,1)S(1)} %near.3.refs_0_), channel_id=1, source_target_pairs={{0,8},{1,9},{2,10},{3,11},{4,20},{5,21},{6,22},{7,23},{8,0},{9,1},... | collective-permute-start | bytes 2654216 | tf_op jit(solution)/shard_map/ppermute | solution.py:213
  60.2 9.9 %collective-permute-start.12 = (bf16[256,768]{1,0:T(8,128)(2,1)}, bf16[256,768]{1,0:T(8,128)(2,1)S(1)}, u32[]{:S(2)}, u32[]{:S(2)}) collective-permute-start(bf16[256,768]{1,0:T(8,128)(2,1)} %bitcast.18.b0), channel_id=1, source_target_pairs={{5,6},{6,7},{13,14},{14,15},{21,22},{22,23},{29,30},{30,31},{2,1},... | collective-permute-start | bytes 1179656 | tf_op jit(solution)/shard_map/ppermute | solution.py:213
  74.6 21.6 %copy-start.23 = (s32[3]{0:T(128)S(1)}, s32[3]{0:T(128)}, u32[]{:S(2)}) copy-start(s32[3]{0:T(128)} %pad_add_fusion.5.scalars) | copy-start | bytes 40
  74.6 28.2 %collective-permute-start.18 = (bf16[6,576,256]{2,1,0:T(8,128)(2,1)}, bf16[6,576,256]{2,1,0:T(8,128)(2,1)}, u32[]{:S(2)}, u32[]{:S(2)}) collective-permute-start(bf16[6,576,256]{2,1,0:T(8,128)(2,1)} %nearest.3.near_ref), channel_id=1, source_target_pairs={{0,16},{1,17},{2,18},{3,19},{4,12},{5,13},{6,14},{7,15},{8,24},{9,... | collective-permute-start | bytes 5308424 | tf_op jit(solution)/shard_map/ppermute | solution.py:213
  76.1 20.0 %collective-permute-start.16 = (bf16[256,768]{1,0:T(8,128)(2,1)}, bf16[256,768]{1,0:T(8,128)(2,1)S(1)}, u32[]{:S(2)}, u32[]{:S(2)}) collective-permute-start(bf16[256,768]{1,0:T(8,128)(2,1)} %bitcast.18.b0), channel_id=1, source_target_pairs={{4,7},{7,6},{12,15},{15,14},{20,23},{23,22},{28,31},{31,30},{3,0},... | collective-permute-start | bytes 1179656 | tf_op jit(solution)/shard_map/ppermute | solution.py:213
  79.7 16.4 %collective-permute-start.15 = (bf16[256,768]{1,0:T(8,128)(2,1)}, bf16[256,768]{1,0:T(8,128)(2,1)S(1)}, u32[]{:S(2)}, u32[]{:S(2)}) collective-permute-start(bf16[256,768]{1,0:T(8,128)(2,1)} %bitcast.18.b0), channel_id=1, source_target_pairs={{4,6},{5,7},{12,14},{13,15},{20,22},{21,23},{28,30},{29,31},{3,1},... | collective-permute-start | bytes 1179656 | tf_op jit(solution)/shard_map/ppermute | solution.py:213
  98.6 2.4 collective-permute-start.17
  100.0 13.9 %copy-start.6 = (bf16[768,384]{1,0:T(8,128)(2,1)}, bf16[768,384]{1,0:T(8,128)(2,1)S(1)}, u32[]{:S(2)}) copy-start(bf16[768,384]{1,0:T(8,128)(2,1)S(1)} %slice_bitcast_fusion.w_attn.w_ref) | copy-start | bytes 1769476
  100.0 2.7 %collective-permute-start.14 = (bf16[768,384]{1,0:T(8,128)(2,1)S(1)}, bf16[768,384]{1,0:T(8,128)(2,1)S(1)}, u32[]{:S(2)}, u32[]{:S(2)}) collective-permute-start(bf16[768,384]{1,0:T(8,128)(2,1)S(1)} %slice_bitcast_fusion.w_attn.w_ref), channel_id=1, source_target_pairs={{0,4},{4,0},{1,5},{5,1},{2,6},{6,2},{3,7},{7,3},{8,12},{12,8},{9,1... | collective-permute-start | bytes 1769480 | tf_op jit(solution)/shard_map/ppermute | solution.py:46
  100.6 2.2 collective-permute-start.13
  101.1 13.4 %copy-start.3 = (bf16[512,768]{1,0:T(8,128)(2,1)}, bf16[512,768]{1,0:T(8,128)(2,1)S(1)}, u32[]{:S(2)}) copy-start(bf16[512,768]{1,0:T(8,128)(2,1)S(1)} %broadcast_select_fusion.gy_ref) | copy-start | bytes 2359300
  114.0 8.3 %collective-permute-start.19 = (f32[512,768]{1,0:T(8,128)S(1)}, f32[512,768]{1,0:T(8,128)S(1)}, u32[]{:S(2)}, u32[]{:S(2)}) collective-permute-start(f32[512,768]{1,0:T(8,128)S(1)} %get-tuple-element.136.own_part), channel_id=1, source_target_pairs={{0,4},{4,0},{1,5},{5,1},{2,6},{6,2},{3,7},{7,3},{8,12},{12,8},{9,1... | collective-permute-start | bytes 4718600 | tf_op jit(solution)/shard_map/ppermute | solution.py:46
  119.7 29.2 %collective-permute-start.21 = (bf16[4608,256]{1,0:T(8,128)(2,1)}, bf16[4608,256]{1,0:T(8,128)(2,1)}, u32[]{:S(2)}, u32[]{:S(2)}) collective-permute-start(bf16[4608,256]{1,0:T(8,128)(2,1)} %get-tuple-element.140), channel_id=1, source_target_pairs={{0,8},{1,9},{2,10},{3,11},{4,20},{5,21},{6,22},{7,23},{8,0},{9,1},... | collective-permute-start | bytes 7077896 | tf_op jit(solution)/shard_map/ppermute | solution.py:213
  123.4 14.6 %collective-permute-start.20 = (f32[512,768]{1,0:T(8,128)}, f32[512,768]{1,0:T(8,128)}, u32[]{:S(2)}, u32[]{:S(2)}) collective-permute-start(f32[512,768]{1,0:T(8,128)} %get-tuple-element.147.own_part), channel_id=1, source_target_pairs={{0,4},{4,0},{1,5},{5,1},{2,6},{6,2},{3,7},{7,3},{8,12},{12,8},{9,1... | collective-permute-start | bytes 4718600 | tf_op jit(solution)/shard_map/ppermute | solution.py:46
  151.7 16.5 %collective-permute-start.23 = (bf16[2304,256]{1,0:T(8,128)(2,1)}, bf16[2304,256]{1,0:T(8,128)(2,1)}, u32[]{:S(2)}, u32[]{:S(2)}) collective-permute-start(bf16[2304,256]{1,0:T(8,128)(2,1)} %pass_ffn.1), channel_id=1, source_target_pairs={{0,16},{1,17},{2,18},{3,19},{4,12},{5,13},{6,14},{7,15},{8,24},{9,... | collective-permute-start | bytes 3538952 | tf_op jit(solution)/shard_map/ppermute | solution.py:213
  152.2 14.1 %collective-permute-start.22 = (bf16[512,768]{1,0:T(8,128)(2,1)}, bf16[512,768]{1,0:T(8,128)(2,1)S(1)}, u32[]{:S(2)}, u32[]{:S(2)}) collective-permute-start(bf16[512,768]{1,0:T(8,128)(2,1)} %get-tuple-element.151), channel_id=1, source_target_pairs={{0,1},{1,0},{6,7},{7,6},{8,9},{9,8},{14,15},{15,14},{16,17},{17,16... | collective-permute-start | bytes 2359304 | tf_op jit(solution)/shard_map/ppermute | solution.py:213
  154.1 14.6 %copy-start.25 = (s32[3]{0:T(128)S(1)}, s32[3]{0:T(128)}, u32[]{:S(2)}) copy-start(s32[3]{0:T(128)} %pad_add_fusion.5.scalars) | copy-start | bytes 40
  163.2 25.1 %collective-permute-start.26 = (f32[512,768]{1,0:T(8,128)}, f32[512,768]{1,0:T(8,128)}, u32[]{:S(2)}, u32[]{:S(2)}) collective-permute-start(f32[512,768]{1,0:T(8,128)} %get-tuple-element.156.own_part), channel_id=1, source_target_pairs={{0,4},{4,0},{1,5},{5,1},{2,6},{6,2},{3,7},{7,3},{8,12},{12,8},{9,1... | collective-permute-start | bytes 4718600 | tf_op jit(solution)/shard_map/ppermute | solution.py:46
  168.2 27.6 %collective-permute-start.27 = (bf16[1552,384]{1,0:T(8,128)(2,1)}, bf16[1552,384]{1,0:T(8,128)(2,1)S(1)}, u32[]{:S(2)}, u32[]{:S(2)}) collective-permute-start(bf16[1552,384]{1,0:T(8,128)(2,1)} %get-tuple-element.171.sent), channel_id=1, source_target_pairs={{0,8},{1,9},{2,10},{3,11},{4,20},{5,21},{6,22},{7,23},{8,0},{9,1},... | collective-permute-start | bytes 3575816 | tf_op jit(solution)/shard_map/ppermute | solution.py:213
  171.9 23.3 %collective-permute-start.25 = (bf16[1152,256]{1,0:T(8,128)(2,1)}, bf16[1152,256]{1,0:T(8,128)(2,1)S(1)}, u32[]{:S(2)}, u32[]{:S(2)}) collective-permute-start(bf16[1152,256]{1,0:T(8,128)(2,1)} %get-tuple-element.160), channel_id=1, source_target_pairs={{0,1},{1,0},{2,3},{3,2},{4,5},{5,4},{6,7},{7,6},{8,9},{9,8},{10,11... | collective-permute-start | bytes 1769480 | tf_op jit(solution)/shard_map/ppermute | solution.py:213
  172.9 15.4 %collective-permute-start.24 = (bf16[256,768]{1,0:T(8,128)(2,1)S(1)}, bf16[256,768]{1,0:T(8,128)(2,1)S(1)}, u32[]{:S(2)}, u32[]{:S(2)}) collective-permute-start(bf16[256,768]{1,0:T(8,128)(2,1)S(1)} %add_rows.2), channel_id=1, source_target_pairs={{0,2},{1,3},{6,4},{7,5},{8,10},{9,11},{14,12},{15,13},{16,18},{17,... | collective-permute-start | bytes 1179656 | tf_op jit(solution)/shard_map/ppermute | solution.py:213
  198.4 11.8 %copy-start.32 = (f32[576,256]{1,0:T(8,128)S(1)}, f32[576,256]{1,0:T(8,128)}, u32[]{:S(2)}) copy-start(f32[576,256]{1,0:T(8,128)} %copy-done.31) | copy-start | bytes 1769476
  198.4 10.1 %collective-permute-start.28 = (bf16[784,384]{1,0:T(8,128)(2,1)S(1)}, bf16[784,384]{1,0:T(8,128)(2,1)S(1)}, u32[]{:S(2)}, u32[]{:S(2)}) collective-permute-start(bf16[784,384]{1,0:T(8,128)(2,1)S(1)} %pass_attn.1.passed), channel_id=1, source_target_pairs={{0,16},{1,17},{2,18},{3,19},{4,12},{5,13},{6,14},{7,15},{8,24},{9,... | collective-permute-start | bytes 1806344 | tf_op jit(solution)/shard_map/ppermute | solution.py:213
  199.3 11.0 %collective-permute-start.31 = (bf16[576,256]{1,0:T(8,128)(2,1)S(1)}, bf16[576,256]{1,0:T(8,128)(2,1)S(1)}, u32[]{:S(2)}, u32[]{:S(2)}) collective-permute-start(bf16[576,256]{1,0:T(8,128)(2,1)S(1)} %far_ffn.1), channel_id=1, source_target_pairs={{0,3},{1,2},{2,1},{3,0},{4,7},{5,6},{6,5},{7,4},{8,11},{9,10},{10,... | collective-permute-start | bytes 884744 | tf_op jit(solution)/shard_map/ppermute | solution.py:213
  209.3 9.0 %collective-permute-start.29 = (bf16[416,384]{1,0:T(8,128)(2,1)S(1)}, bf16[416,384]{1,0:T(8,128)(2,1)S(1)}, u32[]{:S(2)}, u32[]{:S(2)}) collective-permute-start(bf16[416,384]{1,0:T(8,128)(2,1)S(1)} %get-tuple-element.174), channel_id=1, source_target_pairs={{0,1},{1,0},{2,3},{3,2},{4,5},{5,4},{6,7},{7,6},{8,9},{9,8},{10,11... | collective-permute-start | bytes 958472 | tf_op jit(solution)/shard_map/ppermute | solution.py:213
  210.9 8.0 %collective-permute-start.32 = (bf16[576,256]{1,0:T(8,128)(2,1)S(1)}, bf16[576,256]{1,0:T(8,128)(2,1)S(1)}, u32[]{:S(2)}, u32[]{:S(2)}) collective-permute-start(bf16[576,256]{1,0:T(8,128)(2,1)S(1)} %total_ffn.1.refs_0_), channel_id=1, source_target_pairs={{0,8},{1,9},{2,10},{3,11},{4,20},{5,21},{6,22},{7,23},{8,0},{9,1},... | collective-permute-start | bytes 884744 | tf_op jit(solution)/shard_map/ppermute | solution.py:213
  219.5 9.9 %collective-permute-start.33 = (bf16[2,576,256]{2,1,0:T(8,128)(2,1)S(1)}, bf16[2,576,256]{2,1,0:T(8,128)(2,1)S(1)}, u32[]{:S(2)}, u32[]{:S(2)}) collective-permute-start(bf16[2,576,256]{2,1,0:T(8,128)(2,1)S(1)} %pair_ffn.1.refs_0_), channel_id=1, source_target_pairs={{0,16},{1,17},{2,18},{3,19},{4,12},{5,13},{6,14},{7,15},{8,24},{9,... | collective-permute-start | bytes 1769480 | tf_op jit(solution)/shard_map/ppermute | solution.py:213
  219.8 9.5 %collective-permute-start.30 = (bf16[208,384]{1,0:T(8,128)(2,1)S(1)}, bf16[208,384]{1,0:T(8,128)(2,1)S(1)}, u32[]{:S(2)}, u32[]{:S(2)}) collective-permute-start(bf16[208,384]{1,0:T(8,128)(2,1)S(1)} %far_attn.1), channel_id=1, source_target_pairs={{0,3},{1,2},{2,1},{3,0},{4,7},{5,6},{6,5},{7,4},{8,11},{9,10},{10,... | collective-permute-start | bytes 479240 | tf_op jit(solution)/shard_map/ppermute | solution.py:213
  230.1 9.6 %collective-permute-start.35 = (bf16[4,576,256]{2,1,0:T(8,128)(2,1)S(1)}, bf16[4,576,256]{2,1,0:T(8,128)(2,1)}, u32[]{:S(2)}, u32[]{:S(2)}) collective-permute-start(bf16[4,576,256]{2,1,0:T(8,128)(2,1)S(1)} %stack_ffn.1.refs_3_), channel_id=1, source_target_pairs={{0,4},{4,0},{1,5},{5,1},{2,6},{6,2},{3,7},{7,3},{8,12},{12,8},{9,1... | collective-permute-start | bytes 3538952 | tf_op jit(solution)/shard_map/ppermute | solution.py:46
  230.9 18.6 %collective-permute-start.34 = (bf16[512,768]{1,0:T(8,128)(2,1)S(1)}, bf16[512,768]{1,0:T(8,128)(2,1)S(1)}, u32[]{:S(2)}, u32[]{:S(2)}) collective-permute-start(bf16[512,768]{1,0:T(8,128)(2,1)S(1)} %copy-done.55), channel_id=1, source_target_pairs={{0,1},{1,0},{6,7},{7,6},{8,9},{9,8},{14,15},{15,14},{16,17},{17,16... | collective-permute-start | bytes 2359304 | tf_op jit(solution)/shard_map/ppermute | solution.py:213
  238.2 10.0 %collective-permute-start.37 = (bf16[192,384]{1,0:T(8,128)(2,1)S(1)}, bf16[192,384]{1,0:T(8,128)(2,1)S(1)}, u32[]{:S(2)}, u32[]{:S(2)}) collective-permute-start(bf16[192,384]{1,0:T(8,128)(2,1)S(1)} %get-tuple-element.189.refs_0_), channel_id=1, source_target_pairs={{0,8},{1,9},{2,10},{3,11},{4,20},{5,21},{6,22},{7,23},{8,0},{9,1},... | collective-permute-start | bytes 442376 | tf_op jit(solution)/shard_map/ppermute | solution.py:213
  248.8 10.4 %collective-permute-start.38 = (bf16[2,192,384]{2,1,0:T(8,128)(2,1)S(1)}, bf16[2,192,384]{2,1,0:T(8,128)(2,1)S(1)}, u32[]{:S(2)}, u32[]{:S(2)}) collective-permute-start(bf16[2,192,384]{2,1,0:T(8,128)(2,1)S(1)} %pair_attn.1.refs_0_), channel_id=1, source_target_pairs={{0,16},{1,17},{2,18},{3,19},{4,12},{5,13},{6,14},{7,15},{8,24},{9,... | collective-permute-start | bytes 884744 | tf_op jit(solution)/shard_map/ppermute | solution.py:213
  250.1 13.2 %collective-permute-start.36 = (bf16[256,768]{1,0:T(8,128)(2,1)S(1)}, bf16[256,768]{1,0:T(8,128)(2,1)}, u32[]{:S(2)}, u32[]{:S(2)}) collective-permute-start(bf16[256,768]{1,0:T(8,128)(2,1)S(1)} %add_rows.3), channel_id=1, source_target_pairs={{0,2},{1,3},{6,4},{7,5},{8,10},{9,11},{14,12},{15,13},{16,18},{17,... | collective-permute-start | bytes 1179656 | tf_op jit(solution)/shard_map/ppermute | solution.py:213
  259.8 5.3 %collective-permute-start.39 = (bf16[4,192,384]{2,1,0:T(8,128)(2,1)S(1)}, bf16[4,192,384]{2,1,0:T(8,128)(2,1)S(1)}, u32[]{:S(2)}, u32[]{:S(2)}) collective-permute-start(bf16[4,192,384]{2,1,0:T(8,128)(2,1)S(1)} %stack_attn.1.refs_3_), channel_id=1, source_target_pairs={{0,4},{4,0},{1,5},{5,1},{2,6},{6,2},{3,7},{7,3},{8,12},{12,8},{9,1... | collective-permute-start | bytes 1769480 | tf_op jit(solution)/shard_map/ppermute | solution.py:46
  259.9 2.0 collective-permute-start.40
  (49 other events, 264.9 us)

commit v5 on v4

--- a/solution.py
+++ b/solution.py
@@ -1057,7 +1057,6 @@
         [((576, 256), full), ((1152, 256), low), ((576, 256), full)], [], "sum_ffn", 0, 8,
     )
     ffn_near = across(ffn_two, 1)
-    y_far = rows_far(y_rows, after(y_near, ffn_two))
     x_rows = call(
         spread_x_kernel, spot,
         [(part_one,), (swap(part_one),), (x_low,), gains, (grad_mid,), wanted_x, token_row],
@@ -1070,10 +1069,8 @@
     )
     ffn_send = call(far_kernel, spot, [ffn_far, after(ffn_near, *x_rows)], [((576, 256), low)], [], "far_ffn", 0, 8)[0]
     ffn_last = across(ffn_send, 3)
-    y_far = after(y_far, ffn_send)
-    attn_first_came = after(plane_first(after(attn_send, ffn_second)), ffn_send, y_far, *x_rows)
+    attn_first_came = after(plane_first(after(attn_send, ffn_second)), ffn_send, *x_rows)
     passed = one_out(pass_attn_kernel, [attn_keep, attn_send, attn_first_came], (784, 384), "pass_attn")
-    layer_out = y_rows[1] + y_near[:256] + y_far
     attn_second_came = plane_second(passed)
     attn_own, attn_two, attn_far = call(
         sum_attn_kernel, spot, [attn_keep, passed, attn_first_came, attn_second_came],
@@ -1105,6 +1102,8 @@
     attn_stack = cat(spot, [attn_near, after(plane_second(attn_near), ffout_res[0])], 192, "stack_attn")
     attn_sum = (attn_stack, swap(attn_stack))
     x_rows = [after(value, small) for value in x_rows]
+    y_far = rows_far(y_rows, after(y_near, small), ffin_res[0])
+    layer_out = y_rows[1] + y_near[:256] + y_far
     input_grad, _ = rows_back(x_rows, ffin_res[0], ffout_res[0])
     small_other = swap(small)
     square = (4, 192, 768)

time: 274 us -> 268 us (0.978)
  waiting for transfers between devices: 63.8 us -> 56.6 us
    ppermute x30, waiting for transfers between devices: 61.1 us -> 53 us  [send(): lax.ppermute(value, ('plane', 'core', 'shard'), [((p * 2 + c) * 4 + z, (q...]
    unnamed x112 -> x102, local copies, waits for them, and re-layouts: 6.03 us -> 5.96 us
  transfers between devices with their start and end apart: 41 -> 41, of which waited for: 19 -> 20; matrix products, arithmetic and copies ran while one was open for 5% -> 5% of each run, Pallas kernels for 35% -> 36%
where the time goes in v5:
time: 268 us; the launch traced here: 267 us
  Pallas kernels  124 us (46%)
  starting transfers between devices  60.9 us (23%)
  waiting for transfers between devices  56.6 us (21%)
  local copies, waits for them, and re-layouts  12.2 us (5%)
  other arithmetic  8.69 us (3%)
  between operations  4.47 us (2%)
    pallas_call x38, Pallas kernels, call(): pl.pallas_call(kernel, in_specs=[pl.BlockSpec(memory_space=pltpu.SMEM)] +...  124 us
    ppermute x30, starting transfers between devices, send(): lax.ppermute(value, ('plane', 'core', 'shard'), [((p * 2 + c) * 4 + z, (q...  59 us
    ppermute x30, waiting for transfers between devices, send(): lax.ppermute(value, ('plane', 'core', 'shard'), [((p * 2 + c) * 4 + z, (q...  53 us
    unnamed x102, local copies, waits for them, and re-layouts  5.96 us
  transfers between devices with their start and end apart: 41, of which 20 were waited for; matrix products, arithmetic and copies ran while one was open for 5% of the time, Pallas kernels for 36%

profile of v5, /device:TPU:0, one launch (start us, length us, event | category | flops | bytes accessed | tf_op | source)
XLA Modules:
  0.0 266.8 jit_solution(14374351632315534557)
XLA Ops:
  1.3 2.3 pack_attn.1.refs_0_.r0
  3.7 5.1 %collective-permute-start.4 = (bf16[208,384]{1,0:T(8,128)(2,1)}, bf16[208,384]{1,0:T(8,128)(2,1)S(1)}, u32[]{:S(2)}, u32[]{:S(2)}) collective-permute-start(bf16[208,384]{1,0:T(8,128)(2,1)} %pack_attn.1.refs_0_.r0), channel_id=1, source_target_pairs={{0,3},{1,2},{2,1},{3,0},{4,7},{5,6},{6,5},{7,4},{8,11},{9,10},{10,... | collective-permute-start | bytes 479240 | tf_op jit(solution)/shard_map/ppermute | solution.py:213
  10.5 2.7 %pack_ffn.1.refs_0_ = bf16[576,256]{1,0:T(8,128)(2,1)} custom-call(s32[3]{0:T(128)} %pad_add_fusion.5.scalars, f32[2,192,2048]{2,1,0:T(8,128)} %refs_0_.3, f32[512,768]{1,0:T(8,128)} %refs_0_.4), custom_call_target="tpu_custom_call" | custom-call | tf_op jit(solution)/shard_map/pack_ffn/pallas_call | solution.py:257
  14.2 3.0 %collective-permute-start.5 = (bf16[2,208,384]{2,1,0:T(8,128)(2,1)S(1)}, bf16[2,208,384]{2,1,0:T(8,128)(2,1)S(1)}, u32[]{:S(2)}, u32[]{:S(2)}) collective-permute-start(bf16[2,208,384]{2,1,0:T(8,128)(2,1)S(1)} %pair_attn_in.1), channel_id=1, source_target_pairs={{0,1},{1,0},{2,3},{3,2},{4,5},{5,4},{6,7},{7,6},{8,9},{9,8},{10,11... | collective-permute-start | bytes 958472 | tf_op jit(solution)/shard_map/ppermute | solution.py:213
  21.4 3.3 %collective-permute-start.7 = (bf16[576,256]{1,0:T(8,128)(2,1)}, bf16[576,256]{1,0:T(8,128)(2,1)S(1)}, u32[]{:S(2)}, u32[]{:S(2)}) collective-permute-start(bf16[576,256]{1,0:T(8,128)(2,1)} %pack_ffn.1.refs_0_), channel_id=1, source_target_pairs={{0,3},{1,2},{2,1},{3,0},{4,7},{5,6},{6,5},{7,4},{8,11},{9,10},{10,... | collective-permute-start | bytes 884744 | tf_op jit(solution)/shard_map/ppermute | solution.py:213
  29.9 2.0 collective-permute-done.7.refs_1_
  32.5 2.8 %collective-permute-done.6.refs_1_ = bf16[3,192,384]{2,1,0:T(8,128)(2,1)} collective-permute-done((bf16[3,192,384]{2,1,0:T(8,128)(2,1)S(1)}, bf16[3,192,384]{2,1,0:T(8,128)(2,1)}, u32[]{:S(2)}, u32[]{:S(2)}) %collective-permute-start.6) | collective-permute-done | bytes 442400 | tf_op jit(solution)/shard_map/ppermute | solution.py:213
  36.4 1.6 collective-permute-start.8
  38.6 2.4 collective-permute-start.9
  41.0 1.9 collective-permute-start.2
  45.1 11.5 %collective-permute-done.2.b3 = bf16[256,768]{1,0:T(8,128)(2,1)S(1)} collective-permute-done((bf16[256,768]{1,0:T(8,128)(2,1)S(1)}, bf16[256,768]{1,0:T(8,128)(2,1)S(1)}, u32[]{:S(2)}, u32[]{:S(2)}) %collective-permute-start.2) | collective-permute-done | bytes 393248 | tf_op jit(solution)/shard_map/ppermute | solution.py:213
  56.6 2.3 pick.2
  63.4 5.2 %project.1 = (bf16[4,768,384]{2,1,0:T(8,128)(2,1)}, bf16[512,768]{1,0:T(8,128)(2,1)}, bf16[512,384]{1,0:T(8,128)(2,1)}, bf16[512,384]{1,0:T(8,128)(2,1)}, bf16[512,384]{1,0:T(8,128)(2,1)}) custom-call(s32[3]{0:T(128)} %pad_add_fusion.5.scalars, bf16[512,768]{1,0:T(8,128)(2,1)} %broadcast_select_fusion.1.x_ref, f32[2,768]{1,0:T(2,128)} %copy-done.34, ...), custom_call_target="tpu_custom_call" | custom-call | tf_op jit(solution)/shard_map/project/pallas_call | solution.py:257
  70.1 2.6 collective-permute-done.11.refs_1_
  72.7 1.9 nearest.3.near_ref
  76.1 3.6 %collective-permute-start.16 = (bf16[256,768]{1,0:T(8,128)(2,1)}, bf16[256,768]{1,0:T(8,128)(2,1)S(1)}, u32[]{:S(2)}, u32[]{:S(2)}) collective-permute-start(bf16[256,768]{1,0:T(8,128)(2,1)} %bitcast.18.b0), channel_id=1, source_target_pairs={{4,7},{7,6},{12,15},{15,14},{20,23},{23,22},{28,31},{31,30},{3,0},... | collective-permute-start | bytes 1179656 | tf_op jit(solution)/shard_map/ppermute | solution.py:213
  82.9 13.3 %attend.1 = (bf16[512,384]{1,0:T(8,128)(2,1)}, bf16[6,512,512]{2,1,0:T(8,128)(2,1)}) custom-call(s32[3]{0:T(128)} %pad_add_fusion.5.scalars, bf16[512,384]{1,0:T(8,128)(2,1)} %get-tuple-element.124.q_ref, bf16[512,384]{1,0:T(8,128)(2,1)} %get-tuple-element.125.k_ref, bf16[512,384]{1,0:T(8,128)(2,1)} %get-tuple-element.126.v_ref, s32[512,1]{1,0:T(8,128)} %copy.43.qseg_ref, ...), custom_call_target="tpu_custom_call" | custom-call | tf_op jit(solution)/shard_map/attend/pallas_call | solution.py:257
  96.2 2.4 pick.3
  101.1 1.7 collective-permute-done.13.mix_other
  102.8 11.1 %feed.1 = (f32[512,768]{1,0:T(8,128)S(1)}, bf16[512,768]{1,0:T(8,128)(2,1)S(1)}, bf16[512,1024]{1,0:T(8,128)(2,1)S(1)}, f32[512,768]{1,0:T(8,128)S(1)}, f32[512,...) custom-call(s32[3]{0:T(128)S(1)} %copy-done.22, bf16[512,768]{1,0:T(8,128)(2,1)S(1)} %copy-done.1, ...), custom_call_target="tpu_custom_call" | custom-call | tf_op jit(solution)/shard_map/feed/pallas_call | solution.py:257
  114.4 5.3 %sent.1 = (bf16[4608,256]{1,0:T(8,128)(2,1)}, bf16[1536,256]{1,0:T(8,128)(2,1)S(1)}) custom-call(s32[3]{0:T(128)S(1)} %copy-done.22, bf16[512,768]{1,0:T(8,128)(2,1)S(1)} %get-tuple-element.137.act_ref, bf16[4,512,512]{2,1,0:T(8,128)(2,1)S(1)} %get-tuple-element.141.grad_ref, bf16[512,1024]{1,0:T(8,128)(2,1)S(1)} %get-tuple-element.139.hid_ref, ...), custom_call_target="tpu_custom_call" | custom-call | tf_op jit(solution)/shard_map/sent/pallas_call | solution.py:257
  120.3 2.0 kept.1.keep
  124.5 13.6 %back.1 = (f32[512,768]{1,0:T(8,128)}, bf16[4,512,384]{2,1,0:T(8,128)(2,1)}, f32[3,2,1024]{2,1,0:T(2,128)}, f32[1,768]{1,0:T(1,128)}) custom-call(s32[3]{0:T(128)} %pad_add_fusion.5.scalars, f32[512,768]{1,0:T(8,128)} %copy-done.16, f32[512,768]{1,0:T(8,128)} %copy-done.43, f32[512,768]{1,0:T(8,128)} %copy-done.5, bf16[512,768]{1,0:T(8,128)(2,1)} %copy-done.3, ...), custom_call_target="tpu_custom_call" | custom-call | tf_op jit(solution)/shard_map/back/pallas_call | solution.py:257
  138.1 5.4 %spread_y.1 = (bf16[512,768]{1,0:T(8,128)(2,1)}, bf16[256,768]{1,0:T(8,128)(2,1)}, bf16[256,768]{1,0:T(8,128)(2,1)}) custom-call(s32[3]{0:T(128)} %pad_add_fusion.5.scalars, f32[512,768]{1,0:T(8,128)} %copy-done.5, f32[512,768]{1,0:T(8,128)} %get-tuple-element.147.own_part, f32[512,768]{1,0:T(8,128)} %collective-permute-done.20.other_part, ...), custom_call_target="tpu_custom_call" | custom-call | tf_op jit(solution)/shard_map/spread_y/pallas_call | solution.py:257
  143.5 5.4 %collective-permute-done.21.first = bf16[4608,256]{1,0:T(8,128)(2,1)} collective-permute-done((bf16[4608,256]{1,0:T(8,128)(2,1)}, bf16[4608,256]{1,0:T(8,128)(2,1)}, u32[]{:S(2)}, u32[]{:S(2)}) %collective-permute-start.21) | collective-permute-done | bytes 2359328 | tf_op jit(solution)/shard_map/ppermute | solution.py:213
  148.9 2.8 %pass_ffn.1 = bf16[2304,256]{1,0:T(8,128)(2,1)} custom-call(s32[3]{0:T(128)S(1)} %copy-done.23, bf16[4608,256]{1,0:T(8,128)(2,1)S(1)} %kept.1.keep, bf16[4608,256]{1,0:T(8,128)(2,1)} %collective-permute-done.21.first), custom_call_target="tpu_custom_call" | custom-call | tf_op jit(solution)/shard_map/pass_ffn/pallas_call | solution.py:257
  152.2 1.9 collective-permute-start.22
  154.1 9.0 %last.1 = (bf16[1552,384]{1,0:T(8,128)(2,1)}, bf16[1536,384]{1,0:T(8,128)(2,1)}, f32[512,768]{1,0:T(8,128)}) custom-call(s32[3]{0:T(128)} %pad_add_fusion.5.scalars, bf16[512,768]{1,0:T(8,128)(2,1)} %get-tuple-element.153.act_ref, bf16[512,384]{1,0:T(8,128)(2,1)} %get-tuple-element.128.mix_own, bf16[512,384]{1,0:T(8,128)(2,1)} %copy-done.14, ...), custom_call_target="tpu_custom_call" | custom-call | tf_op jit(solution)/shard_map/last/pallas_call | solution.py:257
  163.3 3.0 %collective-permute-done.22.more_ref = bf16[512,768]{1,0:T(8,128)(2,1)S(1)} collective-permute-done((bf16[512,768]{1,0:T(8,128)(2,1)}, bf16[512,768]{1,0:T(8,128)(2,1)S(1)}, u32[]{:S(2)}, u32[]{:S(2)}) %collective-permute-start.22) | collective-permute-done | bytes 786464 | tf_op jit(solution)/shard_map/ppermute | solution.py:213
  168.8 3.1 %sum_ffn.1 = (f32[576,256]{1,0:T(8,128)S(1)}, bf16[1152,256]{1,0:T(8,128)(2,1)}, f32[576,256]{1,0:T(8,128)S(1)}) custom-call(s32[3]{0:T(128)S(1)} %copy-done.24, bf16[4608,256]{1,0:T(8,128)(2,1)S(1)} %kept.1.keep, bf16[4608,256]{1,0:T(8,128)(2,1)} %collective-permute-done.21.first, bf16[2304,256]{1,0:T(8,128)(2,1)} %collective-permute-done.23.second), custom_call_target="tpu_custom_call" | custom-call | tf_op jit(solution)/shard_map/sum_ffn/pallas_call | solution.py:257
  173.5 1.7 copy.45.wanted_ref
  175.3 6.1 %spread_x.1 = (bf16[512,768]{1,0:T(8,128)(2,1)}, bf16[256,768]{1,0:T(8,128)(2,1)}, bf16[256,768]{1,0:T(8,128)(2,1)}) custom-call(s32[3]{0:T(128)} %pad_add_fusion.5.scalars, f32[512,768]{1,0:T(8,128)} %get-tuple-element.156.own_part, f32[512,768]{1,0:T(8,128)} %collective-permute-done.26.other_part, bf16[512,768]{1,0:T(8,128)(2,1)} %broadcast_select_fusion.1.x_ref, ...), custom_call_target="tpu_custom_call" | custom-call | tf_op jit(solution)/shard_map/spread_x/pallas_call | solution.py:257
  181.4 5.7 %collective-permute-done.25.came.near = bf16[1152,256]{1,0:T(8,128)(2,1)S(1)} collective-permute-done((bf16[1152,256]{1,0:T(8,128)(2,1)}, bf16[1152,256]{1,0:T(8,128)(2,1)S(1)}, u32[]{:S(2)}, u32[]{:S(2)}) %collective-permute-start.25) | collective-permute-done | bytes 589856 | tf_op jit(solution)/shard_map/ppermute | solution.py:213
  189.7 1.6 collective-permute-start.27
  191.3 3.3 %collective-permute-start.30 = (bf16[576,256]{1,0:T(8,128)(2,1)S(1)}, bf16[576,256]{1,0:T(8,128)(2,1)S(1)}, u32[]{:S(2)}, u32[]{:S(2)}) collective-permute-start(bf16[576,256]{1,0:T(8,128)(2,1)S(1)} %far_ffn.1), channel_id=1, source_target_pairs={{0,3},{1,2},{2,1},{3,0},{4,7},{5,6},{6,5},{7,4},{8,11},{9,10},{10,... | collective-permute-start | bytes 884744 | tf_op jit(solution)/shard_map/ppermute | solution.py:213
  194.6 5.2 %collective-permute-done.27.second = bf16[784,384]{1,0:T(8,128)(2,1)S(1)} collective-permute-done((bf16[784,384]{1,0:T(8,128)(2,1)S(1)}, bf16[784,384]{1,0:T(8,128)(2,1)S(1)}, u32[]{:S(2)}, u32[]{:S(2)}) %collective-permute-start.27) | collective-permute-done | bytes 602144 | tf_op jit(solution)/shard_map/ppermute | solution.py:213
  203.0 4.6 %collective-permute-done.28.came.near = bf16[416,384]{1,0:T(8,128)(2,1)S(1)} collective-permute-done((bf16[416,384]{1,0:T(8,128)(2,1)S(1)}, bf16[416,384]{1,0:T(8,128)(2,1)S(1)}, u32[]{:S(2)}, u32[]{:S(2)}) %collective-permute-start.28) | collective-permute-done | bytes 319520 | tf_op jit(solution)/shard_map/ppermute | solution.py:213
  211.7 4.0 %collective-permute-start.29 = (bf16[208,384]{1,0:T(8,128)(2,1)S(1)}, bf16[208,384]{1,0:T(8,128)(2,1)S(1)}, u32[]{:S(2)}, u32[]{:S(2)}) collective-permute-start(bf16[208,384]{1,0:T(8,128)(2,1)S(1)} %far_attn.1), channel_id=1, source_target_pairs={{0,3},{1,2},{2,1},{3,0},{4,7},{5,6},{6,5},{7,4},{8,11},{9,10},{10,... | collective-permute-start | bytes 479240 | tf_op jit(solution)/shard_map/ppermute | solution.py:213
  215.7 3.4 %collective-permute-done.29.far = bf16[208,384]{1,0:T(8,128)(2,1)S(1)} collective-permute-done((bf16[208,384]{1,0:T(8,128)(2,1)S(1)}, bf16[208,384]{1,0:T(8,128)(2,1)S(1)}, u32[]{:S(2)}, u32[]{:S(2)}) %collective-permute-start.29) | collective-permute-done | bytes 159776 | tf_op jit(solution)/shard_map/ppermute | solution.py:213
  221.4 5.0 %collective-permute-start.35 = (bf16[512,768]{1,0:T(8,128)(2,1)}, bf16[512,768]{1,0:T(8,128)(2,1)S(1)}, u32[]{:S(2)}, u32[]{:S(2)}) collective-permute-start(bf16[512,768]{1,0:T(8,128)(2,1)} %get-tuple-element.184), channel_id=1, source_target_pairs={{0,1},{1,0},{6,7},{7,6},{8,9},{9,8},{14,15},{15,14},{16,17},{17,16... | collective-permute-start | bytes 2359304 | tf_op jit(solution)/shard_map/ppermute | solution.py:213
  226.4 1.7 collective-permute-start.37
  229.5 2.8 %collective-permute-start.33 = (bf16[256,768]{1,0:T(8,128)(2,1)}, bf16[256,768]{1,0:T(8,128)(2,1)}, u32[]{:S(2)}, u32[]{:S(2)}) collective-permute-start(bf16[256,768]{1,0:T(8,128)(2,1)} %add_rows.2), channel_id=1, source_target_pairs={{0,2},{1,3},{6,4},{7,5},{8,10},{9,11},{14,12},{15,13},{16,18},{17,... | collective-permute-start | bytes 1179656 | tf_op jit(solution)/shard_map/ppermute | solution.py:213
  232.3 8.5 %adam_ffin.1 = (f32[2,192,2048]{2,1,0:T(8,128)}, f32[2,192,2048]{2,1,0:T(8,128)}, f32[2,192,2048]{2,1,0:T(8,128)}, bf16[2,192,2048]{2,1,0:T(8,128)(2,1)}) custom-call(s32[3]{0:T(128)} %pad_add_fusion.5.scalars, f32[2,192,2048]{2,1,0:T(8,128)} %refs_0_.3, f32[2,192,2048]{2,1,0:T(8,128)} %refs_1_.3, f32[2,192,2048]{2,1,0:T(8,128)} %refs_2_.3, ...), custom_call_target="tpu_custom_call" | custom-call | tf_op jit(solution)/shard_map/adam_ffin/pallas_call | solution.py:257
  241.3 2.1 collective-permute-start.38
  244.1 1.7 collective-permute-start.36
  245.8 6.2 %adam_ffout.1 = (f32[512,768]{1,0:T(8,128)}, f32[512,768]{1,0:T(8,128)}, f32[512,768]{1,0:T(8,128)}, bf16[512,768]{1,0:T(8,128)(2,1)}) custom-call(s32[3]{0:T(128)} %pad_add_fusion.5.scalars, f32[512,768]{1,0:T(8,128)} %refs_0_.4, f32[512,768]{1,0:T(8,128)} %refs_1_.4, f32[512,768]{1,0:T(8,128)} %refs_2_.4, bf16[4,576,256]{2,1,0:T(8,128)(2,1)} %copy-done.4, ...), custom_call_target="tpu_custom_call" | custom-call | tf_op jit(solution)/shard_map/adam_ffout/pallas_call | solution.py:257
  256.2 1.8 add_bitcast_fusion.1
  259.7 7.0 %adam_attn.1 = (f32[4,192,768]{2,1,0:T(8,128)}, f32[4,192,768]{2,1,0:T(8,128)}, f32[3,192,768]{2,1,0:T(8,128)}, f32[192,768]{1,0:T(8,128)}, bf16[4,192,768]{2,1,0:T(8,128)(2,1)}) custom-call(s32[3]{0:T(128)} %pad_add_fusion.5.scalars, f32[4,192,768]{2,1,0:T(8,128)} %refs_0_.5, f32[4,192,768]{2,1,0:T(8,128)} %refs_1_.5, f32[4,192,768]{2,1,0:T(8,128)} %refs_2_.5, ...), custom_call_target="tpu_custom_call" | custom-call | tf_op jit(solution)/shard_map/adam_attn/pallas_call | solution.py:257
  (216 shorter events, 55.6 us)
Async XLA Ops:
  3.7 9.9 %collective-permute-start.4 = (bf16[208,384]{1,0:T(8,128)(2,1)}, bf16[208,384]{1,0:T(8,128)(2,1)S(1)}, u32[]{:S(2)}, u32[]{:S(2)}) collective-permute-start(bf16[208,384]{1,0:T(8,128)(2,1)} %pack_attn.1.refs_0_.r0), channel_id=1, source_target_pairs={{0,3},{1,2},{2,1},{3,0},{4,7},{5,6},{6,5},{7,4},{8,11},{9,10},{10,... | collective-permute-start | bytes 479240 | tf_op jit(solution)/shard_map/ppermute | solution.py:213
  8.8 19.5 %collective-permute-start.3 = (s32[1028]{0:T(1024)S(1)}, s32[1028]{0:T(1024)S(1)}, u32[]{:S(2)}, u32[]{:S(2)}) collective-permute-start(s32[1028]{0:T(1024)S(1)} %pad_add_fusion), channel_id=1, source_target_pairs={{0,4},{4,0},{1,5},{5,1},{2,6},{6,2},{3,7},{7,3},{8,12},{12,8},{9,1... | collective-permute-start | bytes 12344 | tf_op jit(solution)/shard_map/ppermute | solution.py:46
  8.9 19.5 %collective-permute-start = (bf16[256,768]{1,0:T(8,128)(2,1)S(1)}, bf16[256,768]{1,0:T(8,128)(2,1)}, u32[]{:S(2)}, u32[]{:S(2)}) collective-permute-start(bf16[256,768]{1,0:T(8,128)(2,1)S(1)} %bitcast.32), channel_id=1, source_target_pairs={{4,5},{5,6},{6,7},{12,13},{13,14},{14,15},{20,21},{21,22},{22,23},... | collective-permute-start | bytes 1179656 | tf_op jit(solution)/shard_map/ppermute | solution.py:213
  13.2 18.6 %copy-start.19 = (bf16[576,256]{1,0:T(8,128)(2,1)S(1)}, bf16[576,256]{1,0:T(8,128)(2,1)}, u32[]{:S(2)}) copy-start(bf16[576,256]{1,0:T(8,128)(2,1)} %pack_ffn.1.refs_0_) | copy-start | bytes 884740
  14.2 12.0 %collective-permute-start.5 = (bf16[2,208,384]{2,1,0:T(8,128)(2,1)S(1)}, bf16[2,208,384]{2,1,0:T(8,128)(2,1)S(1)}, u32[]{:S(2)}, u32[]{:S(2)}) collective-permute-start(bf16[2,208,384]{2,1,0:T(8,128)(2,1)S(1)} %pair_attn_in.1), channel_id=1, source_target_pairs={{0,1},{1,0},{2,3},{3,2},{4,5},{5,4},{6,7},{7,6},{8,9},{9,8},{10,11... | collective-permute-start | bytes 958472 | tf_op jit(solution)/shard_map/ppermute | solution.py:213
  21.4 10.5 %collective-permute-start.7 = (bf16[576,256]{1,0:T(8,128)(2,1)}, bf16[576,256]{1,0:T(8,128)(2,1)S(1)}, u32[]{:S(2)}, u32[]{:S(2)}) collective-permute-start(bf16[576,256]{1,0:T(8,128)(2,1)} %pack_ffn.1.refs_0_), channel_id=1, source_target_pairs={{0,3},{1,2},{2,1},{3,0},{4,7},{5,6},{6,5},{7,4},{8,11},{9,10},{10,... | collective-permute-start | bytes 884744 | tf_op jit(solution)/shard_map/ppermute | solution.py:213
  26.8 8.5 %collective-permute-start.6 = (bf16[3,192,384]{2,1,0:T(8,128)(2,1)S(1)}, bf16[3,192,384]{2,1,0:T(8,128)(2,1)}, u32[]{:S(2)}, u32[]{:S(2)}) collective-permute-start(bf16[3,192,384]{2,1,0:T(8,128)(2,1)S(1)} %near.2.refs_0_), channel_id=1, source_target_pairs={{0,8},{1,9},{2,10},{3,11},{4,20},{5,21},{6,22},{7,23},{8,0},{9,1},... | collective-permute-start | bytes 1327112 | tf_op jit(solution)/shard_map/ppermute | solution.py:213
  28.4 12.6 %collective-permute-start.1 = (bf16[256,768]{1,0:T(8,128)(2,1)}, bf16[256,768]{1,0:T(8,128)(2,1)S(1)}, u32[]{:S(2)}, u32[]{:S(2)}) collective-permute-start(bf16[256,768]{1,0:T(8,128)(2,1)} %collective-permute-done.b1), channel_id=1, source_target_pairs={{5,6},{6,7},{13,14},{14,15},{21,22},{22,23},{29,30},{30,31},{2,1},... | collective-permute-start | bytes 1179656 | tf_op jit(solution)/shard_map/ppermute | solution.py:213
  36.3 22.5 %copy-start.8 = (bf16[6,192,384]{2,1,0:T(8,128)(2,1)}, bf16[6,192,384]{2,1,0:T(8,128)(2,1)S(1)}, u32[]{:S(2)}) copy-start(bf16[6,192,384]{2,1,0:T(8,128)(2,1)S(1)} %nearest.2.near_ref) | copy-start | bytes 2654212
  36.4 22.5 %collective-permute-start.8 = (bf16[6,192,384]{2,1,0:T(8,128)(2,1)S(1)}, bf16[6,192,384]{2,1,0:T(8,128)(2,1)S(1)}, u32[]{:S(2)}, u32[]{:S(2)}) collective-permute-start(bf16[6,192,384]{2,1,0:T(8,128)(2,1)S(1)} %nearest.2.near_ref), channel_id=1, source_target_pairs={{0,16},{1,17},{2,18},{3,19},{4,12},{5,13},{6,14},{7,15},{8,24},{9,... | collective-permute-start | bytes 2654216 | tf_op jit(solution)/shard_map/ppermute | solution.py:213
  38.6 20.3 %collective-permute-start.9 = (bf16[2,576,256]{2,1,0:T(8,128)(2,1)S(1)}, bf16[2,576,256]{2,1,0:T(8,128)(2,1)S(1)}, u32[]{:S(2)}, u32[]{:S(2)}) collective-permute-start(bf16[2,576,256]{2,1,0:T(8,128)(2,1)S(1)} %pair_ffn_in.1), channel_id=1, source_target_pairs={{0,1},{1,0},{2,3},{3,2},{4,5},{5,4},{6,7},{7,6},{8,9},{9,8},{10,11... | collective-permute-start | bytes 1769480 | tf_op jit(solution)/shard_map/ppermute | solution.py:213
  41.0 15.6 %collective-permute-start.2 = (bf16[256,768]{1,0:T(8,128)(2,1)S(1)}, bf16[256,768]{1,0:T(8,128)(2,1)S(1)}, u32[]{:S(2)}, u32[]{:S(2)}) collective-permute-start(bf16[256,768]{1,0:T(8,128)(2,1)S(1)} %broadcast_select_fusion.2), channel_id=1, source_target_pairs={{6,7},{7,6},{14,15},{15,14},{22,23},{23,22},{30,31},{31,30},{1,0},... | collective-permute-start | bytes 1179656 | tf_op jit(solution)/shard_map/ppermute | solution.py:213
  58.9 3.4 %collective-permute-start.10 = (bf16[512,768]{1,0:T(8,128)(2,1)S(1)}, bf16[512,768]{1,0:T(8,128)(2,1)S(1)}, u32[]{:S(2)}, u32[]{:S(2)}) collective-permute-start(bf16[512,768]{1,0:T(8,128)(2,1)S(1)} %pick.2), channel_id=1, source_target_pairs={{0,4},{4,0},{1,5},{5,1},{2,6},{6,2},{3,7},{7,3},{8,12},{12,8},{9,1... | collective-permute-start | bytes 2359304 | tf_op jit(solution)/shard_map/ppermute | solution.py:46
  59.6 13.1 %collective-permute-start.11 = (bf16[3,576,256]{2,1,0:T(8,128)(2,1)S(1)}, bf16[3,576,256]{2,1,0:T(8,128)(2,1)S(1)}, u32[]{:S(2)}, u32[]{:S(2)}) collective-permute-start(bf16[3,576,256]{2,1,0:T(8,128)(2,1)S(1)} %near.3.refs_0_), channel_id=1, source_target_pairs={{0,8},{1,9},{2,10},{3,11},{4,20},{5,21},{6,22},{7,23},{8,0},{9,1},... | collective-permute-start | bytes 2654216 | tf_op jit(solution)/shard_map/ppermute | solution.py:213
  60.2 9.9 %collective-permute-start.12 = (bf16[256,768]{1,0:T(8,128)(2,1)}, bf16[256,768]{1,0:T(8,128)(2,1)S(1)}, u32[]{:S(2)}, u32[]{:S(2)}) collective-permute-start(bf16[256,768]{1,0:T(8,128)(2,1)} %bitcast.18.b0), channel_id=1, source_target_pairs={{5,6},{6,7},{13,14},{14,15},{21,22},{22,23},{29,30},{30,31},{2,1},... | collective-permute-start | bytes 1179656 | tf_op jit(solution)/shard_map/ppermute | solution.py:213
  74.6 21.6 %copy-start.22 = (s32[3]{0:T(128)S(1)}, s32[3]{0:T(128)}, u32[]{:S(2)}) copy-start(s32[3]{0:T(128)} %pad_add_fusion.5.scalars) | copy-start | bytes 40
  74.6 28.2 %collective-permute-start.18 = (bf16[6,576,256]{2,1,0:T(8,128)(2,1)}, bf16[6,576,256]{2,1,0:T(8,128)(2,1)}, u32[]{:S(2)}, u32[]{:S(2)}) collective-permute-start(bf16[6,576,256]{2,1,0:T(8,128)(2,1)} %nearest.3.near_ref), channel_id=1, source_target_pairs={{0,16},{1,17},{2,18},{3,19},{4,12},{5,13},{6,14},{7,15},{8,24},{9,... | collective-permute-start | bytes 5308424 | tf_op jit(solution)/shard_map/ppermute | solution.py:213
  76.1 20.0 %collective-permute-start.16 = (bf16[256,768]{1,0:T(8,128)(2,1)}, bf16[256,768]{1,0:T(8,128)(2,1)S(1)}, u32[]{:S(2)}, u32[]{:S(2)}) collective-permute-start(bf16[256,768]{1,0:T(8,128)(2,1)} %bitcast.18.b0), channel_id=1, source_target_pairs={{4,7},{7,6},{12,15},{15,14},{20,23},{23,22},{28,31},{31,30},{3,0},... | collective-permute-start | bytes 1179656 | tf_op jit(solution)/shard_map/ppermute | solution.py:213
  79.8 16.4 %collective-permute-start.15 = (bf16[256,768]{1,0:T(8,128)(2,1)}, bf16[256,768]{1,0:T(8,128)(2,1)S(1)}, u32[]{:S(2)}, u32[]{:S(2)}) collective-permute-start(bf16[256,768]{1,0:T(8,128)(2,1)} %bitcast.18.b0), channel_id=1, source_target_pairs={{4,6},{5,7},{12,14},{13,15},{20,22},{21,23},{28,30},{29,31},{3,1},... | collective-permute-start | bytes 1179656 | tf_op jit(solution)/shard_map/ppermute | solution.py:213
  98.6 2.4 collective-permute-start.17
  100.0 2.7 %collective-permute-start.14 = (bf16[768,384]{1,0:T(8,128)(2,1)S(1)}, bf16[768,384]{1,0:T(8,128)(2,1)S(1)}, u32[]{:S(2)}, u32[]{:S(2)}) collective-permute-start(bf16[768,384]{1,0:T(8,128)(2,1)S(1)} %slice_bitcast_fusion.w_attn.w_ref), channel_id=1, source_target_pairs={{0,4},{4,0},{1,5},{5,1},{2,6},{6,2},{3,7},{7,3},{8,12},{12,8},{9,1... | collective-permute-start | bytes 1769480 | tf_op jit(solution)/shard_map/ppermute | solution.py:46
  100.6 2.2 collective-permute-start.13
  114.0 8.3 %collective-permute-start.19 = (f32[512,768]{1,0:T(8,128)S(1)}, f32[512,768]{1,0:T(8,128)S(1)}, u32[]{:S(2)}, u32[]{:S(2)}) collective-permute-start(f32[512,768]{1,0:T(8,128)S(1)} %get-tuple-element.136.own_part), channel_id=1, source_target_pairs={{0,4},{4,0},{1,5},{5,1},{2,6},{6,2},{3,7},{7,3},{8,12},{12,8},{9,1... | collective-permute-start | bytes 4718600 | tf_op jit(solution)/shard_map/ppermute | solution.py:46
  119.7 29.2 %collective-permute-start.21 = (bf16[4608,256]{1,0:T(8,128)(2,1)}, bf16[4608,256]{1,0:T(8,128)(2,1)}, u32[]{:S(2)}, u32[]{:S(2)}) collective-permute-start(bf16[4608,256]{1,0:T(8,128)(2,1)} %get-tuple-element.140), channel_id=1, source_target_pairs={{0,8},{1,9},{2,10},{3,11},{4,20},{5,21},{6,22},{7,23},{8,0},{9,1},... | collective-permute-start | bytes 7077896 | tf_op jit(solution)/shard_map/ppermute | solution.py:213
  123.4 14.6 %collective-permute-start.20 = (f32[512,768]{1,0:T(8,128)}, f32[512,768]{1,0:T(8,128)}, u32[]{:S(2)}, u32[]{:S(2)}) collective-permute-start(f32[512,768]{1,0:T(8,128)} %get-tuple-element.147.own_part), channel_id=1, source_target_pairs={{0,4},{4,0},{1,5},{5,1},{2,6},{6,2},{3,7},{7,3},{8,12},{12,8},{9,1... | collective-permute-start | bytes 4718600 | tf_op jit(solution)/shard_map/ppermute | solution.py:46
  151.7 16.5 %collective-permute-start.23 = (bf16[2304,256]{1,0:T(8,128)(2,1)}, bf16[2304,256]{1,0:T(8,128)(2,1)}, u32[]{:S(2)}, u32[]{:S(2)}) collective-permute-start(bf16[2304,256]{1,0:T(8,128)(2,1)} %pass_ffn.1), channel_id=1, source_target_pairs={{0,16},{1,17},{2,18},{3,19},{4,12},{5,13},{6,14},{7,15},{8,24},{9,... | collective-permute-start | bytes 3538952 | tf_op jit(solution)/shard_map/ppermute | solution.py:213
  152.2 14.1 %collective-permute-start.22 = (bf16[512,768]{1,0:T(8,128)(2,1)}, bf16[512,768]{1,0:T(8,128)(2,1)S(1)}, u32[]{:S(2)}, u32[]{:S(2)}) collective-permute-start(bf16[512,768]{1,0:T(8,128)(2,1)} %get-tuple-element.151), channel_id=1, source_target_pairs={{0,1},{1,0},{6,7},{7,6},{8,9},{9,8},{14,15},{15,14},{16,17},{17,16... | collective-permute-start | bytes 2359304 | tf_op jit(solution)/shard_map/ppermute | solution.py:213
  154.1 14.6 %copy-start.24 = (s32[3]{0:T(128)S(1)}, s32[3]{0:T(128)}, u32[]{:S(2)}) copy-start(s32[3]{0:T(128)} %pad_add_fusion.5.scalars) | copy-start | bytes 40
  163.2 12.1 %collective-permute-start.26 = (f32[512,768]{1,0:T(8,128)}, f32[512,768]{1,0:T(8,128)}, u32[]{:S(2)}, u32[]{:S(2)}) collective-permute-start(f32[512,768]{1,0:T(8,128)} %get-tuple-element.156.own_part), channel_id=1, source_target_pairs={{0,4},{4,0},{1,5},{5,1},{2,6},{6,2},{3,7},{7,3},{8,12},{12,8},{9,1... | collective-permute-start | bytes 4718600 | tf_op jit(solution)/shard_map/ppermute | solution.py:46
  168.2 19.5 %collective-permute-start.24 = (bf16[1552,384]{1,0:T(8,128)(2,1)}, bf16[1552,384]{1,0:T(8,128)(2,1)S(1)}, u32[]{:S(2)}, u32[]{:S(2)}) collective-permute-start(bf16[1552,384]{1,0:T(8,128)(2,1)} %get-tuple-element.162.sent), channel_id=1, source_target_pairs={{0,8},{1,9},{2,10},{3,11},{4,20},{5,21},{6,22},{7,23},{8,0},{9,1},... | collective-permute-start | bytes 3575816 | tf_op jit(solution)/shard_map/ppermute | solution.py:213
  173.5 13.6 %collective-permute-start.25 = (bf16[1152,256]{1,0:T(8,128)(2,1)}, bf16[1152,256]{1,0:T(8,128)(2,1)S(1)}, u32[]{:S(2)}, u32[]{:S(2)}) collective-permute-start(bf16[1152,256]{1,0:T(8,128)(2,1)} %get-tuple-element.164), channel_id=1, source_target_pairs={{0,1},{1,0},{2,3},{3,2},{4,5},{5,4},{6,7},{7,6},{8,9},{9,8},{10,11... | collective-permute-start | bytes 1769480 | tf_op jit(solution)/shard_map/ppermute | solution.py:213
  189.7 10.1 %collective-permute-start.27 = (bf16[784,384]{1,0:T(8,128)(2,1)S(1)}, bf16[784,384]{1,0:T(8,128)(2,1)S(1)}, u32[]{:S(2)}, u32[]{:S(2)}) collective-permute-start(bf16[784,384]{1,0:T(8,128)(2,1)S(1)} %pass_attn.1.passed), channel_id=1, source_target_pairs={{0,16},{1,17},{2,18},{3,19},{4,12},{5,13},{6,14},{7,15},{8,24},{9,... | collective-permute-start | bytes 1806344 | tf_op jit(solution)/shard_map/ppermute | solution.py:213
  191.3 10.4 %collective-permute-start.30 = (bf16[576,256]{1,0:T(8,128)(2,1)S(1)}, bf16[576,256]{1,0:T(8,128)(2,1)S(1)}, u32[]{:S(2)}, u32[]{:S(2)}) collective-permute-start(bf16[576,256]{1,0:T(8,128)(2,1)S(1)} %far_ffn.1), channel_id=1, source_target_pairs={{0,3},{1,2},{2,1},{3,0},{4,7},{5,6},{6,5},{7,4},{8,11},{9,10},{10,... | collective-permute-start | bytes 884744 | tf_op jit(solution)/shard_map/ppermute | solution.py:213
  200.6 7.1 %collective-permute-start.28 = (bf16[416,384]{1,0:T(8,128)(2,1)S(1)}, bf16[416,384]{1,0:T(8,128)(2,1)S(1)}, u32[]{:S(2)}, u32[]{:S(2)}) collective-permute-start(bf16[416,384]{1,0:T(8,128)(2,1)S(1)} %get-tuple-element.172), channel_id=1, source_target_pairs={{0,1},{1,0},{2,3},{3,2},{4,5},{5,4},{6,7},{7,6},{8,9},{9,8},{10,11... | collective-permute-start | bytes 958472 | tf_op jit(solution)/shard_map/ppermute | solution.py:213
  202.3 7.2 %collective-permute-start.31 = (bf16[576,256]{1,0:T(8,128)(2,1)S(1)}, bf16[576,256]{1,0:T(8,128)(2,1)S(1)}, u32[]{:S(2)}, u32[]{:S(2)}) collective-permute-start(bf16[576,256]{1,0:T(8,128)(2,1)S(1)} %total_ffn.1.refs_0_), channel_id=1, source_target_pairs={{0,8},{1,9},{2,10},{3,11},{4,20},{5,21},{6,22},{7,23},{8,0},{9,1},... | collective-permute-start | bytes 884744 | tf_op jit(solution)/shard_map/ppermute | solution.py:213
  210.1 18.0 %copy-start.12 = (bf16[512,768]{1,0:T(8,128)(2,1)S(1)}, bf16[512,768]{1,0:T(8,128)(2,1)}, u32[]{:S(2)}) copy-start(bf16[512,768]{1,0:T(8,128)(2,1)} %copy-done.11) | copy-start | bytes 2359300
  210.1 18.0 %copy-start.32 = (bf16[256,768]{1,0:T(8,128)(2,1)S(1)}, bf16[256,768]{1,0:T(8,128)(2,1)}, u32[]{:S(2)}) copy-start(bf16[256,768]{1,0:T(8,128)(2,1)} %get-tuple-element.158.value_ref) | copy-start | bytes 1179652
  210.1 9.9 %collective-permute-start.32 = (bf16[2,576,256]{2,1,0:T(8,128)(2,1)S(1)}, bf16[2,576,256]{2,1,0:T(8,128)(2,1)S(1)}, u32[]{:S(2)}, u32[]{:S(2)}) collective-permute-start(bf16[2,576,256]{2,1,0:T(8,128)(2,1)S(1)} %pair_ffn.1.refs_0_), channel_id=1, source_target_pairs={{0,16},{1,17},{2,18},{3,19},{4,12},{5,13},{6,14},{7,15},{8,24},{9,... | collective-permute-start | bytes 1769480 | tf_op jit(solution)/shard_map/ppermute | solution.py:213
  211.7 7.4 %collective-permute-start.29 = (bf16[208,384]{1,0:T(8,128)(2,1)S(1)}, bf16[208,384]{1,0:T(8,128)(2,1)S(1)}, u32[]{:S(2)}, u32[]{:S(2)}) collective-permute-start(bf16[208,384]{1,0:T(8,128)(2,1)S(1)} %far_attn.1), channel_id=1, source_target_pairs={{0,3},{1,2},{2,1},{3,0},{4,7},{5,6},{6,5},{7,4},{8,11},{9,10},{10,... | collective-permute-start | bytes 479240 | tf_op jit(solution)/shard_map/ppermute | solution.py:213
  220.7 11.5 %collective-permute-start.34 = (bf16[4,576,256]{2,1,0:T(8,128)(2,1)S(1)}, bf16[4,576,256]{2,1,0:T(8,128)(2,1)}, u32[]{:S(2)}, u32[]{:S(2)}) collective-permute-start(bf16[4,576,256]{2,1,0:T(8,128)(2,1)S(1)} %stack_ffn.1.refs_3_), channel_id=1, source_target_pairs={{0,4},{4,0},{1,5},{5,1},{2,6},{6,2},{3,7},{7,3},{8,12},{12,8},{9,1... | collective-permute-start | bytes 3538952 | tf_op jit(solution)/shard_map/ppermute | solution.py:46
  221.4 22.0 %collective-permute-start.35 = (bf16[512,768]{1,0:T(8,128)(2,1)}, bf16[512,768]{1,0:T(8,128)(2,1)S(1)}, u32[]{:S(2)}, u32[]{:S(2)}) collective-permute-start(bf16[512,768]{1,0:T(8,128)(2,1)} %get-tuple-element.184), channel_id=1, source_target_pairs={{0,1},{1,0},{6,7},{7,6},{8,9},{9,8},{14,15},{15,14},{16,17},{17,16... | collective-permute-start | bytes 2359304 | tf_op jit(solution)/shard_map/ppermute | solution.py:213
  226.4 14.3 %collective-permute-start.37 = (bf16[192,384]{1,0:T(8,128)(2,1)S(1)}, bf16[192,384]{1,0:T(8,128)(2,1)S(1)}, u32[]{:S(2)}, u32[]{:S(2)}) collective-permute-start(bf16[192,384]{1,0:T(8,128)(2,1)S(1)} %get-tuple-element.189.refs_0_), channel_id=1, source_target_pairs={{0,8},{1,9},{2,10},{3,11},{4,20},{5,21},{6,22},{7,23},{8,0},{9,1},... | collective-permute-start | bytes 442376 | tf_op jit(solution)/shard_map/ppermute | solution.py:213
  229.5 14.0 %copy-start.33 = (bf16[256,768]{1,0:T(8,128)(2,1)S(1)}, bf16[256,768]{1,0:T(8,128)(2,1)}, u32[]{:S(2)}) copy-start(bf16[256,768]{1,0:T(8,128)(2,1)} %get-tuple-element.186.value_ref) | copy-start | bytes 1179652
  229.5 26.7 %collective-permute-start.33 = (bf16[256,768]{1,0:T(8,128)(2,1)}, bf16[256,768]{1,0:T(8,128)(2,1)}, u32[]{:S(2)}, u32[]{:S(2)}) collective-permute-start(bf16[256,768]{1,0:T(8,128)(2,1)} %add_rows.2), channel_id=1, source_target_pairs={{0,2},{1,3},{6,4},{7,5},{8,10},{9,11},{14,12},{15,13},{16,18},{17,... | collective-permute-start | bytes 1179656 | tf_op jit(solution)/shard_map/ppermute | solution.py:213
  241.3 10.7 %collective-permute-start.38 = (bf16[2,192,384]{2,1,0:T(8,128)(2,1)S(1)}, bf16[2,192,384]{2,1,0:T(8,128)(2,1)S(1)}, u32[]{:S(2)}, u32[]{:S(2)}) collective-permute-start(bf16[2,192,384]{2,1,0:T(8,128)(2,1)S(1)} %pair_attn.1.refs_0_), channel_id=1, source_target_pairs={{0,16},{1,17},{2,18},{3,19},{4,12},{5,13},{6,14},{7,15},{8,24},{9,... | collective-permute-start | bytes 884744 | tf_op jit(solution)/shard_map/ppermute | solution.py:213
  244.1 13.9 %collective-permute-start.36 = (bf16[256,768]{1,0:T(8,128)(2,1)S(1)}, bf16[256,768]{1,0:T(8,128)(2,1)S(1)}, u32[]{:S(2)}, u32[]{:S(2)}) collective-permute-start(bf16[256,768]{1,0:T(8,128)(2,1)S(1)} %add_rows.3), channel_id=1, source_target_pairs={{0,2},{1,3},{6,4},{7,5},{8,10},{9,11},{14,12},{15,13},{16,18},{17,... | collective-permute-start | bytes 1179656 | tf_op jit(solution)/shard_map/ppermute | solution.py:213
  252.7 6.1 %collective-permute-start.39 = (bf16[4,192,384]{2,1,0:T(8,128)(2,1)S(1)}, bf16[4,192,384]{2,1,0:T(8,128)(2,1)S(1)}, u32[]{:S(2)}, u32[]{:S(2)}) collective-permute-start(bf16[4,192,384]{2,1,0:T(8,128)(2,1)S(1)} %stack_attn.1.refs_3_), channel_id=1, source_target_pairs={{0,4},{4,0},{1,5},{5,1},{2,6},{6,2},{3,7},{7,3},{8,12},{12,8},{9,1... | collective-permute-start | bytes 1769480 | tf_op jit(solution)/shard_map/ppermute | solution.py:46
  252.8 2.0 collective-permute-start.40
  (44 other events, 316.6 us)

commit v6 on v5

--- a/solution.py
+++ b/solution.py
@@ -350,11 +350,16 @@
     lax.fori_loop(0, 4, one, 0)
 
 
-def sum_ffn_kernel(scalars, keep, first, second, own, pair, far):
-    for step, out in enumerate((own, pair.at[0:576], pair.at[576:1152], far)):
+def sum_ffn_kernel(scalars, keep, first, second, own_out, pair, far_out, own, far, sems):
+    copies = []
+    for step, out in ((0, own), (3, far), (1, pair.at[0:576]), (2, pair.at[576:1152])):
         rows = tile_at(576 * xor(scalars[2], step), 576)
         total = wide(keep[rows, :]) + wide(first[rows, :]) + wide(second[rows, :])
         out[...] = total.astype(out.dtype)
+        if step in (0, 3):
+            copies.append(fetch_part(out, own_out if step == 0 else far_out, sems.at[step // 3]))
+    for copy in copies:
+        copy.wait()
 
 
 def pass_attn_kernel(scalars, keep, sent, first, out):
@@ -1054,7 +1059,9 @@
     ffn_second = after(ffn_second, part_one, y_near)
     ffn_own, ffn_two, ffn_far = call(
         sum_ffn_kernel, spot, [ffn_keep, ffn_first, ffn_second],
-        [((576, 256), full), ((1152, 256), low), ((576, 256), full)], [], "sum_ffn", 0, 8,
+        [((576, 256), full), ((1152, 256), low), ((576, 256), full)],
+        [pltpu.VMEM((576, 256), full), pltpu.VMEM((576, 256), full), pltpu.SemaphoreType.DMA((2,))],
+        "sum_ffn", 0, 8, (0, 2),
     )
     ffn_near = across(ffn_two, 1)
     x_rows = call(

time: 268 us -> 268 us (level)
  no operation moved by 1% of the time
where the time goes in v6:
time: 268 us; the launch traced here: 267 us
  Pallas kernels  124 us (46%)
  starting transfers between devices  60.9 us (23%)
  waiting for transfers between devices  56.6 us (21%)
  local copies, waits for them, and re-layouts  12.2 us (5%)
  other arithmetic  8.69 us (3%)
  between operations  4.49 us (2%)
    pallas_call x38, Pallas kernels, call(): pl.pallas_call(kernel, in_specs=[pl.BlockSpec(memory_space=pltpu.SMEM)] +...  124 us
    ppermute x30, starting transfers between devices, send(): lax.ppermute(value, ('plane', 'core', 'shard'), [((p * 2 + c) * 4 + z, (q...  59 us
    ppermute x30, waiting for transfers between devices, send(): lax.ppermute(value, ('plane', 'core', 'shard'), [((p * 2 + c) * 4 + z, (q...  53 us
    unnamed x102, local copies, waits for them, and re-layouts  5.96 us
  transfers between devices with their start and end apart: 41, of which 20 were waited for; matrix products, arithmetic and copies ran while one was open for 5% of the time, Pallas kernels for 36%

profile of v6, /device:TPU:0, one launch (start us, length us, event | category | flops | bytes accessed | tf_op | source)
XLA Modules:
  0.0 267.2 jit_solution(14184458099872049116)
XLA Ops:
  1.3 2.3 pack_attn.1.refs_0_.r0
  3.7 5.1 %collective-permute-start.4 = (bf16[208,384]{1,0:T(8,128)(2,1)}, bf16[208,384]{1,0:T(8,128)(2,1)S(1)}, u32[]{:S(2)}, u32[]{:S(2)}) collective-permute-start(bf16[208,384]{1,0:T(8,128)(2,1)} %pack_attn.1.refs_0_.r0), channel_id=1, source_target_pairs={{0,3},{1,2},{2,1},{3,0},{4,7},{5,6},{6,5},{7,4},{8,11},{9,10},{10,... | collective-permute-start | bytes 479240 | tf_op jit(solution)/shard_map/ppermute | solution.py:213
  10.5 2.7 %pack_ffn.1.refs_0_ = bf16[576,256]{1,0:T(8,128)(2,1)} custom-call(s32[3]{0:T(128)} %pad_add_fusion.5.scalars, f32[2,192,2048]{2,1,0:T(8,128)} %refs_0_.3, f32[512,768]{1,0:T(8,128)} %refs_0_.4), custom_call_target="tpu_custom_call" | custom-call | tf_op jit(solution)/shard_map/pack_ffn/pallas_call | solution.py:257
  14.2 3.0 %collective-permute-start.5 = (bf16[2,208,384]{2,1,0:T(8,128)(2,1)S(1)}, bf16[2,208,384]{2,1,0:T(8,128)(2,1)S(1)}, u32[]{:S(2)}, u32[]{:S(2)}) collective-permute-start(bf16[2,208,384]{2,1,0:T(8,128)(2,1)S(1)} %pair_attn_in.1), channel_id=1, source_target_pairs={{0,1},{1,0},{2,3},{3,2},{4,5},{5,4},{6,7},{7,6},{8,9},{9,8},{10,11... | collective-permute-start | bytes 958472 | tf_op jit(solution)/shard_map/ppermute | solution.py:213
  21.4 3.3 %collective-permute-start.7 = (bf16[576,256]{1,0:T(8,128)(2,1)}, bf16[576,256]{1,0:T(8,128)(2,1)S(1)}, u32[]{:S(2)}, u32[]{:S(2)}) collective-permute-start(bf16[576,256]{1,0:T(8,128)(2,1)} %pack_ffn.1.refs_0_), channel_id=1, source_target_pairs={{0,3},{1,2},{2,1},{3,0},{4,7},{5,6},{6,5},{7,4},{8,11},{9,10},{10,... | collective-permute-start | bytes 884744 | tf_op jit(solution)/shard_map/ppermute | solution.py:213
  29.9 2.0 collective-permute-done.7.refs_1_
  32.5 2.8 %collective-permute-done.6.refs_1_ = bf16[3,192,384]{2,1,0:T(8,128)(2,1)} collective-permute-done((bf16[3,192,384]{2,1,0:T(8,128)(2,1)S(1)}, bf16[3,192,384]{2,1,0:T(8,128)(2,1)}, u32[]{:S(2)}, u32[]{:S(2)}) %collective-permute-start.6) | collective-permute-done | bytes 442400 | tf_op jit(solution)/shard_map/ppermute | solution.py:213
  36.4 1.6 collective-permute-start.8
  38.6 2.4 collective-permute-start.9
  41.0 1.9 collective-permute-start.2
  45.1 11.5 %collective-permute-done.2.b3 = bf16[256,768]{1,0:T(8,128)(2,1)S(1)} collective-permute-done((bf16[256,768]{1,0:T(8,128)(2,1)S(1)}, bf16[256,768]{1,0:T(8,128)(2,1)S(1)}, u32[]{:S(2)}, u32[]{:S(2)}) %collective-permute-start.2) | collective-permute-done | bytes 393248 | tf_op jit(solution)/shard_map/ppermute | solution.py:213
  56.6 2.3 pick.2
  63.4 5.2 %project.1 = (bf16[4,768,384]{2,1,0:T(8,128)(2,1)}, bf16[512,768]{1,0:T(8,128)(2,1)}, bf16[512,384]{1,0:T(8,128)(2,1)}, bf16[512,384]{1,0:T(8,128)(2,1)}, bf16[512,384]{1,0:T(8,128)(2,1)}) custom-call(s32[3]{0:T(128)} %pad_add_fusion.5.scalars, bf16[512,768]{1,0:T(8,128)(2,1)} %broadcast_select_fusion.1.x_ref, f32[2,768]{1,0:T(2,128)} %copy-done.34, ...), custom_call_target="tpu_custom_call" | custom-call | tf_op jit(solution)/shard_map/project/pallas_call | solution.py:257
  70.1 2.6 collective-permute-done.11.refs_1_
  72.7 1.9 nearest.3.near_ref
  76.1 3.6 %collective-permute-start.16 = (bf16[256,768]{1,0:T(8,128)(2,1)}, bf16[256,768]{1,0:T(8,128)(2,1)S(1)}, u32[]{:S(2)}, u32[]{:S(2)}) collective-permute-start(bf16[256,768]{1,0:T(8,128)(2,1)} %bitcast.18.b0), channel_id=1, source_target_pairs={{4,7},{7,6},{12,15},{15,14},{20,23},{23,22},{28,31},{31,30},{3,0},... | collective-permute-start | bytes 1179656 | tf_op jit(solution)/shard_map/ppermute | solution.py:213
  82.9 13.3 %attend.1 = (bf16[512,384]{1,0:T(8,128)(2,1)}, bf16[6,512,512]{2,1,0:T(8,128)(2,1)}) custom-call(s32[3]{0:T(128)} %pad_add_fusion.5.scalars, bf16[512,384]{1,0:T(8,128)(2,1)} %get-tuple-element.124.q_ref, bf16[512,384]{1,0:T(8,128)(2,1)} %get-tuple-element.125.k_ref, bf16[512,384]{1,0:T(8,128)(2,1)} %get-tuple-element.126.v_ref, s32[512,1]{1,0:T(8,128)} %copy.43.qseg_ref, ...), custom_call_target="tpu_custom_call" | custom-call | tf_op jit(solution)/shard_map/attend/pallas_call | solution.py:257
  96.2 2.4 pick.3
  101.1 1.7 collective-permute-done.13.mix_other
  102.8 11.1 %feed.1 = (f32[512,768]{1,0:T(8,128)S(1)}, bf16[512,768]{1,0:T(8,128)(2,1)S(1)}, bf16[512,1024]{1,0:T(8,128)(2,1)S(1)}, f32[512,768]{1,0:T(8,128)S(1)}, f32[512,...) custom-call(s32[3]{0:T(128)S(1)} %copy-done.22, bf16[512,768]{1,0:T(8,128)(2,1)S(1)} %copy-done.1, ...), custom_call_target="tpu_custom_call" | custom-call | tf_op jit(solution)/shard_map/feed/pallas_call | solution.py:257
  114.4 5.3 %sent.1 = (bf16[4608,256]{1,0:T(8,128)(2,1)}, bf16[1536,256]{1,0:T(8,128)(2,1)S(1)}) custom-call(s32[3]{0:T(128)S(1)} %copy-done.22, bf16[512,768]{1,0:T(8,128)(2,1)S(1)} %get-tuple-element.137.act_ref, bf16[4,512,512]{2,1,0:T(8,128)(2,1)S(1)} %get-tuple-element.141.grad_ref, bf16[512,1024]{1,0:T(8,128)(2,1)S(1)} %get-tuple-element.139.hid_ref, ...), custom_call_target="tpu_custom_call" | custom-call | tf_op jit(solution)/shard_map/sent/pallas_call | solution.py:257
  120.3 2.0 kept.1.keep
  124.5 13.6 %back.1 = (f32[512,768]{1,0:T(8,128)}, bf16[4,512,384]{2,1,0:T(8,128)(2,1)}, f32[3,2,1024]{2,1,0:T(2,128)}, f32[1,768]{1,0:T(1,128)}) custom-call(s32[3]{0:T(128)} %pad_add_fusion.5.scalars, f32[512,768]{1,0:T(8,128)} %copy-done.16, f32[512,768]{1,0:T(8,128)} %copy-done.43, f32[512,768]{1,0:T(8,128)} %copy-done.5, bf16[512,768]{1,0:T(8,128)(2,1)} %copy-done.3, ...), custom_call_target="tpu_custom_call" | custom-call | tf_op jit(solution)/shard_map/back/pallas_call | solution.py:257
  138.1 5.4 %spread_y.1 = (bf16[512,768]{1,0:T(8,128)(2,1)}, bf16[256,768]{1,0:T(8,128)(2,1)}, bf16[256,768]{1,0:T(8,128)(2,1)}) custom-call(s32[3]{0:T(128)} %pad_add_fusion.5.scalars, f32[512,768]{1,0:T(8,128)} %copy-done.5, f32[512,768]{1,0:T(8,128)} %get-tuple-element.147.own_part, f32[512,768]{1,0:T(8,128)} %collective-permute-done.20.other_part, ...), custom_call_target="tpu_custom_call" | custom-call | tf_op jit(solution)/shard_map/spread_y/pallas_call | solution.py:257
  143.5 5.4 %collective-permute-done.21.first = bf16[4608,256]{1,0:T(8,128)(2,1)} collective-permute-done((bf16[4608,256]{1,0:T(8,128)(2,1)}, bf16[4608,256]{1,0:T(8,128)(2,1)}, u32[]{:S(2)}, u32[]{:S(2)}) %collective-permute-start.21) | collective-permute-done | bytes 2359328 | tf_op jit(solution)/shard_map/ppermute | solution.py:213
  148.9 2.8 %pass_ffn.1 = bf16[2304,256]{1,0:T(8,128)(2,1)} custom-call(s32[3]{0:T(128)S(1)} %copy-done.23, bf16[4608,256]{1,0:T(8,128)(2,1)S(1)} %kept.1.keep, bf16[4608,256]{1,0:T(8,128)(2,1)} %collective-permute-done.21.first), custom_call_target="tpu_custom_call" | custom-call | tf_op jit(solution)/shard_map/pass_ffn/pallas_call | solution.py:257
  152.2 1.9 collective-permute-start.22
  154.1 9.0 %last.1 = (bf16[1552,384]{1,0:T(8,128)(2,1)}, bf16[1536,384]{1,0:T(8,128)(2,1)}, f32[512,768]{1,0:T(8,128)}) custom-call(s32[3]{0:T(128)} %pad_add_fusion.5.scalars, bf16[512,768]{1,0:T(8,128)(2,1)} %get-tuple-element.153.act_ref, bf16[512,384]{1,0:T(8,128)(2,1)} %get-tuple-element.128.mix_own, bf16[512,384]{1,0:T(8,128)(2,1)} %copy-done.14, ...), custom_call_target="tpu_custom_call" | custom-call | tf_op jit(solution)/shard_map/last/pallas_call | solution.py:257
  163.3 3.0 %collective-permute-done.22.more_ref = bf16[512,768]{1,0:T(8,128)(2,1)S(1)} collective-permute-done((bf16[512,768]{1,0:T(8,128)(2,1)}, bf16[512,768]{1,0:T(8,128)(2,1)S(1)}, u32[]{:S(2)}, u32[]{:S(2)}) %collective-permute-start.22) | collective-permute-done | bytes 786464 | tf_op jit(solution)/shard_map/ppermute | solution.py:213
  168.8 3.5 %sum_ffn.1 = (f32[576,256]{1,0:T(8,128)S(1)}, bf16[1152,256]{1,0:T(8,128)(2,1)}, f32[576,256]{1,0:T(8,128)S(1)}) custom-call(s32[3]{0:T(128)S(1)} %copy-done.24, bf16[4608,256]{1,0:T(8,128)(2,1)S(1)} %kept.1.keep, bf16[4608,256]{1,0:T(8,128)(2,1)} %collective-permute-done.21.first, bf16[2304,256]{1,0:T(8,128)(2,1)} %collective-permute-done.23.second), custom_call_target="tpu_custom_call" | custom-call | tf_op jit(solution)/shard_map/sum_ffn/pallas_call | solution.py:257
  173.9 1.7 copy.45.wanted_ref
  175.6 6.1 %spread_x.1 = (bf16[512,768]{1,0:T(8,128)(2,1)}, bf16[256,768]{1,0:T(8,128)(2,1)}, bf16[256,768]{1,0:T(8,128)(2,1)}) custom-call(s32[3]{0:T(128)} %pad_add_fusion.5.scalars, f32[512,768]{1,0:T(8,128)} %get-tuple-element.156.own_part, f32[512,768]{1,0:T(8,128)} %collective-permute-done.26.other_part, bf16[512,768]{1,0:T(8,128)(2,1)} %broadcast_select_fusion.1.x_ref, ...), custom_call_target="tpu_custom_call" | custom-call | tf_op jit(solution)/shard_map/spread_x/pallas_call | solution.py:257
  181.8 5.7 %collective-permute-done.25.came.near = bf16[1152,256]{1,0:T(8,128)(2,1)S(1)} collective-permute-done((bf16[1152,256]{1,0:T(8,128)(2,1)}, bf16[1152,256]{1,0:T(8,128)(2,1)S(1)}, u32[]{:S(2)}, u32[]{:S(2)}) %collective-permute-start.25) | collective-permute-done | bytes 589856 | tf_op jit(solution)/shard_map/ppermute | solution.py:213
  190.1 1.6 collective-permute-start.27
  191.7 3.3 %collective-permute-start.30 = (bf16[576,256]{1,0:T(8,128)(2,1)S(1)}, bf16[576,256]{1,0:T(8,128)(2,1)S(1)}, u32[]{:S(2)}, u32[]{:S(2)}) collective-permute-start(bf16[576,256]{1,0:T(8,128)(2,1)S(1)} %far_ffn.1), channel_id=1, source_target_pairs={{0,3},{1,2},{2,1},{3,0},{4,7},{5,6},{6,5},{7,4},{8,11},{9,10},{10,... | collective-permute-start | bytes 884744 | tf_op jit(solution)/shard_map/ppermute | solution.py:213
  194.9 5.2 %collective-permute-done.27.second = bf16[784,384]{1,0:T(8,128)(2,1)S(1)} collective-permute-done((bf16[784,384]{1,0:T(8,128)(2,1)S(1)}, bf16[784,384]{1,0:T(8,128)(2,1)S(1)}, u32[]{:S(2)}, u32[]{:S(2)}) %collective-permute-start.27) | collective-permute-done | bytes 602144 | tf_op jit(solution)/shard_map/ppermute | solution.py:213
  203.4 4.6 %collective-permute-done.28.came.near = bf16[416,384]{1,0:T(8,128)(2,1)S(1)} collective-permute-done((bf16[416,384]{1,0:T(8,128)(2,1)S(1)}, bf16[416,384]{1,0:T(8,128)(2,1)S(1)}, u32[]{:S(2)}, u32[]{:S(2)}) %collective-permute-start.28) | collective-permute-done | bytes 319520 | tf_op jit(solution)/shard_map/ppermute | solution.py:213
  212.1 4.0 %collective-permute-start.29 = (bf16[208,384]{1,0:T(8,128)(2,1)S(1)}, bf16[208,384]{1,0:T(8,128)(2,1)S(1)}, u32[]{:S(2)}, u32[]{:S(2)}) collective-permute-start(bf16[208,384]{1,0:T(8,128)(2,1)S(1)} %far_attn.1), channel_id=1, source_target_pairs={{0,3},{1,2},{2,1},{3,0},{4,7},{5,6},{6,5},{7,4},{8,11},{9,10},{10,... | collective-permute-start | bytes 479240 | tf_op jit(solution)/shard_map/ppermute | solution.py:213
  216.1 3.4 %collective-permute-done.29.far = bf16[208,384]{1,0:T(8,128)(2,1)S(1)} collective-permute-done((bf16[208,384]{1,0:T(8,128)(2,1)S(1)}, bf16[208,384]{1,0:T(8,128)(2,1)S(1)}, u32[]{:S(2)}, u32[]{:S(2)}) %collective-permute-start.29) | collective-permute-done | bytes 159776 | tf_op jit(solution)/shard_map/ppermute | solution.py:213
  221.8 5.0 %collective-permute-start.35 = (bf16[512,768]{1,0:T(8,128)(2,1)}, bf16[512,768]{1,0:T(8,128)(2,1)S(1)}, u32[]{:S(2)}, u32[]{:S(2)}) collective-permute-start(bf16[512,768]{1,0:T(8,128)(2,1)} %get-tuple-element.184), channel_id=1, source_target_pairs={{0,1},{1,0},{6,7},{7,6},{8,9},{9,8},{14,15},{15,14},{16,17},{17,16... | collective-permute-start | bytes 2359304 | tf_op jit(solution)/shard_map/ppermute | solution.py:213
  226.8 1.7 collective-permute-start.37
  229.8 2.8 %collective-permute-start.33 = (bf16[256,768]{1,0:T(8,128)(2,1)}, bf16[256,768]{1,0:T(8,128)(2,1)}, u32[]{:S(2)}, u32[]{:S(2)}) collective-permute-start(bf16[256,768]{1,0:T(8,128)(2,1)} %add_rows.2), channel_id=1, source_target_pairs={{0,2},{1,3},{6,4},{7,5},{8,10},{9,11},{14,12},{15,13},{16,18},{17,... | collective-permute-start | bytes 1179656 | tf_op jit(solution)/shard_map/ppermute | solution.py:213
  232.6 8.5 %adam_ffin.1 = (f32[2,192,2048]{2,1,0:T(8,128)}, f32[2,192,2048]{2,1,0:T(8,128)}, f32[2,192,2048]{2,1,0:T(8,128)}, bf16[2,192,2048]{2,1,0:T(8,128)(2,1)}) custom-call(s32[3]{0:T(128)} %pad_add_fusion.5.scalars, f32[2,192,2048]{2,1,0:T(8,128)} %refs_0_.3, f32[2,192,2048]{2,1,0:T(8,128)} %refs_1_.3, f32[2,192,2048]{2,1,0:T(8,128)} %refs_2_.3, ...), custom_call_target="tpu_custom_call" | custom-call | tf_op jit(solution)/shard_map/adam_ffin/pallas_call | solution.py:257
  241.7 2.1 collective-permute-start.38
  244.5 1.7 collective-permute-start.36
  246.2 6.2 %adam_ffout.1 = (f32[512,768]{1,0:T(8,128)}, f32[512,768]{1,0:T(8,128)}, f32[512,768]{1,0:T(8,128)}, bf16[512,768]{1,0:T(8,128)(2,1)}) custom-call(s32[3]{0:T(128)} %pad_add_fusion.5.scalars, f32[512,768]{1,0:T(8,128)} %refs_0_.4, f32[512,768]{1,0:T(8,128)} %refs_1_.4, f32[512,768]{1,0:T(8,128)} %refs_2_.4, bf16[4,576,256]{2,1,0:T(8,128)(2,1)} %copy-done.4, ...), custom_call_target="tpu_custom_call" | custom-call | tf_op jit(solution)/shard_map/adam_ffout/pallas_call | solution.py:257
  256.6 1.8 add_bitcast_fusion.1
  260.0 7.0 %adam_attn.1 = (f32[4,192,768]{2,1,0:T(8,128)}, f32[4,192,768]{2,1,0:T(8,128)}, f32[3,192,768]{2,1,0:T(8,128)}, f32[192,768]{1,0:T(8,128)}, bf16[4,192,768]{2,1,0:T(8,128)(2,1)}) custom-call(s32[3]{0:T(128)} %pad_add_fusion.5.scalars, f32[4,192,768]{2,1,0:T(8,128)} %refs_0_.5, f32[4,192,768]{2,1,0:T(8,128)} %refs_1_.5, f32[4,192,768]{2,1,0:T(8,128)} %refs_2_.5, ...), custom_call_target="tpu_custom_call" | custom-call | tf_op jit(solution)/shard_map/adam_attn/pallas_call | solution.py:257
  (216 shorter events, 55.6 us)
Async XLA Ops:
  3.7 9.9 %collective-permute-start.4 = (bf16[208,384]{1,0:T(8,128)(2,1)}, bf16[208,384]{1,0:T(8,128)(2,1)S(1)}, u32[]{:S(2)}, u32[]{:S(2)}) collective-permute-start(bf16[208,384]{1,0:T(8,128)(2,1)} %pack_attn.1.refs_0_.r0), channel_id=1, source_target_pairs={{0,3},{1,2},{2,1},{3,0},{4,7},{5,6},{6,5},{7,4},{8,11},{9,10},{10,... | collective-permute-start | bytes 479240 | tf_op jit(solution)/shard_map/ppermute | solution.py:213
  8.8 19.5 %collective-permute-start.3 = (s32[1028]{0:T(1024)S(1)}, s32[1028]{0:T(1024)S(1)}, u32[]{:S(2)}, u32[]{:S(2)}) collective-permute-start(s32[1028]{0:T(1024)S(1)} %pad_add_fusion), channel_id=1, source_target_pairs={{0,4},{4,0},{1,5},{5,1},{2,6},{6,2},{3,7},{7,3},{8,12},{12,8},{9,1... | collective-permute-start | bytes 12344 | tf_op jit(solution)/shard_map/ppermute | solution.py:46
  8.9 19.5 %collective-permute-start = (bf16[256,768]{1,0:T(8,128)(2,1)S(1)}, bf16[256,768]{1,0:T(8,128)(2,1)}, u32[]{:S(2)}, u32[]{:S(2)}) collective-permute-start(bf16[256,768]{1,0:T(8,128)(2,1)S(1)} %bitcast.32), channel_id=1, source_target_pairs={{4,5},{5,6},{6,7},{12,13},{13,14},{14,15},{20,21},{21,22},{22,23},... | collective-permute-start | bytes 1179656 | tf_op jit(solution)/shard_map/ppermute | solution.py:213
  13.2 18.6 %copy-start.19 = (bf16[576,256]{1,0:T(8,128)(2,1)S(1)}, bf16[576,256]{1,0:T(8,128)(2,1)}, u32[]{:S(2)}) copy-start(bf16[576,256]{1,0:T(8,128)(2,1)} %pack_ffn.1.refs_0_) | copy-start | bytes 884740
  14.2 12.0 %collective-permute-start.5 = (bf16[2,208,384]{2,1,0:T(8,128)(2,1)S(1)}, bf16[2,208,384]{2,1,0:T(8,128)(2,1)S(1)}, u32[]{:S(2)}, u32[]{:S(2)}) collective-permute-start(bf16[2,208,384]{2,1,0:T(8,128)(2,1)S(1)} %pair_attn_in.1), channel_id=1, source_target_pairs={{0,1},{1,0},{2,3},{3,2},{4,5},{5,4},{6,7},{7,6},{8,9},{9,8},{10,11... | collective-permute-start | bytes 958472 | tf_op jit(solution)/shard_map/ppermute | solution.py:213
  21.4 10.5 %collective-permute-start.7 = (bf16[576,256]{1,0:T(8,128)(2,1)}, bf16[576,256]{1,0:T(8,128)(2,1)S(1)}, u32[]{:S(2)}, u32[]{:S(2)}) collective-permute-start(bf16[576,256]{1,0:T(8,128)(2,1)} %pack_ffn.1.refs_0_), channel_id=1, source_target_pairs={{0,3},{1,2},{2,1},{3,0},{4,7},{5,6},{6,5},{7,4},{8,11},{9,10},{10,... | collective-permute-start | bytes 884744 | tf_op jit(solution)/shard_map/ppermute | solution.py:213
  26.8 8.5 %collective-permute-start.6 = (bf16[3,192,384]{2,1,0:T(8,128)(2,1)S(1)}, bf16[3,192,384]{2,1,0:T(8,128)(2,1)}, u32[]{:S(2)}, u32[]{:S(2)}) collective-permute-start(bf16[3,192,384]{2,1,0:T(8,128)(2,1)S(1)} %near.2.refs_0_), channel_id=1, source_target_pairs={{0,8},{1,9},{2,10},{3,11},{4,20},{5,21},{6,22},{7,23},{8,0},{9,1},... | collective-permute-start | bytes 1327112 | tf_op jit(solution)/shard_map/ppermute | solution.py:213
  28.4 12.6 %collective-permute-start.1 = (bf16[256,768]{1,0:T(8,128)(2,1)}, bf16[256,768]{1,0:T(8,128)(2,1)S(1)}, u32[]{:S(2)}, u32[]{:S(2)}) collective-permute-start(bf16[256,768]{1,0:T(8,128)(2,1)} %collective-permute-done.b1), channel_id=1, source_target_pairs={{5,6},{6,7},{13,14},{14,15},{21,22},{22,23},{29,30},{30,31},{2,1},... | collective-permute-start | bytes 1179656 | tf_op jit(solution)/shard_map/ppermute | solution.py:213
  36.3 22.5 %copy-start.8 = (bf16[6,192,384]{2,1,0:T(8,128)(2,1)}, bf16[6,192,384]{2,1,0:T(8,128)(2,1)S(1)}, u32[]{:S(2)}) copy-start(bf16[6,192,384]{2,1,0:T(8,128)(2,1)S(1)} %nearest.2.near_ref) | copy-start | bytes 2654212
  36.4 22.5 %collective-permute-start.8 = (bf16[6,192,384]{2,1,0:T(8,128)(2,1)S(1)}, bf16[6,192,384]{2,1,0:T(8,128)(2,1)S(1)}, u32[]{:S(2)}, u32[]{:S(2)}) collective-permute-start(bf16[6,192,384]{2,1,0:T(8,128)(2,1)S(1)} %nearest.2.near_ref), channel_id=1, source_target_pairs={{0,16},{1,17},{2,18},{3,19},{4,12},{5,13},{6,14},{7,15},{8,24},{9,... | collective-permute-start | bytes 2654216 | tf_op jit(solution)/shard_map/ppermute | solution.py:213
  38.6 20.3 %collective-permute-start.9 = (bf16[2,576,256]{2,1,0:T(8,128)(2,1)S(1)}, bf16[2,576,256]{2,1,0:T(8,128)(2,1)S(1)}, u32[]{:S(2)}, u32[]{:S(2)}) collective-permute-start(bf16[2,576,256]{2,1,0:T(8,128)(2,1)S(1)} %pair_ffn_in.1), channel_id=1, source_target_pairs={{0,1},{1,0},{2,3},{3,2},{4,5},{5,4},{6,7},{7,6},{8,9},{9,8},{10,11... | collective-permute-start | bytes 1769480 | tf_op jit(solution)/shard_map/ppermute | solution.py:213
  41.0 15.6 %collective-permute-start.2 = (bf16[256,768]{1,0:T(8,128)(2,1)S(1)}, bf16[256,768]{1,0:T(8,128)(2,1)S(1)}, u32[]{:S(2)}, u32[]{:S(2)}) collective-permute-start(bf16[256,768]{1,0:T(8,128)(2,1)S(1)} %broadcast_select_fusion.2), channel_id=1, source_target_pairs={{6,7},{7,6},{14,15},{15,14},{22,23},{23,22},{30,31},{31,30},{1,0},... | collective-permute-start | bytes 1179656 | tf_op jit(solution)/shard_map/ppermute | solution.py:213
  58.9 3.4 %collective-permute-start.10 = (bf16[512,768]{1,0:T(8,128)(2,1)S(1)}, bf16[512,768]{1,0:T(8,128)(2,1)S(1)}, u32[]{:S(2)}, u32[]{:S(2)}) collective-permute-start(bf16[512,768]{1,0:T(8,128)(2,1)S(1)} %pick.2), channel_id=1, source_target_pairs={{0,4},{4,0},{1,5},{5,1},{2,6},{6,2},{3,7},{7,3},{8,12},{12,8},{9,1... | collective-permute-start | bytes 2359304 | tf_op jit(solution)/shard_map/ppermute | solution.py:46
  59.6 13.1 %collective-permute-start.11 = (bf16[3,576,256]{2,1,0:T(8,128)(2,1)S(1)}, bf16[3,576,256]{2,1,0:T(8,128)(2,1)S(1)}, u32[]{:S(2)}, u32[]{:S(2)}) collective-permute-start(bf16[3,576,256]{2,1,0:T(8,128)(2,1)S(1)} %near.3.refs_0_), channel_id=1, source_target_pairs={{0,8},{1,9},{2,10},{3,11},{4,20},{5,21},{6,22},{7,23},{8,0},{9,1},... | collective-permute-start | bytes 2654216 | tf_op jit(solution)/shard_map/ppermute | solution.py:213
  60.2 9.9 %collective-permute-start.12 = (bf16[256,768]{1,0:T(8,128)(2,1)}, bf16[256,768]{1,0:T(8,128)(2,1)S(1)}, u32[]{:S(2)}, u32[]{:S(2)}) collective-permute-start(bf16[256,768]{1,0:T(8,128)(2,1)} %bitcast.18.b0), channel_id=1, source_target_pairs={{5,6},{6,7},{13,14},{14,15},{21,22},{22,23},{29,30},{30,31},{2,1},... | collective-permute-start | bytes 1179656 | tf_op jit(solution)/shard_map/ppermute | solution.py:213
  74.6 21.6 %copy-start.22 = (s32[3]{0:T(128)S(1)}, s32[3]{0:T(128)}, u32[]{:S(2)}) copy-start(s32[3]{0:T(128)} %pad_add_fusion.5.scalars) | copy-start | bytes 40
  74.6 28.2 %collective-permute-start.18 = (bf16[6,576,256]{2,1,0:T(8,128)(2,1)}, bf16[6,576,256]{2,1,0:T(8,128)(2,1)}, u32[]{:S(2)}, u32[]{:S(2)}) collective-permute-start(bf16[6,576,256]{2,1,0:T(8,128)(2,1)} %nearest.3.near_ref), channel_id=1, source_target_pairs={{0,16},{1,17},{2,18},{3,19},{4,12},{5,13},{6,14},{7,15},{8,24},{9,... | collective-permute-start | bytes 5308424 | tf_op jit(solution)/shard_map/ppermute | solution.py:213
  76.1 20.0 %collective-permute-start.16 = (bf16[256,768]{1,0:T(8,128)(2,1)}, bf16[256,768]{1,0:T(8,128)(2,1)S(1)}, u32[]{:S(2)}, u32[]{:S(2)}) collective-permute-start(bf16[256,768]{1,0:T(8,128)(2,1)} %bitcast.18.b0), channel_id=1, source_target_pairs={{4,7},{7,6},{12,15},{15,14},{20,23},{23,22},{28,31},{31,30},{3,0},... | collective-permute-start | bytes 1179656 | tf_op jit(solution)/shard_map/ppermute | solution.py:213
  79.8 16.4 %collective-permute-start.15 = (bf16[256,768]{1,0:T(8,128)(2,1)}, bf16[256,768]{1,0:T(8,128)(2,1)S(1)}, u32[]{:S(2)}, u32[]{:S(2)}) collective-permute-start(bf16[256,768]{1,0:T(8,128)(2,1)} %bitcast.18.b0), channel_id=1, source_target_pairs={{4,6},{5,7},{12,14},{13,15},{20,22},{21,23},{28,30},{29,31},{3,1},... | collective-permute-start | bytes 1179656 | tf_op jit(solution)/shard_map/ppermute | solution.py:213
  98.6 2.4 collective-permute-start.17
  100.0 2.7 %collective-permute-start.14 = (bf16[768,384]{1,0:T(8,128)(2,1)S(1)}, bf16[768,384]{1,0:T(8,128)(2,1)S(1)}, u32[]{:S(2)}, u32[]{:S(2)}) collective-permute-start(bf16[768,384]{1,0:T(8,128)(2,1)S(1)} %slice_bitcast_fusion.w_attn.w_ref), channel_id=1, source_target_pairs={{0,4},{4,0},{1,5},{5,1},{2,6},{6,2},{3,7},{7,3},{8,12},{12,8},{9,1... | collective-permute-start | bytes 1769480 | tf_op jit(solution)/shard_map/ppermute | solution.py:46
  100.6 2.2 collective-permute-start.13
  114.0 8.3 %collective-permute-start.19 = (f32[512,768]{1,0:T(8,128)S(1)}, f32[512,768]{1,0:T(8,128)S(1)}, u32[]{:S(2)}, u32[]{:S(2)}) collective-permute-start(f32[512,768]{1,0:T(8,128)S(1)} %get-tuple-element.136.own_part), channel_id=1, source_target_pairs={{0,4},{4,0},{1,5},{5,1},{2,6},{6,2},{3,7},{7,3},{8,12},{12,8},{9,1... | collective-permute-start | bytes 4718600 | tf_op jit(solution)/shard_map/ppermute | solution.py:46
  119.7 29.2 %collective-permute-start.21 = (bf16[4608,256]{1,0:T(8,128)(2,1)}, bf16[4608,256]{1,0:T(8,128)(2,1)}, u32[]{:S(2)}, u32[]{:S(2)}) collective-permute-start(bf16[4608,256]{1,0:T(8,128)(2,1)} %get-tuple-element.140), channel_id=1, source_target_pairs={{0,8},{1,9},{2,10},{3,11},{4,20},{5,21},{6,22},{7,23},{8,0},{9,1},... | collective-permute-start | bytes 7077896 | tf_op jit(solution)/shard_map/ppermute | solution.py:213
  123.4 14.6 %collective-permute-start.20 = (f32[512,768]{1,0:T(8,128)}, f32[512,768]{1,0:T(8,128)}, u32[]{:S(2)}, u32[]{:S(2)}) collective-permute-start(f32[512,768]{1,0:T(8,128)} %get-tuple-element.147.own_part), channel_id=1, source_target_pairs={{0,4},{4,0},{1,5},{5,1},{2,6},{6,2},{3,7},{7,3},{8,12},{12,8},{9,1... | collective-permute-start | bytes 4718600 | tf_op jit(solution)/shard_map/ppermute | solution.py:46
  151.7 16.5 %collective-permute-start.23 = (bf16[2304,256]{1,0:T(8,128)(2,1)}, bf16[2304,256]{1,0:T(8,128)(2,1)}, u32[]{:S(2)}, u32[]{:S(2)}) collective-permute-start(bf16[2304,256]{1,0:T(8,128)(2,1)} %pass_ffn.1), channel_id=1, source_target_pairs={{0,16},{1,17},{2,18},{3,19},{4,12},{5,13},{6,14},{7,15},{8,24},{9,... | collective-permute-start | bytes 3538952 | tf_op jit(solution)/shard_map/ppermute | solution.py:213
  152.2 14.1 %collective-permute-start.22 = (bf16[512,768]{1,0:T(8,128)(2,1)}, bf16[512,768]{1,0:T(8,128)(2,1)S(1)}, u32[]{:S(2)}, u32[]{:S(2)}) collective-permute-start(bf16[512,768]{1,0:T(8,128)(2,1)} %get-tuple-element.151), channel_id=1, source_target_pairs={{0,1},{1,0},{6,7},{7,6},{8,9},{9,8},{14,15},{15,14},{16,17},{17,16... | collective-permute-start | bytes 2359304 | tf_op jit(solution)/shard_map/ppermute | solution.py:213
  154.1 14.6 %copy-start.24 = (s32[3]{0:T(128)S(1)}, s32[3]{0:T(128)}, u32[]{:S(2)}) copy-start(s32[3]{0:T(128)} %pad_add_fusion.5.scalars) | copy-start | bytes 40
  163.2 12.4 %collective-permute-start.26 = (f32[512,768]{1,0:T(8,128)}, f32[512,768]{1,0:T(8,128)}, u32[]{:S(2)}, u32[]{:S(2)}) collective-permute-start(f32[512,768]{1,0:T(8,128)} %get-tuple-element.156.own_part), channel_id=1, source_target_pairs={{0,4},{4,0},{1,5},{5,1},{2,6},{6,2},{3,7},{7,3},{8,12},{12,8},{9,1... | collective-permute-start | bytes 4718600 | tf_op jit(solution)/shard_map/ppermute | solution.py:46
  168.2 19.9 %collective-permute-start.24 = (bf16[1552,384]{1,0:T(8,128)(2,1)}, bf16[1552,384]{1,0:T(8,128)(2,1)S(1)}, u32[]{:S(2)}, u32[]{:S(2)}) collective-permute-start(bf16[1552,384]{1,0:T(8,128)(2,1)} %get-tuple-element.162.sent), channel_id=1, source_target_pairs={{0,8},{1,9},{2,10},{3,11},{4,20},{5,21},{6,22},{7,23},{8,0},{9,1},... | collective-permute-start | bytes 3575816 | tf_op jit(solution)/shard_map/ppermute | solution.py:213
  173.9 13.6 %collective-permute-start.25 = (bf16[1152,256]{1,0:T(8,128)(2,1)}, bf16[1152,256]{1,0:T(8,128)(2,1)S(1)}, u32[]{:S(2)}, u32[]{:S(2)}) collective-permute-start(bf16[1152,256]{1,0:T(8,128)(2,1)} %get-tuple-element.164), channel_id=1, source_target_pairs={{0,1},{1,0},{2,3},{3,2},{4,5},{5,4},{6,7},{7,6},{8,9},{9,8},{10,11... | collective-permute-start | bytes 1769480 | tf_op jit(solution)/shard_map/ppermute | solution.py:213
  190.1 10.1 %collective-permute-start.27 = (bf16[784,384]{1,0:T(8,128)(2,1)S(1)}, bf16[784,384]{1,0:T(8,128)(2,1)S(1)}, u32[]{:S(2)}, u32[]{:S(2)}) collective-permute-start(bf16[784,384]{1,0:T(8,128)(2,1)S(1)} %pass_attn.1.passed), channel_id=1, source_target_pairs={{0,16},{1,17},{2,18},{3,19},{4,12},{5,13},{6,14},{7,15},{8,24},{9,... | collective-permute-start | bytes 1806344 | tf_op jit(solution)/shard_map/ppermute | solution.py:213
  191.7 10.4 %collective-permute-start.30 = (bf16[576,256]{1,0:T(8,128)(2,1)S(1)}, bf16[576,256]{1,0:T(8,128)(2,1)S(1)}, u32[]{:S(2)}, u32[]{:S(2)}) collective-permute-start(bf16[576,256]{1,0:T(8,128)(2,1)S(1)} %far_ffn.1), channel_id=1, source_target_pairs={{0,3},{1,2},{2,1},{3,0},{4,7},{5,6},{6,5},{7,4},{8,11},{9,10},{10,... | collective-permute-start | bytes 884744 | tf_op jit(solution)/shard_map/ppermute | solution.py:213
  201.0 7.1 %collective-permute-start.28 = (bf16[416,384]{1,0:T(8,128)(2,1)S(1)}, bf16[416,384]{1,0:T(8,128)(2,1)S(1)}, u32[]{:S(2)}, u32[]{:S(2)}) collective-permute-start(bf16[416,384]{1,0:T(8,128)(2,1)S(1)} %get-tuple-element.172), channel_id=1, source_target_pairs={{0,1},{1,0},{2,3},{3,2},{4,5},{5,4},{6,7},{7,6},{8,9},{9,8},{10,11... | collective-permute-start | bytes 958472 | tf_op jit(solution)/shard_map/ppermute | solution.py:213
  202.7 7.2 %collective-permute-start.31 = (bf16[576,256]{1,0:T(8,128)(2,1)S(1)}, bf16[576,256]{1,0:T(8,128)(2,1)S(1)}, u32[]{:S(2)}, u32[]{:S(2)}) collective-permute-start(bf16[576,256]{1,0:T(8,128)(2,1)S(1)} %total_ffn.1.refs_0_), channel_id=1, source_target_pairs={{0,8},{1,9},{2,10},{3,11},{4,20},{5,21},{6,22},{7,23},{8,0},{9,1},... | collective-permute-start | bytes 884744 | tf_op jit(solution)/shard_map/ppermute | solution.py:213
  210.5 18.0 %copy-start.12 = (bf16[512,768]{1,0:T(8,128)(2,1)S(1)}, bf16[512,768]{1,0:T(8,128)(2,1)}, u32[]{:S(2)}) copy-start(bf16[512,768]{1,0:T(8,128)(2,1)} %copy-done.11) | copy-start | bytes 2359300
  210.5 18.0 %copy-start.32 = (bf16[256,768]{1,0:T(8,128)(2,1)S(1)}, bf16[256,768]{1,0:T(8,128)(2,1)}, u32[]{:S(2)}) copy-start(bf16[256,768]{1,0:T(8,128)(2,1)} %get-tuple-element.158.value_ref) | copy-start | bytes 1179652
  210.5 9.9 %collective-permute-start.32 = (bf16[2,576,256]{2,1,0:T(8,128)(2,1)S(1)}, bf16[2,576,256]{2,1,0:T(8,128)(2,1)S(1)}, u32[]{:S(2)}, u32[]{:S(2)}) collective-permute-start(bf16[2,576,256]{2,1,0:T(8,128)(2,1)S(1)} %pair_ffn.1.refs_0_), channel_id=1, source_target_pairs={{0,16},{1,17},{2,18},{3,19},{4,12},{5,13},{6,14},{7,15},{8,24},{9,... | collective-permute-start | bytes 1769480 | tf_op jit(solution)/shard_map/ppermute | solution.py:213
  212.1 7.4 %collective-permute-start.29 = (bf16[208,384]{1,0:T(8,128)(2,1)S(1)}, bf16[208,384]{1,0:T(8,128)(2,1)S(1)}, u32[]{:S(2)}, u32[]{:S(2)}) collective-permute-start(bf16[208,384]{1,0:T(8,128)(2,1)S(1)} %far_attn.1), channel_id=1, source_target_pairs={{0,3},{1,2},{2,1},{3,0},{4,7},{5,6},{6,5},{7,4},{8,11},{9,10},{10,... | collective-permute-start | bytes 479240 | tf_op jit(solution)/shard_map/ppermute | solution.py:213
  221.1 11.5 %collective-permute-start.34 = (bf16[4,576,256]{2,1,0:T(8,128)(2,1)S(1)}, bf16[4,576,256]{2,1,0:T(8,128)(2,1)}, u32[]{:S(2)}, u32[]{:S(2)}) collective-permute-start(bf16[4,576,256]{2,1,0:T(8,128)(2,1)S(1)} %stack_ffn.1.refs_3_), channel_id=1, source_target_pairs={{0,4},{4,0},{1,5},{5,1},{2,6},{6,2},{3,7},{7,3},{8,12},{12,8},{9,1... | collective-permute-start | bytes 3538952 | tf_op jit(solution)/shard_map/ppermute | solution.py:46
  221.8 22.0 %collective-permute-start.35 = (bf16[512,768]{1,0:T(8,128)(2,1)}, bf16[512,768]{1,0:T(8,128)(2,1)S(1)}, u32[]{:S(2)}, u32[]{:S(2)}) collective-permute-start(bf16[512,768]{1,0:T(8,128)(2,1)} %get-tuple-element.184), channel_id=1, source_target_pairs={{0,1},{1,0},{6,7},{7,6},{8,9},{9,8},{14,15},{15,14},{16,17},{17,16... | collective-permute-start | bytes 2359304 | tf_op jit(solution)/shard_map/ppermute | solution.py:213
  226.8 14.3 %collective-permute-start.37 = (bf16[192,384]{1,0:T(8,128)(2,1)S(1)}, bf16[192,384]{1,0:T(8,128)(2,1)S(1)}, u32[]{:S(2)}, u32[]{:S(2)}) collective-permute-start(bf16[192,384]{1,0:T(8,128)(2,1)S(1)} %get-tuple-element.189.refs_0_), channel_id=1, source_target_pairs={{0,8},{1,9},{2,10},{3,11},{4,20},{5,21},{6,22},{7,23},{8,0},{9,1},... | collective-permute-start | bytes 442376 | tf_op jit(solution)/shard_map/ppermute | solution.py:213
  229.8 14.0 %copy-start.33 = (bf16[256,768]{1,0:T(8,128)(2,1)S(1)}, bf16[256,768]{1,0:T(8,128)(2,1)}, u32[]{:S(2)}) copy-start(bf16[256,768]{1,0:T(8,128)(2,1)} %get-tuple-element.186.value_ref) | copy-start | bytes 1179652
  229.8 26.7 %collective-permute-start.33 = (bf16[256,768]{1,0:T(8,128)(2,1)}, bf16[256,768]{1,0:T(8,128)(2,1)}, u32[]{:S(2)}, u32[]{:S(2)}) collective-permute-start(bf16[256,768]{1,0:T(8,128)(2,1)} %add_rows.2), channel_id=1, source_target_pairs={{0,2},{1,3},{6,4},{7,5},{8,10},{9,11},{14,12},{15,13},{16,18},{17,... | collective-permute-start | bytes 1179656 | tf_op jit(solution)/shard_map/ppermute | solution.py:213
  241.7 10.7 %collective-permute-start.38 = (bf16[2,192,384]{2,1,0:T(8,128)(2,1)S(1)}, bf16[2,192,384]{2,1,0:T(8,128)(2,1)S(1)}, u32[]{:S(2)}, u32[]{:S(2)}) collective-permute-start(bf16[2,192,384]{2,1,0:T(8,128)(2,1)S(1)} %pair_attn.1.refs_0_), channel_id=1, source_target_pairs={{0,16},{1,17},{2,18},{3,19},{4,12},{5,13},{6,14},{7,15},{8,24},{9,... | collective-permute-start | bytes 884744 | tf_op jit(solution)/shard_map/ppermute | solution.py:213
  244.5 13.9 %collective-permute-start.36 = (bf16[256,768]{1,0:T(8,128)(2,1)S(1)}, bf16[256,768]{1,0:T(8,128)(2,1)S(1)}, u32[]{:S(2)}, u32[]{:S(2)}) collective-permute-start(bf16[256,768]{1,0:T(8,128)(2,1)S(1)} %add_rows.3), channel_id=1, source_target_pairs={{0,2},{1,3},{6,4},{7,5},{8,10},{9,11},{14,12},{15,13},{16,18},{17,... | collective-permute-start | bytes 1179656 | tf_op jit(solution)/shard_map/ppermute | solution.py:213
  253.1 6.1 %collective-permute-start.39 = (bf16[4,192,384]{2,1,0:T(8,128)(2,1)S(1)}, bf16[4,192,384]{2,1,0:T(8,128)(2,1)S(1)}, u32[]{:S(2)}, u32[]{:S(2)}) collective-permute-start(bf16[4,192,384]{2,1,0:T(8,128)(2,1)S(1)} %stack_attn.1.refs_3_), channel_id=1, source_target_pairs={{0,4},{4,0},{1,5},{5,1},{2,6},{6,2},{3,7},{7,3},{8,12},{12,8},{9,1... | collective-permute-start | bytes 1769480 | tf_op jit(solution)/shard_map/ppermute | solution.py:46
  253.2 2.0 collective-permute-start.40
  (44 other events, 316.6 us)
